TPU v7x, 128 devices: a whole 4x4x4 slice. The times are simulated.
128 devices in a mesh: slab: 32 (over y, z, core), col: 4 (over x).
Axes of the slice: x: 4, y: 4, z: 4, core: 2. Of those that a mesh axis runs over, the one named last changes fastest.
Arguments:
- input_map: float32 [64, 64, 192, 128], P('col', 'slab'), may hold values from -24 to 24
- output_map: float32 [64, 64, 192, 128], P('col', 'slab'), may hold values from -24 to 24
- region_ids: int32 [64, 192, 128], P('slab'), may hold values from 0 to 7
- region_cond: float32 [8], replicated, may hold values from 0.3 to 3
- shift_ids: int32 [2], replicated, may hold values from 0 to 7
Outputs:
- ctrl_factor: float32 [2, 64, 64, 192, 128], P(None, None, 'slab', 'col')
- obsv_factor: float32 [2, 64, 64, 192, 128], P(None, None, 'slab', 'col')
- cross_gram: float32 [128, 128], P('slab', 'col')
All inputs are finite; a program needn't handle non-finite values.
Results may differ from a plain program's by a relative error of at most 0.000098.
Values sent between devices are 32-bit elements; how exact they have to be, the bound alone decides.
A program may use at most 192 MiB of HBM per device.

v0:
```python
import math

import jax
import jax.numpy as jnp
from jax import lax
from jax.experimental import pallas as pl
from jax.experimental.pallas import tpu as pltpu
from jax.sharding import PartitionSpec as P

ADI = 2
STEPS = 3


def extended(block, sides, width):
    for axis, dim in sides:
        count = lax.axis_size(axis)
        forward = [(i, i + 1) for i in range(count - 1)]
        backward = [(target, source) for source, target in forward]
        low = lax.ppermute(
            lax.slice_in_dim(block, block.shape[dim] - width, None, axis=dim), axis, forward
        )
        high = lax.ppermute(lax.slice_in_dim(block, 0, width, axis=dim), axis, backward)
        block = jnp.concatenate([low, block, high], axis=dim)
    return block


def scatter_sum_kernel(tiles_ref, out_ref, recv, send_sem, recv_sem):
    count = tiles_ref.shape[0]
    me = lax.axis_index("slab")
    col = lax.axis_index("col")
    recv[pl.ds(me, 1)] = tiles_ref[pl.ds(me, 1)]
    barrier = pltpu.get_barrier_semaphore()

    def greet(k, carry):
        peer = lax.rem(me + k, count)
        pl.semaphore_signal(barrier, inc=1, device_id=(peer, col), device_id_type=pl.DeviceIdType.MESH)
        return carry

    lax.fori_loop(1, count, greet, 0)
    pl.semaphore_wait(barrier, count - 1)

    def copy_to(k):
        peer = lax.rem(me + k, count)
        return pltpu.make_async_remote_copy(
            src_ref=tiles_ref.at[pl.ds(peer, 1)],
            dst_ref=recv.at[pl.ds(me, 1)],
            send_sem=send_sem.at[peer],
            recv_sem=recv_sem.at[me],
            device_id=(peer, col),
            device_id_type=pl.DeviceIdType.MESH,
        )

    def send(k, carry):
        copy_to(k).start()
        return carry

    lax.fori_loop(1, count, send, 0)

    def finish(k, carry):
        peer = lax.rem(me + k, count)
        copy_to(k).wait_send()
        pltpu.make_async_remote_copy(
            src_ref=tiles_ref.at[pl.ds(me, 1)],
            dst_ref=recv.at[pl.ds(peer, 1)],
            send_sem=send_sem.at[me],
            recv_sem=recv_sem.at[peer],
            device_id=(peer, col),
            device_id_type=pl.DeviceIdType.MESH,
        ).wait_recv()
        return carry

    lax.fori_loop(1, count, finish, 0)
    out_ref[...] = jnp.sum(recv[...], axis=0, keepdims=True)


def scatter_sum(tiles):
    count, rows, lanes = tiles.shape
    return pl.pallas_call(
        scatter_sum_kernel,
        out_shape=jax.ShapeDtypeStruct((1, rows, lanes), jnp.float32),
        in_specs=[pl.BlockSpec(memory_space=pltpu.VMEM)],
        out_specs=pl.BlockSpec(memory_space=pltpu.VMEM),
        scratch_shapes=[
            pltpu.VMEM((count, rows, lanes), jnp.float32),
            pltpu.SemaphoreType.DMA((count,)),
            pltpu.SemaphoreType.DMA((count,)),
        ],
        compiler_params=pltpu.CompilerParams(collective_id=0, has_side_effects=True),
    )(tiles)


def lookup(region_ids, region_cond):
    summed = jnp.zeros(region_ids.shape, jnp.float32)
    for region in range(region_cond.shape[0]):
        summed = summed + jnp.where(region_ids == region, region_cond[region], jnp.float32(0.0))
    return summed


def halo_pair(block, axis, dim):
    count = lax.axis_size(axis)
    forward = [(i, i + 1) for i in range(count - 1)]
    backward = [(target, source) for source, target in forward]
    size = block.shape[dim]
    low = lax.ppermute(lax.slice_in_dim(block, size - 1, None, axis=dim), axis, forward)
    high = lax.ppermute(lax.slice_in_dim(block, 0, 1, axis=dim), axis, backward)
    return low, high


def shifted(block, low, high, dim):
    size = block.shape[dim]
    ahead = jnp.concatenate([lax.slice_in_dim(block, 1, None, axis=dim), high], axis=dim)
    behind = jnp.concatenate([low, lax.slice_in_dim(block, 0, size - 1, axis=dim)], axis=dim)
    return ahead, behind


def coefficients(cond_xy):
    cond_mid = cond_xy[1:-1, 1:-1]
    kxp = 0.5 * (cond_mid + cond_xy[2:, 1:-1])
    kxm = 0.5 * (cond_mid + cond_xy[:-2, 1:-1])
    kyp = 0.5 * (cond_mid + cond_xy[1:-1, 2:])
    kym = 0.5 * (cond_mid + cond_xy[1:-1, :-2])
    cond_z = jnp.pad(cond_mid, ((0, 0), (0, 0), (1, 1)))
    kzp = 0.5 * (cond_mid + cond_z[:, :, 2:])
    kzm = 0.5 * (cond_mid + cond_z[:, :, :-2])
    return (kxp, kxm, kyp, kym, kzp, kzm)


def windows(block, rows, count):
    parts = [lax.slice_in_dim(block, c * rows, (c + 1) * rows, axis=2) for c in range(count)]
    received = lax.all_to_all(jnp.stack(parts), "col", 0, 0, tiled=True)
    return received.reshape((-1,) + received.shape[2:])


def conduction(field, coeffs):
    kxp, kxm, kyp, kym, kzp, kzm = coeffs
    xlo, xhi = halo_pair(field, "slab", 1)
    ylo, yhi = halo_pair(field, "col", 2)
    nxp, nxm = shifted(field, xlo, xhi, 1)
    nyp, nym = shifted(field, ylo, yhi, 2)
    field_z = jnp.pad(field, ((0, 0), (0, 0), (0, 0), (1, 1)))
    summed = kxp * (field - nxp)
    summed = summed + kxm * (field - nxm)
    summed = summed + kyp * (field - nyp)
    summed = summed + kym * (field - nym)
    summed = summed + kzp * (field - field_z[..., 2:])
    summed = summed + kzm * (field - field_z[..., :-2])
    return summed


def bounds(shift_val, cond_max):
    high_eig = shift_val + 12.0 * cond_max
    mid_eig = 0.5 * (high_eig + shift_val)
    half_span = 0.5 * (high_eig - shift_val)
    return (mid_eig, half_span, mid_eig / half_span)


def solve_slabs(right_side, shift_val, cond_max, coeffs):
    mid_eig, half_span, ratio_eig = bounds(shift_val, cond_max)
    rho_now = 1.0 / ratio_eig
    solution = jnp.zeros_like(right_side)
    residual = right_side
    direction = right_side / mid_eig
    for sweep_idx in range(STEPS - 1):
        solution = solution + direction
        applied = conduction(direction, coeffs) + shift_val * direction
        residual = residual - applied
        rho_next = 1.0 / (2.0 * ratio_eig - rho_now)
        direction = rho_next * rho_now * direction + 2.0 * rho_next / half_span * residual
        rho_now = rho_next
    return solution + direction


def run_segments(stacked, shifts, solver):
    factors = []
    current = stacked
    for segment_idx in range(ADI):
        shift_val = shifts[segment_idx]
        if segment_idx == 0:
            current = solver(stacked, shift_val)
        else:
            current = current - (shifts[segment_idx - 1] + shift_val) * solver(current, shift_val)
        factors.append(jnp.sqrt(2.0 * shift_val) * current)
    return jnp.stack(factors)


def body(input_map, output_map, region_ids, region_cond, shift_ids):
    col_count = lax.axis_size("col")
    ctrl_in = windows(input_map, input_map.shape[2] // col_count, col_count)
    obsv_in = windows(output_map, output_map.shape[2] // col_count, col_count)
    col_local = ctrl_in.shape[0]
    rows = ctrl_in.shape[2]
    local_x = input_map.shape[1]
    cond_cells = lookup(region_ids, region_cond)
    cond_max = jnp.max(region_cond)
    shifts = 0.25 * jnp.exp2(shift_ids.astype(jnp.float32))
    total_x = local_x * lax.axis_size("slab")
    cond_ypad = jnp.pad(cond_cells, ((0, 0), (1, 1), (0, 0)))
    cond_y = lax.dynamic_slice_in_dim(cond_ypad, lax.axis_index("col") * rows, rows + 2, axis=1)
    cond_xy = extended(cond_y, (("slab", 0),), 1)
    coeffs = coefficients(cond_xy)
    solver = lambda rhs, shift_val: solve_slabs(rhs, shift_val, cond_max, coeffs)
    ctrl_cols = run_segments(ctrl_in, shifts, solver)
    obsv_cols = run_segments(obsv_in, shifts, solver)
    row_count = ctrl_cols.shape[0] * ctrl_cols.shape[1]
    ctrl_flat = ctrl_cols.reshape(row_count, -1)
    obsv_flat = obsv_cols.reshape(row_count, -1)
    partial_value = lax.dot_general(
        ctrl_flat,
        obsv_flat,
        (((1,), (1,)), ((), ())),
        precision=lax.Precision.HIGHEST,
        preferred_element_type=jnp.float32,
    )
    cells_total = total_x * region_ids.shape[1] * region_ids.shape[2]
    norm_scale = 1.0 / math.sqrt(cells_total)
    slab_count = lax.axis_size("slab")
    col_count = lax.axis_size("col")
    tile_rows = row_count // slab_count
    tile_cols = row_count // col_count
    col_parts = partial_value.reshape(row_count, col_count, tile_cols).transpose(1, 0, 2)
    col_sum = jnp.sum(lax.all_to_all(col_parts, "col", 0, 0, tiled=True), axis=0)
    row_parts = col_sum.reshape(slab_count, 1, tile_rows * tile_cols)
    own_tile = scatter_sum(row_parts).reshape(tile_rows, tile_cols)
    return (ctrl_cols, obsv_cols, own_tile * norm_scale)


def solution(mesh):
    placed = (
        P("col", "slab", None, None),
        P("col", "slab", None, None),
        P("slab", None, None),
        P(),
        P(),
    )
    return jax.shard_map(
        body,
        mesh=mesh,
        in_specs=placed,
        out_specs=(
            P(None, None, "slab", "col", None),
            P(None, None, "slab", "col", None),
            P("slab", "col"),
        ),
        check_vma=False,
    )
```

profile of v0, /device:TPU:1, one launch (start us, length us, event | category | flops | bytes accessed | tf_op | source)
XLA Modules:
  0.0 353.7 jit_solution(5779163176662310728)
XLA Ops:
  4.7 4.8 %all-to-all-start.1 = ((f32[4,16,2,48,128]{4,3,2,1,0:T(8,128)}), f32[4,16,2,48,128]{4,3,2,1,0:T(8,128)S(1)}, u32[]{:S(2)}, u32[]{:S(2)}) async-start(f32[4,16,2,48,128]{4,3,2,1,0:T(8,128)} %pad_maximum_fusion.3), calls=%async_computation.1 | async-start | bytes 6291456 | tf_op jit(solution)/shard_map/all_to_all | solution.py:130
  13.5 32.6 %all-to-all-done.1 = f32[4,16,2,48,128]{4,3,2,1,0:T(8,128)S(1)} async-done(((f32[4,16,2,48,128]{4,3,2,1,0:T(8,128)}), f32[4,16,2,48,128]{4,3,2,1,0:T(8,128)S(1)}, u32[]{:S(2)}, u32[]{:S(2)}) %all-to-all-start.1) | async-done | bytes 3145760 | tf_op jit(solution)/shard_map/all_to_all | solution.py:130
  46.2 4.7 %all-to-all-start = ((f32[4,16,2,48,128]{4,3,2,1,0:T(8,128)}), f32[4,16,2,48,128]{4,3,2,1,0:T(8,128)}, u32[]{:S(2)}, u32[]{:S(2)}) async-start(f32[4,16,2,48,128]{4,3,2,1,0:T(8,128)} %pad_maximum_fusion.2), calls=%async_computation | async-start | bytes 6291456 | tf_op jit(solution)/shard_map/all_to_all | solution.py:130
  51.5 5.2 %select_add_fusion = f32[2,192,128]{2,1,0:T(8,128)S(1)} fusion(s32[2,192,128]{2,1,0:T(8,128)S(1)} %copy-done.14, f32[]{:T(128)} %bitcast.13, f32[]{:T(128)} %bitcast.12, f32[]{:T(128)} %bitcast.11, f32[]{:T(128)} %bitcast.10, f32[]{:T(128)} %bitcast.9, f32[]{:T(128)} %bitcast.8, f32[]{:T(128)} %bitcast.7, f32[]{:T(128)} %bitcast.6), kind=kLoop, calls=%fused_computation.211 | loop fusion | flops 1130496 | bytes 393248 | tf_op jit(solution)/shard_map/add | solution.py:95
  74.7 11.9 %all-to-all-done = f32[4,16,2,48,128]{4,3,2,1,0:T(8,128)} async-done(((f32[4,16,2,48,128]{4,3,2,1,0:T(8,128)}), f32[4,16,2,48,128]{4,3,2,1,0:T(8,128)}, u32[]{:S(2)}, u32[]{:S(2)}) %all-to-all-start) | async-done | bytes 3145760 | tf_op jit(solution)/shard_map/all_to_all | solution.py:130
  89.8 6.2 %collective-permute-start.3 = (f32[64,1,48,128]{3,2,1,0:T(8,128)S(1)}, f32[64,1,48,128]{3,2,1,0:T(8,128)S(1)}, u32[]{:S(2)}, u32[]{:S(2)}) collective-permute-start(f32[64,1,48,128]{3,2,1,0:T(8,128)S(1)} %get-tuple-element.63), channel_id=1, source_target_pairs={{0,4},{4,8},{8,12},{12,16},{16,20},{20,24},{24,28},{28,32},{32,36}... | collective-permute-start | bytes 4718600 | tf_op jit(solution)/shard_map/ppermute | solution.py:104
  106.7 4.0 %collective-permute-start.21 = (f32[64,2,1,128]{3,2,1,0:T(1,128)}, f32[64,2,1,128]{3,2,1,0:T(1,128)S(1)}, u32[]{:S(2)}, u32[]{:S(2)}) collective-permute-start(f32[64,2,1,128]{3,2,1,0:T(1,128)} %get-tuple-element.40), channel_id=1, source_target_pairs={{0,1},{1,2},{2,3},{4,5},{5,6},{6,7},{8,9},{9,10},{10,11},{12,13},{... | collective-permute-start | bytes 196616 | tf_op jit(solution)/shard_map/ppermute | solution.py:104
  112.0 4.5 %collective-permute-start.19 = (f32[64,1,48,128]{3,2,1,0:T(8,128)S(1)}, f32[64,1,48,128]{3,2,1,0:T(8,128)}, u32[]{:S(2)}, u32[]{:S(2)}) collective-permute-start(f32[64,1,48,128]{3,2,1,0:T(8,128)S(1)} %get-tuple-element.35), channel_id=1, source_target_pairs={{0,4},{4,8},{8,12},{12,16},{16,20},{20,24},{24,28},{28,32},{32,36}... | collective-permute-start | bytes 4718600 | tf_op jit(solution)/shard_map/ppermute | solution.py:104
  119.7 8.0 %multiply_add_fusion.3 = (f32[64,2,48,128]{3,2,1,0:T(8,128)S(1)}, f32[64,2,48,128]{3,2,1,0:T(8,128)}) fusion(f32[64,2,48,128]{3,2,1,0:T(8,128)S(1)} %get-tuple-element.93, f32[]{:T(128)S(6)} %div.73, f32[]{:T(128)S(6)} %mul.258, f32[]{:T(128)} %bitcast, f32[2,48,128]{2,1,0:T(8,128)S(1)} %get-tuple-element.78, f32[2,48,128]{2,1,0:T(8,128)S(1)} %copy-done.10, ...), kind=kLoop, calls=%fused_computation.199 | loop fusion | flops 21233664 | bytes 25460748 | tf_op jit(solution)/shard_map/add | solution.py:168
  130.3 4.3 %collective-permute-start.9 = (f32[64,2,1,128]{3,2,1,0:T(1,128)}, f32[64,2,1,128]{3,2,1,0:T(1,128)S(1)}, u32[]{:S(2)}, u32[]{:S(2)}) collective-permute-start(f32[64,2,1,128]{3,2,1,0:T(1,128)} %get-tuple-element.62), channel_id=1, source_target_pairs={{0,1},{1,2},{2,3},{4,5},{5,6},{6,7},{8,9},{9,10},{10,11},{12,13},{... | collective-permute-start | bytes 196616 | tf_op jit(solution)/shard_map/ppermute | solution.py:104
  135.9 3.9 %collective-permute-start.7 = (f32[64,1,48,128]{3,2,1,0:T(8,128)}, f32[64,1,48,128]{3,2,1,0:T(8,128)}, u32[]{:S(2)}, u32[]{:S(2)}) collective-permute-start(f32[64,1,48,128]{3,2,1,0:T(8,128)} %get-tuple-element.57), channel_id=1, source_target_pairs={{0,4},{4,8},{8,12},{12,16},{16,20},{20,24},{24,28},{28,32},{32,36}... | collective-permute-start | bytes 4718600 | tf_op jit(solution)/shard_map/ppermute | solution.py:104
  141.7 7.6 %multiply_add_fusion.1 = (f32[64,2,48,128]{3,2,1,0:T(8,128)S(1)}, f32[64,2,48,128]{3,2,1,0:T(8,128)}) fusion(f32[64,2,48,128]{3,2,1,0:T(8,128)S(1)} %get-tuple-element.92, f32[]{:T(128)S(6)} %div.73, f32[]{:T(128)S(6)} %mul.258, f32[]{:T(128)} %bitcast, f32[2,48,128]{2,1,0:T(8,128)S(1)} %get-tuple-element.78, f32[2,48,128]{2,1,0:T(8,128)S(1)} %copy-done.10, ...), kind=kLoop, calls=%fused_computation.196 | loop fusion | flops 21233664 | bytes 25460748 | tf_op jit(solution)/shard_map/add | solution.py:168
  157.2 4.3 %collective-permute-start.25 = (f32[64,2,1,128]{3,2,1,0:T(1,128)S(1)}, f32[64,2,1,128]{3,2,1,0:T(1,128)S(1)}, u32[]{:S(2)}, u32[]{:S(2)}) collective-permute-start(f32[64,2,1,128]{3,2,1,0:T(1,128)S(1)} %get-tuple-element.34), channel_id=1, source_target_pairs={{0,1},{1,2},{2,3},{4,5},{5,6},{6,7},{8,9},{9,10},{10,11},{12,13},{... | collective-permute-start | bytes 196616 | tf_op jit(solution)/shard_map/ppermute | solution.py:104
  162.8 3.9 %collective-permute-start.23 = (f32[64,1,48,128]{3,2,1,0:T(8,128)S(1)}, f32[64,1,48,128]{3,2,1,0:T(8,128)}, u32[]{:S(2)}, u32[]{:S(2)}) collective-permute-start(f32[64,1,48,128]{3,2,1,0:T(8,128)S(1)} %get-tuple-element.29), channel_id=1, source_target_pairs={{0,4},{4,8},{8,12},{12,16},{16,20},{20,24},{24,28},{28,32},{32,36}... | collective-permute-start | bytes 4718600 | tf_op jit(solution)/shard_map/ppermute | solution.py:104
  168.9 9.1 %multiply_bitcast_fusion.1 = (f32[1,64,2,48,128]{4,3,2,1,0:T(8,128)}, f32[64,2,48,128]{3,2,1,0:T(8,128)S(1)}) fusion(f32[]{:T(128)S(6)} %sqrt.8, f32[64,2,48,128]{3,2,1,0:T(8,128)} %get-tuple-element.14, f32[64,2,48,128]{3,2,1,0:T(8,128)S(1)} %get-tuple-element.13, f32[]{:T(128)} %bitcast, f32[2,48,128]{2,1,0:T(8,128)S(1)} %get-tuple-element.78, ...), kind=kLoop, calls=%fused_computation.198 | loop fusion | flops 23592960 | bytes 28606480 | tf_op jit(solution)/shard_map/stack | solution.py:183
  181.0 4.3 %collective-permute-start.13 = (f32[64,2,1,128]{3,2,1,0:T(1,128)}, f32[64,2,1,128]{3,2,1,0:T(1,128)S(1)}, u32[]{:S(2)}, u32[]{:S(2)}) collective-permute-start(f32[64,2,1,128]{3,2,1,0:T(1,128)} %get-tuple-element.56), channel_id=1, source_target_pairs={{0,1},{1,2},{2,3},{4,5},{5,6},{6,7},{8,9},{9,10},{10,11},{12,13},{... | collective-permute-start | bytes 196616 | tf_op jit(solution)/shard_map/ppermute | solution.py:104
  186.6 3.9 %collective-permute-start.11 = (f32[64,1,48,128]{3,2,1,0:T(8,128)}, f32[64,1,48,128]{3,2,1,0:T(8,128)}, u32[]{:S(2)}, u32[]{:S(2)}) collective-permute-start(f32[64,1,48,128]{3,2,1,0:T(8,128)} %get-tuple-element.51), channel_id=1, source_target_pairs={{0,4},{4,8},{8,12},{12,16},{16,20},{20,24},{24,28},{28,32},{32,36}... | collective-permute-start | bytes 4718600 | tf_op jit(solution)/shard_map/ppermute | solution.py:104
  192.5 8.2 %multiply_bitcast_fusion = (f32[1,64,2,48,128]{4,3,2,1,0:T(8,128)}, f32[64,2,48,128]{3,2,1,0:T(8,128)S(1)}) fusion(f32[]{:T(128)S(6)} %sqrt.8, f32[64,2,48,128]{3,2,1,0:T(8,128)} %get-tuple-element.8, f32[64,2,48,128]{3,2,1,0:T(8,128)S(1)} %get-tuple-element.7, f32[]{:T(128)} %bitcast, f32[2,48,128]{2,1,0:T(8,128)S(1)} %get-tuple-element.78, ...), kind=kLoop, calls=%fused_computation.195 | loop fusion | flops 23592960 | bytes 28606480 | tf_op jit(solution)/shard_map/stack | solution.py:183
  207.9 4.3 %collective-permute-start.29 = (f32[64,2,1,128]{3,2,1,0:T(1,128)}, f32[64,2,1,128]{3,2,1,0:T(1,128)S(1)}, u32[]{:S(2)}, u32[]{:S(2)}) collective-permute-start(f32[64,2,1,128]{3,2,1,0:T(1,128)} %get-tuple-element.28), channel_id=1, source_target_pairs={{0,1},{1,2},{2,3},{4,5},{5,6},{6,7},{8,9},{9,10},{10,11},{12,13},{... | collective-permute-start | bytes 196616 | tf_op jit(solution)/shard_map/ppermute | solution.py:104
  213.5 3.9 %collective-permute-start.27 = (f32[64,1,48,128]{3,2,1,0:T(8,128)S(1)}, f32[64,1,48,128]{3,2,1,0:T(8,128)}, u32[]{:S(2)}, u32[]{:S(2)}) collective-permute-start(f32[64,1,48,128]{3,2,1,0:T(8,128)S(1)} %get-tuple-element.23), channel_id=1, source_target_pairs={{0,4},{4,8},{8,12},{12,16},{16,20},{20,24},{24,28},{28,32},{32,36}... | collective-permute-start | bytes 4718600 | tf_op jit(solution)/shard_map/ppermute | solution.py:104
  219.4 7.7 %multiply_add_fusion.2 = (f32[64,2,48,128]{3,2,1,0:T(8,128)S(1)}, f32[64,2,48,128]{3,2,1,0:T(8,128)}) fusion(f32[]{:T(128)S(6)} %div.81, f32[]{:T(128)S(6)} %mul.607, f32[64,2,48,128]{3,2,1,0:T(8,128)S(1)} %get-tuple-element.10, f32[]{:T(128)S(6)} %mul.604, f32[64,2,48,128]{3,2,1,0:T(8,128)S(1)} %broadcast_divide_fusion.1, f32[]{:T(128)} %bitcast.15, ...), kind=kLoop, calls=%fused_computation.197 | loop fusion | flops 22020096 | bytes 25460752 | tf_op jit(solution)/shard_map/add | solution.py:168
  236.8 5.1 %collective-permute-start.17 = (f32[64,2,1,128]{3,2,1,0:T(1,128)S(1)}, f32[64,2,1,128]{3,2,1,0:T(1,128)S(1)}, u32[]{:S(2)}, u32[]{:S(2)}) collective-permute-start(f32[64,2,1,128]{3,2,1,0:T(1,128)S(1)} %get-tuple-element.45), channel_id=1, source_target_pairs={{0,1},{1,2},{2,3},{4,5},{5,6},{6,7},{8,9},{9,10},{10,11},{12,13},{... | collective-permute-start | bytes 196616 | tf_op jit(solution)/shard_map/ppermute | solution.py:104
  242.0 7.9 %multiply_add_fusion = (f32[64,2,48,128]{3,2,1,0:T(8,128)S(1)}, f32[64,2,48,128]{3,2,1,0:T(8,128)}) fusion(f32[]{:T(128)S(6)} %div.81, f32[]{:T(128)S(6)} %mul.607, f32[64,2,48,128]{3,2,1,0:T(8,128)S(1)} %get-tuple-element.4, f32[]{:T(128)S(6)} %mul.604, f32[64,2,48,128]{3,2,1,0:T(8,128)S(1)} %broadcast_divide_fusion, f32[]{:T(128)} %bitcast.15, ...), kind=kLoop, calls=%fused_computation.194 | loop fusion | flops 22020096 | bytes 25460752 | tf_op jit(solution)/shard_map/add | solution.py:168
  263.8 4.6 %collective-permute-start.33 = (f32[64,2,1,128]{3,2,1,0:T(1,128)}, f32[64,2,1,128]{3,2,1,0:T(1,128)}, u32[]{:S(2)}, u32[]{:S(2)}) collective-permute-start(f32[64,2,1,128]{3,2,1,0:T(1,128)} %get-tuple-element.17), channel_id=1, source_target_pairs={{0,1},{1,2},{2,3},{4,5},{5,6},{6,7},{8,9},{9,10},{10,11},{12,13},{... | collective-permute-start | bytes 196616 | tf_op jit(solution)/shard_map/ppermute | solution.py:104
  268.4 8.7 %fusion.39 = f32[1,64,2,48,128]{4,3,2,1,0:T(8,128)} fusion(f32[64,2,48,128]{3,2,1,0:T(8,128)S(1)} %get-tuple-element.10, f32[64,2,48,128]{3,2,1,0:T(8,128)S(1)} %copy-done.2, f32[64,2,48,128]{3,2,1,0:T(8,128)S(1)} %get-tuple-element.11, f32[64,1,48,128]{3,2,1,0:T(8,128)} %collective-permute-done.14, f32[64,1,48,128]{3,2,1,0:T(8,128)} %get-tuple-element.49, ...), kind=kLoop, calls=%fused_computation.57 | loop fusion | flops 25952256 | bytes 25460760 | tf_op jit(solution)/shard_map/stack | solution.py:183
  277.1 5.2 %pad_maximum_fusion = f32[2,64,2,48,128]{4,3,2,1,0:T(8,128)} fusion(f32[1,64,2,48,128]{4,3,2,1,0:T(8,128)} %fusion.39, f32[1,64,2,48,128]{4,3,2,1,0:T(8,128)S(1)} %copy-done.3), kind=kLoop, calls=%fused_computation.16 | loop fusion | flops 1572864 | bytes 12582912 | tf_op jit(solution)/shard_map/stack | solution.py:183
  282.3 7.5 %reshape.35 = f32[128,12288,1]{1,0,2:T(8,128)} reshape(f32[2,64,2,48,128]{4,3,2,1,0:T(8,128)} %pad_maximum_fusion) | data formatting | bytes 12582912 | tf_op jit(solution)/shard_map/reshape | solution.py:205
  289.8 9.2 %fusion.81 = f32[1,64,2,48,128]{4,3,2,1,0:T(8,128)S(1)} fusion(f32[64,2,48,128]{3,2,1,0:T(8,128)} %copy-done, f32[64,2,48,128]{3,2,1,0:T(8,128)} %get-tuple-element.6, f32[64,2,48,128]{3,2,1,0:T(8,128)S(1)} %get-tuple-element.5, f32[64,1,48,128]{3,2,1,0:T(8,128)} %collective-permute-done.30, f32[64,1,48,128]{3,2,1,0:T(8,128)} %get-tuple-element.21, ...), kind=kLoop, calls=%fused_computation.99 | loop fusion | flops 25952256 | bytes 25460760 | tf_op jit(solution)/shard_map/stack | solution.py:183
  302.3 7.4 %dot_general.5 = f32[4,32,12288]{2,1,0:T(8,128)} reshape(f32[2,64,2,48,128]{4,3,2,1,0:T(8,128)} %pad_maximum_fusion.1) | data formatting | bytes 12582912 | tf_op jit(solution)/shard_map/dot_general | solution.py:207
  309.7 8.2 %convolution_bitcast_fusion = f32[4,128,32]{1,2,0:T(8,128)S(1)} fusion(f32[128,12288,1]{1,0,2:T(8,128)} %reshape.35, f32[4,32,12288]{2,1,0:T(8,128)} %dot_general.5), kind=kOutput, calls=%fused_computation.202 | convolution fusion | flops 2415919104 | bytes 12648448 | tf_op jit(solution)/shard_map/dot_general | solution.py:207
  317.9 8.5 %all_to_all.15 = f32[4,128,32]{1,2,0:T(8,128)S(1)} all-to-all(f32[4,128,32]{1,2,0:T(8,128)S(1)} %convolution_bitcast_fusion), channel_id=1, replica_groups=mesh['slab'=32,'col'=4] {'col'}, dimensions={0} | all-to-all | bytes 131072 | tf_op jit(solution)/shard_map/all_to_all | solution.py:221
  327.2 25.2 %shard_map.76 = f32[1,1,128]{2,1,0:T(1,128)} custom-call(f32[32,1,128]{2,1,0:T(1,128)} %bitcast.51), custom_call_target="tpu_custom_call" | custom-call | tf_op jit(solution)/shard_map/pallas_call | solution.py:78
  (140 shorter events, 100.1 us)
Async XLA Ops:
  4.7 41.5 %all-to-all-start.1 = ((f32[4,16,2,48,128]{4,3,2,1,0:T(8,128)}), f32[4,16,2,48,128]{4,3,2,1,0:T(8,128)S(1)}, u32[]{:S(2)}, u32[]{:S(2)}) async-start(f32[4,16,2,48,128]{4,3,2,1,0:T(8,128)} %pad_maximum_fusion.3), calls=%async_computation.1 | async-start | bytes 6291456 | tf_op jit(solution)/shard_map/all_to_all | solution.py:130
  46.2 40.5 %all-to-all-start = ((f32[4,16,2,48,128]{4,3,2,1,0:T(8,128)}), f32[4,16,2,48,128]{4,3,2,1,0:T(8,128)}, u32[]{:S(2)}, u32[]{:S(2)}) async-start(f32[4,16,2,48,128]{4,3,2,1,0:T(8,128)} %pad_maximum_fusion.2), calls=%async_computation | async-start | bytes 6291456 | tf_op jit(solution)/shard_map/all_to_all | solution.py:130
  89.8 26.7 %collective-permute-start.3 = (f32[64,1,48,128]{3,2,1,0:T(8,128)S(1)}, f32[64,1,48,128]{3,2,1,0:T(8,128)S(1)}, u32[]{:S(2)}, u32[]{:S(2)}) collective-permute-start(f32[64,1,48,128]{3,2,1,0:T(8,128)S(1)} %get-tuple-element.63), channel_id=1, source_target_pairs={{0,4},{4,8},{8,12},{12,16},{16,20},{20,24},{24,28},{28,32},{32,36}... | collective-permute-start | bytes 4718600 | tf_op jit(solution)/shard_map/ppermute | solution.py:104
  96.0 22.5 %collective-permute-start.1 = (f32[64,1,48,128]{3,2,1,0:T(8,128)S(1)}, f32[64,1,48,128]{3,2,1,0:T(8,128)S(1)}, u32[]{:S(2)}, u32[]{:S(2)}) collective-permute-start(f32[64,1,48,128]{3,2,1,0:T(8,128)S(1)} %get-tuple-element.64), channel_id=1, source_target_pairs={{4,0},{8,4},{12,8},{16,12},{20,16},{24,20},{28,24},{32,28},{36,32}... | collective-permute-start | bytes 4718600 | tf_op jit(solution)/shard_map/ppermute | solution.py:105
  106.7 27.8 %collective-permute-start.21 = (f32[64,2,1,128]{3,2,1,0:T(1,128)}, f32[64,2,1,128]{3,2,1,0:T(1,128)S(1)}, u32[]{:S(2)}, u32[]{:S(2)}) collective-permute-start(f32[64,2,1,128]{3,2,1,0:T(1,128)} %get-tuple-element.40), channel_id=1, source_target_pairs={{0,1},{1,2},{2,3},{4,5},{5,6},{6,7},{8,9},{9,10},{10,11},{12,13},{... | collective-permute-start | bytes 196616 | tf_op jit(solution)/shard_map/ppermute | solution.py:104
  110.7 25.1 %collective-permute-start.20 = (f32[64,2,1,128]{3,2,1,0:T(1,128)}, f32[64,2,1,128]{3,2,1,0:T(1,128)S(1)}, u32[]{:S(2)}, u32[]{:S(2)}) collective-permute-start(f32[64,2,1,128]{3,2,1,0:T(1,128)} %get-tuple-element.39), channel_id=1, source_target_pairs={{1,0},{2,1},{3,2},{5,4},{6,5},{7,6},{9,8},{10,9},{11,10},{13,12},{... | collective-permute-start | bytes 196616 | tf_op jit(solution)/shard_map/ppermute | solution.py:105
  112.0 27.7 %collective-permute-start.19 = (f32[64,1,48,128]{3,2,1,0:T(8,128)S(1)}, f32[64,1,48,128]{3,2,1,0:T(8,128)}, u32[]{:S(2)}, u32[]{:S(2)}) collective-permute-start(f32[64,1,48,128]{3,2,1,0:T(8,128)S(1)} %get-tuple-element.35), channel_id=1, source_target_pairs={{0,4},{4,8},{8,12},{12,16},{16,20},{20,24},{24,28},{28,32},{32,36}... | collective-permute-start | bytes 4718600 | tf_op jit(solution)/shard_map/ppermute | solution.py:104
  116.6 25.2 %collective-permute-start.18 = (f32[64,1,48,128]{3,2,1,0:T(8,128)}, f32[64,1,48,128]{3,2,1,0:T(8,128)}, u32[]{:S(2)}, u32[]{:S(2)}) collective-permute-start(f32[64,1,48,128]{3,2,1,0:T(8,128)} %get-tuple-element.36), channel_id=1, source_target_pairs={{4,0},{8,4},{12,8},{16,12},{20,16},{24,20},{28,24},{32,28},{36,32}... | collective-permute-start | bytes 4718600 | tf_op jit(solution)/shard_map/ppermute | solution.py:105
  130.3 31.2 %collective-permute-start.9 = (f32[64,2,1,128]{3,2,1,0:T(1,128)}, f32[64,2,1,128]{3,2,1,0:T(1,128)S(1)}, u32[]{:S(2)}, u32[]{:S(2)}) collective-permute-start(f32[64,2,1,128]{3,2,1,0:T(1,128)} %get-tuple-element.62), channel_id=1, source_target_pairs={{0,1},{1,2},{2,3},{4,5},{5,6},{6,7},{8,9},{9,10},{10,11},{12,13},{... | collective-permute-start | bytes 196616 | tf_op jit(solution)/shard_map/ppermute | solution.py:104
  134.5 28.3 %collective-permute-start.8 = (f32[64,2,1,128]{3,2,1,0:T(1,128)}, f32[64,2,1,128]{3,2,1,0:T(1,128)}, u32[]{:S(2)}, u32[]{:S(2)}) collective-permute-start(f32[64,2,1,128]{3,2,1,0:T(1,128)} %get-tuple-element.61), channel_id=1, source_target_pairs={{1,0},{2,1},{3,2},{5,4},{6,5},{7,6},{9,8},{10,9},{11,10},{13,12},{... | collective-permute-start | bytes 196616 | tf_op jit(solution)/shard_map/ppermute | solution.py:105
  135.9 30.9 %collective-permute-start.7 = (f32[64,1,48,128]{3,2,1,0:T(8,128)}, f32[64,1,48,128]{3,2,1,0:T(8,128)}, u32[]{:S(2)}, u32[]{:S(2)}) collective-permute-start(f32[64,1,48,128]{3,2,1,0:T(8,128)} %get-tuple-element.57), channel_id=1, source_target_pairs={{0,4},{4,8},{8,12},{12,16},{16,20},{20,24},{24,28},{28,32},{32,36}... | collective-permute-start | bytes 4718600 | tf_op jit(solution)/shard_map/ppermute | solution.py:104
  139.8 29.1 %collective-permute-start.6 = (f32[64,1,48,128]{3,2,1,0:T(8,128)}, f32[64,1,48,128]{3,2,1,0:T(8,128)}, u32[]{:S(2)}, u32[]{:S(2)}) collective-permute-start(f32[64,1,48,128]{3,2,1,0:T(8,128)} %get-tuple-element.58), channel_id=1, source_target_pairs={{4,0},{8,4},{12,8},{16,12},{20,16},{24,20},{28,24},{32,28},{36,32}... | collective-permute-start | bytes 4718600 | tf_op jit(solution)/shard_map/ppermute | solution.py:105
  157.2 28.0 %collective-permute-start.25 = (f32[64,2,1,128]{3,2,1,0:T(1,128)S(1)}, f32[64,2,1,128]{3,2,1,0:T(1,128)S(1)}, u32[]{:S(2)}, u32[]{:S(2)}) collective-permute-start(f32[64,2,1,128]{3,2,1,0:T(1,128)S(1)} %get-tuple-element.34), channel_id=1, source_target_pairs={{0,1},{1,2},{2,3},{4,5},{5,6},{6,7},{8,9},{9,10},{10,11},{12,13},{... | collective-permute-start | bytes 196616 | tf_op jit(solution)/shard_map/ppermute | solution.py:104
  161.5 25.1 %collective-permute-start.24 = (f32[64,2,1,128]{3,2,1,0:T(1,128)}, f32[64,2,1,128]{3,2,1,0:T(1,128)}, u32[]{:S(2)}, u32[]{:S(2)}) collective-permute-start(f32[64,2,1,128]{3,2,1,0:T(1,128)} %get-tuple-element.33), channel_id=1, source_target_pairs={{1,0},{2,1},{3,2},{5,4},{6,5},{7,6},{9,8},{10,9},{11,10},{13,12},{... | collective-permute-start | bytes 196616 | tf_op jit(solution)/shard_map/ppermute | solution.py:105
  162.8 27.7 %collective-permute-start.23 = (f32[64,1,48,128]{3,2,1,0:T(8,128)S(1)}, f32[64,1,48,128]{3,2,1,0:T(8,128)}, u32[]{:S(2)}, u32[]{:S(2)}) collective-permute-start(f32[64,1,48,128]{3,2,1,0:T(8,128)S(1)} %get-tuple-element.29), channel_id=1, source_target_pairs={{0,4},{4,8},{8,12},{12,16},{16,20},{20,24},{24,28},{28,32},{32,36}... | collective-permute-start | bytes 4718600 | tf_op jit(solution)/shard_map/ppermute | solution.py:104
  166.8 25.7 %collective-permute-start.22 = (f32[64,1,48,128]{3,2,1,0:T(8,128)}, f32[64,1,48,128]{3,2,1,0:T(8,128)}, u32[]{:S(2)}, u32[]{:S(2)}) collective-permute-start(f32[64,1,48,128]{3,2,1,0:T(8,128)} %get-tuple-element.30), channel_id=1, source_target_pairs={{4,0},{8,4},{12,8},{16,12},{20,16},{24,20},{28,24},{32,28},{36,32}... | collective-permute-start | bytes 4718600 | tf_op jit(solution)/shard_map/ppermute | solution.py:105
  181.0 31.2 %collective-permute-start.13 = (f32[64,2,1,128]{3,2,1,0:T(1,128)}, f32[64,2,1,128]{3,2,1,0:T(1,128)S(1)}, u32[]{:S(2)}, u32[]{:S(2)}) collective-permute-start(f32[64,2,1,128]{3,2,1,0:T(1,128)} %get-tuple-element.56), channel_id=1, source_target_pairs={{0,1},{1,2},{2,3},{4,5},{5,6},{6,7},{8,9},{9,10},{10,11},{12,13},{... | collective-permute-start | bytes 196616 | tf_op jit(solution)/shard_map/ppermute | solution.py:104
  185.3 28.2 %collective-permute-start.12 = (f32[64,2,1,128]{3,2,1,0:T(1,128)}, f32[64,2,1,128]{3,2,1,0:T(1,128)S(1)}, u32[]{:S(2)}, u32[]{:S(2)}) collective-permute-start(f32[64,2,1,128]{3,2,1,0:T(1,128)} %get-tuple-element.55), channel_id=1, source_target_pairs={{1,0},{2,1},{3,2},{5,4},{6,5},{7,6},{9,8},{10,9},{11,10},{13,12},{... | collective-permute-start | bytes 196616 | tf_op jit(solution)/shard_map/ppermute | solution.py:105
  186.6 30.9 %collective-permute-start.11 = (f32[64,1,48,128]{3,2,1,0:T(8,128)}, f32[64,1,48,128]{3,2,1,0:T(8,128)}, u32[]{:S(2)}, u32[]{:S(2)}) collective-permute-start(f32[64,1,48,128]{3,2,1,0:T(8,128)} %get-tuple-element.51), channel_id=1, source_target_pairs={{0,4},{4,8},{8,12},{12,16},{16,20},{20,24},{24,28},{28,32},{32,36}... | collective-permute-start | bytes 4718600 | tf_op jit(solution)/shard_map/ppermute | solution.py:104
  190.5 28.9 %collective-permute-start.10 = (f32[64,1,48,128]{3,2,1,0:T(8,128)}, f32[64,1,48,128]{3,2,1,0:T(8,128)}, u32[]{:S(2)}, u32[]{:S(2)}) collective-permute-start(f32[64,1,48,128]{3,2,1,0:T(8,128)} %get-tuple-element.52), channel_id=1, source_target_pairs={{4,0},{8,4},{12,8},{16,12},{20,16},{24,20},{28,24},{32,28},{36,32}... | collective-permute-start | bytes 4718600 | tf_op jit(solution)/shard_map/ppermute | solution.py:105
  207.9 23.8 %collective-permute-start.29 = (f32[64,2,1,128]{3,2,1,0:T(1,128)}, f32[64,2,1,128]{3,2,1,0:T(1,128)S(1)}, u32[]{:S(2)}, u32[]{:S(2)}) collective-permute-start(f32[64,2,1,128]{3,2,1,0:T(1,128)} %get-tuple-element.28), channel_id=1, source_target_pairs={{0,1},{1,2},{2,3},{4,5},{5,6},{6,7},{8,9},{9,10},{10,11},{12,13},{... | collective-permute-start | bytes 196616 | tf_op jit(solution)/shard_map/ppermute | solution.py:104
  212.2 23.2 %collective-permute-start.28 = (f32[64,2,1,128]{3,2,1,0:T(1,128)}, f32[64,2,1,128]{3,2,1,0:T(1,128)}, u32[]{:S(2)}, u32[]{:S(2)}) collective-permute-start(f32[64,2,1,128]{3,2,1,0:T(1,128)} %get-tuple-element.27), channel_id=1, source_target_pairs={{1,0},{2,1},{3,2},{5,4},{6,5},{7,6},{9,8},{10,9},{11,10},{13,12},{... | collective-permute-start | bytes 196616 | tf_op jit(solution)/shard_map/ppermute | solution.py:105
  213.5 23.2 %collective-permute-start.27 = (f32[64,1,48,128]{3,2,1,0:T(8,128)S(1)}, f32[64,1,48,128]{3,2,1,0:T(8,128)}, u32[]{:S(2)}, u32[]{:S(2)}) collective-permute-start(f32[64,1,48,128]{3,2,1,0:T(8,128)S(1)} %get-tuple-element.23), channel_id=1, source_target_pairs={{0,4},{4,8},{8,12},{12,16},{16,20},{20,24},{24,28},{28,32},{32,36}... | collective-permute-start | bytes 4718600 | tf_op jit(solution)/shard_map/ppermute | solution.py:104
  217.5 24.4 %collective-permute-start.26 = (f32[64,1,48,128]{3,2,1,0:T(8,128)}, f32[64,1,48,128]{3,2,1,0:T(8,128)}, u32[]{:S(2)}, u32[]{:S(2)}) collective-permute-start(f32[64,1,48,128]{3,2,1,0:T(8,128)} %get-tuple-element.24), channel_id=1, source_target_pairs={{4,0},{8,4},{12,8},{16,12},{20,16},{24,20},{28,24},{32,28},{36,32}... | collective-permute-start | bytes 4718600 | tf_op jit(solution)/shard_map/ppermute | solution.py:105
  229.9 33.9 %collective-permute-start.14 = (f32[64,1,48,128]{3,2,1,0:T(8,128)}, f32[64,1,48,128]{3,2,1,0:T(8,128)}, u32[]{:S(2)}, u32[]{:S(2)}) collective-permute-start(f32[64,1,48,128]{3,2,1,0:T(8,128)} %get-tuple-element.50), channel_id=1, source_target_pairs={{4,0},{8,4},{12,8},{16,12},{20,16},{24,20},{28,24},{32,28},{36,32}... | collective-permute-start | bytes 4718600 | tf_op jit(solution)/shard_map/ppermute | solution.py:105
  231.8 36.6 %collective-permute-start.15 = (f32[64,1,48,128]{3,2,1,0:T(8,128)}, f32[64,1,48,128]{3,2,1,0:T(8,128)}, u32[]{:S(2)}, u32[]{:S(2)}) collective-permute-start(f32[64,1,48,128]{3,2,1,0:T(8,128)} %get-tuple-element.49), channel_id=1, source_target_pairs={{0,4},{4,8},{8,12},{12,16},{16,20},{20,24},{24,28},{28,32},{32,36}... | collective-permute-start | bytes 4718600 | tf_op jit(solution)/shard_map/ppermute | solution.py:104
  235.5 23.5 %collective-permute-start.16 = (f32[64,2,1,128]{3,2,1,0:T(1,128)}, f32[64,2,1,128]{3,2,1,0:T(1,128)S(1)}, u32[]{:S(2)}, u32[]{:S(2)}) collective-permute-start(f32[64,2,1,128]{3,2,1,0:T(1,128)} %get-tuple-element.46), channel_id=1, source_target_pairs={{1,0},{2,1},{3,2},{5,4},{6,5},{7,6},{9,8},{10,9},{11,10},{13,12},{... | collective-permute-start | bytes 196616 | tf_op jit(solution)/shard_map/ppermute | solution.py:105
  236.8 25.7 %collective-permute-start.17 = (f32[64,2,1,128]{3,2,1,0:T(1,128)S(1)}, f32[64,2,1,128]{3,2,1,0:T(1,128)S(1)}, u32[]{:S(2)}, u32[]{:S(2)}) collective-permute-start(f32[64,2,1,128]{3,2,1,0:T(1,128)S(1)} %get-tuple-element.45), channel_id=1, source_target_pairs={{0,1},{1,2},{2,3},{4,5},{5,6},{6,7},{8,9},{9,10},{10,11},{12,13},{... | collective-permute-start | bytes 196616 | tf_op jit(solution)/shard_map/ppermute | solution.py:104
  256.9 32.9 %collective-permute-start.30 = (f32[64,1,48,128]{3,2,1,0:T(8,128)}, f32[64,1,48,128]{3,2,1,0:T(8,128)}, u32[]{:S(2)}, u32[]{:S(2)}) collective-permute-start(f32[64,1,48,128]{3,2,1,0:T(8,128)} %get-tuple-element.22), channel_id=1, source_target_pairs={{4,0},{8,4},{12,8},{16,12},{20,16},{24,20},{28,24},{32,28},{36,32}... | collective-permute-start | bytes 4718600 | tf_op jit(solution)/shard_map/ppermute | solution.py:105
  259.0 30.8 %collective-permute-start.31 = (f32[64,1,48,128]{3,2,1,0:T(8,128)}, f32[64,1,48,128]{3,2,1,0:T(8,128)}, u32[]{:S(2)}, u32[]{:S(2)}) collective-permute-start(f32[64,1,48,128]{3,2,1,0:T(8,128)} %get-tuple-element.21), channel_id=1, source_target_pairs={{0,4},{4,8},{8,12},{12,16},{16,20},{20,24},{24,28},{28,32},{32,36}... | collective-permute-start | bytes 4718600 | tf_op jit(solution)/shard_map/ppermute | solution.py:104
  262.5 27.3 %collective-permute-start.32 = (f32[64,2,1,128]{3,2,1,0:T(1,128)}, f32[64,2,1,128]{3,2,1,0:T(1,128)}, u32[]{:S(2)}, u32[]{:S(2)}) collective-permute-start(f32[64,2,1,128]{3,2,1,0:T(1,128)} %get-tuple-element.18), channel_id=1, source_target_pairs={{1,0},{2,1},{3,2},{5,4},{6,5},{7,6},{9,8},{10,9},{11,10},{13,12},{... | collective-permute-start | bytes 196616 | tf_op jit(solution)/shard_map/ppermute | solution.py:105
  263.8 26.0 %collective-permute-start.33 = (f32[64,2,1,128]{3,2,1,0:T(1,128)}, f32[64,2,1,128]{3,2,1,0:T(1,128)}, u32[]{:S(2)}, u32[]{:S(2)}) collective-permute-start(f32[64,2,1,128]{3,2,1,0:T(1,128)} %get-tuple-element.17), channel_id=1, source_target_pairs={{0,1},{1,2},{2,3},{4,5},{5,6},{6,7},{8,9},{9,10},{10,11},{12,13},{... | collective-permute-start | bytes 196616 | tf_op jit(solution)/shard_map/ppermute | solution.py:104
  (24 other events, 377.7 us)
where the time goes:
time: 356 us; the launch traced here: 354 us
  starting transfers between devices  109 us (31%)
  other arithmetic  90.2 us (25%)
  local copies, waits for them, and re-layouts  59.1 us (17%)
  waiting for transfers between devices  44.6 us (13%)
  Pallas kernels  25.2 us (7%)
  between operations  8.76 us (2%)
  blocking collectives  8.48 us (2%)
  matrix products  8.21 us (2%)
    ppermute x16, starting transfers between devices, halo_pair(): lax.ppermute(lax.slice_in_dim(block, size - 1, None, axis=dim), axis, for...  66.4 us
    all_to_all x2, waiting for transfers between devices, windows(): received = lax.all_to_all(jnp.stack(parts), 'col', 0, 0, tiled=True)  44.5 us
    another operation x6, other arithmetic, run_segments(): return jnp.stack(factors)  43.6 us
    add x4, other arithmetic, solve_slabs(): rho_next * rho_now * direction + 2.0 * rho_next / half_span * residual  31.2 us
    ppermute x16, starting transfers between devices, halo_pair(): high = lax.ppermute(lax.slice_in_dim(block, 0, 1, axis=dim), axis, backward)  26.1 us
    slice x14, local copies, waits for them, and re-layouts, shifted(): lax.slice_in_dim(block, 1, None, axis=dim)  25.9 us
    pallas_call x1, Pallas kernels, scatter_sum(): pl.pallas_call(scatter_sum_kernel, out_shape=jax.ShapeDtypeStruct((1, row...  25.2 us
    all_to_all x2, starting transfers between devices, windows(): received = lax.all_to_all(jnp.stack(parts), 'col', 0, 0, tiled=True)  9.51 us
  transfers between devices with their start and end apart: 36, of which 2 were waited for; matrix products, arithmetic and copies ran while one was open for 33% of the time, Pallas kernels for 0%

commit v1 on v0

--- a/solution.py
+++ b/solution.py
@@ -87,6 +87,38 @@
         ],
         compiler_params=pltpu.CompilerParams(collective_id=0, has_side_effects=True),
     )(tiles)
+
+
+def gram_kernel(a_ref, b_ref, out_ref):
+    @pl.when((pl.program_id(0) == 0) & (pl.program_id(1) == 0))
+    def _():
+        out_ref[...] = jnp.zeros_like(out_ref)
+
+    total = out_ref[...]
+    for row in range(a_ref.shape[2]):
+        total = total + lax.dot_general(
+            a_ref[:, 0, row, :],
+            b_ref[:, 0, row, :],
+            (((1,), (1,)), ((), ())),
+            precision=lax.Precision.HIGHEST,
+            preferred_element_type=jnp.float32,
+        )
+    out_ref[...] = total
+
+
+def gram(a, b, rows_per_step=8):
+    count, depth, rows, lanes = a.shape
+    spec = pl.BlockSpec((count, 1, rows_per_step, lanes), lambda i, j: (0, i, j, 0))
+    return pl.pallas_call(
+        gram_kernel,
+        grid=(depth, rows // rows_per_step),
+        in_specs=[spec, spec],
+        out_specs=pl.BlockSpec((count, count), lambda i, j: (0, 0)),
+        out_shape=jax.ShapeDtypeStruct((count, count), jnp.float32),
+        cost_estimate=pl.CostEstimate(
+            flops=2 * count * count * a.size // count, bytes_accessed=8 * a.size, transcendentals=0
+        ),
+    )(a, b)
 
 
 def lookup(region_ids, region_cond):
@@ -202,14 +234,9 @@
     ctrl_cols = run_segments(ctrl_in, shifts, solver)
     obsv_cols = run_segments(obsv_in, shifts, solver)
     row_count = ctrl_cols.shape[0] * ctrl_cols.shape[1]
-    ctrl_flat = ctrl_cols.reshape(row_count, -1)
-    obsv_flat = obsv_cols.reshape(row_count, -1)
-    partial_value = lax.dot_general(
-        ctrl_flat,
-        obsv_flat,
-        (((1,), (1,)), ((), ())),
-        precision=lax.Precision.HIGHEST,
-        preferred_element_type=jnp.float32,
+    partial_value = gram(
+        ctrl_cols.reshape((row_count,) + ctrl_cols.shape[2:]),
+        obsv_cols.reshape((row_count,) + obsv_cols.shape[2:]),
     )
     cells_total = total_x * region_ids.shape[1] * region_ids.shape[2]
     norm_scale = 1.0 / math.sqrt(cells_total)

time: 356 us -> 351 us (0.986)
  Pallas kernels: 25.2 us -> 45.3 us
  local copies, waits for them, and re-layouts: 59.1 us -> 46.3 us
  matrix products: 8.21 us -> 0 us
    pallas_call x0 -> x1, Pallas kernels: none -> 18.6 us  [gram(): pl.pallas_call(gram_kernel, grid=(depth, rows // rows_per_step), in_specs...]
    ppermute x16, starting transfers between devices: 26.1 us -> 37.7 us  [halo_pair(): high = lax.ppermute(lax.slice_in_dim(block, 0, 1, axis=dim), axis, backward)]
    ppermute x16, starting transfers between devices: 66.4 us -> 54.9 us  [halo_pair(): lax.ppermute(lax.slice_in_dim(block, size - 1, None, axis=dim), axis, for...]
    dot_general x1 -> x0, matrix products: 8.21 us -> none  [body(): lax.dot_general(ctrl_flat, obsv_flat, (((1,), (1,)), ((), ())), precision...]
    reshape x1 -> x0, local copies, waits for them, and re-layouts: 7.49 us -> none  [body(): ctrl_flat = ctrl_cols.reshape(row_count, -1)]
    dot_general x1 -> x0, local copies, waits for them, and re-layouts: 7.42 us -> none  [body(): lax.dot_general(ctrl_flat, obsv_flat, (((1,), (1,)), ((), ())), precision...]
  transfers between devices with their start and end apart: 36 -> 36, of which waited for: 2 -> 2; matrix products, arithmetic and copies ran while one was open for 33% -> 32% of each run, Pallas kernels for 0% -> 0%
where the time goes in v1:
time: 351 us; the launch traced here: 349 us
  starting transfers between devices  109 us (31%)
  other arithmetic  88.2 us (25%)
  local copies, waits for them, and re-layouts  46.3 us (13%)
  Pallas kernels  45.3 us (13%)
  waiting for transfers between devices  44.4 us (13%)
  between operations  8.79 us (3%)
  blocking collectives  6.84 us (2%)
    ppermute x16, starting transfers between devices, halo_pair(): lax.ppermute(lax.slice_in_dim(block, size - 1, None, axis=dim), axis, for...  54.9 us
    all_to_all x2, waiting for transfers between devices, windows(): received = lax.all_to_all(jnp.stack(parts), 'col', 0, 0, tiled=True)  44.3 us
    another operation x6, other arithmetic, run_segments(): return jnp.stack(factors)  41.9 us
    ppermute x16, starting transfers between devices, halo_pair(): high = lax.ppermute(lax.slice_in_dim(block, 0, 1, axis=dim), axis, backward)  37.7 us
    add x4, other arithmetic, solve_slabs(): rho_next * rho_now * direction + 2.0 * rho_next / half_span * residual  31.1 us
    pallas_call x1, Pallas kernels, scatter_sum(): pl.pallas_call(scatter_sum_kernel, out_shape=jax.ShapeDtypeStruct((1, row...  26.6 us
    slice x14, local copies, waits for them, and re-layouts, shifted(): lax.slice_in_dim(block, 1, None, axis=dim)  24.9 us
    pallas_call x1, Pallas kernels, gram(): pl.pallas_call(gram_kernel, grid=(depth, rows // rows_per_step), in_specs...  18.6 us
  transfers between devices with their start and end apart: 36, of which 2 were waited for; matrix products, arithmetic and copies ran while one was open for 32% of the time, Pallas kernels for 0%

profile of v1, /device:TPU:1, one launch (start us, length us, event | category | flops | bytes accessed | tf_op | source)
XLA Modules:
  0.0 349.3 jit_solution(10082299996817504856)
XLA Ops:
  4.7 4.8 %all-to-all-start = ((f32[4,16,2,48,128]{4,3,2,1,0:T(8,128)}), f32[4,16,2,48,128]{4,3,2,1,0:T(8,128)S(1)}, u32[]{:S(2)}, u32[]{:S(2)}) async-start(f32[4,16,2,48,128]{4,3,2,1,0:T(8,128)} %pad_maximum_fusion.2), calls=%async_computation | async-start | bytes 6291456 | tf_op jit(solution)/shard_map/all_to_all | solution.py:162
  13.5 32.6 %all-to-all-done = f32[4,16,2,48,128]{4,3,2,1,0:T(8,128)S(1)} async-done(((f32[4,16,2,48,128]{4,3,2,1,0:T(8,128)}), f32[4,16,2,48,128]{4,3,2,1,0:T(8,128)S(1)}, u32[]{:S(2)}, u32[]{:S(2)}) %all-to-all-start) | async-done | bytes 3145760 | tf_op jit(solution)/shard_map/all_to_all | solution.py:162
  46.2 4.7 %all-to-all-start.1 = ((f32[4,16,2,48,128]{4,3,2,1,0:T(8,128)}), f32[4,16,2,48,128]{4,3,2,1,0:T(8,128)}, u32[]{:S(2)}, u32[]{:S(2)}) async-start(f32[4,16,2,48,128]{4,3,2,1,0:T(8,128)} %pad_maximum_fusion.3), calls=%async_computation.1 | async-start | bytes 6291456 | tf_op jit(solution)/shard_map/all_to_all | solution.py:162
  51.5 5.2 %select_add_fusion = f32[2,192,128]{2,1,0:T(8,128)S(1)} fusion(s32[2,192,128]{2,1,0:T(8,128)S(1)} %copy-done.13, f32[]{:T(128)} %bitcast.13, f32[]{:T(128)} %bitcast.12, f32[]{:T(128)} %bitcast.11, f32[]{:T(128)} %bitcast.10, f32[]{:T(128)} %bitcast.9, f32[]{:T(128)} %bitcast.8, f32[]{:T(128)} %bitcast.7, f32[]{:T(128)} %bitcast.6), kind=kLoop, calls=%fused_computation.210 | loop fusion | flops 1130496 | bytes 393248 | tf_op jit(solution)/shard_map/add | solution.py:127
  56.8 3.8 %collective-permute-start = (f32[1,50,128]{2,1,0:T(8,128)S(1)}, f32[1,50,128]{2,1,0:T(8,128)S(1)}, u32[]{:S(2)}, u32[]{:S(2)}) collective-permute-start(f32[1,50,128]{2,1,0:T(8,128)S(1)} %get-tuple-element.76), channel_id=1, source_target_pairs={{4,0},{8,4},{12,8},{16,12},{20,16},{24,20},{28,24},{32,28},{36,32}... | collective-permute-start | bytes 76808 | tf_op jit(solution)/shard_map/ppermute | solution.py:22
  74.9 11.7 %all-to-all-done.1 = f32[4,16,2,48,128]{4,3,2,1,0:T(8,128)} async-done(((f32[4,16,2,48,128]{4,3,2,1,0:T(8,128)}), f32[4,16,2,48,128]{4,3,2,1,0:T(8,128)}, u32[]{:S(2)}, u32[]{:S(2)}) %all-to-all-start.1) | async-done | bytes 3145760 | tf_op jit(solution)/shard_map/all_to_all | solution.py:162
  89.6 4.7 %collective-permute-start.18 = (f32[64,1,48,128]{3,2,1,0:T(8,128)S(1)}, f32[64,1,48,128]{3,2,1,0:T(8,128)S(1)}, u32[]{:S(2)}, u32[]{:S(2)}) collective-permute-start(f32[64,1,48,128]{3,2,1,0:T(8,128)S(1)} %get-tuple-element.36), channel_id=1, source_target_pairs={{4,0},{8,4},{12,8},{16,12},{20,16},{24,20},{28,24},{32,28},{36,32}... | collective-permute-start | bytes 4718600 | tf_op jit(solution)/shard_map/ppermute | solution.py:137
  99.2 4.0 %collective-permute-start.21 = (f32[64,2,1,128]{3,2,1,0:T(1,128)S(1)}, f32[64,2,1,128]{3,2,1,0:T(1,128)S(1)}, u32[]{:S(2)}, u32[]{:S(2)}) collective-permute-start(f32[64,2,1,128]{3,2,1,0:T(1,128)S(1)} %get-tuple-element.40), channel_id=1, source_target_pairs={{0,1},{1,2},{2,3},{4,5},{5,6},{6,7},{8,9},{9,10},{10,11},{12,13},{... | collective-permute-start | bytes 196616 | tf_op jit(solution)/shard_map/ppermute | solution.py:136
  110.2 3.6 %collective-permute-start.3 = (f32[64,1,48,128]{3,2,1,0:T(8,128)S(1)}, f32[64,1,48,128]{3,2,1,0:T(8,128)}, u32[]{:S(2)}, u32[]{:S(2)}) collective-permute-start(f32[64,1,48,128]{3,2,1,0:T(8,128)S(1)} %get-tuple-element.63), channel_id=1, source_target_pairs={{0,4},{4,8},{8,12},{12,16},{16,20},{20,24},{24,28},{28,32},{32,36}... | collective-permute-start | bytes 4718600 | tf_op jit(solution)/shard_map/ppermute | solution.py:136
  115.8 4.0 %collective-permute-start.5 = (f32[64,2,1,128]{3,2,1,0:T(1,128)}, f32[64,2,1,128]{3,2,1,0:T(1,128)S(1)}, u32[]{:S(2)}, u32[]{:S(2)}) collective-permute-start(f32[64,2,1,128]{3,2,1,0:T(1,128)} %get-tuple-element.68), channel_id=1, source_target_pairs={{0,1},{1,2},{2,3},{4,5},{5,6},{6,7},{8,9},{9,10},{10,11},{12,13},{... | collective-permute-start | bytes 196616 | tf_op jit(solution)/shard_map/ppermute | solution.py:136
  120.9 8.0 %multiply_add_fusion.1 = (f32[64,2,48,128]{3,2,1,0:T(8,128)S(1)}, f32[64,2,48,128]{3,2,1,0:T(8,128)}) fusion(f32[64,2,48,128]{3,2,1,0:T(8,128)S(1)} %get-tuple-element.92, f32[]{:T(128)S(6)} %div.73, f32[]{:T(128)S(6)} %mul.258, f32[]{:T(128)} %bitcast, f32[2,48,128]{2,1,0:T(8,128)S(1)} %get-tuple-element.78, f32[2,48,128]{2,1,0:T(8,128)S(1)} %copy-done.9, ...), kind=kLoop, calls=%fused_computation.196 | loop fusion | flops 21233664 | bytes 25460748 | tf_op jit(solution)/shard_map/add | solution.py:200
  138.5 4.6 %collective-permute-start.25 = (f32[64,2,1,128]{3,2,1,0:T(1,128)}, f32[64,2,1,128]{3,2,1,0:T(1,128)}, u32[]{:S(2)}, u32[]{:S(2)}) collective-permute-start(f32[64,2,1,128]{3,2,1,0:T(1,128)} %get-tuple-element.34), channel_id=1, source_target_pairs={{0,1},{1,2},{2,3},{4,5},{5,6},{6,7},{8,9},{9,10},{10,11},{12,13},{... | collective-permute-start | bytes 196616 | tf_op jit(solution)/shard_map/ppermute | solution.py:136
  143.1 7.5 %multiply_add_fusion.3 = (f32[64,2,48,128]{3,2,1,0:T(8,128)S(1)}, f32[64,2,48,128]{3,2,1,0:T(8,128)}) fusion(f32[64,2,48,128]{3,2,1,0:T(8,128)S(1)} %get-tuple-element.93, f32[]{:T(128)S(6)} %div.73, f32[]{:T(128)S(6)} %mul.258, f32[]{:T(128)} %bitcast, f32[2,48,128]{2,1,0:T(8,128)S(1)} %get-tuple-element.78, f32[2,48,128]{2,1,0:T(8,128)S(1)} %copy-done.9, ...), kind=kLoop, calls=%fused_computation.199 | loop fusion | flops 21233664 | bytes 25460748 | tf_op jit(solution)/shard_map/add | solution.py:200
  152.0 3.5 fusion.165
  165.5 4.2 %collective-permute-start.9 = (f32[64,2,1,128]{3,2,1,0:T(1,128)}, f32[64,2,1,128]{3,2,1,0:T(1,128)S(1)}, u32[]{:S(2)}, u32[]{:S(2)}) collective-permute-start(f32[64,2,1,128]{3,2,1,0:T(1,128)} %get-tuple-element.62), channel_id=1, source_target_pairs={{0,1},{1,2},{2,3},{4,5},{5,6},{6,7},{8,9},{9,10},{10,11},{12,13},{... | collective-permute-start | bytes 196616 | tf_op jit(solution)/shard_map/ppermute | solution.py:136
  169.7 9.1 %multiply_bitcast_fusion = (f32[1,64,2,48,128]{4,3,2,1,0:T(8,128)}, f32[64,2,48,128]{3,2,1,0:T(8,128)S(1)}) fusion(f32[]{:T(128)S(6)} %sqrt.8, f32[64,2,48,128]{3,2,1,0:T(8,128)} %get-tuple-element.8, f32[64,2,48,128]{3,2,1,0:T(8,128)S(1)} %get-tuple-element.7, f32[]{:T(128)} %bitcast, f32[2,48,128]{2,1,0:T(8,128)S(1)} %get-tuple-element.78, ...), kind=kLoop, calls=%fused_computation.195 | loop fusion | flops 23592960 | bytes 28606480 | tf_op jit(solution)/shard_map/stack | solution.py:215
  188.7 4.0 %collective-permute-start.29 = (f32[64,2,1,128]{3,2,1,0:T(1,128)}, f32[64,2,1,128]{3,2,1,0:T(1,128)S(1)}, u32[]{:S(2)}, u32[]{:S(2)}) collective-permute-start(f32[64,2,1,128]{3,2,1,0:T(1,128)} %get-tuple-element.28), channel_id=1, source_target_pairs={{0,1},{1,2},{2,3},{4,5},{5,6},{6,7},{8,9},{9,10},{10,11},{12,13},{... | collective-permute-start | bytes 196616 | tf_op jit(solution)/shard_map/ppermute | solution.py:136
  192.7 8.3 %multiply_bitcast_fusion.1 = (f32[1,64,2,48,128]{4,3,2,1,0:T(8,128)}, f32[64,2,48,128]{3,2,1,0:T(8,128)S(1)}) fusion(f32[]{:T(128)S(6)} %sqrt.8, f32[64,2,48,128]{3,2,1,0:T(8,128)} %get-tuple-element.14, f32[64,2,48,128]{3,2,1,0:T(8,128)S(1)} %get-tuple-element.13, f32[]{:T(128)} %bitcast, f32[2,48,128]{2,1,0:T(8,128)S(1)} %get-tuple-element.78, ...), kind=kLoop, calls=%fused_computation.198 | loop fusion | flops 23592960 | bytes 28606480 | tf_op jit(solution)/shard_map/stack | solution.py:215
  208.0 3.9 %collective-permute-start.10 = (f32[64,1,48,128]{3,2,1,0:T(8,128)}, f32[64,1,48,128]{3,2,1,0:T(8,128)}, u32[]{:S(2)}, u32[]{:S(2)}) collective-permute-start(f32[64,1,48,128]{3,2,1,0:T(8,128)} %get-tuple-element.52), channel_id=1, source_target_pairs={{4,0},{8,4},{12,8},{16,12},{20,16},{24,20},{28,24},{32,28},{36,32}... | collective-permute-start | bytes 4718600 | tf_op jit(solution)/shard_map/ppermute | solution.py:137
  215.1 4.6 %collective-permute-start.13 = (f32[64,2,1,128]{3,2,1,0:T(1,128)}, f32[64,2,1,128]{3,2,1,0:T(1,128)}, u32[]{:S(2)}, u32[]{:S(2)}) collective-permute-start(f32[64,2,1,128]{3,2,1,0:T(1,128)} %get-tuple-element.56), channel_id=1, source_target_pairs={{0,1},{1,2},{2,3},{4,5},{5,6},{6,7},{8,9},{9,10},{10,11},{12,13},{... | collective-permute-start | bytes 196616 | tf_op jit(solution)/shard_map/ppermute | solution.py:136
  219.8 7.7 %multiply_add_fusion = (f32[64,2,48,128]{3,2,1,0:T(8,128)S(1)}, f32[64,2,48,128]{3,2,1,0:T(8,128)}) fusion(f32[]{:T(128)S(6)} %div.81, f32[]{:T(128)S(6)} %mul.607, f32[64,2,48,128]{3,2,1,0:T(8,128)S(1)} %get-tuple-element.4, f32[]{:T(128)S(6)} %mul.604, f32[64,2,48,128]{3,2,1,0:T(8,128)S(1)} %broadcast_divide_fusion, f32[]{:T(128)} %bitcast.15, ...), kind=kLoop, calls=%fused_computation.194 | loop fusion | flops 22020096 | bytes 25460752 | tf_op jit(solution)/shard_map/add | solution.py:200
  230.1 4.1 %collective-permute-start.30 = (f32[64,1,48,128]{3,2,1,0:T(8,128)}, f32[64,1,48,128]{3,2,1,0:T(8,128)}, u32[]{:S(2)}, u32[]{:S(2)}) collective-permute-start(f32[64,1,48,128]{3,2,1,0:T(8,128)} %get-tuple-element.22), channel_id=1, source_target_pairs={{4,0},{8,4},{12,8},{16,12},{20,16},{24,20},{28,24},{32,28},{36,32}... | collective-permute-start | bytes 4718600 | tf_op jit(solution)/shard_map/ppermute | solution.py:137
  237.5 4.2 %collective-permute-start.33 = (f32[64,2,1,128]{3,2,1,0:T(1,128)}, f32[64,2,1,128]{3,2,1,0:T(1,128)S(1)}, u32[]{:S(2)}, u32[]{:S(2)}) collective-permute-start(f32[64,2,1,128]{3,2,1,0:T(1,128)} %get-tuple-element.17), channel_id=1, source_target_pairs={{0,1},{1,2},{2,3},{4,5},{5,6},{6,7},{8,9},{9,10},{10,11},{12,13},{... | collective-permute-start | bytes 196616 | tf_op jit(solution)/shard_map/ppermute | solution.py:136
  241.7 7.8 %multiply_add_fusion.2 = (f32[64,2,48,128]{3,2,1,0:T(8,128)S(1)}, f32[64,2,48,128]{3,2,1,0:T(8,128)}) fusion(f32[]{:T(128)S(6)} %div.81, f32[]{:T(128)S(6)} %mul.607, f32[64,2,48,128]{3,2,1,0:T(8,128)S(1)} %get-tuple-element.10, f32[]{:T(128)S(6)} %mul.604, f32[64,2,48,128]{3,2,1,0:T(8,128)S(1)} %broadcast_divide_fusion.1, f32[]{:T(128)} %bitcast.15, ...), kind=kLoop, calls=%fused_computation.197 | loop fusion | flops 22020096 | bytes 25460752 | tf_op jit(solution)/shard_map/add | solution.py:200
  257.5 4.1 %collective-permute-start.14 = (f32[64,1,48,128]{3,2,1,0:T(8,128)}, f32[64,1,48,128]{3,2,1,0:T(8,128)}, u32[]{:S(2)}, u32[]{:S(2)}) collective-permute-start(f32[64,1,48,128]{3,2,1,0:T(8,128)} %get-tuple-element.50), channel_id=1, source_target_pairs={{4,0},{8,4},{12,8},{16,12},{20,16},{24,20},{28,24},{32,28},{36,32}... | collective-permute-start | bytes 4718600 | tf_op jit(solution)/shard_map/ppermute | solution.py:137
  264.9 4.6 %collective-permute-start.17 = (f32[64,2,1,128]{3,2,1,0:T(1,128)}, f32[64,2,1,128]{3,2,1,0:T(1,128)}, u32[]{:S(2)}, u32[]{:S(2)}) collective-permute-start(f32[64,2,1,128]{3,2,1,0:T(1,128)} %get-tuple-element.45), channel_id=1, source_target_pairs={{0,1},{1,2},{2,3},{4,5},{5,6},{6,7},{8,9},{9,10},{10,11},{12,13},{... | collective-permute-start | bytes 196616 | tf_op jit(solution)/shard_map/ppermute | solution.py:136
  269.5 8.8 %fusion.81 = f32[1,64,2,48,128]{4,3,2,1,0:T(8,128)} fusion(f32[64,2,48,128]{3,2,1,0:T(8,128)S(1)} %get-tuple-element.4, f32[64,2,48,128]{3,2,1,0:T(8,128)S(1)} %copy-done.1, f32[64,2,48,128]{3,2,1,0:T(8,128)S(1)} %get-tuple-element.5, f32[64,1,48,128]{3,2,1,0:T(8,128)} %collective-permute-done.30, f32[64,1,48,128]{3,2,1,0:T(8,128)} %get-tuple-element.21, ...), kind=kLoop, calls=%fused_computation.99 | loop fusion | flops 25952256 | bytes 25460760 | tf_op jit(solution)/shard_map/stack | solution.py:215
  278.4 5.3 %pad_maximum_fusion.1 = f32[2,64,2,48,128]{4,3,2,1,0:T(8,128)} fusion(f32[1,64,2,48,128]{4,3,2,1,0:T(8,128)} %fusion.81, f32[1,64,2,48,128]{4,3,2,1,0:T(8,128)S(1)} %copy-done.3), kind=kLoop, calls=%fused_computation.17 | loop fusion | flops 1572864 | bytes 12582912 | tf_op jit(solution)/shard_map/stack | solution.py:215
  283.7 7.3 %fusion.39 = f32[1,64,2,48,128]{4,3,2,1,0:T(8,128)S(1)} fusion(f32[64,2,48,128]{3,2,1,0:T(8,128)S(1)} %get-tuple-element.10, f32[64,2,48,128]{3,2,1,0:T(8,128)S(1)} %copy-done.2, f32[64,2,48,128]{3,2,1,0:T(8,128)S(1)} %get-tuple-element.11, f32[64,1,48,128]{3,2,1,0:T(8,128)} %collective-permute-done.14, f32[64,1,48,128]{3,2,1,0:T(8,128)S(1)} %get-tuple-element.49, ...), kind=kLoop, calls=%fused_computation.57 | loop fusion | flops 25952256 | bytes 25460760 | tf_op jit(solution)/shard_map/stack | solution.py:215
  294.1 18.6 %shard_map.76 = f32[128,128]{1,0:T(8,128)} custom-call(f32[128,2,48,128]{3,2,1,0:T(8,128)} %bitcast.49, f32[128,2,48,128]{3,2,1,0:T(8,128)} %bitcast.48), custom_call_target="tpu_custom_call" | custom-call | flops 402653184 | bytes 12582912 | tf_op jit(solution)/shard_map/pallas_call | solution.py:112
  313.7 6.8 %all_to_all.15 = f32[4,128,32]{1,2,0:T(8,128)S(1)} all-to-all(f32[4,128,32]{1,2,0:T(8,128)S(1)} %bitcast.50), channel_id=1, replica_groups=mesh['slab'=32,'col'=4] {'col'}, dimensions={0} | all-to-all | bytes 131072 | tf_op jit(solution)/shard_map/all_to_all | solution.py:248
  321.4 26.6 %shard_map.77 = f32[1,1,128]{2,1,0:T(1,128)} custom-call(f32[32,1,128]{2,1,0:T(1,128)} %bitcast.51), custom_call_target="tpu_custom_call" | custom-call | tf_op jit(solution)/shard_map/pallas_call | solution.py:78
  (137 shorter events, 97.6 us)
Async XLA Ops:
  4.7 41.5 %all-to-all-start = ((f32[4,16,2,48,128]{4,3,2,1,0:T(8,128)}), f32[4,16,2,48,128]{4,3,2,1,0:T(8,128)S(1)}, u32[]{:S(2)}, u32[]{:S(2)}) async-start(f32[4,16,2,48,128]{4,3,2,1,0:T(8,128)} %pad_maximum_fusion.2), calls=%async_computation | async-start | bytes 6291456 | tf_op jit(solution)/shard_map/all_to_all | solution.py:162
  46.2 40.5 %all-to-all-start.1 = ((f32[4,16,2,48,128]{4,3,2,1,0:T(8,128)}), f32[4,16,2,48,128]{4,3,2,1,0:T(8,128)}, u32[]{:S(2)}, u32[]{:S(2)}) async-start(f32[4,16,2,48,128]{4,3,2,1,0:T(8,128)} %pad_maximum_fusion.3), calls=%async_computation.1 | async-start | bytes 6291456 | tf_op jit(solution)/shard_map/all_to_all | solution.py:162
  89.6 26.2 %collective-permute-start.18 = (f32[64,1,48,128]{3,2,1,0:T(8,128)S(1)}, f32[64,1,48,128]{3,2,1,0:T(8,128)S(1)}, u32[]{:S(2)}, u32[]{:S(2)}) collective-permute-start(f32[64,1,48,128]{3,2,1,0:T(8,128)S(1)} %get-tuple-element.36), channel_id=1, source_target_pairs={{4,0},{8,4},{12,8},{16,12},{20,16},{24,20},{28,24},{32,28},{36,32}... | collective-permute-start | bytes 4718600 | tf_op jit(solution)/shard_map/ppermute | solution.py:137
  94.3 25.5 %collective-permute-start.19 = (f32[64,1,48,128]{3,2,1,0:T(8,128)S(1)}, f32[64,1,48,128]{3,2,1,0:T(8,128)S(1)}, u32[]{:S(2)}, u32[]{:S(2)}) collective-permute-start(f32[64,1,48,128]{3,2,1,0:T(8,128)S(1)} %get-tuple-element.35), channel_id=1, source_target_pairs={{0,4},{4,8},{8,12},{12,16},{16,20},{20,24},{24,28},{28,32},{32,36}... | collective-permute-start | bytes 4718600 | tf_op jit(solution)/shard_map/ppermute | solution.py:136
  108.2 30.3 %collective-permute-start.1 = (f32[64,1,48,128]{3,2,1,0:T(8,128)}, f32[64,1,48,128]{3,2,1,0:T(8,128)}, u32[]{:S(2)}, u32[]{:S(2)}) collective-permute-start(f32[64,1,48,128]{3,2,1,0:T(8,128)} %get-tuple-element.64), channel_id=1, source_target_pairs={{4,0},{8,4},{12,8},{16,12},{20,16},{24,20},{28,24},{32,28},{36,32}... | collective-permute-start | bytes 4718600 | tf_op jit(solution)/shard_map/ppermute | solution.py:137
  110.2 33.0 %collective-permute-start.3 = (f32[64,1,48,128]{3,2,1,0:T(8,128)S(1)}, f32[64,1,48,128]{3,2,1,0:T(8,128)}, u32[]{:S(2)}, u32[]{:S(2)}) collective-permute-start(f32[64,1,48,128]{3,2,1,0:T(8,128)S(1)} %get-tuple-element.63), channel_id=1, source_target_pairs={{0,4},{4,8},{8,12},{12,16},{16,20},{20,24},{24,28},{28,32},{32,36}... | collective-permute-start | bytes 4718600 | tf_op jit(solution)/shard_map/ppermute | solution.py:136
  114.5 19.6 %collective-permute-start.4 = (f32[64,2,1,128]{3,2,1,0:T(1,128)}, f32[64,2,1,128]{3,2,1,0:T(1,128)S(1)}, u32[]{:S(2)}, u32[]{:S(2)}) collective-permute-start(f32[64,2,1,128]{3,2,1,0:T(1,128)} %get-tuple-element.67), channel_id=1, source_target_pairs={{1,0},{2,1},{3,2},{5,4},{6,5},{7,6},{9,8},{10,9},{11,10},{13,12},{... | collective-permute-start | bytes 196616 | tf_op jit(solution)/shard_map/ppermute | solution.py:137
  115.8 21.4 %collective-permute-start.5 = (f32[64,2,1,128]{3,2,1,0:T(1,128)}, f32[64,2,1,128]{3,2,1,0:T(1,128)S(1)}, u32[]{:S(2)}, u32[]{:S(2)}) collective-permute-start(f32[64,2,1,128]{3,2,1,0:T(1,128)} %get-tuple-element.68), channel_id=1, source_target_pairs={{0,1},{1,2},{2,3},{4,5},{5,6},{6,7},{8,9},{9,10},{10,11},{12,13},{... | collective-permute-start | bytes 196616 | tf_op jit(solution)/shard_map/ppermute | solution.py:136
  131.6 33.9 %collective-permute-start.22 = (f32[64,1,48,128]{3,2,1,0:T(8,128)}, f32[64,1,48,128]{3,2,1,0:T(8,128)}, u32[]{:S(2)}, u32[]{:S(2)}) collective-permute-start(f32[64,1,48,128]{3,2,1,0:T(8,128)} %get-tuple-element.30), channel_id=1, source_target_pairs={{4,0},{8,4},{12,8},{16,12},{20,16},{24,20},{28,24},{32,28},{36,32}... | collective-permute-start | bytes 4718600 | tf_op jit(solution)/shard_map/ppermute | solution.py:137
  134.1 35.6 %collective-permute-start.23 = (f32[64,1,48,128]{3,2,1,0:T(8,128)}, f32[64,1,48,128]{3,2,1,0:T(8,128)}, u32[]{:S(2)}, u32[]{:S(2)}) collective-permute-start(f32[64,1,48,128]{3,2,1,0:T(8,128)} %get-tuple-element.29), channel_id=1, source_target_pairs={{0,4},{4,8},{8,12},{12,16},{16,20},{20,24},{24,28},{28,32},{32,36}... | collective-permute-start | bytes 4718600 | tf_op jit(solution)/shard_map/ppermute | solution.py:136
  137.2 24.3 %collective-permute-start.24 = (f32[64,2,1,128]{3,2,1,0:T(1,128)}, f32[64,2,1,128]{3,2,1,0:T(1,128)S(1)}, u32[]{:S(2)}, u32[]{:S(2)}) collective-permute-start(f32[64,2,1,128]{3,2,1,0:T(1,128)} %get-tuple-element.33), channel_id=1, source_target_pairs={{1,0},{2,1},{3,2},{5,4},{6,5},{7,6},{9,8},{10,9},{11,10},{13,12},{... | collective-permute-start | bytes 196616 | tf_op jit(solution)/shard_map/ppermute | solution.py:137
  138.5 25.6 %collective-permute-start.25 = (f32[64,2,1,128]{3,2,1,0:T(1,128)}, f32[64,2,1,128]{3,2,1,0:T(1,128)}, u32[]{:S(2)}, u32[]{:S(2)}) collective-permute-start(f32[64,2,1,128]{3,2,1,0:T(1,128)} %get-tuple-element.34), channel_id=1, source_target_pairs={{0,1},{1,2},{2,3},{4,5},{5,6},{6,7},{8,9},{9,10},{10,11},{12,13},{... | collective-permute-start | bytes 196616 | tf_op jit(solution)/shard_map/ppermute | solution.py:136
  158.6 30.1 %collective-permute-start.6 = (f32[64,1,48,128]{3,2,1,0:T(8,128)}, f32[64,1,48,128]{3,2,1,0:T(8,128)}, u32[]{:S(2)}, u32[]{:S(2)}) collective-permute-start(f32[64,1,48,128]{3,2,1,0:T(8,128)} %get-tuple-element.58), channel_id=1, source_target_pairs={{4,0},{8,4},{12,8},{16,12},{20,16},{24,20},{28,24},{32,28},{36,32}... | collective-permute-start | bytes 4718600 | tf_op jit(solution)/shard_map/ppermute | solution.py:137
  161.5 31.2 %collective-permute-start.7 = (f32[64,1,48,128]{3,2,1,0:T(8,128)S(1)}, f32[64,1,48,128]{3,2,1,0:T(8,128)}, u32[]{:S(2)}, u32[]{:S(2)}) collective-permute-start(f32[64,1,48,128]{3,2,1,0:T(8,128)S(1)} %get-tuple-element.57), channel_id=1, source_target_pairs={{0,4},{4,8},{8,12},{12,16},{16,20},{20,24},{24,28},{28,32},{32,36}... | collective-permute-start | bytes 4718600 | tf_op jit(solution)/shard_map/ppermute | solution.py:136
  164.2 21.0 %collective-permute-start.8 = (f32[64,2,1,128]{3,2,1,0:T(1,128)}, f32[64,2,1,128]{3,2,1,0:T(1,128)S(1)}, u32[]{:S(2)}, u32[]{:S(2)}) collective-permute-start(f32[64,2,1,128]{3,2,1,0:T(1,128)} %get-tuple-element.61), channel_id=1, source_target_pairs={{1,0},{2,1},{3,2},{5,4},{6,5},{7,6},{9,8},{10,9},{11,10},{13,12},{... | collective-permute-start | bytes 196616 | tf_op jit(solution)/shard_map/ppermute | solution.py:137
  165.5 21.9 %collective-permute-start.9 = (f32[64,2,1,128]{3,2,1,0:T(1,128)}, f32[64,2,1,128]{3,2,1,0:T(1,128)S(1)}, u32[]{:S(2)}, u32[]{:S(2)}) collective-permute-start(f32[64,2,1,128]{3,2,1,0:T(1,128)} %get-tuple-element.62), channel_id=1, source_target_pairs={{0,1},{1,2},{2,3},{4,5},{5,6},{6,7},{8,9},{9,10},{10,11},{12,13},{... | collective-permute-start | bytes 196616 | tf_op jit(solution)/shard_map/ppermute | solution.py:136
  181.8 33.3 %collective-permute-start.26 = (f32[64,1,48,128]{3,2,1,0:T(8,128)}, f32[64,1,48,128]{3,2,1,0:T(8,128)}, u32[]{:S(2)}, u32[]{:S(2)}) collective-permute-start(f32[64,1,48,128]{3,2,1,0:T(8,128)} %get-tuple-element.24), channel_id=1, source_target_pairs={{4,0},{8,4},{12,8},{16,12},{20,16},{24,20},{28,24},{32,28},{36,32}... | collective-permute-start | bytes 4718600 | tf_op jit(solution)/shard_map/ppermute | solution.py:137
  185.2 34.5 %collective-permute-start.27 = (f32[64,1,48,128]{3,2,1,0:T(8,128)}, f32[64,1,48,128]{3,2,1,0:T(8,128)}, u32[]{:S(2)}, u32[]{:S(2)}) collective-permute-start(f32[64,1,48,128]{3,2,1,0:T(8,128)} %get-tuple-element.23), channel_id=1, source_target_pairs={{0,4},{4,8},{8,12},{12,16},{16,20},{20,24},{24,28},{28,32},{32,36}... | collective-permute-start | bytes 4718600 | tf_op jit(solution)/shard_map/ppermute | solution.py:136
  187.4 24.5 %collective-permute-start.28 = (f32[64,2,1,128]{3,2,1,0:T(1,128)}, f32[64,2,1,128]{3,2,1,0:T(1,128)S(1)}, u32[]{:S(2)}, u32[]{:S(2)}) collective-permute-start(f32[64,2,1,128]{3,2,1,0:T(1,128)} %get-tuple-element.27), channel_id=1, source_target_pairs={{1,0},{2,1},{3,2},{5,4},{6,5},{7,6},{9,8},{10,9},{11,10},{13,12},{... | collective-permute-start | bytes 196616 | tf_op jit(solution)/shard_map/ppermute | solution.py:137
  188.7 25.1 %collective-permute-start.29 = (f32[64,2,1,128]{3,2,1,0:T(1,128)}, f32[64,2,1,128]{3,2,1,0:T(1,128)S(1)}, u32[]{:S(2)}, u32[]{:S(2)}) collective-permute-start(f32[64,2,1,128]{3,2,1,0:T(1,128)} %get-tuple-element.28), channel_id=1, source_target_pairs={{0,1},{1,2},{2,3},{4,5},{5,6},{6,7},{8,9},{9,10},{10,11},{12,13},{... | collective-permute-start | bytes 196616 | tf_op jit(solution)/shard_map/ppermute | solution.py:136
  208.0 29.5 %collective-permute-start.10 = (f32[64,1,48,128]{3,2,1,0:T(8,128)}, f32[64,1,48,128]{3,2,1,0:T(8,128)}, u32[]{:S(2)}, u32[]{:S(2)}) collective-permute-start(f32[64,1,48,128]{3,2,1,0:T(8,128)} %get-tuple-element.52), channel_id=1, source_target_pairs={{4,0},{8,4},{12,8},{16,12},{20,16},{24,20},{28,24},{32,28},{36,32}... | collective-permute-start | bytes 4718600 | tf_op jit(solution)/shard_map/ppermute | solution.py:137
  211.9 29.8 %collective-permute-start.11 = (f32[64,1,48,128]{3,2,1,0:T(8,128)S(1)}, f32[64,1,48,128]{3,2,1,0:T(8,128)}, u32[]{:S(2)}, u32[]{:S(2)}) collective-permute-start(f32[64,1,48,128]{3,2,1,0:T(8,128)S(1)} %get-tuple-element.51), channel_id=1, source_target_pairs={{0,4},{4,8},{8,12},{12,16},{16,20},{20,24},{24,28},{28,32},{32,36}... | collective-permute-start | bytes 4718600 | tf_op jit(solution)/shard_map/ppermute | solution.py:136
  213.8 20.4 %collective-permute-start.12 = (f32[64,2,1,128]{3,2,1,0:T(1,128)}, f32[64,2,1,128]{3,2,1,0:T(1,128)S(1)}, u32[]{:S(2)}, u32[]{:S(2)}) collective-permute-start(f32[64,2,1,128]{3,2,1,0:T(1,128)} %get-tuple-element.55), channel_id=1, source_target_pairs={{1,0},{2,1},{3,2},{5,4},{6,5},{7,6},{9,8},{10,9},{11,10},{13,12},{... | collective-permute-start | bytes 196616 | tf_op jit(solution)/shard_map/ppermute | solution.py:137
  215.1 21.0 %collective-permute-start.13 = (f32[64,2,1,128]{3,2,1,0:T(1,128)}, f32[64,2,1,128]{3,2,1,0:T(1,128)}, u32[]{:S(2)}, u32[]{:S(2)}) collective-permute-start(f32[64,2,1,128]{3,2,1,0:T(1,128)} %get-tuple-element.56), channel_id=1, source_target_pairs={{0,1},{1,2},{2,3},{4,5},{5,6},{6,7},{8,9},{9,10},{10,11},{12,13},{... | collective-permute-start | bytes 196616 | tf_op jit(solution)/shard_map/ppermute | solution.py:136
  230.1 34.8 %collective-permute-start.30 = (f32[64,1,48,128]{3,2,1,0:T(8,128)}, f32[64,1,48,128]{3,2,1,0:T(8,128)}, u32[]{:S(2)}, u32[]{:S(2)}) collective-permute-start(f32[64,1,48,128]{3,2,1,0:T(8,128)} %get-tuple-element.22), channel_id=1, source_target_pairs={{4,0},{8,4},{12,8},{16,12},{20,16},{24,20},{28,24},{32,28},{36,32}... | collective-permute-start | bytes 4718600 | tf_op jit(solution)/shard_map/ppermute | solution.py:137
  234.2 35.3 %collective-permute-start.31 = (f32[64,1,48,128]{3,2,1,0:T(8,128)}, f32[64,1,48,128]{3,2,1,0:T(8,128)}, u32[]{:S(2)}, u32[]{:S(2)}) collective-permute-start(f32[64,1,48,128]{3,2,1,0:T(8,128)} %get-tuple-element.21), channel_id=1, source_target_pairs={{0,4},{4,8},{8,12},{12,16},{16,20},{20,24},{24,28},{28,32},{32,36}... | collective-permute-start | bytes 4718600 | tf_op jit(solution)/shard_map/ppermute | solution.py:136
  236.2 25.5 %collective-permute-start.32 = (f32[64,2,1,128]{3,2,1,0:T(1,128)}, f32[64,2,1,128]{3,2,1,0:T(1,128)S(1)}, u32[]{:S(2)}, u32[]{:S(2)}) collective-permute-start(f32[64,2,1,128]{3,2,1,0:T(1,128)} %get-tuple-element.18), channel_id=1, source_target_pairs={{1,0},{2,1},{3,2},{5,4},{6,5},{7,6},{9,8},{10,9},{11,10},{13,12},{... | collective-permute-start | bytes 196616 | tf_op jit(solution)/shard_map/ppermute | solution.py:137
  237.5 26.1 %collective-permute-start.33 = (f32[64,2,1,128]{3,2,1,0:T(1,128)}, f32[64,2,1,128]{3,2,1,0:T(1,128)S(1)}, u32[]{:S(2)}, u32[]{:S(2)}) collective-permute-start(f32[64,2,1,128]{3,2,1,0:T(1,128)} %get-tuple-element.17), channel_id=1, source_target_pairs={{0,1},{1,2},{2,3},{4,5},{5,6},{6,7},{8,9},{9,10},{10,11},{12,13},{... | collective-permute-start | bytes 196616 | tf_op jit(solution)/shard_map/ppermute | solution.py:136
  257.5 26.1 %collective-permute-start.14 = (f32[64,1,48,128]{3,2,1,0:T(8,128)}, f32[64,1,48,128]{3,2,1,0:T(8,128)}, u32[]{:S(2)}, u32[]{:S(2)}) collective-permute-start(f32[64,1,48,128]{3,2,1,0:T(8,128)} %get-tuple-element.50), channel_id=1, source_target_pairs={{4,0},{8,4},{12,8},{16,12},{20,16},{24,20},{28,24},{32,28},{36,32}... | collective-permute-start | bytes 4718600 | tf_op jit(solution)/shard_map/ppermute | solution.py:137
  261.7 22.0 %collective-permute-start.15 = (f32[64,1,48,128]{3,2,1,0:T(8,128)S(1)}, f32[64,1,48,128]{3,2,1,0:T(8,128)}, u32[]{:S(2)}, u32[]{:S(2)}) collective-permute-start(f32[64,1,48,128]{3,2,1,0:T(8,128)S(1)} %get-tuple-element.49), channel_id=1, source_target_pairs={{0,4},{4,8},{8,12},{12,16},{16,20},{20,24},{24,28},{28,32},{32,36}... | collective-permute-start | bytes 4718600 | tf_op jit(solution)/shard_map/ppermute | solution.py:136
  263.6 20.0 %collective-permute-start.16 = (f32[64,2,1,128]{3,2,1,0:T(1,128)}, f32[64,2,1,128]{3,2,1,0:T(1,128)S(1)}, u32[]{:S(2)}, u32[]{:S(2)}) collective-permute-start(f32[64,2,1,128]{3,2,1,0:T(1,128)} %get-tuple-element.46), channel_id=1, source_target_pairs={{1,0},{2,1},{3,2},{5,4},{6,5},{7,6},{9,8},{10,9},{11,10},{13,12},{... | collective-permute-start | bytes 196616 | tf_op jit(solution)/shard_map/ppermute | solution.py:137
  264.9 18.7 %collective-permute-start.17 = (f32[64,2,1,128]{3,2,1,0:T(1,128)}, f32[64,2,1,128]{3,2,1,0:T(1,128)}, u32[]{:S(2)}, u32[]{:S(2)}) collective-permute-start(f32[64,2,1,128]{3,2,1,0:T(1,128)} %get-tuple-element.45), channel_id=1, source_target_pairs={{0,1},{1,2},{2,3},{4,5},{5,6},{6,7},{8,9},{9,10},{10,11},{12,13},{... | collective-permute-start | bytes 196616 | tf_op jit(solution)/shard_map/ppermute | solution.py:136
  (23 other events, 311.6 us)

commit v2 on v1

--- a/solution.py
+++ b/solution.py
@@ -94,19 +94,19 @@
     def _():
         out_ref[...] = jnp.zeros_like(out_ref)
 
-    total = out_ref[...]
-    for row in range(a_ref.shape[2]):
-        total = total + lax.dot_general(
-            a_ref[:, 0, row, :],
-            b_ref[:, 0, row, :],
-            (((1,), (1,)), ((), ())),
-            precision=lax.Precision.HIGHEST,
-            preferred_element_type=jnp.float32,
-        )
-    out_ref[...] = total
-
-
-def gram(a, b, rows_per_step=8):
+    rows = a_ref.shape[2]
+    left = jnp.concatenate([a_ref[:, 0, row, :] for row in range(rows)], axis=1)
+    right = jnp.concatenate([b_ref[:, 0, row, :] for row in range(rows)], axis=1)
+    out_ref[...] += lax.dot_general(
+        left,
+        right,
+        (((1,), (1,)), ((), ())),
+        precision=lax.Precision.HIGHEST,
+        preferred_element_type=jnp.float32,
+    )
+
+
+def gram(a, b, rows_per_step=16):
     count, depth, rows, lanes = a.shape
     spec = pl.BlockSpec((count, 1, rows_per_step, lanes), lambda i, j: (0, i, j, 0))
     return pl.pallas_call(

time: 351 us -> 346 us (0.986)
  Pallas kernels: 45.3 us -> 39.8 us
    pallas_call x1, Pallas kernels: 18.6 us -> 13.2 us  [gram(): pl.pallas_call(gram_kernel, grid=(depth, rows // rows_per_step), in_specs...]
where the time goes in v2:
time: 346 us; the launch traced here: 344 us
  starting transfers between devices  109 us (32%)
  other arithmetic  88.2 us (25%)
  local copies, waits for them, and re-layouts  46.3 us (13%)
  waiting for transfers between devices  44.4 us (13%)
  Pallas kernels  39.8 us (12%)
  between operations  8.79 us (3%)
  blocking collectives  6.84 us (2%)
    ppermute x16, starting transfers between devices, halo_pair(): lax.ppermute(lax.slice_in_dim(block, size - 1, None, axis=dim), axis, for...  54.9 us
    all_to_all x2, waiting for transfers between devices, windows(): received = lax.all_to_all(jnp.stack(parts), 'col', 0, 0, tiled=True)  44.3 us
    another operation x6, other arithmetic, run_segments(): return jnp.stack(factors)  41.9 us
    ppermute x16, starting transfers between devices, halo_pair(): high = lax.ppermute(lax.slice_in_dim(block, 0, 1, axis=dim), axis, backward)  37.7 us
    add x4, other arithmetic, solve_slabs(): rho_next * rho_now * direction + 2.0 * rho_next / half_span * residual  31.1 us
    pallas_call x1, Pallas kernels, scatter_sum(): pl.pallas_call(scatter_sum_kernel, out_shape=jax.ShapeDtypeStruct((1, row...  26.6 us
    slice x14, local copies, waits for them, and re-layouts, shifted(): lax.slice_in_dim(block, 1, None, axis=dim)  24.9 us
    pallas_call x1, Pallas kernels, gram(): pl.pallas_call(gram_kernel, grid=(depth, rows // rows_per_step), in_specs...  13.2 us
  transfers between devices with their start and end apart: 36, of which 2 were waited for; matrix products, arithmetic and copies ran while one was open for 32% of the time, Pallas kernels for 0%

profile of v2, /device:TPU:1, one launch (start us, length us, event | category | flops | bytes accessed | tf_op | source)
XLA Modules:
  0.0 343.8 jit_solution(12567480714537430637)
XLA Ops:
  4.7 4.8 %all-to-all-start = ((f32[4,16,2,48,128]{4,3,2,1,0:T(8,128)}), f32[4,16,2,48,128]{4,3,2,1,0:T(8,128)S(1)}, u32[]{:S(2)}, u32[]{:S(2)}) async-start(f32[4,16,2,48,128]{4,3,2,1,0:T(8,128)} %pad_maximum_fusion.2), calls=%async_computation | async-start | bytes 6291456 | tf_op jit(solution)/shard_map/all_to_all | solution.py:162
  13.5 32.6 %all-to-all-done = f32[4,16,2,48,128]{4,3,2,1,0:T(8,128)S(1)} async-done(((f32[4,16,2,48,128]{4,3,2,1,0:T(8,128)}), f32[4,16,2,48,128]{4,3,2,1,0:T(8,128)S(1)}, u32[]{:S(2)}, u32[]{:S(2)}) %all-to-all-start) | async-done | bytes 3145760 | tf_op jit(solution)/shard_map/all_to_all | solution.py:162
  46.2 4.7 %all-to-all-start.1 = ((f32[4,16,2,48,128]{4,3,2,1,0:T(8,128)}), f32[4,16,2,48,128]{4,3,2,1,0:T(8,128)}, u32[]{:S(2)}, u32[]{:S(2)}) async-start(f32[4,16,2,48,128]{4,3,2,1,0:T(8,128)} %pad_maximum_fusion.3), calls=%async_computation.1 | async-start | bytes 6291456 | tf_op jit(solution)/shard_map/all_to_all | solution.py:162
  51.5 5.2 %select_add_fusion = f32[2,192,128]{2,1,0:T(8,128)S(1)} fusion(s32[2,192,128]{2,1,0:T(8,128)S(1)} %copy-done.13, f32[]{:T(128)} %bitcast.13, f32[]{:T(128)} %bitcast.12, f32[]{:T(128)} %bitcast.11, f32[]{:T(128)} %bitcast.10, f32[]{:T(128)} %bitcast.9, f32[]{:T(128)} %bitcast.8, f32[]{:T(128)} %bitcast.7, f32[]{:T(128)} %bitcast.6), kind=kLoop, calls=%fused_computation.210 | loop fusion | flops 1130496 | bytes 393248 | tf_op jit(solution)/shard_map/add | solution.py:127
  56.8 3.8 %collective-permute-start = (f32[1,50,128]{2,1,0:T(8,128)S(1)}, f32[1,50,128]{2,1,0:T(8,128)S(1)}, u32[]{:S(2)}, u32[]{:S(2)}) collective-permute-start(f32[1,50,128]{2,1,0:T(8,128)S(1)} %get-tuple-element.76), channel_id=1, source_target_pairs={{4,0},{8,4},{12,8},{16,12},{20,16},{24,20},{28,24},{32,28},{36,32}... | collective-permute-start | bytes 76808 | tf_op jit(solution)/shard_map/ppermute | solution.py:22
  74.9 11.7 %all-to-all-done.1 = f32[4,16,2,48,128]{4,3,2,1,0:T(8,128)} async-done(((f32[4,16,2,48,128]{4,3,2,1,0:T(8,128)}), f32[4,16,2,48,128]{4,3,2,1,0:T(8,128)}, u32[]{:S(2)}, u32[]{:S(2)}) %all-to-all-start.1) | async-done | bytes 3145760 | tf_op jit(solution)/shard_map/all_to_all | solution.py:162
  89.6 4.7 %collective-permute-start.18 = (f32[64,1,48,128]{3,2,1,0:T(8,128)S(1)}, f32[64,1,48,128]{3,2,1,0:T(8,128)S(1)}, u32[]{:S(2)}, u32[]{:S(2)}) collective-permute-start(f32[64,1,48,128]{3,2,1,0:T(8,128)S(1)} %get-tuple-element.36), channel_id=1, source_target_pairs={{4,0},{8,4},{12,8},{16,12},{20,16},{24,20},{28,24},{32,28},{36,32}... | collective-permute-start | bytes 4718600 | tf_op jit(solution)/shard_map/ppermute | solution.py:137
  99.2 4.0 %collective-permute-start.21 = (f32[64,2,1,128]{3,2,1,0:T(1,128)S(1)}, f32[64,2,1,128]{3,2,1,0:T(1,128)S(1)}, u32[]{:S(2)}, u32[]{:S(2)}) collective-permute-start(f32[64,2,1,128]{3,2,1,0:T(1,128)S(1)} %get-tuple-element.40), channel_id=1, source_target_pairs={{0,1},{1,2},{2,3},{4,5},{5,6},{6,7},{8,9},{9,10},{10,11},{12,13},{... | collective-permute-start | bytes 196616 | tf_op jit(solution)/shard_map/ppermute | solution.py:136
  110.2 3.6 %collective-permute-start.3 = (f32[64,1,48,128]{3,2,1,0:T(8,128)S(1)}, f32[64,1,48,128]{3,2,1,0:T(8,128)}, u32[]{:S(2)}, u32[]{:S(2)}) collective-permute-start(f32[64,1,48,128]{3,2,1,0:T(8,128)S(1)} %get-tuple-element.63), channel_id=1, source_target_pairs={{0,4},{4,8},{8,12},{12,16},{16,20},{20,24},{24,28},{28,32},{32,36}... | collective-permute-start | bytes 4718600 | tf_op jit(solution)/shard_map/ppermute | solution.py:136
  115.8 4.0 %collective-permute-start.5 = (f32[64,2,1,128]{3,2,1,0:T(1,128)}, f32[64,2,1,128]{3,2,1,0:T(1,128)S(1)}, u32[]{:S(2)}, u32[]{:S(2)}) collective-permute-start(f32[64,2,1,128]{3,2,1,0:T(1,128)} %get-tuple-element.68), channel_id=1, source_target_pairs={{0,1},{1,2},{2,3},{4,5},{5,6},{6,7},{8,9},{9,10},{10,11},{12,13},{... | collective-permute-start | bytes 196616 | tf_op jit(solution)/shard_map/ppermute | solution.py:136
  120.9 8.0 %multiply_add_fusion.1 = (f32[64,2,48,128]{3,2,1,0:T(8,128)S(1)}, f32[64,2,48,128]{3,2,1,0:T(8,128)}) fusion(f32[64,2,48,128]{3,2,1,0:T(8,128)S(1)} %get-tuple-element.92, f32[]{:T(128)S(6)} %div.73, f32[]{:T(128)S(6)} %mul.258, f32[]{:T(128)} %bitcast, f32[2,48,128]{2,1,0:T(8,128)S(1)} %get-tuple-element.78, f32[2,48,128]{2,1,0:T(8,128)S(1)} %copy-done.9, ...), kind=kLoop, calls=%fused_computation.196 | loop fusion | flops 21233664 | bytes 25460748 | tf_op jit(solution)/shard_map/add | solution.py:200
  138.5 4.6 %collective-permute-start.25 = (f32[64,2,1,128]{3,2,1,0:T(1,128)}, f32[64,2,1,128]{3,2,1,0:T(1,128)}, u32[]{:S(2)}, u32[]{:S(2)}) collective-permute-start(f32[64,2,1,128]{3,2,1,0:T(1,128)} %get-tuple-element.34), channel_id=1, source_target_pairs={{0,1},{1,2},{2,3},{4,5},{5,6},{6,7},{8,9},{9,10},{10,11},{12,13},{... | collective-permute-start | bytes 196616 | tf_op jit(solution)/shard_map/ppermute | solution.py:136
  143.1 7.5 %multiply_add_fusion.3 = (f32[64,2,48,128]{3,2,1,0:T(8,128)S(1)}, f32[64,2,48,128]{3,2,1,0:T(8,128)}) fusion(f32[64,2,48,128]{3,2,1,0:T(8,128)S(1)} %get-tuple-element.93, f32[]{:T(128)S(6)} %div.73, f32[]{:T(128)S(6)} %mul.258, f32[]{:T(128)} %bitcast, f32[2,48,128]{2,1,0:T(8,128)S(1)} %get-tuple-element.78, f32[2,48,128]{2,1,0:T(8,128)S(1)} %copy-done.9, ...), kind=kLoop, calls=%fused_computation.199 | loop fusion | flops 21233664 | bytes 25460748 | tf_op jit(solution)/shard_map/add | solution.py:200
  152.0 3.5 %fusion.165 = (f32[64,2,47,128]{3,2,1,0:T(8,128)}, f32[64,2,47,128]{3,2,1,0:T(8,128)}) fusion(f32[64,2,48,128]{3,2,1,0:T(8,128)S(1)} %get-tuple-element.7), kind=kLoop, calls=%fused_computation.242 | loop fusion | bytes 12320768 | tf_op jit(solution)/shard_map/slice | solution.py:143
  165.5 4.2 %collective-permute-start.9 = (f32[64,2,1,128]{3,2,1,0:T(1,128)}, f32[64,2,1,128]{3,2,1,0:T(1,128)S(1)}, u32[]{:S(2)}, u32[]{:S(2)}) collective-permute-start(f32[64,2,1,128]{3,2,1,0:T(1,128)} %get-tuple-element.62), channel_id=1, source_target_pairs={{0,1},{1,2},{2,3},{4,5},{5,6},{6,7},{8,9},{9,10},{10,11},{12,13},{... | collective-permute-start | bytes 196616 | tf_op jit(solution)/shard_map/ppermute | solution.py:136
  169.7 9.1 %multiply_bitcast_fusion = (f32[1,64,2,48,128]{4,3,2,1,0:T(8,128)}, f32[64,2,48,128]{3,2,1,0:T(8,128)S(1)}) fusion(f32[]{:T(128)S(6)} %sqrt.8, f32[64,2,48,128]{3,2,1,0:T(8,128)} %get-tuple-element.8, f32[64,2,48,128]{3,2,1,0:T(8,128)S(1)} %get-tuple-element.7, f32[]{:T(128)} %bitcast, f32[2,48,128]{2,1,0:T(8,128)S(1)} %get-tuple-element.78, ...), kind=kLoop, calls=%fused_computation.195 | loop fusion | flops 23592960 | bytes 28606480 | tf_op jit(solution)/shard_map/stack | solution.py:215
  188.7 4.0 %collective-permute-start.29 = (f32[64,2,1,128]{3,2,1,0:T(1,128)}, f32[64,2,1,128]{3,2,1,0:T(1,128)S(1)}, u32[]{:S(2)}, u32[]{:S(2)}) collective-permute-start(f32[64,2,1,128]{3,2,1,0:T(1,128)} %get-tuple-element.28), channel_id=1, source_target_pairs={{0,1},{1,2},{2,3},{4,5},{5,6},{6,7},{8,9},{9,10},{10,11},{12,13},{... | collective-permute-start | bytes 196616 | tf_op jit(solution)/shard_map/ppermute | solution.py:136
  192.7 8.3 %multiply_bitcast_fusion.1 = (f32[1,64,2,48,128]{4,3,2,1,0:T(8,128)}, f32[64,2,48,128]{3,2,1,0:T(8,128)S(1)}) fusion(f32[]{:T(128)S(6)} %sqrt.8, f32[64,2,48,128]{3,2,1,0:T(8,128)} %get-tuple-element.14, f32[64,2,48,128]{3,2,1,0:T(8,128)S(1)} %get-tuple-element.13, f32[]{:T(128)} %bitcast, f32[2,48,128]{2,1,0:T(8,128)S(1)} %get-tuple-element.78, ...), kind=kLoop, calls=%fused_computation.198 | loop fusion | flops 23592960 | bytes 28606480 | tf_op jit(solution)/shard_map/stack | solution.py:215
  208.0 3.9 %collective-permute-start.10 = (f32[64,1,48,128]{3,2,1,0:T(8,128)}, f32[64,1,48,128]{3,2,1,0:T(8,128)}, u32[]{:S(2)}, u32[]{:S(2)}) collective-permute-start(f32[64,1,48,128]{3,2,1,0:T(8,128)} %get-tuple-element.52), channel_id=1, source_target_pairs={{4,0},{8,4},{12,8},{16,12},{20,16},{24,20},{28,24},{32,28},{36,32}... | collective-permute-start | bytes 4718600 | tf_op jit(solution)/shard_map/ppermute | solution.py:137
  215.1 4.6 %collective-permute-start.13 = (f32[64,2,1,128]{3,2,1,0:T(1,128)}, f32[64,2,1,128]{3,2,1,0:T(1,128)}, u32[]{:S(2)}, u32[]{:S(2)}) collective-permute-start(f32[64,2,1,128]{3,2,1,0:T(1,128)} %get-tuple-element.56), channel_id=1, source_target_pairs={{0,1},{1,2},{2,3},{4,5},{5,6},{6,7},{8,9},{9,10},{10,11},{12,13},{... | collective-permute-start | bytes 196616 | tf_op jit(solution)/shard_map/ppermute | solution.py:136
  219.8 7.7 %multiply_add_fusion = (f32[64,2,48,128]{3,2,1,0:T(8,128)S(1)}, f32[64,2,48,128]{3,2,1,0:T(8,128)}) fusion(f32[]{:T(128)S(6)} %div.81, f32[]{:T(128)S(6)} %mul.607, f32[64,2,48,128]{3,2,1,0:T(8,128)S(1)} %get-tuple-element.4, f32[]{:T(128)S(6)} %mul.604, f32[64,2,48,128]{3,2,1,0:T(8,128)S(1)} %broadcast_divide_fusion, f32[]{:T(128)} %bitcast.15, ...), kind=kLoop, calls=%fused_computation.194 | loop fusion | flops 22020096 | bytes 25460752 | tf_op jit(solution)/shard_map/add | solution.py:200
  230.1 4.1 %collective-permute-start.30 = (f32[64,1,48,128]{3,2,1,0:T(8,128)}, f32[64,1,48,128]{3,2,1,0:T(8,128)}, u32[]{:S(2)}, u32[]{:S(2)}) collective-permute-start(f32[64,1,48,128]{3,2,1,0:T(8,128)} %get-tuple-element.22), channel_id=1, source_target_pairs={{4,0},{8,4},{12,8},{16,12},{20,16},{24,20},{28,24},{32,28},{36,32}... | collective-permute-start | bytes 4718600 | tf_op jit(solution)/shard_map/ppermute | solution.py:137
  237.5 4.2 %collective-permute-start.33 = (f32[64,2,1,128]{3,2,1,0:T(1,128)}, f32[64,2,1,128]{3,2,1,0:T(1,128)S(1)}, u32[]{:S(2)}, u32[]{:S(2)}) collective-permute-start(f32[64,2,1,128]{3,2,1,0:T(1,128)} %get-tuple-element.17), channel_id=1, source_target_pairs={{0,1},{1,2},{2,3},{4,5},{5,6},{6,7},{8,9},{9,10},{10,11},{12,13},{... | collective-permute-start | bytes 196616 | tf_op jit(solution)/shard_map/ppermute | solution.py:136
  241.7 7.8 %multiply_add_fusion.2 = (f32[64,2,48,128]{3,2,1,0:T(8,128)S(1)}, f32[64,2,48,128]{3,2,1,0:T(8,128)}) fusion(f32[]{:T(128)S(6)} %div.81, f32[]{:T(128)S(6)} %mul.607, f32[64,2,48,128]{3,2,1,0:T(8,128)S(1)} %get-tuple-element.10, f32[]{:T(128)S(6)} %mul.604, f32[64,2,48,128]{3,2,1,0:T(8,128)S(1)} %broadcast_divide_fusion.1, f32[]{:T(128)} %bitcast.15, ...), kind=kLoop, calls=%fused_computation.197 | loop fusion | flops 22020096 | bytes 25460752 | tf_op jit(solution)/shard_map/add | solution.py:200
  257.5 4.1 %collective-permute-start.14 = (f32[64,1,48,128]{3,2,1,0:T(8,128)}, f32[64,1,48,128]{3,2,1,0:T(8,128)}, u32[]{:S(2)}, u32[]{:S(2)}) collective-permute-start(f32[64,1,48,128]{3,2,1,0:T(8,128)} %get-tuple-element.50), channel_id=1, source_target_pairs={{4,0},{8,4},{12,8},{16,12},{20,16},{24,20},{28,24},{32,28},{36,32}... | collective-permute-start | bytes 4718600 | tf_op jit(solution)/shard_map/ppermute | solution.py:137
  264.9 4.6 %collective-permute-start.17 = (f32[64,2,1,128]{3,2,1,0:T(1,128)}, f32[64,2,1,128]{3,2,1,0:T(1,128)}, u32[]{:S(2)}, u32[]{:S(2)}) collective-permute-start(f32[64,2,1,128]{3,2,1,0:T(1,128)} %get-tuple-element.45), channel_id=1, source_target_pairs={{0,1},{1,2},{2,3},{4,5},{5,6},{6,7},{8,9},{9,10},{10,11},{12,13},{... | collective-permute-start | bytes 196616 | tf_op jit(solution)/shard_map/ppermute | solution.py:136
  269.5 8.8 %fusion.81 = f32[1,64,2,48,128]{4,3,2,1,0:T(8,128)} fusion(f32[64,2,48,128]{3,2,1,0:T(8,128)S(1)} %get-tuple-element.4, f32[64,2,48,128]{3,2,1,0:T(8,128)S(1)} %copy-done.1, f32[64,2,48,128]{3,2,1,0:T(8,128)S(1)} %get-tuple-element.5, f32[64,1,48,128]{3,2,1,0:T(8,128)} %collective-permute-done.30, f32[64,1,48,128]{3,2,1,0:T(8,128)} %get-tuple-element.21, ...), kind=kLoop, calls=%fused_computation.99 | loop fusion | flops 25952256 | bytes 25460760 | tf_op jit(solution)/shard_map/stack | solution.py:215
  278.4 5.3 %pad_maximum_fusion.1 = f32[2,64,2,48,128]{4,3,2,1,0:T(8,128)} fusion(f32[1,64,2,48,128]{4,3,2,1,0:T(8,128)} %fusion.81, f32[1,64,2,48,128]{4,3,2,1,0:T(8,128)S(1)} %copy-done.3), kind=kLoop, calls=%fused_computation.17 | loop fusion | flops 1572864 | bytes 12582912 | tf_op jit(solution)/shard_map/stack | solution.py:215
  283.7 7.3 %fusion.39 = f32[1,64,2,48,128]{4,3,2,1,0:T(8,128)S(1)} fusion(f32[64,2,48,128]{3,2,1,0:T(8,128)S(1)} %get-tuple-element.10, f32[64,2,48,128]{3,2,1,0:T(8,128)S(1)} %copy-done.2, f32[64,2,48,128]{3,2,1,0:T(8,128)S(1)} %get-tuple-element.11, f32[64,1,48,128]{3,2,1,0:T(8,128)} %collective-permute-done.14, f32[64,1,48,128]{3,2,1,0:T(8,128)S(1)} %get-tuple-element.49, ...), kind=kLoop, calls=%fused_computation.57 | loop fusion | flops 25952256 | bytes 25460760 | tf_op jit(solution)/shard_map/stack | solution.py:215
  294.1 13.2 %shard_map.76 = f32[128,128]{1,0:T(8,128)} custom-call(f32[128,2,48,128]{3,2,1,0:T(8,128)} %bitcast.49, f32[128,2,48,128]{3,2,1,0:T(8,128)} %bitcast.48), custom_call_target="tpu_custom_call" | custom-call | flops 402653184 | bytes 12582912 | tf_op jit(solution)/shard_map/pallas_call | solution.py:112
  308.3 6.8 %all_to_all.15 = f32[4,128,32]{1,2,0:T(8,128)S(1)} all-to-all(f32[4,128,32]{1,2,0:T(8,128)S(1)} %bitcast.50), channel_id=1, replica_groups=mesh['slab'=32,'col'=4] {'col'}, dimensions={0} | all-to-all | bytes 131072 | tf_op jit(solution)/shard_map/all_to_all | solution.py:248
  315.9 26.6 %shard_map.77 = f32[1,1,128]{2,1,0:T(1,128)} custom-call(f32[32,1,128]{2,1,0:T(1,128)} %bitcast.51), custom_call_target="tpu_custom_call" | custom-call | tf_op jit(solution)/shard_map/pallas_call | solution.py:78
  (137 shorter events, 97.6 us)
Async XLA Ops:
  4.7 41.5 %all-to-all-start = ((f32[4,16,2,48,128]{4,3,2,1,0:T(8,128)}), f32[4,16,2,48,128]{4,3,2,1,0:T(8,128)S(1)}, u32[]{:S(2)}, u32[]{:S(2)}) async-start(f32[4,16,2,48,128]{4,3,2,1,0:T(8,128)} %pad_maximum_fusion.2), calls=%async_computation | async-start | bytes 6291456 | tf_op jit(solution)/shard_map/all_to_all | solution.py:162
  46.2 40.5 %all-to-all-start.1 = ((f32[4,16,2,48,128]{4,3,2,1,0:T(8,128)}), f32[4,16,2,48,128]{4,3,2,1,0:T(8,128)}, u32[]{:S(2)}, u32[]{:S(2)}) async-start(f32[4,16,2,48,128]{4,3,2,1,0:T(8,128)} %pad_maximum_fusion.3), calls=%async_computation.1 | async-start | bytes 6291456 | tf_op jit(solution)/shard_map/all_to_all | solution.py:162
  89.6 26.2 %collective-permute-start.18 = (f32[64,1,48,128]{3,2,1,0:T(8,128)S(1)}, f32[64,1,48,128]{3,2,1,0:T(8,128)S(1)}, u32[]{:S(2)}, u32[]{:S(2)}) collective-permute-start(f32[64,1,48,128]{3,2,1,0:T(8,128)S(1)} %get-tuple-element.36), channel_id=1, source_target_pairs={{4,0},{8,4},{12,8},{16,12},{20,16},{24,20},{28,24},{32,28},{36,32}... | collective-permute-start | bytes 4718600 | tf_op jit(solution)/shard_map/ppermute | solution.py:137
  94.3 25.5 %collective-permute-start.19 = (f32[64,1,48,128]{3,2,1,0:T(8,128)S(1)}, f32[64,1,48,128]{3,2,1,0:T(8,128)S(1)}, u32[]{:S(2)}, u32[]{:S(2)}) collective-permute-start(f32[64,1,48,128]{3,2,1,0:T(8,128)S(1)} %get-tuple-element.35), channel_id=1, source_target_pairs={{0,4},{4,8},{8,12},{12,16},{16,20},{20,24},{24,28},{28,32},{32,36}... | collective-permute-start | bytes 4718600 | tf_op jit(solution)/shard_map/ppermute | solution.py:136
  108.2 30.3 %collective-permute-start.1 = (f32[64,1,48,128]{3,2,1,0:T(8,128)}, f32[64,1,48,128]{3,2,1,0:T(8,128)}, u32[]{:S(2)}, u32[]{:S(2)}) collective-permute-start(f32[64,1,48,128]{3,2,1,0:T(8,128)} %get-tuple-element.64), channel_id=1, source_target_pairs={{4,0},{8,4},{12,8},{16,12},{20,16},{24,20},{28,24},{32,28},{36,32}... | collective-permute-start | bytes 4718600 | tf_op jit(solution)/shard_map/ppermute | solution.py:137
  110.2 33.0 %collective-permute-start.3 = (f32[64,1,48,128]{3,2,1,0:T(8,128)S(1)}, f32[64,1,48,128]{3,2,1,0:T(8,128)}, u32[]{:S(2)}, u32[]{:S(2)}) collective-permute-start(f32[64,1,48,128]{3,2,1,0:T(8,128)S(1)} %get-tuple-element.63), channel_id=1, source_target_pairs={{0,4},{4,8},{8,12},{12,16},{16,20},{20,24},{24,28},{28,32},{32,36}... | collective-permute-start | bytes 4718600 | tf_op jit(solution)/shard_map/ppermute | solution.py:136
  114.5 19.6 %collective-permute-start.4 = (f32[64,2,1,128]{3,2,1,0:T(1,128)}, f32[64,2,1,128]{3,2,1,0:T(1,128)S(1)}, u32[]{:S(2)}, u32[]{:S(2)}) collective-permute-start(f32[64,2,1,128]{3,2,1,0:T(1,128)} %get-tuple-element.67), channel_id=1, source_target_pairs={{1,0},{2,1},{3,2},{5,4},{6,5},{7,6},{9,8},{10,9},{11,10},{13,12},{... | collective-permute-start | bytes 196616 | tf_op jit(solution)/shard_map/ppermute | solution.py:137
  115.8 21.4 %collective-permute-start.5 = (f32[64,2,1,128]{3,2,1,0:T(1,128)}, f32[64,2,1,128]{3,2,1,0:T(1,128)S(1)}, u32[]{:S(2)}, u32[]{:S(2)}) collective-permute-start(f32[64,2,1,128]{3,2,1,0:T(1,128)} %get-tuple-element.68), channel_id=1, source_target_pairs={{0,1},{1,2},{2,3},{4,5},{5,6},{6,7},{8,9},{9,10},{10,11},{12,13},{... | collective-permute-start | bytes 196616 | tf_op jit(solution)/shard_map/ppermute | solution.py:136
  131.6 33.9 %collective-permute-start.22 = (f32[64,1,48,128]{3,2,1,0:T(8,128)}, f32[64,1,48,128]{3,2,1,0:T(8,128)}, u32[]{:S(2)}, u32[]{:S(2)}) collective-permute-start(f32[64,1,48,128]{3,2,1,0:T(8,128)} %get-tuple-element.30), channel_id=1, source_target_pairs={{4,0},{8,4},{12,8},{16,12},{20,16},{24,20},{28,24},{32,28},{36,32}... | collective-permute-start | bytes 4718600 | tf_op jit(solution)/shard_map/ppermute | solution.py:137
  134.1 35.6 %collective-permute-start.23 = (f32[64,1,48,128]{3,2,1,0:T(8,128)}, f32[64,1,48,128]{3,2,1,0:T(8,128)}, u32[]{:S(2)}, u32[]{:S(2)}) collective-permute-start(f32[64,1,48,128]{3,2,1,0:T(8,128)} %get-tuple-element.29), channel_id=1, source_target_pairs={{0,4},{4,8},{8,12},{12,16},{16,20},{20,24},{24,28},{28,32},{32,36}... | collective-permute-start | bytes 4718600 | tf_op jit(solution)/shard_map/ppermute | solution.py:136
  137.2 24.3 %collective-permute-start.24 = (f32[64,2,1,128]{3,2,1,0:T(1,128)}, f32[64,2,1,128]{3,2,1,0:T(1,128)S(1)}, u32[]{:S(2)}, u32[]{:S(2)}) collective-permute-start(f32[64,2,1,128]{3,2,1,0:T(1,128)} %get-tuple-element.33), channel_id=1, source_target_pairs={{1,0},{2,1},{3,2},{5,4},{6,5},{7,6},{9,8},{10,9},{11,10},{13,12},{... | collective-permute-start | bytes 196616 | tf_op jit(solution)/shard_map/ppermute | solution.py:137
  138.5 25.6 %collective-permute-start.25 = (f32[64,2,1,128]{3,2,1,0:T(1,128)}, f32[64,2,1,128]{3,2,1,0:T(1,128)}, u32[]{:S(2)}, u32[]{:S(2)}) collective-permute-start(f32[64,2,1,128]{3,2,1,0:T(1,128)} %get-tuple-element.34), channel_id=1, source_target_pairs={{0,1},{1,2},{2,3},{4,5},{5,6},{6,7},{8,9},{9,10},{10,11},{12,13},{... | collective-permute-start | bytes 196616 | tf_op jit(solution)/shard_map/ppermute | solution.py:136
  158.6 30.1 %collective-permute-start.6 = (f32[64,1,48,128]{3,2,1,0:T(8,128)}, f32[64,1,48,128]{3,2,1,0:T(8,128)}, u32[]{:S(2)}, u32[]{:S(2)}) collective-permute-start(f32[64,1,48,128]{3,2,1,0:T(8,128)} %get-tuple-element.58), channel_id=1, source_target_pairs={{4,0},{8,4},{12,8},{16,12},{20,16},{24,20},{28,24},{32,28},{36,32}... | collective-permute-start | bytes 4718600 | tf_op jit(solution)/shard_map/ppermute | solution.py:137
  161.5 31.2 %collective-permute-start.7 = (f32[64,1,48,128]{3,2,1,0:T(8,128)S(1)}, f32[64,1,48,128]{3,2,1,0:T(8,128)}, u32[]{:S(2)}, u32[]{:S(2)}) collective-permute-start(f32[64,1,48,128]{3,2,1,0:T(8,128)S(1)} %get-tuple-element.57), channel_id=1, source_target_pairs={{0,4},{4,8},{8,12},{12,16},{16,20},{20,24},{24,28},{28,32},{32,36}... | collective-permute-start | bytes 4718600 | tf_op jit(solution)/shard_map/ppermute | solution.py:136
  164.2 21.0 %collective-permute-start.8 = (f32[64,2,1,128]{3,2,1,0:T(1,128)}, f32[64,2,1,128]{3,2,1,0:T(1,128)S(1)}, u32[]{:S(2)}, u32[]{:S(2)}) collective-permute-start(f32[64,2,1,128]{3,2,1,0:T(1,128)} %get-tuple-element.61), channel_id=1, source_target_pairs={{1,0},{2,1},{3,2},{5,4},{6,5},{7,6},{9,8},{10,9},{11,10},{13,12},{... | collective-permute-start | bytes 196616 | tf_op jit(solution)/shard_map/ppermute | solution.py:137
  165.5 21.9 %collective-permute-start.9 = (f32[64,2,1,128]{3,2,1,0:T(1,128)}, f32[64,2,1,128]{3,2,1,0:T(1,128)S(1)}, u32[]{:S(2)}, u32[]{:S(2)}) collective-permute-start(f32[64,2,1,128]{3,2,1,0:T(1,128)} %get-tuple-element.62), channel_id=1, source_target_pairs={{0,1},{1,2},{2,3},{4,5},{5,6},{6,7},{8,9},{9,10},{10,11},{12,13},{... | collective-permute-start | bytes 196616 | tf_op jit(solution)/shard_map/ppermute | solution.py:136
  181.8 33.3 %collective-permute-start.26 = (f32[64,1,48,128]{3,2,1,0:T(8,128)}, f32[64,1,48,128]{3,2,1,0:T(8,128)}, u32[]{:S(2)}, u32[]{:S(2)}) collective-permute-start(f32[64,1,48,128]{3,2,1,0:T(8,128)} %get-tuple-element.24), channel_id=1, source_target_pairs={{4,0},{8,4},{12,8},{16,12},{20,16},{24,20},{28,24},{32,28},{36,32}... | collective-permute-start | bytes 4718600 | tf_op jit(solution)/shard_map/ppermute | solution.py:137
  185.2 34.5 %collective-permute-start.27 = (f32[64,1,48,128]{3,2,1,0:T(8,128)}, f32[64,1,48,128]{3,2,1,0:T(8,128)}, u32[]{:S(2)}, u32[]{:S(2)}) collective-permute-start(f32[64,1,48,128]{3,2,1,0:T(8,128)} %get-tuple-element.23), channel_id=1, source_target_pairs={{0,4},{4,8},{8,12},{12,16},{16,20},{20,24},{24,28},{28,32},{32,36}... | collective-permute-start | bytes 4718600 | tf_op jit(solution)/shard_map/ppermute | solution.py:136
  187.4 24.5 %collective-permute-start.28 = (f32[64,2,1,128]{3,2,1,0:T(1,128)}, f32[64,2,1,128]{3,2,1,0:T(1,128)S(1)}, u32[]{:S(2)}, u32[]{:S(2)}) collective-permute-start(f32[64,2,1,128]{3,2,1,0:T(1,128)} %get-tuple-element.27), channel_id=1, source_target_pairs={{1,0},{2,1},{3,2},{5,4},{6,5},{7,6},{9,8},{10,9},{11,10},{13,12},{... | collective-permute-start | bytes 196616 | tf_op jit(solution)/shard_map/ppermute | solution.py:137
  188.7 25.1 %collective-permute-start.29 = (f32[64,2,1,128]{3,2,1,0:T(1,128)}, f32[64,2,1,128]{3,2,1,0:T(1,128)S(1)}, u32[]{:S(2)}, u32[]{:S(2)}) collective-permute-start(f32[64,2,1,128]{3,2,1,0:T(1,128)} %get-tuple-element.28), channel_id=1, source_target_pairs={{0,1},{1,2},{2,3},{4,5},{5,6},{6,7},{8,9},{9,10},{10,11},{12,13},{... | collective-permute-start | bytes 196616 | tf_op jit(solution)/shard_map/ppermute | solution.py:136
  208.0 29.5 %collective-permute-start.10 = (f32[64,1,48,128]{3,2,1,0:T(8,128)}, f32[64,1,48,128]{3,2,1,0:T(8,128)}, u32[]{:S(2)}, u32[]{:S(2)}) collective-permute-start(f32[64,1,48,128]{3,2,1,0:T(8,128)} %get-tuple-element.52), channel_id=1, source_target_pairs={{4,0},{8,4},{12,8},{16,12},{20,16},{24,20},{28,24},{32,28},{36,32}... | collective-permute-start | bytes 4718600 | tf_op jit(solution)/shard_map/ppermute | solution.py:137
  211.9 29.8 %collective-permute-start.11 = (f32[64,1,48,128]{3,2,1,0:T(8,128)S(1)}, f32[64,1,48,128]{3,2,1,0:T(8,128)}, u32[]{:S(2)}, u32[]{:S(2)}) collective-permute-start(f32[64,1,48,128]{3,2,1,0:T(8,128)S(1)} %get-tuple-element.51), channel_id=1, source_target_pairs={{0,4},{4,8},{8,12},{12,16},{16,20},{20,24},{24,28},{28,32},{32,36}... | collective-permute-start | bytes 4718600 | tf_op jit(solution)/shard_map/ppermute | solution.py:136
  213.8 20.4 %collective-permute-start.12 = (f32[64,2,1,128]{3,2,1,0:T(1,128)}, f32[64,2,1,128]{3,2,1,0:T(1,128)S(1)}, u32[]{:S(2)}, u32[]{:S(2)}) collective-permute-start(f32[64,2,1,128]{3,2,1,0:T(1,128)} %get-tuple-element.55), channel_id=1, source_target_pairs={{1,0},{2,1},{3,2},{5,4},{6,5},{7,6},{9,8},{10,9},{11,10},{13,12},{... | collective-permute-start | bytes 196616 | tf_op jit(solution)/shard_map/ppermute | solution.py:137
  215.1 21.0 %collective-permute-start.13 = (f32[64,2,1,128]{3,2,1,0:T(1,128)}, f32[64,2,1,128]{3,2,1,0:T(1,128)}, u32[]{:S(2)}, u32[]{:S(2)}) collective-permute-start(f32[64,2,1,128]{3,2,1,0:T(1,128)} %get-tuple-element.56), channel_id=1, source_target_pairs={{0,1},{1,2},{2,3},{4,5},{5,6},{6,7},{8,9},{9,10},{10,11},{12,13},{... | collective-permute-start | bytes 196616 | tf_op jit(solution)/shard_map/ppermute | solution.py:136
  230.1 34.8 %collective-permute-start.30 = (f32[64,1,48,128]{3,2,1,0:T(8,128)}, f32[64,1,48,128]{3,2,1,0:T(8,128)}, u32[]{:S(2)}, u32[]{:S(2)}) collective-permute-start(f32[64,1,48,128]{3,2,1,0:T(8,128)} %get-tuple-element.22), channel_id=1, source_target_pairs={{4,0},{8,4},{12,8},{16,12},{20,16},{24,20},{28,24},{32,28},{36,32}... | collective-permute-start | bytes 4718600 | tf_op jit(solution)/shard_map/ppermute | solution.py:137
  234.2 35.3 %collective-permute-start.31 = (f32[64,1,48,128]{3,2,1,0:T(8,128)}, f32[64,1,48,128]{3,2,1,0:T(8,128)}, u32[]{:S(2)}, u32[]{:S(2)}) collective-permute-start(f32[64,1,48,128]{3,2,1,0:T(8,128)} %get-tuple-element.21), channel_id=1, source_target_pairs={{0,4},{4,8},{8,12},{12,16},{16,20},{20,24},{24,28},{28,32},{32,36}... | collective-permute-start | bytes 4718600 | tf_op jit(solution)/shard_map/ppermute | solution.py:136
  236.2 25.5 %collective-permute-start.32 = (f32[64,2,1,128]{3,2,1,0:T(1,128)}, f32[64,2,1,128]{3,2,1,0:T(1,128)S(1)}, u32[]{:S(2)}, u32[]{:S(2)}) collective-permute-start(f32[64,2,1,128]{3,2,1,0:T(1,128)} %get-tuple-element.18), channel_id=1, source_target_pairs={{1,0},{2,1},{3,2},{5,4},{6,5},{7,6},{9,8},{10,9},{11,10},{13,12},{... | collective-permute-start | bytes 196616 | tf_op jit(solution)/shard_map/ppermute | solution.py:137
  237.5 26.1 %collective-permute-start.33 = (f32[64,2,1,128]{3,2,1,0:T(1,128)}, f32[64,2,1,128]{3,2,1,0:T(1,128)S(1)}, u32[]{:S(2)}, u32[]{:S(2)}) collective-permute-start(f32[64,2,1,128]{3,2,1,0:T(1,128)} %get-tuple-element.17), channel_id=1, source_target_pairs={{0,1},{1,2},{2,3},{4,5},{5,6},{6,7},{8,9},{9,10},{10,11},{12,13},{... | collective-permute-start | bytes 196616 | tf_op jit(solution)/shard_map/ppermute | solution.py:136
  257.5 26.1 %collective-permute-start.14 = (f32[64,1,48,128]{3,2,1,0:T(8,128)}, f32[64,1,48,128]{3,2,1,0:T(8,128)}, u32[]{:S(2)}, u32[]{:S(2)}) collective-permute-start(f32[64,1,48,128]{3,2,1,0:T(8,128)} %get-tuple-element.50), channel_id=1, source_target_pairs={{4,0},{8,4},{12,8},{16,12},{20,16},{24,20},{28,24},{32,28},{36,32}... | collective-permute-start | bytes 4718600 | tf_op jit(solution)/shard_map/ppermute | solution.py:137
  261.7 22.0 %collective-permute-start.15 = (f32[64,1,48,128]{3,2,1,0:T(8,128)S(1)}, f32[64,1,48,128]{3,2,1,0:T(8,128)}, u32[]{:S(2)}, u32[]{:S(2)}) collective-permute-start(f32[64,1,48,128]{3,2,1,0:T(8,128)S(1)} %get-tuple-element.49), channel_id=1, source_target_pairs={{0,4},{4,8},{8,12},{12,16},{16,20},{20,24},{24,28},{28,32},{32,36}... | collective-permute-start | bytes 4718600 | tf_op jit(solution)/shard_map/ppermute | solution.py:136
  263.6 20.0 %collective-permute-start.16 = (f32[64,2,1,128]{3,2,1,0:T(1,128)}, f32[64,2,1,128]{3,2,1,0:T(1,128)S(1)}, u32[]{:S(2)}, u32[]{:S(2)}) collective-permute-start(f32[64,2,1,128]{3,2,1,0:T(1,128)} %get-tuple-element.46), channel_id=1, source_target_pairs={{1,0},{2,1},{3,2},{5,4},{6,5},{7,6},{9,8},{10,9},{11,10},{13,12},{... | collective-permute-start | bytes 196616 | tf_op jit(solution)/shard_map/ppermute | solution.py:137
  264.9 18.7 %collective-permute-start.17 = (f32[64,2,1,128]{3,2,1,0:T(1,128)}, f32[64,2,1,128]{3,2,1,0:T(1,128)}, u32[]{:S(2)}, u32[]{:S(2)}) collective-permute-start(f32[64,2,1,128]{3,2,1,0:T(1,128)} %get-tuple-element.45), channel_id=1, source_target_pairs={{0,1},{1,2},{2,3},{4,5},{5,6},{6,7},{8,9},{9,10},{10,11},{12,13},{... | collective-permute-start | bytes 196616 | tf_op jit(solution)/shard_map/ppermute | solution.py:136
  (23 other events, 311.6 us)

commit v3 on v2

--- a/solution.py
+++ b/solution.py
@@ -24,66 +24,90 @@
     return block
 
 
-def scatter_sum_kernel(tiles_ref, out_ref, recv, send_sem, recv_sem):
-    count = tiles_ref.shape[0]
-    me = lax.axis_index("slab")
-    col = lax.axis_index("col")
-    recv[pl.ds(me, 1)] = tiles_ref[pl.ds(me, 1)]
+def reduce_kernel(tiles_ref, out_ref, recv1, stage, recv2, send1, rsem1, send2, rsem2):
+    ncol = tiles_ref.shape[0]
+    nslab = recv2.shape[0]
+    my_slab = lax.axis_index("slab")
+    my_col = lax.axis_index("col")
+    mesh = pl.DeviceIdType.MESH
+    recv1[pl.ds(my_col, 1)] = tiles_ref[pl.ds(my_col, 1)]
     barrier = pltpu.get_barrier_semaphore()
+    for k in range(1, ncol):
+        peer = lax.rem(my_col + k, ncol)
+        pl.semaphore_signal(barrier, inc=1, device_id=(my_slab, peer), device_id_type=mesh)
 
     def greet(k, carry):
-        peer = lax.rem(me + k, count)
-        pl.semaphore_signal(barrier, inc=1, device_id=(peer, col), device_id_type=pl.DeviceIdType.MESH)
+        peer = lax.rem(my_slab + k, nslab)
+        pl.semaphore_signal(barrier, inc=1, device_id=(peer, my_col), device_id_type=mesh)
         return carry
 
-    lax.fori_loop(1, count, greet, 0)
-    pl.semaphore_wait(barrier, count - 1)
-
-    def copy_to(k):
-        peer = lax.rem(me + k, count)
+    lax.fori_loop(1, nslab, greet, 0)
+    pl.semaphore_wait(barrier, ncol - 1 + nslab - 1)
+
+    def col_copy(peer, src, dst):
         return pltpu.make_async_remote_copy(
-            src_ref=tiles_ref.at[pl.ds(peer, 1)],
-            dst_ref=recv.at[pl.ds(me, 1)],
-            send_sem=send_sem.at[peer],
-            recv_sem=recv_sem.at[me],
-            device_id=(peer, col),
-            device_id_type=pl.DeviceIdType.MESH,
+            src_ref=tiles_ref.at[pl.ds(src, 1)],
+            dst_ref=recv1.at[pl.ds(dst, 1)],
+            send_sem=send1.at[src],
+            recv_sem=rsem1.at[dst],
+            device_id=(my_slab, peer),
+            device_id_type=mesh,
         )
 
+    for k in range(1, ncol):
+        peer = lax.rem(my_col + k, ncol)
+        col_copy(peer, peer, my_col).start()
+    for k in range(1, ncol):
+        peer = lax.rem(my_col + k, ncol)
+        col_copy(peer, peer, my_col).wait_send()
+        col_copy(peer, my_col, peer).wait_recv()
+    summed = jnp.sum(recv1[...], axis=0)
+    for k in range(nslab):
+        stage[k] = summed[k:k + 1]
+    recv2[pl.ds(my_slab, 1)] = stage[pl.ds(my_slab, 1)]
+
+    def slab_copy(peer, src, dst):
+        return pltpu.make_async_remote_copy(
+            src_ref=stage.at[pl.ds(src, 1)],
+            dst_ref=recv2.at[pl.ds(dst, 1)],
+            send_sem=send2.at[src],
+            recv_sem=rsem2.at[dst],
+            device_id=(peer, my_col),
+            device_id_type=mesh,
+        )
+
     def send(k, carry):
-        copy_to(k).start()
+        peer = lax.rem(my_slab + k, nslab)
+        slab_copy(peer, peer, my_slab).start()
         return carry
 
-    lax.fori_loop(1, count, send, 0)
+    lax.fori_loop(1, nslab, send, 0)
 
     def finish(k, carry):
-        peer = lax.rem(me + k, count)
-        copy_to(k).wait_send()
-        pltpu.make_async_remote_copy(
-            src_ref=tiles_ref.at[pl.ds(me, 1)],
-            dst_ref=recv.at[pl.ds(peer, 1)],
-            send_sem=send_sem.at[me],
-            recv_sem=recv_sem.at[peer],
-            device_id=(peer, col),
-            device_id_type=pl.DeviceIdType.MESH,
-        ).wait_recv()
+        peer = lax.rem(my_slab + k, nslab)
+        slab_copy(peer, peer, my_slab).wait_send()
+        slab_copy(peer, my_slab, peer).wait_recv()
         return carry
 
-    lax.fori_loop(1, count, finish, 0)
-    out_ref[...] = jnp.sum(recv[...], axis=0, keepdims=True)
-
-
-def scatter_sum(tiles):
-    count, rows, lanes = tiles.shape
+    lax.fori_loop(1, nslab, finish, 0)
+    out_ref[...] = jnp.sum(recv2[...], axis=0, keepdims=True)
+
+
+def reduce_scatter(tiles, nslab):
+    ncol, rows, lanes = tiles.shape
     return pl.pallas_call(
-        scatter_sum_kernel,
-        out_shape=jax.ShapeDtypeStruct((1, rows, lanes), jnp.float32),
+        reduce_kernel,
+        out_shape=jax.ShapeDtypeStruct((1, 1, lanes), jnp.float32),
         in_specs=[pl.BlockSpec(memory_space=pltpu.VMEM)],
         out_specs=pl.BlockSpec(memory_space=pltpu.VMEM),
         scratch_shapes=[
-            pltpu.VMEM((count, rows, lanes), jnp.float32),
-            pltpu.SemaphoreType.DMA((count,)),
-            pltpu.SemaphoreType.DMA((count,)),
+            pltpu.VMEM((ncol, rows, lanes), jnp.float32),
+            pltpu.VMEM((nslab, 1, lanes), jnp.float32),
+            pltpu.VMEM((nslab, 1, lanes), jnp.float32),
+            pltpu.SemaphoreType.DMA((ncol,)),
+            pltpu.SemaphoreType.DMA((ncol,)),
+            pltpu.SemaphoreType.DMA((nslab,)),
+            pltpu.SemaphoreType.DMA((nslab,)),
         ],
         compiler_params=pltpu.CompilerParams(collective_id=0, has_side_effects=True),
     )(tiles)
@@ -244,10 +268,9 @@
     col_count = lax.axis_size("col")
     tile_rows = row_count // slab_count
     tile_cols = row_count // col_count
-    col_parts = partial_value.reshape(row_count, col_count, tile_cols).transpose(1, 0, 2)
-    col_sum = jnp.sum(lax.all_to_all(col_parts, "col", 0, 0, tiled=True), axis=0)
-    row_parts = col_sum.reshape(slab_count, 1, tile_rows * tile_cols)
-    own_tile = scatter_sum(row_parts).reshape(tile_rows, tile_cols)
+    tiles = partial_value.reshape(row_count, col_count, tile_cols).transpose(1, 0, 2)
+    tiles = tiles.reshape(col_count, slab_count, tile_rows * tile_cols)
+    own_tile = reduce_scatter(tiles, slab_count).reshape(tile_rows, tile_cols)
     return (ctrl_cols, obsv_cols, own_tile * norm_scale)
 
 

time: 346 us -> 340 us (0.983)
  blocking collectives: 6.84 us -> 0 us
    all_to_all x1 -> x0, blocking collectives: 6.84 us -> none  [body(): lax.all_to_all(col_parts, 'col', 0, 0, tiled=True)]
  transfers between devices with their start and end apart: 36 -> 36, of which waited for: 2 -> 2; matrix products, arithmetic and copies ran while one was open for 32% -> 33% of each run, Pallas kernels for 0% -> 0%
where the time goes in v3:
time: 340 us; the launch traced here: 338 us
  starting transfers between devices  109 us (32%)
  other arithmetic  88.1 us (26%)
  local copies, waits for them, and re-layouts  46.4 us (14%)
  waiting for transfers between devices  44.4 us (13%)
  Pallas kernels  41.2 us (12%)
  between operations  9.03 us (3%)
    ppermute x16, starting transfers between devices, halo_pair(): lax.ppermute(lax.slice_in_dim(block, size - 1, None, axis=dim), axis, for...  54.4 us
    all_to_all x2, waiting for transfers between devices, windows(): received = lax.all_to_all(jnp.stack(parts), 'col', 0, 0, tiled=True)  44.3 us
    another operation x6, other arithmetic, run_segments(): return jnp.stack(factors)  42.1 us
    ppermute x16, starting transfers between devices, halo_pair(): high = lax.ppermute(lax.slice_in_dim(block, 0, 1, axis=dim), axis, backward)  37.6 us
    add x4, other arithmetic, solve_slabs(): rho_next * rho_now * direction + 2.0 * rho_next / half_span * residual  31.2 us
    pallas_call x1, Pallas kernels, reduce_scatter(): pl.pallas_call(reduce_kernel, out_shape=jax.ShapeDtypeStruct((1, 1, lanes...  28 us
    slice x14, local copies, waits for them, and re-layouts, shifted(): lax.slice_in_dim(block, 1, None, axis=dim)  24.9 us
    pallas_call x1, Pallas kernels, gram(): pl.pallas_call(gram_kernel, grid=(depth, rows // rows_per_step), in_specs...  13.2 us
  transfers between devices with their start and end apart: 36, of which 2 were waited for; matrix products, arithmetic and copies ran while one was open for 33% of the time, Pallas kernels for 0%

profile of v3, /device:TPU:1, one launch (start us, length us, event | category | flops | bytes accessed | tf_op | source)
XLA Modules:
  0.0 337.9 jit_solution(3089263251573491106)
XLA Ops:
  4.6 4.8 %all-to-all-start = ((f32[4,16,2,48,128]{4,3,2,1,0:T(8,128)}), f32[4,16,2,48,128]{4,3,2,1,0:T(8,128)S(1)}, u32[]{:S(2)}, u32[]{:S(2)}) async-start(f32[4,16,2,48,128]{4,3,2,1,0:T(8,128)} %pad_maximum_fusion.2), calls=%async_computation | async-start | bytes 6291456 | tf_op jit(solution)/shard_map/all_to_all | solution.py:186
  13.4 32.6 %all-to-all-done = f32[4,16,2,48,128]{4,3,2,1,0:T(8,128)S(1)} async-done(((f32[4,16,2,48,128]{4,3,2,1,0:T(8,128)}), f32[4,16,2,48,128]{4,3,2,1,0:T(8,128)S(1)}, u32[]{:S(2)}, u32[]{:S(2)}) %all-to-all-start) | async-done | bytes 3145760 | tf_op jit(solution)/shard_map/all_to_all | solution.py:186
  46.1 4.6 %all-to-all-start.1 = ((f32[4,16,2,48,128]{4,3,2,1,0:T(8,128)}), f32[4,16,2,48,128]{4,3,2,1,0:T(8,128)}, u32[]{:S(2)}, u32[]{:S(2)}) async-start(f32[4,16,2,48,128]{4,3,2,1,0:T(8,128)} %pad_maximum_fusion.3), calls=%async_computation.1 | async-start | bytes 6291456 | tf_op jit(solution)/shard_map/all_to_all | solution.py:186
  51.4 5.1 %select_add_fusion = f32[2,192,128]{2,1,0:T(8,128)S(1)} fusion(s32[2,192,128]{2,1,0:T(8,128)S(1)} %copy-done.13, f32[]{:T(128)} %bitcast.13, f32[]{:T(128)} %bitcast.12, f32[]{:T(128)} %bitcast.11, f32[]{:T(128)} %bitcast.10, f32[]{:T(128)} %bitcast.9, f32[]{:T(128)} %bitcast.8, f32[]{:T(128)} %bitcast.7, f32[]{:T(128)} %bitcast.6), kind=kLoop, calls=%fused_computation.210 | loop fusion | flops 1130496 | bytes 393248 | tf_op jit(solution)/shard_map/add | solution.py:151
  56.6 3.8 %collective-permute-start = (f32[1,50,128]{2,1,0:T(8,128)S(1)}, f32[1,50,128]{2,1,0:T(8,128)S(1)}, u32[]{:S(2)}, u32[]{:S(2)}) collective-permute-start(f32[1,50,128]{2,1,0:T(8,128)S(1)} %get-tuple-element.76), channel_id=1, source_target_pairs={{4,0},{8,4},{12,8},{16,12},{20,16},{24,20},{28,24},{32,28},{36,32}... | collective-permute-start | bytes 76808 | tf_op jit(solution)/shard_map/ppermute | solution.py:22
  74.8 11.7 %all-to-all-done.1 = f32[4,16,2,48,128]{4,3,2,1,0:T(8,128)} async-done(((f32[4,16,2,48,128]{4,3,2,1,0:T(8,128)}), f32[4,16,2,48,128]{4,3,2,1,0:T(8,128)}, u32[]{:S(2)}, u32[]{:S(2)}) %all-to-all-start.1) | async-done | bytes 3145760 | tf_op jit(solution)/shard_map/all_to_all | solution.py:186
  89.5 4.7 %collective-permute-start.18 = (f32[64,1,48,128]{3,2,1,0:T(8,128)S(1)}, f32[64,1,48,128]{3,2,1,0:T(8,128)S(1)}, u32[]{:S(2)}, u32[]{:S(2)}) collective-permute-start(f32[64,1,48,128]{3,2,1,0:T(8,128)S(1)} %get-tuple-element.36), channel_id=1, source_target_pairs={{4,0},{8,4},{12,8},{16,12},{20,16},{24,20},{28,24},{32,28},{36,32}... | collective-permute-start | bytes 4718600 | tf_op jit(solution)/shard_map/ppermute | solution.py:161
  99.0 4.0 %collective-permute-start.21 = (f32[64,2,1,128]{3,2,1,0:T(1,128)S(1)}, f32[64,2,1,128]{3,2,1,0:T(1,128)S(1)}, u32[]{:S(2)}, u32[]{:S(2)}) collective-permute-start(f32[64,2,1,128]{3,2,1,0:T(1,128)S(1)} %get-tuple-element.40), channel_id=1, source_target_pairs={{0,1},{1,2},{2,3},{4,5},{5,6},{6,7},{8,9},{9,10},{10,11},{12,13},{... | collective-permute-start | bytes 196616 | tf_op jit(solution)/shard_map/ppermute | solution.py:160
  110.0 3.6 %collective-permute-start.3 = (f32[64,1,48,128]{3,2,1,0:T(8,128)S(1)}, f32[64,1,48,128]{3,2,1,0:T(8,128)}, u32[]{:S(2)}, u32[]{:S(2)}) collective-permute-start(f32[64,1,48,128]{3,2,1,0:T(8,128)S(1)} %get-tuple-element.63), channel_id=1, source_target_pairs={{0,4},{4,8},{8,12},{12,16},{16,20},{20,24},{24,28},{28,32},{32,36}... | collective-permute-start | bytes 4718600 | tf_op jit(solution)/shard_map/ppermute | solution.py:160
  115.0 4.0 %collective-permute-start.5 = (f32[64,2,1,128]{3,2,1,0:T(1,128)}, f32[64,2,1,128]{3,2,1,0:T(1,128)S(1)}, u32[]{:S(2)}, u32[]{:S(2)}) collective-permute-start(f32[64,2,1,128]{3,2,1,0:T(1,128)} %get-tuple-element.68), channel_id=1, source_target_pairs={{0,1},{1,2},{2,3},{4,5},{5,6},{6,7},{8,9},{9,10},{10,11},{12,13},{... | collective-permute-start | bytes 196616 | tf_op jit(solution)/shard_map/ppermute | solution.py:160
  120.2 8.0 %multiply_add_fusion.1 = (f32[64,2,48,128]{3,2,1,0:T(8,128)S(1)}, f32[64,2,48,128]{3,2,1,0:T(8,128)}) fusion(f32[64,2,48,128]{3,2,1,0:T(8,128)S(1)} %get-tuple-element.92, f32[]{:T(128)S(6)} %div.73, f32[]{:T(128)S(6)} %mul.258, f32[]{:T(128)} %bitcast, f32[2,48,128]{2,1,0:T(8,128)S(1)} %get-tuple-element.78, f32[2,48,128]{2,1,0:T(8,128)S(1)} %copy-done.9, ...), kind=kLoop, calls=%fused_computation.196 | loop fusion | flops 21233664 | bytes 25460748 | tf_op jit(solution)/shard_map/add | solution.py:224
  138.4 4.0 %collective-permute-start.25 = (f32[64,2,1,128]{3,2,1,0:T(1,128)}, f32[64,2,1,128]{3,2,1,0:T(1,128)S(1)}, u32[]{:S(2)}, u32[]{:S(2)}) collective-permute-start(f32[64,2,1,128]{3,2,1,0:T(1,128)} %get-tuple-element.34), channel_id=1, source_target_pairs={{0,1},{1,2},{2,3},{4,5},{5,6},{6,7},{8,9},{9,10},{10,11},{12,13},{... | collective-permute-start | bytes 196616 | tf_op jit(solution)/shard_map/ppermute | solution.py:160
  142.4 7.6 %multiply_add_fusion.3 = (f32[64,2,48,128]{3,2,1,0:T(8,128)S(1)}, f32[64,2,48,128]{3,2,1,0:T(8,128)}) fusion(f32[64,2,48,128]{3,2,1,0:T(8,128)S(1)} %get-tuple-element.93, f32[]{:T(128)S(6)} %div.73, f32[]{:T(128)S(6)} %mul.258, f32[]{:T(128)} %bitcast, f32[2,48,128]{2,1,0:T(8,128)S(1)} %get-tuple-element.78, f32[2,48,128]{2,1,0:T(8,128)S(1)} %copy-done.9, ...), kind=kLoop, calls=%fused_computation.199 | loop fusion | flops 21233664 | bytes 25460748 | tf_op jit(solution)/shard_map/add | solution.py:224
  151.4 3.5 %fusion.165 = (f32[64,2,47,128]{3,2,1,0:T(8,128)}, f32[64,2,47,128]{3,2,1,0:T(8,128)}) fusion(f32[64,2,48,128]{3,2,1,0:T(8,128)S(1)} %get-tuple-element.7), kind=kLoop, calls=%fused_computation.242 | loop fusion | bytes 12320768 | tf_op jit(solution)/shard_map/slice | solution.py:167
  164.9 4.2 %collective-permute-start.9 = (f32[64,2,1,128]{3,2,1,0:T(1,128)}, f32[64,2,1,128]{3,2,1,0:T(1,128)S(1)}, u32[]{:S(2)}, u32[]{:S(2)}) collective-permute-start(f32[64,2,1,128]{3,2,1,0:T(1,128)} %get-tuple-element.62), channel_id=1, source_target_pairs={{0,1},{1,2},{2,3},{4,5},{5,6},{6,7},{8,9},{9,10},{10,11},{12,13},{... | collective-permute-start | bytes 196616 | tf_op jit(solution)/shard_map/ppermute | solution.py:160
  169.0 9.2 %multiply_bitcast_fusion = (f32[1,64,2,48,128]{4,3,2,1,0:T(8,128)}, f32[64,2,48,128]{3,2,1,0:T(8,128)S(1)}) fusion(f32[]{:T(128)S(6)} %sqrt.8, f32[64,2,48,128]{3,2,1,0:T(8,128)} %get-tuple-element.8, f32[64,2,48,128]{3,2,1,0:T(8,128)S(1)} %get-tuple-element.7, f32[]{:T(128)} %bitcast, f32[2,48,128]{2,1,0:T(8,128)S(1)} %get-tuple-element.78, ...), kind=kLoop, calls=%fused_computation.195 | loop fusion | flops 23592960 | bytes 28606480 | tf_op jit(solution)/shard_map/stack | solution.py:239
  188.2 4.0 %collective-permute-start.29 = (f32[64,2,1,128]{3,2,1,0:T(1,128)}, f32[64,2,1,128]{3,2,1,0:T(1,128)S(1)}, u32[]{:S(2)}, u32[]{:S(2)}) collective-permute-start(f32[64,2,1,128]{3,2,1,0:T(1,128)} %get-tuple-element.28), channel_id=1, source_target_pairs={{0,1},{1,2},{2,3},{4,5},{5,6},{6,7},{8,9},{9,10},{10,11},{12,13},{... | collective-permute-start | bytes 196616 | tf_op jit(solution)/shard_map/ppermute | solution.py:160
  192.2 8.3 %multiply_bitcast_fusion.1 = (f32[1,64,2,48,128]{4,3,2,1,0:T(8,128)}, f32[64,2,48,128]{3,2,1,0:T(8,128)S(1)}) fusion(f32[]{:T(128)S(6)} %sqrt.8, f32[64,2,48,128]{3,2,1,0:T(8,128)} %get-tuple-element.14, f32[64,2,48,128]{3,2,1,0:T(8,128)S(1)} %get-tuple-element.13, f32[]{:T(128)} %bitcast, f32[2,48,128]{2,1,0:T(8,128)S(1)} %get-tuple-element.78, ...), kind=kLoop, calls=%fused_computation.198 | loop fusion | flops 23592960 | bytes 28606480 | tf_op jit(solution)/shard_map/stack | solution.py:239
  207.5 3.8 %collective-permute-start.10 = (f32[64,1,48,128]{3,2,1,0:T(8,128)}, f32[64,1,48,128]{3,2,1,0:T(8,128)}, u32[]{:S(2)}, u32[]{:S(2)}) collective-permute-start(f32[64,1,48,128]{3,2,1,0:T(8,128)} %get-tuple-element.52), channel_id=1, source_target_pairs={{4,0},{8,4},{12,8},{16,12},{20,16},{24,20},{28,24},{32,28},{36,32}... | collective-permute-start | bytes 4718600 | tf_op jit(solution)/shard_map/ppermute | solution.py:161
  214.6 4.6 %collective-permute-start.13 = (f32[64,2,1,128]{3,2,1,0:T(1,128)}, f32[64,2,1,128]{3,2,1,0:T(1,128)}, u32[]{:S(2)}, u32[]{:S(2)}) collective-permute-start(f32[64,2,1,128]{3,2,1,0:T(1,128)} %get-tuple-element.56), channel_id=1, source_target_pairs={{0,1},{1,2},{2,3},{4,5},{5,6},{6,7},{8,9},{9,10},{10,11},{12,13},{... | collective-permute-start | bytes 196616 | tf_op jit(solution)/shard_map/ppermute | solution.py:160
  219.2 7.7 %multiply_add_fusion = (f32[64,2,48,128]{3,2,1,0:T(8,128)S(1)}, f32[64,2,48,128]{3,2,1,0:T(8,128)}) fusion(f32[]{:T(128)S(6)} %div.81, f32[]{:T(128)S(6)} %mul.607, f32[64,2,48,128]{3,2,1,0:T(8,128)S(1)} %get-tuple-element.4, f32[]{:T(128)S(6)} %mul.604, f32[64,2,48,128]{3,2,1,0:T(8,128)S(1)} %broadcast_divide_fusion, f32[]{:T(128)} %bitcast.15, ...), kind=kLoop, calls=%fused_computation.194 | loop fusion | flops 22020096 | bytes 25460752 | tf_op jit(solution)/shard_map/add | solution.py:224
  229.5 4.1 %collective-permute-start.30 = (f32[64,1,48,128]{3,2,1,0:T(8,128)}, f32[64,1,48,128]{3,2,1,0:T(8,128)}, u32[]{:S(2)}, u32[]{:S(2)}) collective-permute-start(f32[64,1,48,128]{3,2,1,0:T(8,128)} %get-tuple-element.22), channel_id=1, source_target_pairs={{4,0},{8,4},{12,8},{16,12},{20,16},{24,20},{28,24},{32,28},{36,32}... | collective-permute-start | bytes 4718600 | tf_op jit(solution)/shard_map/ppermute | solution.py:161
  236.9 4.2 %collective-permute-start.33 = (f32[64,2,1,128]{3,2,1,0:T(1,128)}, f32[64,2,1,128]{3,2,1,0:T(1,128)S(1)}, u32[]{:S(2)}, u32[]{:S(2)}) collective-permute-start(f32[64,2,1,128]{3,2,1,0:T(1,128)} %get-tuple-element.17), channel_id=1, source_target_pairs={{0,1},{1,2},{2,3},{4,5},{5,6},{6,7},{8,9},{9,10},{10,11},{12,13},{... | collective-permute-start | bytes 196616 | tf_op jit(solution)/shard_map/ppermute | solution.py:160
  241.1 7.8 %multiply_add_fusion.2 = (f32[64,2,48,128]{3,2,1,0:T(8,128)S(1)}, f32[64,2,48,128]{3,2,1,0:T(8,128)}) fusion(f32[]{:T(128)S(6)} %div.81, f32[]{:T(128)S(6)} %mul.607, f32[64,2,48,128]{3,2,1,0:T(8,128)S(1)} %get-tuple-element.10, f32[]{:T(128)S(6)} %mul.604, f32[64,2,48,128]{3,2,1,0:T(8,128)S(1)} %broadcast_divide_fusion.1, f32[]{:T(128)} %bitcast.15, ...), kind=kLoop, calls=%fused_computation.197 | loop fusion | flops 22020096 | bytes 25460752 | tf_op jit(solution)/shard_map/add | solution.py:224
  250.3 3.5 %fusion.159 = (f32[64,2,47,128]{3,2,1,0:T(8,128)}, f32[64,2,47,128]{3,2,1,0:T(8,128)}) fusion(f32[64,2,48,128]{3,2,1,0:T(8,128)S(1)} %get-tuple-element.5), kind=kLoop, calls=%fused_computation.236 | loop fusion | bytes 12320768 | tf_op jit(solution)/shard_map/slice | solution.py:168
  256.9 4.1 %collective-permute-start.14 = (f32[64,1,48,128]{3,2,1,0:T(8,128)}, f32[64,1,48,128]{3,2,1,0:T(8,128)}, u32[]{:S(2)}, u32[]{:S(2)}) collective-permute-start(f32[64,1,48,128]{3,2,1,0:T(8,128)} %get-tuple-element.50), channel_id=1, source_target_pairs={{4,0},{8,4},{12,8},{16,12},{20,16},{24,20},{28,24},{32,28},{36,32}... | collective-permute-start | bytes 4718600 | tf_op jit(solution)/shard_map/ppermute | solution.py:161
  264.3 4.6 %collective-permute-start.17 = (f32[64,2,1,128]{3,2,1,0:T(1,128)}, f32[64,2,1,128]{3,2,1,0:T(1,128)}, u32[]{:S(2)}, u32[]{:S(2)}) collective-permute-start(f32[64,2,1,128]{3,2,1,0:T(1,128)} %get-tuple-element.45), channel_id=1, source_target_pairs={{0,1},{1,2},{2,3},{4,5},{5,6},{6,7},{8,9},{9,10},{10,11},{12,13},{... | collective-permute-start | bytes 196616 | tf_op jit(solution)/shard_map/ppermute | solution.py:160
  268.9 8.8 %fusion.81 = f32[1,64,2,48,128]{4,3,2,1,0:T(8,128)} fusion(f32[64,2,48,128]{3,2,1,0:T(8,128)S(1)} %get-tuple-element.4, f32[64,2,48,128]{3,2,1,0:T(8,128)S(1)} %copy-done.1, f32[64,2,48,128]{3,2,1,0:T(8,128)S(1)} %get-tuple-element.5, f32[64,1,48,128]{3,2,1,0:T(8,128)} %collective-permute-done.30, f32[64,1,48,128]{3,2,1,0:T(8,128)} %get-tuple-element.21, ...), kind=kLoop, calls=%fused_computation.99 | loop fusion | flops 25952256 | bytes 25460760 | tf_op jit(solution)/shard_map/stack | solution.py:239
  277.8 5.3 %pad_maximum_fusion.1 = f32[2,64,2,48,128]{4,3,2,1,0:T(8,128)} fusion(f32[1,64,2,48,128]{4,3,2,1,0:T(8,128)} %fusion.81, f32[1,64,2,48,128]{4,3,2,1,0:T(8,128)S(1)} %copy-done.3), kind=kLoop, calls=%fused_computation.17 | loop fusion | flops 1572864 | bytes 12582912 | tf_op jit(solution)/shard_map/stack | solution.py:239
  283.1 7.2 %fusion.39 = f32[1,64,2,48,128]{4,3,2,1,0:T(8,128)S(1)} fusion(f32[64,2,48,128]{3,2,1,0:T(8,128)S(1)} %get-tuple-element.10, f32[64,2,48,128]{3,2,1,0:T(8,128)S(1)} %copy-done.2, f32[64,2,48,128]{3,2,1,0:T(8,128)S(1)} %get-tuple-element.11, f32[64,1,48,128]{3,2,1,0:T(8,128)} %collective-permute-done.14, f32[64,1,48,128]{3,2,1,0:T(8,128)S(1)} %get-tuple-element.49, ...), kind=kLoop, calls=%fused_computation.57 | loop fusion | flops 25952256 | bytes 25460760 | tf_op jit(solution)/shard_map/stack | solution.py:239
  293.5 13.2 %shard_map.76 = f32[128,128]{1,0:T(8,128)} custom-call(f32[128,2,48,128]{3,2,1,0:T(8,128)} %bitcast.48, f32[128,2,48,128]{3,2,1,0:T(8,128)} %bitcast.47), custom_call_target="tpu_custom_call" | custom-call | flops 402653184 | bytes 12582912 | tf_op jit(solution)/shard_map/pallas_call | solution.py:136
  308.5 28.0 %shard_map.77 = f32[1,1,128]{2,1,0:T(1,128)} custom-call(f32[4,32,128]{2,1,0:T(8,128)} %reshape.38.tiles_ref), custom_call_target="tpu_custom_call" | custom-call | tf_op jit(solution)/shard_map/pallas_call | solution.py:98
  (139 shorter events, 94.1 us)
Async XLA Ops:
  4.6 41.5 %all-to-all-start = ((f32[4,16,2,48,128]{4,3,2,1,0:T(8,128)}), f32[4,16,2,48,128]{4,3,2,1,0:T(8,128)S(1)}, u32[]{:S(2)}, u32[]{:S(2)}) async-start(f32[4,16,2,48,128]{4,3,2,1,0:T(8,128)} %pad_maximum_fusion.2), calls=%async_computation | async-start | bytes 6291456 | tf_op jit(solution)/shard_map/all_to_all | solution.py:186
  46.1 40.4 %all-to-all-start.1 = ((f32[4,16,2,48,128]{4,3,2,1,0:T(8,128)}), f32[4,16,2,48,128]{4,3,2,1,0:T(8,128)}, u32[]{:S(2)}, u32[]{:S(2)}) async-start(f32[4,16,2,48,128]{4,3,2,1,0:T(8,128)} %pad_maximum_fusion.3), calls=%async_computation.1 | async-start | bytes 6291456 | tf_op jit(solution)/shard_map/all_to_all | solution.py:186
  89.5 25.5 %collective-permute-start.18 = (f32[64,1,48,128]{3,2,1,0:T(8,128)S(1)}, f32[64,1,48,128]{3,2,1,0:T(8,128)S(1)}, u32[]{:S(2)}, u32[]{:S(2)}) collective-permute-start(f32[64,1,48,128]{3,2,1,0:T(8,128)S(1)} %get-tuple-element.36), channel_id=1, source_target_pairs={{4,0},{8,4},{12,8},{16,12},{20,16},{24,20},{28,24},{32,28},{36,32}... | collective-permute-start | bytes 4718600 | tf_op jit(solution)/shard_map/ppermute | solution.py:161
  94.2 24.9 %collective-permute-start.19 = (f32[64,1,48,128]{3,2,1,0:T(8,128)S(1)}, f32[64,1,48,128]{3,2,1,0:T(8,128)S(1)}, u32[]{:S(2)}, u32[]{:S(2)}) collective-permute-start(f32[64,1,48,128]{3,2,1,0:T(8,128)S(1)} %get-tuple-element.35), channel_id=1, source_target_pairs={{0,4},{4,8},{8,12},{12,16},{16,20},{20,24},{24,28},{28,32},{32,36}... | collective-permute-start | bytes 4718600 | tf_op jit(solution)/shard_map/ppermute | solution.py:160
  108.1 30.2 %collective-permute-start.1 = (f32[64,1,48,128]{3,2,1,0:T(8,128)}, f32[64,1,48,128]{3,2,1,0:T(8,128)}, u32[]{:S(2)}, u32[]{:S(2)}) collective-permute-start(f32[64,1,48,128]{3,2,1,0:T(8,128)} %get-tuple-element.64), channel_id=1, source_target_pairs={{4,0},{8,4},{12,8},{16,12},{20,16},{24,20},{28,24},{32,28},{36,32}... | collective-permute-start | bytes 4718600 | tf_op jit(solution)/shard_map/ppermute | solution.py:161
  110.0 32.3 %collective-permute-start.3 = (f32[64,1,48,128]{3,2,1,0:T(8,128)S(1)}, f32[64,1,48,128]{3,2,1,0:T(8,128)}, u32[]{:S(2)}, u32[]{:S(2)}) collective-permute-start(f32[64,1,48,128]{3,2,1,0:T(8,128)S(1)} %get-tuple-element.63), channel_id=1, source_target_pairs={{0,4},{4,8},{8,12},{12,16},{16,20},{20,24},{24,28},{28,32},{32,36}... | collective-permute-start | bytes 4718600 | tf_op jit(solution)/shard_map/ppermute | solution.py:160
  113.7 19.6 %collective-permute-start.4 = (f32[64,2,1,128]{3,2,1,0:T(1,128)}, f32[64,2,1,128]{3,2,1,0:T(1,128)S(1)}, u32[]{:S(2)}, u32[]{:S(2)}) collective-permute-start(f32[64,2,1,128]{3,2,1,0:T(1,128)} %get-tuple-element.67), channel_id=1, source_target_pairs={{1,0},{2,1},{3,2},{5,4},{6,5},{7,6},{9,8},{10,9},{11,10},{13,12},{... | collective-permute-start | bytes 196616 | tf_op jit(solution)/shard_map/ppermute | solution.py:161
  115.0 21.4 %collective-permute-start.5 = (f32[64,2,1,128]{3,2,1,0:T(1,128)}, f32[64,2,1,128]{3,2,1,0:T(1,128)S(1)}, u32[]{:S(2)}, u32[]{:S(2)}) collective-permute-start(f32[64,2,1,128]{3,2,1,0:T(1,128)} %get-tuple-element.68), channel_id=1, source_target_pairs={{0,1},{1,2},{2,3},{4,5},{5,6},{6,7},{8,9},{9,10},{10,11},{12,13},{... | collective-permute-start | bytes 196616 | tf_op jit(solution)/shard_map/ppermute | solution.py:160
  130.8 34.0 %collective-permute-start.22 = (f32[64,1,48,128]{3,2,1,0:T(8,128)}, f32[64,1,48,128]{3,2,1,0:T(8,128)}, u32[]{:S(2)}, u32[]{:S(2)}) collective-permute-start(f32[64,1,48,128]{3,2,1,0:T(8,128)} %get-tuple-element.30), channel_id=1, source_target_pairs={{4,0},{8,4},{12,8},{16,12},{20,16},{24,20},{28,24},{32,28},{36,32}... | collective-permute-start | bytes 4718600 | tf_op jit(solution)/shard_map/ppermute | solution.py:161
  133.3 35.8 %collective-permute-start.23 = (f32[64,1,48,128]{3,2,1,0:T(8,128)}, f32[64,1,48,128]{3,2,1,0:T(8,128)}, u32[]{:S(2)}, u32[]{:S(2)}) collective-permute-start(f32[64,1,48,128]{3,2,1,0:T(8,128)} %get-tuple-element.29), channel_id=1, source_target_pairs={{0,4},{4,8},{8,12},{12,16},{16,20},{20,24},{24,28},{28,32},{32,36}... | collective-permute-start | bytes 4718600 | tf_op jit(solution)/shard_map/ppermute | solution.py:160
  137.1 23.8 %collective-permute-start.24 = (f32[64,2,1,128]{3,2,1,0:T(1,128)}, f32[64,2,1,128]{3,2,1,0:T(1,128)S(1)}, u32[]{:S(2)}, u32[]{:S(2)}) collective-permute-start(f32[64,2,1,128]{3,2,1,0:T(1,128)} %get-tuple-element.33), channel_id=1, source_target_pairs={{1,0},{2,1},{3,2},{5,4},{6,5},{7,6},{9,8},{10,9},{11,10},{13,12},{... | collective-permute-start | bytes 196616 | tf_op jit(solution)/shard_map/ppermute | solution.py:161
  138.4 25.2 %collective-permute-start.25 = (f32[64,2,1,128]{3,2,1,0:T(1,128)}, f32[64,2,1,128]{3,2,1,0:T(1,128)S(1)}, u32[]{:S(2)}, u32[]{:S(2)}) collective-permute-start(f32[64,2,1,128]{3,2,1,0:T(1,128)} %get-tuple-element.34), channel_id=1, source_target_pairs={{0,1},{1,2},{2,3},{4,5},{5,6},{6,7},{8,9},{9,10},{10,11},{12,13},{... | collective-permute-start | bytes 196616 | tf_op jit(solution)/shard_map/ppermute | solution.py:160
  157.9 30.2 %collective-permute-start.6 = (f32[64,1,48,128]{3,2,1,0:T(8,128)}, f32[64,1,48,128]{3,2,1,0:T(8,128)}, u32[]{:S(2)}, u32[]{:S(2)}) collective-permute-start(f32[64,1,48,128]{3,2,1,0:T(8,128)} %get-tuple-element.58), channel_id=1, source_target_pairs={{4,0},{8,4},{12,8},{16,12},{20,16},{24,20},{28,24},{32,28},{36,32}... | collective-permute-start | bytes 4718600 | tf_op jit(solution)/shard_map/ppermute | solution.py:161
  160.8 31.3 %collective-permute-start.7 = (f32[64,1,48,128]{3,2,1,0:T(8,128)S(1)}, f32[64,1,48,128]{3,2,1,0:T(8,128)}, u32[]{:S(2)}, u32[]{:S(2)}) collective-permute-start(f32[64,1,48,128]{3,2,1,0:T(8,128)S(1)} %get-tuple-element.57), channel_id=1, source_target_pairs={{0,4},{4,8},{8,12},{12,16},{16,20},{20,24},{24,28},{28,32},{32,36}... | collective-permute-start | bytes 4718600 | tf_op jit(solution)/shard_map/ppermute | solution.py:160
  163.5 21.1 %collective-permute-start.8 = (f32[64,2,1,128]{3,2,1,0:T(1,128)}, f32[64,2,1,128]{3,2,1,0:T(1,128)S(1)}, u32[]{:S(2)}, u32[]{:S(2)}) collective-permute-start(f32[64,2,1,128]{3,2,1,0:T(1,128)} %get-tuple-element.61), channel_id=1, source_target_pairs={{1,0},{2,1},{3,2},{5,4},{6,5},{7,6},{9,8},{10,9},{11,10},{13,12},{... | collective-permute-start | bytes 196616 | tf_op jit(solution)/shard_map/ppermute | solution.py:161
  164.9 22.0 %collective-permute-start.9 = (f32[64,2,1,128]{3,2,1,0:T(1,128)}, f32[64,2,1,128]{3,2,1,0:T(1,128)S(1)}, u32[]{:S(2)}, u32[]{:S(2)}) collective-permute-start(f32[64,2,1,128]{3,2,1,0:T(1,128)} %get-tuple-element.62), channel_id=1, source_target_pairs={{0,1},{1,2},{2,3},{4,5},{5,6},{6,7},{8,9},{9,10},{10,11},{12,13},{... | collective-permute-start | bytes 196616 | tf_op jit(solution)/shard_map/ppermute | solution.py:160
  181.2 33.3 %collective-permute-start.26 = (f32[64,1,48,128]{3,2,1,0:T(8,128)}, f32[64,1,48,128]{3,2,1,0:T(8,128)}, u32[]{:S(2)}, u32[]{:S(2)}) collective-permute-start(f32[64,1,48,128]{3,2,1,0:T(8,128)} %get-tuple-element.24), channel_id=1, source_target_pairs={{4,0},{8,4},{12,8},{16,12},{20,16},{24,20},{28,24},{32,28},{36,32}... | collective-permute-start | bytes 4718600 | tf_op jit(solution)/shard_map/ppermute | solution.py:161
  184.6 34.6 %collective-permute-start.27 = (f32[64,1,48,128]{3,2,1,0:T(8,128)}, f32[64,1,48,128]{3,2,1,0:T(8,128)}, u32[]{:S(2)}, u32[]{:S(2)}) collective-permute-start(f32[64,1,48,128]{3,2,1,0:T(8,128)} %get-tuple-element.23), channel_id=1, source_target_pairs={{0,4},{4,8},{8,12},{12,16},{16,20},{20,24},{24,28},{28,32},{32,36}... | collective-permute-start | bytes 4718600 | tf_op jit(solution)/shard_map/ppermute | solution.py:160
  186.8 24.5 %collective-permute-start.28 = (f32[64,2,1,128]{3,2,1,0:T(1,128)}, f32[64,2,1,128]{3,2,1,0:T(1,128)S(1)}, u32[]{:S(2)}, u32[]{:S(2)}) collective-permute-start(f32[64,2,1,128]{3,2,1,0:T(1,128)} %get-tuple-element.27), channel_id=1, source_target_pairs={{1,0},{2,1},{3,2},{5,4},{6,5},{7,6},{9,8},{10,9},{11,10},{13,12},{... | collective-permute-start | bytes 196616 | tf_op jit(solution)/shard_map/ppermute | solution.py:161
  188.2 25.1 %collective-permute-start.29 = (f32[64,2,1,128]{3,2,1,0:T(1,128)}, f32[64,2,1,128]{3,2,1,0:T(1,128)S(1)}, u32[]{:S(2)}, u32[]{:S(2)}) collective-permute-start(f32[64,2,1,128]{3,2,1,0:T(1,128)} %get-tuple-element.28), channel_id=1, source_target_pairs={{0,1},{1,2},{2,3},{4,5},{5,6},{6,7},{8,9},{9,10},{10,11},{12,13},{... | collective-permute-start | bytes 196616 | tf_op jit(solution)/shard_map/ppermute | solution.py:160
  207.5 29.4 %collective-permute-start.10 = (f32[64,1,48,128]{3,2,1,0:T(8,128)}, f32[64,1,48,128]{3,2,1,0:T(8,128)}, u32[]{:S(2)}, u32[]{:S(2)}) collective-permute-start(f32[64,1,48,128]{3,2,1,0:T(8,128)} %get-tuple-element.52), channel_id=1, source_target_pairs={{4,0},{8,4},{12,8},{16,12},{20,16},{24,20},{28,24},{32,28},{36,32}... | collective-permute-start | bytes 4718600 | tf_op jit(solution)/shard_map/ppermute | solution.py:161
  211.3 29.8 %collective-permute-start.11 = (f32[64,1,48,128]{3,2,1,0:T(8,128)S(1)}, f32[64,1,48,128]{3,2,1,0:T(8,128)}, u32[]{:S(2)}, u32[]{:S(2)}) collective-permute-start(f32[64,1,48,128]{3,2,1,0:T(8,128)S(1)} %get-tuple-element.51), channel_id=1, source_target_pairs={{0,4},{4,8},{8,12},{12,16},{16,20},{20,24},{24,28},{28,32},{32,36}... | collective-permute-start | bytes 4718600 | tf_op jit(solution)/shard_map/ppermute | solution.py:160
  213.3 20.3 %collective-permute-start.12 = (f32[64,2,1,128]{3,2,1,0:T(1,128)}, f32[64,2,1,128]{3,2,1,0:T(1,128)S(1)}, u32[]{:S(2)}, u32[]{:S(2)}) collective-permute-start(f32[64,2,1,128]{3,2,1,0:T(1,128)} %get-tuple-element.55), channel_id=1, source_target_pairs={{1,0},{2,1},{3,2},{5,4},{6,5},{7,6},{9,8},{10,9},{11,10},{13,12},{... | collective-permute-start | bytes 196616 | tf_op jit(solution)/shard_map/ppermute | solution.py:161
  214.6 21.0 %collective-permute-start.13 = (f32[64,2,1,128]{3,2,1,0:T(1,128)}, f32[64,2,1,128]{3,2,1,0:T(1,128)}, u32[]{:S(2)}, u32[]{:S(2)}) collective-permute-start(f32[64,2,1,128]{3,2,1,0:T(1,128)} %get-tuple-element.56), channel_id=1, source_target_pairs={{0,1},{1,2},{2,3},{4,5},{5,6},{6,7},{8,9},{9,10},{10,11},{12,13},{... | collective-permute-start | bytes 196616 | tf_op jit(solution)/shard_map/ppermute | solution.py:160
  229.5 34.8 %collective-permute-start.30 = (f32[64,1,48,128]{3,2,1,0:T(8,128)}, f32[64,1,48,128]{3,2,1,0:T(8,128)}, u32[]{:S(2)}, u32[]{:S(2)}) collective-permute-start(f32[64,1,48,128]{3,2,1,0:T(8,128)} %get-tuple-element.22), channel_id=1, source_target_pairs={{4,0},{8,4},{12,8},{16,12},{20,16},{24,20},{28,24},{32,28},{36,32}... | collective-permute-start | bytes 4718600 | tf_op jit(solution)/shard_map/ppermute | solution.py:161
  233.6 35.3 %collective-permute-start.31 = (f32[64,1,48,128]{3,2,1,0:T(8,128)}, f32[64,1,48,128]{3,2,1,0:T(8,128)}, u32[]{:S(2)}, u32[]{:S(2)}) collective-permute-start(f32[64,1,48,128]{3,2,1,0:T(8,128)} %get-tuple-element.21), channel_id=1, source_target_pairs={{0,4},{4,8},{8,12},{12,16},{16,20},{20,24},{24,28},{28,32},{32,36}... | collective-permute-start | bytes 4718600 | tf_op jit(solution)/shard_map/ppermute | solution.py:160
  235.6 25.5 %collective-permute-start.32 = (f32[64,2,1,128]{3,2,1,0:T(1,128)}, f32[64,2,1,128]{3,2,1,0:T(1,128)S(1)}, u32[]{:S(2)}, u32[]{:S(2)}) collective-permute-start(f32[64,2,1,128]{3,2,1,0:T(1,128)} %get-tuple-element.18), channel_id=1, source_target_pairs={{1,0},{2,1},{3,2},{5,4},{6,5},{7,6},{9,8},{10,9},{11,10},{13,12},{... | collective-permute-start | bytes 196616 | tf_op jit(solution)/shard_map/ppermute | solution.py:161
  236.9 26.1 %collective-permute-start.33 = (f32[64,2,1,128]{3,2,1,0:T(1,128)}, f32[64,2,1,128]{3,2,1,0:T(1,128)S(1)}, u32[]{:S(2)}, u32[]{:S(2)}) collective-permute-start(f32[64,2,1,128]{3,2,1,0:T(1,128)} %get-tuple-element.17), channel_id=1, source_target_pairs={{0,1},{1,2},{2,3},{4,5},{5,6},{6,7},{8,9},{9,10},{10,11},{12,13},{... | collective-permute-start | bytes 196616 | tf_op jit(solution)/shard_map/ppermute | solution.py:160
  256.9 26.1 %collective-permute-start.14 = (f32[64,1,48,128]{3,2,1,0:T(8,128)}, f32[64,1,48,128]{3,2,1,0:T(8,128)}, u32[]{:S(2)}, u32[]{:S(2)}) collective-permute-start(f32[64,1,48,128]{3,2,1,0:T(8,128)} %get-tuple-element.50), channel_id=1, source_target_pairs={{4,0},{8,4},{12,8},{16,12},{20,16},{24,20},{28,24},{32,28},{36,32}... | collective-permute-start | bytes 4718600 | tf_op jit(solution)/shard_map/ppermute | solution.py:161
  261.0 22.0 %collective-permute-start.15 = (f32[64,1,48,128]{3,2,1,0:T(8,128)S(1)}, f32[64,1,48,128]{3,2,1,0:T(8,128)}, u32[]{:S(2)}, u32[]{:S(2)}) collective-permute-start(f32[64,1,48,128]{3,2,1,0:T(8,128)S(1)} %get-tuple-element.49), channel_id=1, source_target_pairs={{0,4},{4,8},{8,12},{12,16},{16,20},{20,24},{24,28},{28,32},{32,36}... | collective-permute-start | bytes 4718600 | tf_op jit(solution)/shard_map/ppermute | solution.py:160
  263.0 20.1 %collective-permute-start.16 = (f32[64,2,1,128]{3,2,1,0:T(1,128)}, f32[64,2,1,128]{3,2,1,0:T(1,128)S(1)}, u32[]{:S(2)}, u32[]{:S(2)}) collective-permute-start(f32[64,2,1,128]{3,2,1,0:T(1,128)} %get-tuple-element.46), channel_id=1, source_target_pairs={{1,0},{2,1},{3,2},{5,4},{6,5},{7,6},{9,8},{10,9},{11,10},{13,12},{... | collective-permute-start | bytes 196616 | tf_op jit(solution)/shard_map/ppermute | solution.py:161
  264.3 18.8 %collective-permute-start.17 = (f32[64,2,1,128]{3,2,1,0:T(1,128)}, f32[64,2,1,128]{3,2,1,0:T(1,128)}, u32[]{:S(2)}, u32[]{:S(2)}) collective-permute-start(f32[64,2,1,128]{3,2,1,0:T(1,128)} %get-tuple-element.45), channel_id=1, source_target_pairs={{0,1},{1,2},{2,3},{4,5},{5,6},{6,7},{8,9},{9,10},{10,11},{12,13},{... | collective-permute-start | bytes 196616 | tf_op jit(solution)/shard_map/ppermute | solution.py:160
  (25 other events, 313.1 us)

commit v4 on v3

--- a/solution.py
+++ b/solution.py
@@ -125,7 +125,7 @@
         left,
         right,
         (((1,), (1,)), ((), ())),
-        precision=lax.Precision.HIGHEST,
+        precision=lax.Precision.HIGH,
         preferred_element_type=jnp.float32,
     )
 

time: 340 us -> 338 us (level)
  no operation moved by 1% of the time
where the time goes in v4:
time: 338 us; the launch traced here: 336 us
  starting transfers between devices  109 us (32%)
  other arithmetic  88.1 us (26%)
  local copies, waits for them, and re-layouts  46.4 us (14%)
  waiting for transfers between devices  44.4 us (13%)
  Pallas kernels  39.2 us (12%)
  between operations  9.03 us (3%)
    ppermute x16, starting transfers between devices, halo_pair(): lax.ppermute(lax.slice_in_dim(block, size - 1, None, axis=dim), axis, for...  54.4 us
    all_to_all x2, waiting for transfers between devices, windows(): received = lax.all_to_all(jnp.stack(parts), 'col', 0, 0, tiled=True)  44.3 us
    another operation x6, other arithmetic, run_segments(): return jnp.stack(factors)  42.1 us
    ppermute x16, starting transfers between devices, halo_pair(): high = lax.ppermute(lax.slice_in_dim(block, 0, 1, axis=dim), axis, backward)  37.6 us
    add x4, other arithmetic, solve_slabs(): rho_next * rho_now * direction + 2.0 * rho_next / half_span * residual  31.2 us
    pallas_call x1, Pallas kernels, reduce_scatter(): pl.pallas_call(reduce_kernel, out_shape=jax.ShapeDtypeStruct((1, 1, lanes...  28 us
    slice x14, local copies, waits for them, and re-layouts, shifted(): lax.slice_in_dim(block, 1, None, axis=dim)  24.9 us
    pallas_call x1, Pallas kernels, gram(): pl.pallas_call(gram_kernel, grid=(depth, rows // rows_per_step), in_specs...  11.1 us
  transfers between devices with their start and end apart: 36, of which 2 were waited for; matrix products, arithmetic and copies ran while one was open for 33% of the time, Pallas kernels for 0%

profile of v4, /device:TPU:1, one launch (start us, length us, event | category | flops | bytes accessed | tf_op | source)
XLA Modules:
  0.0 335.9 jit_solution(8192922899918989094)
XLA Ops:
  4.6 4.8 %all-to-all-start = ((f32[4,16,2,48,128]{4,3,2,1,0:T(8,128)}), f32[4,16,2,48,128]{4,3,2,1,0:T(8,128)S(1)}, u32[]{:S(2)}, u32[]{:S(2)}) async-start(f32[4,16,2,48,128]{4,3,2,1,0:T(8,128)} %pad_maximum_fusion.2), calls=%async_computation | async-start | bytes 6291456 | tf_op jit(solution)/shard_map/all_to_all | solution.py:186
  13.4 32.6 %all-to-all-done = f32[4,16,2,48,128]{4,3,2,1,0:T(8,128)S(1)} async-done(((f32[4,16,2,48,128]{4,3,2,1,0:T(8,128)}), f32[4,16,2,48,128]{4,3,2,1,0:T(8,128)S(1)}, u32[]{:S(2)}, u32[]{:S(2)}) %all-to-all-start) | async-done | bytes 3145760 | tf_op jit(solution)/shard_map/all_to_all | solution.py:186
  46.1 4.6 %all-to-all-start.1 = ((f32[4,16,2,48,128]{4,3,2,1,0:T(8,128)}), f32[4,16,2,48,128]{4,3,2,1,0:T(8,128)}, u32[]{:S(2)}, u32[]{:S(2)}) async-start(f32[4,16,2,48,128]{4,3,2,1,0:T(8,128)} %pad_maximum_fusion.3), calls=%async_computation.1 | async-start | bytes 6291456 | tf_op jit(solution)/shard_map/all_to_all | solution.py:186
  51.4 5.1 %select_add_fusion = f32[2,192,128]{2,1,0:T(8,128)S(1)} fusion(s32[2,192,128]{2,1,0:T(8,128)S(1)} %copy-done.13, f32[]{:T(128)} %bitcast.13, f32[]{:T(128)} %bitcast.12, f32[]{:T(128)} %bitcast.11, f32[]{:T(128)} %bitcast.10, f32[]{:T(128)} %bitcast.9, f32[]{:T(128)} %bitcast.8, f32[]{:T(128)} %bitcast.7, f32[]{:T(128)} %bitcast.6), kind=kLoop, calls=%fused_computation.210 | loop fusion | flops 1130496 | bytes 393248 | tf_op jit(solution)/shard_map/add | solution.py:151
  56.6 3.8 %collective-permute-start = (f32[1,50,128]{2,1,0:T(8,128)S(1)}, f32[1,50,128]{2,1,0:T(8,128)S(1)}, u32[]{:S(2)}, u32[]{:S(2)}) collective-permute-start(f32[1,50,128]{2,1,0:T(8,128)S(1)} %get-tuple-element.76), channel_id=1, source_target_pairs={{4,0},{8,4},{12,8},{16,12},{20,16},{24,20},{28,24},{32,28},{36,32}... | collective-permute-start | bytes 76808 | tf_op jit(solution)/shard_map/ppermute | solution.py:22
  74.8 11.7 %all-to-all-done.1 = f32[4,16,2,48,128]{4,3,2,1,0:T(8,128)} async-done(((f32[4,16,2,48,128]{4,3,2,1,0:T(8,128)}), f32[4,16,2,48,128]{4,3,2,1,0:T(8,128)}, u32[]{:S(2)}, u32[]{:S(2)}) %all-to-all-start.1) | async-done | bytes 3145760 | tf_op jit(solution)/shard_map/all_to_all | solution.py:186
  89.5 4.7 %collective-permute-start.18 = (f32[64,1,48,128]{3,2,1,0:T(8,128)S(1)}, f32[64,1,48,128]{3,2,1,0:T(8,128)S(1)}, u32[]{:S(2)}, u32[]{:S(2)}) collective-permute-start(f32[64,1,48,128]{3,2,1,0:T(8,128)S(1)} %get-tuple-element.36), channel_id=1, source_target_pairs={{4,0},{8,4},{12,8},{16,12},{20,16},{24,20},{28,24},{32,28},{36,32}... | collective-permute-start | bytes 4718600 | tf_op jit(solution)/shard_map/ppermute | solution.py:161
  99.0 4.0 %collective-permute-start.21 = (f32[64,2,1,128]{3,2,1,0:T(1,128)S(1)}, f32[64,2,1,128]{3,2,1,0:T(1,128)S(1)}, u32[]{:S(2)}, u32[]{:S(2)}) collective-permute-start(f32[64,2,1,128]{3,2,1,0:T(1,128)S(1)} %get-tuple-element.40), channel_id=1, source_target_pairs={{0,1},{1,2},{2,3},{4,5},{5,6},{6,7},{8,9},{9,10},{10,11},{12,13},{... | collective-permute-start | bytes 196616 | tf_op jit(solution)/shard_map/ppermute | solution.py:160
  110.0 3.6 %collective-permute-start.3 = (f32[64,1,48,128]{3,2,1,0:T(8,128)S(1)}, f32[64,1,48,128]{3,2,1,0:T(8,128)}, u32[]{:S(2)}, u32[]{:S(2)}) collective-permute-start(f32[64,1,48,128]{3,2,1,0:T(8,128)S(1)} %get-tuple-element.63), channel_id=1, source_target_pairs={{0,4},{4,8},{8,12},{12,16},{16,20},{20,24},{24,28},{28,32},{32,36}... | collective-permute-start | bytes 4718600 | tf_op jit(solution)/shard_map/ppermute | solution.py:160
  115.0 4.0 %collective-permute-start.5 = (f32[64,2,1,128]{3,2,1,0:T(1,128)}, f32[64,2,1,128]{3,2,1,0:T(1,128)S(1)}, u32[]{:S(2)}, u32[]{:S(2)}) collective-permute-start(f32[64,2,1,128]{3,2,1,0:T(1,128)} %get-tuple-element.68), channel_id=1, source_target_pairs={{0,1},{1,2},{2,3},{4,5},{5,6},{6,7},{8,9},{9,10},{10,11},{12,13},{... | collective-permute-start | bytes 196616 | tf_op jit(solution)/shard_map/ppermute | solution.py:160
  120.2 8.0 %multiply_add_fusion.1 = (f32[64,2,48,128]{3,2,1,0:T(8,128)S(1)}, f32[64,2,48,128]{3,2,1,0:T(8,128)}) fusion(f32[64,2,48,128]{3,2,1,0:T(8,128)S(1)} %get-tuple-element.92, f32[]{:T(128)S(6)} %div.73, f32[]{:T(128)S(6)} %mul.258, f32[]{:T(128)} %bitcast, f32[2,48,128]{2,1,0:T(8,128)S(1)} %get-tuple-element.78, f32[2,48,128]{2,1,0:T(8,128)S(1)} %copy-done.9, ...), kind=kLoop, calls=%fused_computation.196 | loop fusion | flops 21233664 | bytes 25460748 | tf_op jit(solution)/shard_map/add | solution.py:224
  138.4 4.0 %collective-permute-start.25 = (f32[64,2,1,128]{3,2,1,0:T(1,128)}, f32[64,2,1,128]{3,2,1,0:T(1,128)S(1)}, u32[]{:S(2)}, u32[]{:S(2)}) collective-permute-start(f32[64,2,1,128]{3,2,1,0:T(1,128)} %get-tuple-element.34), channel_id=1, source_target_pairs={{0,1},{1,2},{2,3},{4,5},{5,6},{6,7},{8,9},{9,10},{10,11},{12,13},{... | collective-permute-start | bytes 196616 | tf_op jit(solution)/shard_map/ppermute | solution.py:160
  142.4 7.6 %multiply_add_fusion.3 = (f32[64,2,48,128]{3,2,1,0:T(8,128)S(1)}, f32[64,2,48,128]{3,2,1,0:T(8,128)}) fusion(f32[64,2,48,128]{3,2,1,0:T(8,128)S(1)} %get-tuple-element.93, f32[]{:T(128)S(6)} %div.73, f32[]{:T(128)S(6)} %mul.258, f32[]{:T(128)} %bitcast, f32[2,48,128]{2,1,0:T(8,128)S(1)} %get-tuple-element.78, f32[2,48,128]{2,1,0:T(8,128)S(1)} %copy-done.9, ...), kind=kLoop, calls=%fused_computation.199 | loop fusion | flops 21233664 | bytes 25460748 | tf_op jit(solution)/shard_map/add | solution.py:224
  151.4 3.5 %fusion.165 = (f32[64,2,47,128]{3,2,1,0:T(8,128)}, f32[64,2,47,128]{3,2,1,0:T(8,128)}) fusion(f32[64,2,48,128]{3,2,1,0:T(8,128)S(1)} %get-tuple-element.7), kind=kLoop, calls=%fused_computation.242 | loop fusion | bytes 12320768 | tf_op jit(solution)/shard_map/slice | solution.py:167
  164.9 4.2 %collective-permute-start.9 = (f32[64,2,1,128]{3,2,1,0:T(1,128)}, f32[64,2,1,128]{3,2,1,0:T(1,128)S(1)}, u32[]{:S(2)}, u32[]{:S(2)}) collective-permute-start(f32[64,2,1,128]{3,2,1,0:T(1,128)} %get-tuple-element.62), channel_id=1, source_target_pairs={{0,1},{1,2},{2,3},{4,5},{5,6},{6,7},{8,9},{9,10},{10,11},{12,13},{... | collective-permute-start | bytes 196616 | tf_op jit(solution)/shard_map/ppermute | solution.py:160
  169.0 9.2 %multiply_bitcast_fusion = (f32[1,64,2,48,128]{4,3,2,1,0:T(8,128)}, f32[64,2,48,128]{3,2,1,0:T(8,128)S(1)}) fusion(f32[]{:T(128)S(6)} %sqrt.8, f32[64,2,48,128]{3,2,1,0:T(8,128)} %get-tuple-element.8, f32[64,2,48,128]{3,2,1,0:T(8,128)S(1)} %get-tuple-element.7, f32[]{:T(128)} %bitcast, f32[2,48,128]{2,1,0:T(8,128)S(1)} %get-tuple-element.78, ...), kind=kLoop, calls=%fused_computation.195 | loop fusion | flops 23592960 | bytes 28606480 | tf_op jit(solution)/shard_map/stack | solution.py:239
  188.2 4.0 %collective-permute-start.29 = (f32[64,2,1,128]{3,2,1,0:T(1,128)}, f32[64,2,1,128]{3,2,1,0:T(1,128)S(1)}, u32[]{:S(2)}, u32[]{:S(2)}) collective-permute-start(f32[64,2,1,128]{3,2,1,0:T(1,128)} %get-tuple-element.28), channel_id=1, source_target_pairs={{0,1},{1,2},{2,3},{4,5},{5,6},{6,7},{8,9},{9,10},{10,11},{12,13},{... | collective-permute-start | bytes 196616 | tf_op jit(solution)/shard_map/ppermute | solution.py:160
  192.2 8.3 %multiply_bitcast_fusion.1 = (f32[1,64,2,48,128]{4,3,2,1,0:T(8,128)}, f32[64,2,48,128]{3,2,1,0:T(8,128)S(1)}) fusion(f32[]{:T(128)S(6)} %sqrt.8, f32[64,2,48,128]{3,2,1,0:T(8,128)} %get-tuple-element.14, f32[64,2,48,128]{3,2,1,0:T(8,128)S(1)} %get-tuple-element.13, f32[]{:T(128)} %bitcast, f32[2,48,128]{2,1,0:T(8,128)S(1)} %get-tuple-element.78, ...), kind=kLoop, calls=%fused_computation.198 | loop fusion | flops 23592960 | bytes 28606480 | tf_op jit(solution)/shard_map/stack | solution.py:239
  207.5 3.8 %collective-permute-start.10 = (f32[64,1,48,128]{3,2,1,0:T(8,128)}, f32[64,1,48,128]{3,2,1,0:T(8,128)}, u32[]{:S(2)}, u32[]{:S(2)}) collective-permute-start(f32[64,1,48,128]{3,2,1,0:T(8,128)} %get-tuple-element.52), channel_id=1, source_target_pairs={{4,0},{8,4},{12,8},{16,12},{20,16},{24,20},{28,24},{32,28},{36,32}... | collective-permute-start | bytes 4718600 | tf_op jit(solution)/shard_map/ppermute | solution.py:161
  214.6 4.6 %collective-permute-start.13 = (f32[64,2,1,128]{3,2,1,0:T(1,128)}, f32[64,2,1,128]{3,2,1,0:T(1,128)}, u32[]{:S(2)}, u32[]{:S(2)}) collective-permute-start(f32[64,2,1,128]{3,2,1,0:T(1,128)} %get-tuple-element.56), channel_id=1, source_target_pairs={{0,1},{1,2},{2,3},{4,5},{5,6},{6,7},{8,9},{9,10},{10,11},{12,13},{... | collective-permute-start | bytes 196616 | tf_op jit(solution)/shard_map/ppermute | solution.py:160
  219.2 7.7 %multiply_add_fusion = (f32[64,2,48,128]{3,2,1,0:T(8,128)S(1)}, f32[64,2,48,128]{3,2,1,0:T(8,128)}) fusion(f32[]{:T(128)S(6)} %div.81, f32[]{:T(128)S(6)} %mul.607, f32[64,2,48,128]{3,2,1,0:T(8,128)S(1)} %get-tuple-element.4, f32[]{:T(128)S(6)} %mul.604, f32[64,2,48,128]{3,2,1,0:T(8,128)S(1)} %broadcast_divide_fusion, f32[]{:T(128)} %bitcast.15, ...), kind=kLoop, calls=%fused_computation.194 | loop fusion | flops 22020096 | bytes 25460752 | tf_op jit(solution)/shard_map/add | solution.py:224
  229.5 4.1 %collective-permute-start.30 = (f32[64,1,48,128]{3,2,1,0:T(8,128)}, f32[64,1,48,128]{3,2,1,0:T(8,128)}, u32[]{:S(2)}, u32[]{:S(2)}) collective-permute-start(f32[64,1,48,128]{3,2,1,0:T(8,128)} %get-tuple-element.22), channel_id=1, source_target_pairs={{4,0},{8,4},{12,8},{16,12},{20,16},{24,20},{28,24},{32,28},{36,32}... | collective-permute-start | bytes 4718600 | tf_op jit(solution)/shard_map/ppermute | solution.py:161
  236.9 4.2 %collective-permute-start.33 = (f32[64,2,1,128]{3,2,1,0:T(1,128)}, f32[64,2,1,128]{3,2,1,0:T(1,128)S(1)}, u32[]{:S(2)}, u32[]{:S(2)}) collective-permute-start(f32[64,2,1,128]{3,2,1,0:T(1,128)} %get-tuple-element.17), channel_id=1, source_target_pairs={{0,1},{1,2},{2,3},{4,5},{5,6},{6,7},{8,9},{9,10},{10,11},{12,13},{... | collective-permute-start | bytes 196616 | tf_op jit(solution)/shard_map/ppermute | solution.py:160
  241.1 7.8 %multiply_add_fusion.2 = (f32[64,2,48,128]{3,2,1,0:T(8,128)S(1)}, f32[64,2,48,128]{3,2,1,0:T(8,128)}) fusion(f32[]{:T(128)S(6)} %div.81, f32[]{:T(128)S(6)} %mul.607, f32[64,2,48,128]{3,2,1,0:T(8,128)S(1)} %get-tuple-element.10, f32[]{:T(128)S(6)} %mul.604, f32[64,2,48,128]{3,2,1,0:T(8,128)S(1)} %broadcast_divide_fusion.1, f32[]{:T(128)} %bitcast.15, ...), kind=kLoop, calls=%fused_computation.197 | loop fusion | flops 22020096 | bytes 25460752 | tf_op jit(solution)/shard_map/add | solution.py:224
  250.3 3.5 %fusion.159 = (f32[64,2,47,128]{3,2,1,0:T(8,128)}, f32[64,2,47,128]{3,2,1,0:T(8,128)}) fusion(f32[64,2,48,128]{3,2,1,0:T(8,128)S(1)} %get-tuple-element.5), kind=kLoop, calls=%fused_computation.236 | loop fusion | bytes 12320768 | tf_op jit(solution)/shard_map/slice | solution.py:168
  256.9 4.1 %collective-permute-start.14 = (f32[64,1,48,128]{3,2,1,0:T(8,128)}, f32[64,1,48,128]{3,2,1,0:T(8,128)}, u32[]{:S(2)}, u32[]{:S(2)}) collective-permute-start(f32[64,1,48,128]{3,2,1,0:T(8,128)} %get-tuple-element.50), channel_id=1, source_target_pairs={{4,0},{8,4},{12,8},{16,12},{20,16},{24,20},{28,24},{32,28},{36,32}... | collective-permute-start | bytes 4718600 | tf_op jit(solution)/shard_map/ppermute | solution.py:161
  264.3 4.6 %collective-permute-start.17 = (f32[64,2,1,128]{3,2,1,0:T(1,128)}, f32[64,2,1,128]{3,2,1,0:T(1,128)}, u32[]{:S(2)}, u32[]{:S(2)}) collective-permute-start(f32[64,2,1,128]{3,2,1,0:T(1,128)} %get-tuple-element.45), channel_id=1, source_target_pairs={{0,1},{1,2},{2,3},{4,5},{5,6},{6,7},{8,9},{9,10},{10,11},{12,13},{... | collective-permute-start | bytes 196616 | tf_op jit(solution)/shard_map/ppermute | solution.py:160
  268.9 8.8 %fusion.81 = f32[1,64,2,48,128]{4,3,2,1,0:T(8,128)} fusion(f32[64,2,48,128]{3,2,1,0:T(8,128)S(1)} %get-tuple-element.4, f32[64,2,48,128]{3,2,1,0:T(8,128)S(1)} %copy-done.1, f32[64,2,48,128]{3,2,1,0:T(8,128)S(1)} %get-tuple-element.5, f32[64,1,48,128]{3,2,1,0:T(8,128)} %collective-permute-done.30, f32[64,1,48,128]{3,2,1,0:T(8,128)} %get-tuple-element.21, ...), kind=kLoop, calls=%fused_computation.99 | loop fusion | flops 25952256 | bytes 25460760 | tf_op jit(solution)/shard_map/stack | solution.py:239
  277.8 5.3 %pad_maximum_fusion.1 = f32[2,64,2,48,128]{4,3,2,1,0:T(8,128)} fusion(f32[1,64,2,48,128]{4,3,2,1,0:T(8,128)} %fusion.81, f32[1,64,2,48,128]{4,3,2,1,0:T(8,128)S(1)} %copy-done.3), kind=kLoop, calls=%fused_computation.17 | loop fusion | flops 1572864 | bytes 12582912 | tf_op jit(solution)/shard_map/stack | solution.py:239
  283.1 7.2 %fusion.39 = f32[1,64,2,48,128]{4,3,2,1,0:T(8,128)S(1)} fusion(f32[64,2,48,128]{3,2,1,0:T(8,128)S(1)} %get-tuple-element.10, f32[64,2,48,128]{3,2,1,0:T(8,128)S(1)} %copy-done.2, f32[64,2,48,128]{3,2,1,0:T(8,128)S(1)} %get-tuple-element.11, f32[64,1,48,128]{3,2,1,0:T(8,128)} %collective-permute-done.14, f32[64,1,48,128]{3,2,1,0:T(8,128)S(1)} %get-tuple-element.49, ...), kind=kLoop, calls=%fused_computation.57 | loop fusion | flops 25952256 | bytes 25460760 | tf_op jit(solution)/shard_map/stack | solution.py:239
  293.5 11.1 %shard_map.76 = f32[128,128]{1,0:T(8,128)} custom-call(f32[128,2,48,128]{3,2,1,0:T(8,128)} %bitcast.48, f32[128,2,48,128]{3,2,1,0:T(8,128)} %bitcast.47), custom_call_target="tpu_custom_call" | custom-call | flops 402653184 | bytes 12582912 | tf_op jit(solution)/shard_map/pallas_call | solution.py:136
  306.5 28.0 %shard_map.77 = f32[1,1,128]{2,1,0:T(1,128)} custom-call(f32[4,32,128]{2,1,0:T(8,128)} %reshape.38.tiles_ref), custom_call_target="tpu_custom_call" | custom-call | tf_op jit(solution)/shard_map/pallas_call | solution.py:98
  (139 shorter events, 94.1 us)
Async XLA Ops:
  4.6 41.5 %all-to-all-start = ((f32[4,16,2,48,128]{4,3,2,1,0:T(8,128)}), f32[4,16,2,48,128]{4,3,2,1,0:T(8,128)S(1)}, u32[]{:S(2)}, u32[]{:S(2)}) async-start(f32[4,16,2,48,128]{4,3,2,1,0:T(8,128)} %pad_maximum_fusion.2), calls=%async_computation | async-start | bytes 6291456 | tf_op jit(solution)/shard_map/all_to_all | solution.py:186
  46.1 40.4 %all-to-all-start.1 = ((f32[4,16,2,48,128]{4,3,2,1,0:T(8,128)}), f32[4,16,2,48,128]{4,3,2,1,0:T(8,128)}, u32[]{:S(2)}, u32[]{:S(2)}) async-start(f32[4,16,2,48,128]{4,3,2,1,0:T(8,128)} %pad_maximum_fusion.3), calls=%async_computation.1 | async-start | bytes 6291456 | tf_op jit(solution)/shard_map/all_to_all | solution.py:186
  89.5 25.5 %collective-permute-start.18 = (f32[64,1,48,128]{3,2,1,0:T(8,128)S(1)}, f32[64,1,48,128]{3,2,1,0:T(8,128)S(1)}, u32[]{:S(2)}, u32[]{:S(2)}) collective-permute-start(f32[64,1,48,128]{3,2,1,0:T(8,128)S(1)} %get-tuple-element.36), channel_id=1, source_target_pairs={{4,0},{8,4},{12,8},{16,12},{20,16},{24,20},{28,24},{32,28},{36,32}... | collective-permute-start | bytes 4718600 | tf_op jit(solution)/shard_map/ppermute | solution.py:161
  94.2 24.9 %collective-permute-start.19 = (f32[64,1,48,128]{3,2,1,0:T(8,128)S(1)}, f32[64,1,48,128]{3,2,1,0:T(8,128)S(1)}, u32[]{:S(2)}, u32[]{:S(2)}) collective-permute-start(f32[64,1,48,128]{3,2,1,0:T(8,128)S(1)} %get-tuple-element.35), channel_id=1, source_target_pairs={{0,4},{4,8},{8,12},{12,16},{16,20},{20,24},{24,28},{28,32},{32,36}... | collective-permute-start | bytes 4718600 | tf_op jit(solution)/shard_map/ppermute | solution.py:160
  108.1 30.2 %collective-permute-start.1 = (f32[64,1,48,128]{3,2,1,0:T(8,128)}, f32[64,1,48,128]{3,2,1,0:T(8,128)}, u32[]{:S(2)}, u32[]{:S(2)}) collective-permute-start(f32[64,1,48,128]{3,2,1,0:T(8,128)} %get-tuple-element.64), channel_id=1, source_target_pairs={{4,0},{8,4},{12,8},{16,12},{20,16},{24,20},{28,24},{32,28},{36,32}... | collective-permute-start | bytes 4718600 | tf_op jit(solution)/shard_map/ppermute | solution.py:161
  110.0 32.3 %collective-permute-start.3 = (f32[64,1,48,128]{3,2,1,0:T(8,128)S(1)}, f32[64,1,48,128]{3,2,1,0:T(8,128)}, u32[]{:S(2)}, u32[]{:S(2)}) collective-permute-start(f32[64,1,48,128]{3,2,1,0:T(8,128)S(1)} %get-tuple-element.63), channel_id=1, source_target_pairs={{0,4},{4,8},{8,12},{12,16},{16,20},{20,24},{24,28},{28,32},{32,36}... | collective-permute-start | bytes 4718600 | tf_op jit(solution)/shard_map/ppermute | solution.py:160
  113.7 19.6 %collective-permute-start.4 = (f32[64,2,1,128]{3,2,1,0:T(1,128)}, f32[64,2,1,128]{3,2,1,0:T(1,128)S(1)}, u32[]{:S(2)}, u32[]{:S(2)}) collective-permute-start(f32[64,2,1,128]{3,2,1,0:T(1,128)} %get-tuple-element.67), channel_id=1, source_target_pairs={{1,0},{2,1},{3,2},{5,4},{6,5},{7,6},{9,8},{10,9},{11,10},{13,12},{... | collective-permute-start | bytes 196616 | tf_op jit(solution)/shard_map/ppermute | solution.py:161
  115.0 21.4 %collective-permute-start.5 = (f32[64,2,1,128]{3,2,1,0:T(1,128)}, f32[64,2,1,128]{3,2,1,0:T(1,128)S(1)}, u32[]{:S(2)}, u32[]{:S(2)}) collective-permute-start(f32[64,2,1,128]{3,2,1,0:T(1,128)} %get-tuple-element.68), channel_id=1, source_target_pairs={{0,1},{1,2},{2,3},{4,5},{5,6},{6,7},{8,9},{9,10},{10,11},{12,13},{... | collective-permute-start | bytes 196616 | tf_op jit(solution)/shard_map/ppermute | solution.py:160
  130.8 34.0 %collective-permute-start.22 = (f32[64,1,48,128]{3,2,1,0:T(8,128)}, f32[64,1,48,128]{3,2,1,0:T(8,128)}, u32[]{:S(2)}, u32[]{:S(2)}) collective-permute-start(f32[64,1,48,128]{3,2,1,0:T(8,128)} %get-tuple-element.30), channel_id=1, source_target_pairs={{4,0},{8,4},{12,8},{16,12},{20,16},{24,20},{28,24},{32,28},{36,32}... | collective-permute-start | bytes 4718600 | tf_op jit(solution)/shard_map/ppermute | solution.py:161
  133.3 35.8 %collective-permute-start.23 = (f32[64,1,48,128]{3,2,1,0:T(8,128)}, f32[64,1,48,128]{3,2,1,0:T(8,128)}, u32[]{:S(2)}, u32[]{:S(2)}) collective-permute-start(f32[64,1,48,128]{3,2,1,0:T(8,128)} %get-tuple-element.29), channel_id=1, source_target_pairs={{0,4},{4,8},{8,12},{12,16},{16,20},{20,24},{24,28},{28,32},{32,36}... | collective-permute-start | bytes 4718600 | tf_op jit(solution)/shard_map/ppermute | solution.py:160
  137.1 23.8 %collective-permute-start.24 = (f32[64,2,1,128]{3,2,1,0:T(1,128)}, f32[64,2,1,128]{3,2,1,0:T(1,128)S(1)}, u32[]{:S(2)}, u32[]{:S(2)}) collective-permute-start(f32[64,2,1,128]{3,2,1,0:T(1,128)} %get-tuple-element.33), channel_id=1, source_target_pairs={{1,0},{2,1},{3,2},{5,4},{6,5},{7,6},{9,8},{10,9},{11,10},{13,12},{... | collective-permute-start | bytes 196616 | tf_op jit(solution)/shard_map/ppermute | solution.py:161
  138.4 25.2 %collective-permute-start.25 = (f32[64,2,1,128]{3,2,1,0:T(1,128)}, f32[64,2,1,128]{3,2,1,0:T(1,128)S(1)}, u32[]{:S(2)}, u32[]{:S(2)}) collective-permute-start(f32[64,2,1,128]{3,2,1,0:T(1,128)} %get-tuple-element.34), channel_id=1, source_target_pairs={{0,1},{1,2},{2,3},{4,5},{5,6},{6,7},{8,9},{9,10},{10,11},{12,13},{... | collective-permute-start | bytes 196616 | tf_op jit(solution)/shard_map/ppermute | solution.py:160
  157.9 30.2 %collective-permute-start.6 = (f32[64,1,48,128]{3,2,1,0:T(8,128)}, f32[64,1,48,128]{3,2,1,0:T(8,128)}, u32[]{:S(2)}, u32[]{:S(2)}) collective-permute-start(f32[64,1,48,128]{3,2,1,0:T(8,128)} %get-tuple-element.58), channel_id=1, source_target_pairs={{4,0},{8,4},{12,8},{16,12},{20,16},{24,20},{28,24},{32,28},{36,32}... | collective-permute-start | bytes 4718600 | tf_op jit(solution)/shard_map/ppermute | solution.py:161
  160.8 31.3 %collective-permute-start.7 = (f32[64,1,48,128]{3,2,1,0:T(8,128)S(1)}, f32[64,1,48,128]{3,2,1,0:T(8,128)}, u32[]{:S(2)}, u32[]{:S(2)}) collective-permute-start(f32[64,1,48,128]{3,2,1,0:T(8,128)S(1)} %get-tuple-element.57), channel_id=1, source_target_pairs={{0,4},{4,8},{8,12},{12,16},{16,20},{20,24},{24,28},{28,32},{32,36}... | collective-permute-start | bytes 4718600 | tf_op jit(solution)/shard_map/ppermute | solution.py:160
  163.5 21.1 %collective-permute-start.8 = (f32[64,2,1,128]{3,2,1,0:T(1,128)}, f32[64,2,1,128]{3,2,1,0:T(1,128)S(1)}, u32[]{:S(2)}, u32[]{:S(2)}) collective-permute-start(f32[64,2,1,128]{3,2,1,0:T(1,128)} %get-tuple-element.61), channel_id=1, source_target_pairs={{1,0},{2,1},{3,2},{5,4},{6,5},{7,6},{9,8},{10,9},{11,10},{13,12},{... | collective-permute-start | bytes 196616 | tf_op jit(solution)/shard_map/ppermute | solution.py:161
  164.9 22.0 %collective-permute-start.9 = (f32[64,2,1,128]{3,2,1,0:T(1,128)}, f32[64,2,1,128]{3,2,1,0:T(1,128)S(1)}, u32[]{:S(2)}, u32[]{:S(2)}) collective-permute-start(f32[64,2,1,128]{3,2,1,0:T(1,128)} %get-tuple-element.62), channel_id=1, source_target_pairs={{0,1},{1,2},{2,3},{4,5},{5,6},{6,7},{8,9},{9,10},{10,11},{12,13},{... | collective-permute-start | bytes 196616 | tf_op jit(solution)/shard_map/ppermute | solution.py:160
  181.2 33.3 %collective-permute-start.26 = (f32[64,1,48,128]{3,2,1,0:T(8,128)}, f32[64,1,48,128]{3,2,1,0:T(8,128)}, u32[]{:S(2)}, u32[]{:S(2)}) collective-permute-start(f32[64,1,48,128]{3,2,1,0:T(8,128)} %get-tuple-element.24), channel_id=1, source_target_pairs={{4,0},{8,4},{12,8},{16,12},{20,16},{24,20},{28,24},{32,28},{36,32}... | collective-permute-start | bytes 4718600 | tf_op jit(solution)/shard_map/ppermute | solution.py:161
  184.6 34.6 %collective-permute-start.27 = (f32[64,1,48,128]{3,2,1,0:T(8,128)}, f32[64,1,48,128]{3,2,1,0:T(8,128)}, u32[]{:S(2)}, u32[]{:S(2)}) collective-permute-start(f32[64,1,48,128]{3,2,1,0:T(8,128)} %get-tuple-element.23), channel_id=1, source_target_pairs={{0,4},{4,8},{8,12},{12,16},{16,20},{20,24},{24,28},{28,32},{32,36}... | collective-permute-start | bytes 4718600 | tf_op jit(solution)/shard_map/ppermute | solution.py:160
  186.8 24.5 %collective-permute-start.28 = (f32[64,2,1,128]{3,2,1,0:T(1,128)}, f32[64,2,1,128]{3,2,1,0:T(1,128)S(1)}, u32[]{:S(2)}, u32[]{:S(2)}) collective-permute-start(f32[64,2,1,128]{3,2,1,0:T(1,128)} %get-tuple-element.27), channel_id=1, source_target_pairs={{1,0},{2,1},{3,2},{5,4},{6,5},{7,6},{9,8},{10,9},{11,10},{13,12},{... | collective-permute-start | bytes 196616 | tf_op jit(solution)/shard_map/ppermute | solution.py:161
  188.2 25.1 %collective-permute-start.29 = (f32[64,2,1,128]{3,2,1,0:T(1,128)}, f32[64,2,1,128]{3,2,1,0:T(1,128)S(1)}, u32[]{:S(2)}, u32[]{:S(2)}) collective-permute-start(f32[64,2,1,128]{3,2,1,0:T(1,128)} %get-tuple-element.28), channel_id=1, source_target_pairs={{0,1},{1,2},{2,3},{4,5},{5,6},{6,7},{8,9},{9,10},{10,11},{12,13},{... | collective-permute-start | bytes 196616 | tf_op jit(solution)/shard_map/ppermute | solution.py:160
  207.5 29.4 %collective-permute-start.10 = (f32[64,1,48,128]{3,2,1,0:T(8,128)}, f32[64,1,48,128]{3,2,1,0:T(8,128)}, u32[]{:S(2)}, u32[]{:S(2)}) collective-permute-start(f32[64,1,48,128]{3,2,1,0:T(8,128)} %get-tuple-element.52), channel_id=1, source_target_pairs={{4,0},{8,4},{12,8},{16,12},{20,16},{24,20},{28,24},{32,28},{36,32}... | collective-permute-start | bytes 4718600 | tf_op jit(solution)/shard_map/ppermute | solution.py:161
  211.3 29.8 %collective-permute-start.11 = (f32[64,1,48,128]{3,2,1,0:T(8,128)S(1)}, f32[64,1,48,128]{3,2,1,0:T(8,128)}, u32[]{:S(2)}, u32[]{:S(2)}) collective-permute-start(f32[64,1,48,128]{3,2,1,0:T(8,128)S(1)} %get-tuple-element.51), channel_id=1, source_target_pairs={{0,4},{4,8},{8,12},{12,16},{16,20},{20,24},{24,28},{28,32},{32,36}... | collective-permute-start | bytes 4718600 | tf_op jit(solution)/shard_map/ppermute | solution.py:160
  213.3 20.3 %collective-permute-start.12 = (f32[64,2,1,128]{3,2,1,0:T(1,128)}, f32[64,2,1,128]{3,2,1,0:T(1,128)S(1)}, u32[]{:S(2)}, u32[]{:S(2)}) collective-permute-start(f32[64,2,1,128]{3,2,1,0:T(1,128)} %get-tuple-element.55), channel_id=1, source_target_pairs={{1,0},{2,1},{3,2},{5,4},{6,5},{7,6},{9,8},{10,9},{11,10},{13,12},{... | collective-permute-start | bytes 196616 | tf_op jit(solution)/shard_map/ppermute | solution.py:161
  214.6 21.0 %collective-permute-start.13 = (f32[64,2,1,128]{3,2,1,0:T(1,128)}, f32[64,2,1,128]{3,2,1,0:T(1,128)}, u32[]{:S(2)}, u32[]{:S(2)}) collective-permute-start(f32[64,2,1,128]{3,2,1,0:T(1,128)} %get-tuple-element.56), channel_id=1, source_target_pairs={{0,1},{1,2},{2,3},{4,5},{5,6},{6,7},{8,9},{9,10},{10,11},{12,13},{... | collective-permute-start | bytes 196616 | tf_op jit(solution)/shard_map/ppermute | solution.py:160
  229.5 34.8 %collective-permute-start.30 = (f32[64,1,48,128]{3,2,1,0:T(8,128)}, f32[64,1,48,128]{3,2,1,0:T(8,128)}, u32[]{:S(2)}, u32[]{:S(2)}) collective-permute-start(f32[64,1,48,128]{3,2,1,0:T(8,128)} %get-tuple-element.22), channel_id=1, source_target_pairs={{4,0},{8,4},{12,8},{16,12},{20,16},{24,20},{28,24},{32,28},{36,32}... | collective-permute-start | bytes 4718600 | tf_op jit(solution)/shard_map/ppermute | solution.py:161
  233.6 35.3 %collective-permute-start.31 = (f32[64,1,48,128]{3,2,1,0:T(8,128)}, f32[64,1,48,128]{3,2,1,0:T(8,128)}, u32[]{:S(2)}, u32[]{:S(2)}) collective-permute-start(f32[64,1,48,128]{3,2,1,0:T(8,128)} %get-tuple-element.21), channel_id=1, source_target_pairs={{0,4},{4,8},{8,12},{12,16},{16,20},{20,24},{24,28},{28,32},{32,36}... | collective-permute-start | bytes 4718600 | tf_op jit(solution)/shard_map/ppermute | solution.py:160
  235.6 25.5 %collective-permute-start.32 = (f32[64,2,1,128]{3,2,1,0:T(1,128)}, f32[64,2,1,128]{3,2,1,0:T(1,128)S(1)}, u32[]{:S(2)}, u32[]{:S(2)}) collective-permute-start(f32[64,2,1,128]{3,2,1,0:T(1,128)} %get-tuple-element.18), channel_id=1, source_target_pairs={{1,0},{2,1},{3,2},{5,4},{6,5},{7,6},{9,8},{10,9},{11,10},{13,12},{... | collective-permute-start | bytes 196616 | tf_op jit(solution)/shard_map/ppermute | solution.py:161
  236.9 26.1 %collective-permute-start.33 = (f32[64,2,1,128]{3,2,1,0:T(1,128)}, f32[64,2,1,128]{3,2,1,0:T(1,128)S(1)}, u32[]{:S(2)}, u32[]{:S(2)}) collective-permute-start(f32[64,2,1,128]{3,2,1,0:T(1,128)} %get-tuple-element.17), channel_id=1, source_target_pairs={{0,1},{1,2},{2,3},{4,5},{5,6},{6,7},{8,9},{9,10},{10,11},{12,13},{... | collective-permute-start | bytes 196616 | tf_op jit(solution)/shard_map/ppermute | solution.py:160
  256.9 26.1 %collective-permute-start.14 = (f32[64,1,48,128]{3,2,1,0:T(8,128)}, f32[64,1,48,128]{3,2,1,0:T(8,128)}, u32[]{:S(2)}, u32[]{:S(2)}) collective-permute-start(f32[64,1,48,128]{3,2,1,0:T(8,128)} %get-tuple-element.50), channel_id=1, source_target_pairs={{4,0},{8,4},{12,8},{16,12},{20,16},{24,20},{28,24},{32,28},{36,32}... | collective-permute-start | bytes 4718600 | tf_op jit(solution)/shard_map/ppermute | solution.py:161
  261.0 22.0 %collective-permute-start.15 = (f32[64,1,48,128]{3,2,1,0:T(8,128)S(1)}, f32[64,1,48,128]{3,2,1,0:T(8,128)}, u32[]{:S(2)}, u32[]{:S(2)}) collective-permute-start(f32[64,1,48,128]{3,2,1,0:T(8,128)S(1)} %get-tuple-element.49), channel_id=1, source_target_pairs={{0,4},{4,8},{8,12},{12,16},{16,20},{20,24},{24,28},{28,32},{32,36}... | collective-permute-start | bytes 4718600 | tf_op jit(solution)/shard_map/ppermute | solution.py:160
  263.0 20.1 %collective-permute-start.16 = (f32[64,2,1,128]{3,2,1,0:T(1,128)}, f32[64,2,1,128]{3,2,1,0:T(1,128)S(1)}, u32[]{:S(2)}, u32[]{:S(2)}) collective-permute-start(f32[64,2,1,128]{3,2,1,0:T(1,128)} %get-tuple-element.46), channel_id=1, source_target_pairs={{1,0},{2,1},{3,2},{5,4},{6,5},{7,6},{9,8},{10,9},{11,10},{13,12},{... | collective-permute-start | bytes 196616 | tf_op jit(solution)/shard_map/ppermute | solution.py:161
  264.3 18.8 %collective-permute-start.17 = (f32[64,2,1,128]{3,2,1,0:T(1,128)}, f32[64,2,1,128]{3,2,1,0:T(1,128)}, u32[]{:S(2)}, u32[]{:S(2)}) collective-permute-start(f32[64,2,1,128]{3,2,1,0:T(1,128)} %get-tuple-element.45), channel_id=1, source_target_pairs={{0,1},{1,2},{2,3},{4,5},{5,6},{6,7},{8,9},{9,10},{10,11},{12,13},{... | collective-permute-start | bytes 196616 | tf_op jit(solution)/shard_map/ppermute | solution.py:160
  (25 other events, 313.1 us)

commit v5 on v3

--- a/solution.py
+++ b/solution.py
@@ -113,6 +113,53 @@
     )(tiles)
 
 
+def exchange_kernel(x_ref, o_ref, send_sem, recv_sem):
+    ncol = o_ref.shape[0] // x_ref.shape[0]
+    cols = x_ref.shape[0]
+    rows = o_ref.shape[2]
+    my_slab = lax.axis_index("slab")
+    my_col = lax.axis_index("col")
+    mesh = pl.DeviceIdType.MESH
+    barrier = pltpu.get_barrier_semaphore()
+    for k in range(1, ncol):
+        peer = lax.rem(my_col + k, ncol)
+        pl.semaphore_signal(barrier, inc=1, device_id=(my_slab, peer), device_id_type=mesh)
+    pl.semaphore_wait(barrier, ncol - 1)
+
+    def chunk_copy(peer, src, dst):
+        return pltpu.make_async_remote_copy(
+            src_ref=x_ref.at[:, :, pl.ds(pl.multiple_of(src * rows, 8), rows), :],
+            dst_ref=o_ref.at[pl.ds(dst * cols, cols)],
+            send_sem=send_sem.at[src],
+            recv_sem=recv_sem.at[dst],
+            device_id=(my_slab, peer),
+            device_id_type=mesh,
+        )
+
+    for k in range(1, ncol):
+        peer = lax.rem(my_col + k, ncol)
+        chunk_copy(peer, peer, my_col).start()
+    for k in range(1, ncol):
+        peer = lax.rem(my_col + k, ncol)
+        chunk_copy(peer, peer, my_col).wait_send()
+        chunk_copy(peer, my_col, peer).wait_recv()
+
+
+def exchange(block, ncol):
+    cols, depth, rows, lanes = block.shape
+    received = pl.pallas_call(
+        exchange_kernel,
+        out_shape=jax.ShapeDtypeStruct((cols * ncol, depth, rows // ncol, lanes), block.dtype),
+        in_specs=[pl.BlockSpec(memory_space=pl.ANY)],
+        out_specs=pl.BlockSpec(memory_space=pl.ANY),
+        scratch_shapes=[pltpu.SemaphoreType.DMA((ncol,)), pltpu.SemaphoreType.DMA((ncol,))],
+        compiler_params=pltpu.CompilerParams(collective_id=1, has_side_effects=True),
+    )(block)
+    me = lax.axis_index("col")
+    own = lax.dynamic_slice_in_dim(block, me * (rows // ncol), rows // ncol, axis=2)
+    return lax.dynamic_update_slice_in_dim(received, own, me * cols, axis=0)
+
+
 def gram_kernel(a_ref, b_ref, out_ref):
     @pl.when((pl.program_id(0) == 0) & (pl.program_id(1) == 0))
     def _():
@@ -241,7 +288,7 @@
 
 def body(input_map, output_map, region_ids, region_cond, shift_ids):
     col_count = lax.axis_size("col")
-    ctrl_in = windows(input_map, input_map.shape[2] // col_count, col_count)
+    ctrl_in = exchange(input_map, col_count)
     obsv_in = windows(output_map, output_map.shape[2] // col_count, col_count)
     col_local = ctrl_in.shape[0]
     rows = ctrl_in.shape[2]

time: 340 us -> 349 us (1.026)
  Pallas kernels: 41.2 us -> 101 us
  waiting for transfers between devices: 44.4 us -> 0.09 us
  starting transfers between devices: 109 us -> 103 us
    pallas_call x0 -> x1, Pallas kernels: none -> 58.3 us  [exchange(): pl.pallas_call(exchange_kernel, out_shape=jax.ShapeDtypeStruct((cols * nc...]
    all_to_all x2 -> x1, waiting for transfers between devices: 44.3 us -> 0.01 us  [windows(): received = lax.all_to_all(jnp.stack(parts), 'col', 0, 0, tiled=True)]
    all_to_all x2 -> x1, starting transfers between devices: 9.48 us -> 4.97 us  [windows(): received = lax.all_to_all(jnp.stack(parts), 'col', 0, 0, tiled=True)]
  transfers between devices with their start and end apart: 36 -> 35, of which waited for: 2 -> 0; matrix products, arithmetic and copies ran while one was open for 33% -> 32% of each run, Pallas kernels for 0% -> 17%
where the time goes in v5:
time: 349 us; the launch traced here: 348 us
  starting transfers between devices  103 us (30%)
  Pallas kernels  101 us (29%)
  other arithmetic  86.9 us (25%)
  local copies, waits for them, and re-layouts  47.9 us (14%)
  between operations  9.15 us (3%)
    pallas_call x1, Pallas kernels, exchange(): pl.pallas_call(exchange_kernel, out_shape=jax.ShapeDtypeStruct((cols * nc...  58.3 us
    ppermute x16, starting transfers between devices, halo_pair(): lax.ppermute(lax.slice_in_dim(block, size - 1, None, axis=dim), axis, for...  55.2 us
    another operation x6, other arithmetic, run_segments(): return jnp.stack(factors)  42.1 us
    ppermute x16, starting transfers between devices, halo_pair(): high = lax.ppermute(lax.slice_in_dim(block, 0, 1, axis=dim), axis, backward)  36.6 us
    add x4, other arithmetic, solve_slabs(): rho_next * rho_now * direction + 2.0 * rho_next / half_span * residual  31.5 us
    pallas_call x1, Pallas kernels, reduce_scatter(): pl.pallas_call(reduce_kernel, out_shape=jax.ShapeDtypeStruct((1, 1, lanes...  29.1 us
    slice x14, local copies, waits for them, and re-layouts, shifted(): lax.slice_in_dim(block, 1, None, axis=dim)  25.7 us
    pallas_call x1, Pallas kernels, gram(): pl.pallas_call(gram_kernel, grid=(depth, rows // rows_per_step), in_specs...  13.2 us
  transfers between devices with their start and end apart: 35, of which 0 were waited for; matrix products, arithmetic and copies ran while one was open for 32% of the time, Pallas kernels for 17%

profile of v5, /device:TPU:1, one launch (start us, length us, event | category | flops | bytes accessed | tf_op | source)
XLA Modules:
  0.0 347.7 jit_solution(17676392108682087847)
XLA Ops:
  4.7 5.0 %all-to-all-start = ((f32[4,16,2,48,128]{4,3,2,1,0:T(8,128)}), f32[4,16,2,48,128]{4,3,2,1,0:T(8,128)S(1)}, u32[]{:S(2)}, u32[]{:S(2)}) async-start(f32[4,16,2,48,128]{4,3,2,1,0:T(8,128)} %pad_maximum_fusion.2), calls=%async_computation | async-start | bytes 6291456 | tf_op jit(solution)/shard_map/all_to_all | solution.py:233
  10.3 5.2 %select_add_fusion = f32[2,192,128]{2,1,0:T(8,128)S(1)} fusion(s32[2,192,128]{2,1,0:T(8,128)S(1)} %copy-done.14, f32[]{:T(128)} %bitcast.8, f32[]{:T(128)} %bitcast.7, f32[]{:T(128)} %bitcast.6, f32[]{:T(128)} %bitcast.5, f32[]{:T(128)} %bitcast.4, f32[]{:T(128)} %bitcast.3, f32[]{:T(128)} %bitcast.2, f32[]{:T(128)} %bitcast.1), kind=kLoop, calls=%fused_computation.206 | loop fusion | flops 1130496 | bytes 393248 | tf_op jit(solution)/shard_map/add | solution.py:198
  18.4 3.4 collective-permute-start.2
  21.9 58.3 %shard_map.76 = f32[64,2,48,128]{3,2,1,0:T(8,128)} custom-call(f32[16,2,192,128]{3,2,1,0:T(8,128)} %x_ref.1), custom_call_target="tpu_custom_call" | custom-call | tf_op jit(solution)/shard_map/pallas_call | solution.py:150
  96.6 3.8 %collective-permute-start.18 = (f32[64,1,48,128]{3,2,1,0:T(8,128)S(1)}, f32[64,1,48,128]{3,2,1,0:T(8,128)S(1)}, u32[]{:S(2)}, u32[]{:S(2)}) collective-permute-start(f32[64,1,48,128]{3,2,1,0:T(8,128)S(1)} %get-tuple-element.36), channel_id=1, source_target_pairs={{4,0},{8,4},{12,8},{16,12},{20,16},{24,20},{28,24},{32,28},{36,32}... | collective-permute-start | bytes 4718600 | tf_op jit(solution)/shard_map/ppermute | solution.py:208
  100.4 3.4 collective-permute-start.19
  105.3 4.0 %collective-permute-start.21 = (f32[64,2,1,128]{3,2,1,0:T(1,128)S(1)}, f32[64,2,1,128]{3,2,1,0:T(1,128)S(1)}, u32[]{:S(2)}, u32[]{:S(2)}) collective-permute-start(f32[64,2,1,128]{3,2,1,0:T(1,128)S(1)} %get-tuple-element.40), channel_id=1, source_target_pairs={{0,1},{1,2},{2,3},{4,5},{5,6},{6,7},{8,9},{9,10},{10,11},{12,13},{... | collective-permute-start | bytes 196616 | tf_op jit(solution)/shard_map/ppermute | solution.py:207
  117.1 3.6 %collective-permute-start.3 = (f32[64,1,48,128]{3,2,1,0:T(8,128)}, f32[64,1,48,128]{3,2,1,0:T(8,128)}, u32[]{:S(2)}, u32[]{:S(2)}) collective-permute-start(f32[64,1,48,128]{3,2,1,0:T(8,128)} %get-tuple-element.63), channel_id=1, source_target_pairs={{0,4},{4,8},{8,12},{12,16},{16,20},{20,24},{24,28},{28,32},{32,36}... | collective-permute-start | bytes 4718600 | tf_op jit(solution)/shard_map/ppermute | solution.py:207
  122.1 4.6 %collective-permute-start.5 = (f32[64,2,1,128]{3,2,1,0:T(1,128)}, f32[64,2,1,128]{3,2,1,0:T(1,128)}, u32[]{:S(2)}, u32[]{:S(2)}) collective-permute-start(f32[64,2,1,128]{3,2,1,0:T(1,128)} %get-tuple-element.68), channel_id=1, source_target_pairs={{0,1},{1,2},{2,3},{4,5},{5,6},{6,7},{8,9},{9,10},{10,11},{12,13},{... | collective-permute-start | bytes 196616 | tf_op jit(solution)/shard_map/ppermute | solution.py:207
  127.9 7.8 %multiply_add_fusion.1 = (f32[64,2,48,128]{3,2,1,0:T(8,128)S(1)}, f32[64,2,48,128]{3,2,1,0:T(8,128)}) fusion(f32[64,2,48,128]{3,2,1,0:T(8,128)S(1)} %get-tuple-element.88, f32[]{:T(128)S(6)} %div.73, f32[]{:T(128)S(6)} %mul.262, f32[]{:T(128)} %bitcast, f32[2,48,128]{2,1,0:T(8,128)S(1)} %get-tuple-element.74, f32[2,48,128]{2,1,0:T(8,128)S(1)} %copy-done.10, ...), kind=kLoop, calls=%fused_computation.194 | loop fusion | flops 21233664 | bytes 25460748 | tf_op jit(solution)/shard_map/add | solution.py:271
  145.4 4.0 %collective-permute-start.25 = (f32[64,2,1,128]{3,2,1,0:T(1,128)}, f32[64,2,1,128]{3,2,1,0:T(1,128)S(1)}, u32[]{:S(2)}, u32[]{:S(2)}) collective-permute-start(f32[64,2,1,128]{3,2,1,0:T(1,128)} %get-tuple-element.34), channel_id=1, source_target_pairs={{0,1},{1,2},{2,3},{4,5},{5,6},{6,7},{8,9},{9,10},{10,11},{12,13},{... | collective-permute-start | bytes 196616 | tf_op jit(solution)/shard_map/ppermute | solution.py:207
  149.4 8.1 %multiply_add_fusion.3 = (f32[64,2,48,128]{3,2,1,0:T(8,128)S(1)}, f32[64,2,48,128]{3,2,1,0:T(8,128)}) fusion(f32[64,2,48,128]{3,2,1,0:T(8,128)S(1)} %get-tuple-element.89, f32[]{:T(128)S(6)} %div.73, f32[]{:T(128)S(6)} %mul.262, f32[64,2,48,128]{3,2,1,0:T(8,128)S(1)} %copy-done, f32[]{:T(128)} %bitcast, f32[2,48,128]{2,1,0:T(8,128)S(1)} %get-tuple-element.74, ...), kind=kLoop, calls=%fused_computation.197 | loop fusion | flops 21233664 | bytes 25460748 | tf_op jit(solution)/shard_map/add | solution.py:271
  158.9 3.5 %fusion.165 = (f32[64,2,47,128]{3,2,1,0:T(8,128)}, f32[64,2,47,128]{3,2,1,0:T(8,128)}) fusion(f32[64,2,48,128]{3,2,1,0:T(8,128)S(1)} %get-tuple-element.7), kind=kLoop, calls=%fused_computation.238 | loop fusion | bytes 12320768 | tf_op jit(solution)/shard_map/slice | solution.py:214
  172.9 4.2 %collective-permute-start.9 = (f32[64,2,1,128]{3,2,1,0:T(1,128)}, f32[64,2,1,128]{3,2,1,0:T(1,128)S(1)}, u32[]{:S(2)}, u32[]{:S(2)}) collective-permute-start(f32[64,2,1,128]{3,2,1,0:T(1,128)} %get-tuple-element.62), channel_id=1, source_target_pairs={{0,1},{1,2},{2,3},{4,5},{5,6},{6,7},{8,9},{9,10},{10,11},{12,13},{... | collective-permute-start | bytes 196616 | tf_op jit(solution)/shard_map/ppermute | solution.py:207
  177.1 9.2 %multiply_bitcast_fusion = (f32[1,64,2,48,128]{4,3,2,1,0:T(8,128)}, f32[64,2,48,128]{3,2,1,0:T(8,128)S(1)}) fusion(f32[]{:T(128)S(6)} %sqrt.8, f32[64,2,48,128]{3,2,1,0:T(8,128)} %get-tuple-element.8, f32[64,2,48,128]{3,2,1,0:T(8,128)S(1)} %get-tuple-element.7, f32[]{:T(128)} %bitcast, f32[2,48,128]{2,1,0:T(8,128)S(1)} %get-tuple-element.74, ...), kind=kLoop, calls=%fused_computation.193 | loop fusion | flops 23592960 | bytes 28606480 | tf_op jit(solution)/shard_map/stack | solution.py:286
  189.4 3.3 collective-permute-start.26
  196.9 4.0 %collective-permute-start.29 = (f32[64,2,1,128]{3,2,1,0:T(1,128)}, f32[64,2,1,128]{3,2,1,0:T(1,128)S(1)}, u32[]{:S(2)}, u32[]{:S(2)}) collective-permute-start(f32[64,2,1,128]{3,2,1,0:T(1,128)} %get-tuple-element.28), channel_id=1, source_target_pairs={{0,1},{1,2},{2,3},{4,5},{5,6},{6,7},{8,9},{9,10},{10,11},{12,13},{... | collective-permute-start | bytes 196616 | tf_op jit(solution)/shard_map/ppermute | solution.py:207
  200.9 8.4 %multiply_bitcast_fusion.1 = (f32[1,64,2,48,128]{4,3,2,1,0:T(8,128)}, f32[64,2,48,128]{3,2,1,0:T(8,128)S(1)}) fusion(f32[]{:T(128)S(6)} %sqrt.8, f32[64,2,48,128]{3,2,1,0:T(8,128)} %get-tuple-element.14, f32[64,2,48,128]{3,2,1,0:T(8,128)S(1)} %get-tuple-element.13, f32[]{:T(128)} %bitcast, f32[2,48,128]{2,1,0:T(8,128)S(1)} %get-tuple-element.74, ...), kind=kLoop, calls=%fused_computation.196 | loop fusion | flops 23592960 | bytes 28606480 | tf_op jit(solution)/shard_map/stack | solution.py:286
  216.2 3.8 %collective-permute-start.10 = (f32[64,1,48,128]{3,2,1,0:T(8,128)}, f32[64,1,48,128]{3,2,1,0:T(8,128)}, u32[]{:S(2)}, u32[]{:S(2)}) collective-permute-start(f32[64,1,48,128]{3,2,1,0:T(8,128)} %get-tuple-element.52), channel_id=1, source_target_pairs={{4,0},{8,4},{12,8},{16,12},{20,16},{24,20},{28,24},{32,28},{36,32}... | collective-permute-start | bytes 4718600 | tf_op jit(solution)/shard_map/ppermute | solution.py:208
  223.3 4.6 %collective-permute-start.13 = (f32[64,2,1,128]{3,2,1,0:T(1,128)}, f32[64,2,1,128]{3,2,1,0:T(1,128)}, u32[]{:S(2)}, u32[]{:S(2)}) collective-permute-start(f32[64,2,1,128]{3,2,1,0:T(1,128)} %get-tuple-element.56), channel_id=1, source_target_pairs={{0,1},{1,2},{2,3},{4,5},{5,6},{6,7},{8,9},{9,10},{10,11},{12,13},{... | collective-permute-start | bytes 196616 | tf_op jit(solution)/shard_map/ppermute | solution.py:207
  227.9 7.7 %multiply_add_fusion = (f32[64,2,48,128]{3,2,1,0:T(8,128)S(1)}, f32[64,2,48,128]{3,2,1,0:T(8,128)}) fusion(f32[]{:T(128)S(6)} %div.81, f32[]{:T(128)S(6)} %mul.612, f32[64,2,48,128]{3,2,1,0:T(8,128)S(1)} %get-tuple-element.4, f32[]{:T(128)S(6)} %mul.609, f32[64,2,48,128]{3,2,1,0:T(8,128)S(1)} %broadcast_divide_fusion, f32[]{:T(128)} %bitcast.10, ...), kind=kLoop, calls=%fused_computation.192 | loop fusion | flops 22020096 | bytes 25460752 | tf_op jit(solution)/shard_map/add | solution.py:271
  238.3 4.1 %collective-permute-start.30 = (f32[64,1,48,128]{3,2,1,0:T(8,128)}, f32[64,1,48,128]{3,2,1,0:T(8,128)}, u32[]{:S(2)}, u32[]{:S(2)}) collective-permute-start(f32[64,1,48,128]{3,2,1,0:T(8,128)} %get-tuple-element.22), channel_id=1, source_target_pairs={{4,0},{8,4},{12,8},{16,12},{20,16},{24,20},{28,24},{32,28},{36,32}... | collective-permute-start | bytes 4718600 | tf_op jit(solution)/shard_map/ppermute | solution.py:208
  245.6 4.2 %collective-permute-start.33 = (f32[64,2,1,128]{3,2,1,0:T(1,128)}, f32[64,2,1,128]{3,2,1,0:T(1,128)S(1)}, u32[]{:S(2)}, u32[]{:S(2)}) collective-permute-start(f32[64,2,1,128]{3,2,1,0:T(1,128)} %get-tuple-element.17), channel_id=1, source_target_pairs={{0,1},{1,2},{2,3},{4,5},{5,6},{6,7},{8,9},{9,10},{10,11},{12,13},{... | collective-permute-start | bytes 196616 | tf_op jit(solution)/shard_map/ppermute | solution.py:207
  249.9 7.8 %multiply_add_fusion.2 = (f32[64,2,48,128]{3,2,1,0:T(8,128)S(1)}, f32[64,2,48,128]{3,2,1,0:T(8,128)}) fusion(f32[]{:T(128)S(6)} %div.81, f32[]{:T(128)S(6)} %mul.612, f32[64,2,48,128]{3,2,1,0:T(8,128)S(1)} %get-tuple-element.10, f32[]{:T(128)S(6)} %mul.609, f32[64,2,48,128]{3,2,1,0:T(8,128)S(1)} %broadcast_divide_fusion.1, f32[]{:T(128)} %bitcast.10, ...), kind=kLoop, calls=%fused_computation.195 | loop fusion | flops 22020096 | bytes 25460752 | tf_op jit(solution)/shard_map/add | solution.py:271
  259.1 3.5 fusion.159
  265.7 4.1 %collective-permute-start.14 = (f32[64,1,48,128]{3,2,1,0:T(8,128)}, f32[64,1,48,128]{3,2,1,0:T(8,128)}, u32[]{:S(2)}, u32[]{:S(2)}) collective-permute-start(f32[64,1,48,128]{3,2,1,0:T(8,128)} %get-tuple-element.50), channel_id=1, source_target_pairs={{4,0},{8,4},{12,8},{16,12},{20,16},{24,20},{28,24},{32,28},{36,32}... | collective-permute-start | bytes 4718600 | tf_op jit(solution)/shard_map/ppermute | solution.py:208
  273.0 4.6 %collective-permute-start.17 = (f32[64,2,1,128]{3,2,1,0:T(1,128)}, f32[64,2,1,128]{3,2,1,0:T(1,128)}, u32[]{:S(2)}, u32[]{:S(2)}) collective-permute-start(f32[64,2,1,128]{3,2,1,0:T(1,128)} %get-tuple-element.45), channel_id=1, source_target_pairs={{0,1},{1,2},{2,3},{4,5},{5,6},{6,7},{8,9},{9,10},{10,11},{12,13},{... | collective-permute-start | bytes 196616 | tf_op jit(solution)/shard_map/ppermute | solution.py:207
  277.7 8.8 %fusion.81 = f32[1,64,2,48,128]{4,3,2,1,0:T(8,128)} fusion(f32[64,2,48,128]{3,2,1,0:T(8,128)S(1)} %get-tuple-element.4, f32[64,2,48,128]{3,2,1,0:T(8,128)S(1)} %copy-done.2, f32[64,2,48,128]{3,2,1,0:T(8,128)S(1)} %get-tuple-element.5, f32[64,1,48,128]{3,2,1,0:T(8,128)} %collective-permute-done.30, f32[64,1,48,128]{3,2,1,0:T(8,128)} %get-tuple-element.21, ...), kind=kLoop, calls=%fused_computation.99 | loop fusion | flops 25952256 | bytes 25460760 | tf_op jit(solution)/shard_map/stack | solution.py:286
  286.5 5.3 %pad_maximum_fusion.1 = f32[2,64,2,48,128]{4,3,2,1,0:T(8,128)} fusion(f32[1,64,2,48,128]{4,3,2,1,0:T(8,128)} %fusion.81, f32[1,64,2,48,128]{4,3,2,1,0:T(8,128)S(1)} %copy-done.4), kind=kLoop, calls=%fused_computation.17 | loop fusion | flops 1572864 | bytes 12582912 | tf_op jit(solution)/shard_map/stack | solution.py:286
  291.8 7.3 %fusion.39 = f32[1,64,2,48,128]{4,3,2,1,0:T(8,128)S(1)} fusion(f32[64,2,48,128]{3,2,1,0:T(8,128)S(1)} %get-tuple-element.10, f32[64,2,48,128]{3,2,1,0:T(8,128)S(1)} %copy-done.3, f32[64,2,48,128]{3,2,1,0:T(8,128)S(1)} %get-tuple-element.11, f32[64,1,48,128]{3,2,1,0:T(8,128)} %collective-permute-done.14, f32[64,1,48,128]{3,2,1,0:T(8,128)S(1)} %get-tuple-element.49, ...), kind=kLoop, calls=%fused_computation.57 | loop fusion | flops 25952256 | bytes 25460760 | tf_op jit(solution)/shard_map/stack | solution.py:286
  302.3 13.2 %shard_map.77 = f32[128,128]{1,0:T(8,128)} custom-call(f32[128,2,48,128]{3,2,1,0:T(8,128)} %bitcast.36, f32[128,2,48,128]{3,2,1,0:T(8,128)} %bitcast.35), custom_call_target="tpu_custom_call" | custom-call | flops 402653184 | bytes 12582912 | tf_op jit(solution)/shard_map/pallas_call | solution.py:183
  317.3 29.1 %shard_map.78 = f32[1,1,128]{2,1,0:T(1,128)} custom-call(f32[4,32,128]{2,1,0:T(8,128)} %reshape.34.tiles_ref), custom_call_target="tpu_custom_call" | custom-call | tf_op jit(solution)/shard_map/pallas_call | solution.py:98
  (135 shorter events, 86.7 us)
Async XLA Ops:
  4.7 88.8 %all-to-all-start = ((f32[4,16,2,48,128]{4,3,2,1,0:T(8,128)}), f32[4,16,2,48,128]{4,3,2,1,0:T(8,128)S(1)}, u32[]{:S(2)}, u32[]{:S(2)}) async-start(f32[4,16,2,48,128]{4,3,2,1,0:T(8,128)} %pad_maximum_fusion.2), calls=%async_computation | async-start | bytes 6291456 | tf_op jit(solution)/shard_map/all_to_all | solution.py:233
  15.6 75.8 %collective-permute-start = (f32[1,50,128]{2,1,0:T(8,128)S(1)}, f32[1,50,128]{2,1,0:T(8,128)S(1)}, u32[]{:S(2)}, u32[]{:S(2)}) collective-permute-start(f32[1,50,128]{2,1,0:T(8,128)S(1)} %get-tuple-element.72), channel_id=1, source_target_pairs={{4,0},{8,4},{12,8},{16,12},{20,16},{24,20},{28,24},{32,28},{36,32}... | collective-permute-start | bytes 76808 | tf_op jit(solution)/shard_map/ppermute | solution.py:22
  18.4 73.0 %collective-permute-start.2 = (f32[1,50,128]{2,1,0:T(8,128)S(1)}, f32[1,50,128]{2,1,0:T(8,128)S(1)}, u32[]{:S(2)}, u32[]{:S(2)}) collective-permute-start(f32[1,50,128]{2,1,0:T(8,128)S(1)} %get-tuple-element.71), channel_id=1, source_target_pairs={{0,4},{4,8},{8,12},{12,16},{16,20},{20,24},{24,28},{28,32},{32,36}... | collective-permute-start | bytes 76808 | tf_op jit(solution)/shard_map/ppermute | solution.py:19
  96.6 25.4 %collective-permute-start.18 = (f32[64,1,48,128]{3,2,1,0:T(8,128)S(1)}, f32[64,1,48,128]{3,2,1,0:T(8,128)S(1)}, u32[]{:S(2)}, u32[]{:S(2)}) collective-permute-start(f32[64,1,48,128]{3,2,1,0:T(8,128)S(1)} %get-tuple-element.36), channel_id=1, source_target_pairs={{4,0},{8,4},{12,8},{16,12},{20,16},{24,20},{28,24},{32,28},{36,32}... | collective-permute-start | bytes 4718600 | tf_op jit(solution)/shard_map/ppermute | solution.py:208
  100.4 26.3 %collective-permute-start.19 = (f32[64,1,48,128]{3,2,1,0:T(8,128)S(1)}, f32[64,1,48,128]{3,2,1,0:T(8,128)S(1)}, u32[]{:S(2)}, u32[]{:S(2)}) collective-permute-start(f32[64,1,48,128]{3,2,1,0:T(8,128)S(1)} %get-tuple-element.35), channel_id=1, source_target_pairs={{0,4},{4,8},{8,12},{12,16},{16,20},{20,24},{24,28},{28,32},{32,36}... | collective-permute-start | bytes 4718600 | tf_op jit(solution)/shard_map/ppermute | solution.py:207
  115.2 30.2 %collective-permute-start.1 = (f32[64,1,48,128]{3,2,1,0:T(8,128)}, f32[64,1,48,128]{3,2,1,0:T(8,128)}, u32[]{:S(2)}, u32[]{:S(2)}) collective-permute-start(f32[64,1,48,128]{3,2,1,0:T(8,128)} %get-tuple-element.64), channel_id=1, source_target_pairs={{4,0},{8,4},{12,8},{16,12},{20,16},{24,20},{28,24},{32,28},{36,32}... | collective-permute-start | bytes 4718600 | tf_op jit(solution)/shard_map/ppermute | solution.py:208
  117.1 32.3 %collective-permute-start.3 = (f32[64,1,48,128]{3,2,1,0:T(8,128)}, f32[64,1,48,128]{3,2,1,0:T(8,128)}, u32[]{:S(2)}, u32[]{:S(2)}) collective-permute-start(f32[64,1,48,128]{3,2,1,0:T(8,128)} %get-tuple-element.63), channel_id=1, source_target_pairs={{0,4},{4,8},{8,12},{12,16},{16,20},{20,24},{24,28},{28,32},{32,36}... | collective-permute-start | bytes 4718600 | tf_op jit(solution)/shard_map/ppermute | solution.py:207
  120.8 20.1 %collective-permute-start.4 = (f32[64,2,1,128]{3,2,1,0:T(1,128)}, f32[64,2,1,128]{3,2,1,0:T(1,128)S(1)}, u32[]{:S(2)}, u32[]{:S(2)}) collective-permute-start(f32[64,2,1,128]{3,2,1,0:T(1,128)} %get-tuple-element.67), channel_id=1, source_target_pairs={{1,0},{2,1},{3,2},{5,4},{6,5},{7,6},{9,8},{10,9},{11,10},{13,12},{... | collective-permute-start | bytes 196616 | tf_op jit(solution)/shard_map/ppermute | solution.py:208
  122.1 22.0 %collective-permute-start.5 = (f32[64,2,1,128]{3,2,1,0:T(1,128)}, f32[64,2,1,128]{3,2,1,0:T(1,128)}, u32[]{:S(2)}, u32[]{:S(2)}) collective-permute-start(f32[64,2,1,128]{3,2,1,0:T(1,128)} %get-tuple-element.68), channel_id=1, source_target_pairs={{0,1},{1,2},{2,3},{4,5},{5,6},{6,7},{8,9},{9,10},{10,11},{12,13},{... | collective-permute-start | bytes 196616 | tf_op jit(solution)/shard_map/ppermute | solution.py:207
  138.4 34.6 %collective-permute-start.22 = (f32[64,1,48,128]{3,2,1,0:T(8,128)}, f32[64,1,48,128]{3,2,1,0:T(8,128)}, u32[]{:S(2)}, u32[]{:S(2)}) collective-permute-start(f32[64,1,48,128]{3,2,1,0:T(8,128)} %get-tuple-element.30), channel_id=1, source_target_pairs={{4,0},{8,4},{12,8},{16,12},{20,16},{24,20},{28,24},{32,28},{36,32}... | collective-permute-start | bytes 4718600 | tf_op jit(solution)/shard_map/ppermute | solution.py:208
  140.9 36.2 %collective-permute-start.23 = (f32[64,1,48,128]{3,2,1,0:T(8,128)}, f32[64,1,48,128]{3,2,1,0:T(8,128)}, u32[]{:S(2)}, u32[]{:S(2)}) collective-permute-start(f32[64,1,48,128]{3,2,1,0:T(8,128)} %get-tuple-element.29), channel_id=1, source_target_pairs={{0,4},{4,8},{8,12},{12,16},{16,20},{20,24},{24,28},{28,32},{32,36}... | collective-permute-start | bytes 4718600 | tf_op jit(solution)/shard_map/ppermute | solution.py:207
  144.1 24.2 %collective-permute-start.24 = (f32[64,2,1,128]{3,2,1,0:T(1,128)}, f32[64,2,1,128]{3,2,1,0:T(1,128)S(1)}, u32[]{:S(2)}, u32[]{:S(2)}) collective-permute-start(f32[64,2,1,128]{3,2,1,0:T(1,128)} %get-tuple-element.33), channel_id=1, source_target_pairs={{1,0},{2,1},{3,2},{5,4},{6,5},{7,6},{9,8},{10,9},{11,10},{13,12},{... | collective-permute-start | bytes 196616 | tf_op jit(solution)/shard_map/ppermute | solution.py:208
  145.4 25.6 %collective-permute-start.25 = (f32[64,2,1,128]{3,2,1,0:T(1,128)}, f32[64,2,1,128]{3,2,1,0:T(1,128)S(1)}, u32[]{:S(2)}, u32[]{:S(2)}) collective-permute-start(f32[64,2,1,128]{3,2,1,0:T(1,128)} %get-tuple-element.34), channel_id=1, source_target_pairs={{0,1},{1,2},{2,3},{4,5},{5,6},{6,7},{8,9},{9,10},{10,11},{12,13},{... | collective-permute-start | bytes 196616 | tf_op jit(solution)/shard_map/ppermute | solution.py:207
  165.4 31.5 %collective-permute-start.6 = (f32[64,1,48,128]{3,2,1,0:T(8,128)}, f32[64,1,48,128]{3,2,1,0:T(8,128)}, u32[]{:S(2)}, u32[]{:S(2)}) collective-permute-start(f32[64,1,48,128]{3,2,1,0:T(8,128)} %get-tuple-element.58), channel_id=1, source_target_pairs={{4,0},{8,4},{12,8},{16,12},{20,16},{24,20},{28,24},{32,28},{36,32}... | collective-permute-start | bytes 4718600 | tf_op jit(solution)/shard_map/ppermute | solution.py:208
  168.3 32.6 %collective-permute-start.7 = (f32[64,1,48,128]{3,2,1,0:T(8,128)S(1)}, f32[64,1,48,128]{3,2,1,0:T(8,128)}, u32[]{:S(2)}, u32[]{:S(2)}) collective-permute-start(f32[64,1,48,128]{3,2,1,0:T(8,128)S(1)} %get-tuple-element.57), channel_id=1, source_target_pairs={{0,4},{4,8},{8,12},{12,16},{16,20},{20,24},{24,28},{28,32},{32,36}... | collective-permute-start | bytes 4718600 | tf_op jit(solution)/shard_map/ppermute | solution.py:207
  171.7 21.0 %collective-permute-start.8 = (f32[64,2,1,128]{3,2,1,0:T(1,128)}, f32[64,2,1,128]{3,2,1,0:T(1,128)S(1)}, u32[]{:S(2)}, u32[]{:S(2)}) collective-permute-start(f32[64,2,1,128]{3,2,1,0:T(1,128)} %get-tuple-element.61), channel_id=1, source_target_pairs={{1,0},{2,1},{3,2},{5,4},{6,5},{7,6},{9,8},{10,9},{11,10},{13,12},{... | collective-permute-start | bytes 196616 | tf_op jit(solution)/shard_map/ppermute | solution.py:208
  172.9 22.0 %collective-permute-start.9 = (f32[64,2,1,128]{3,2,1,0:T(1,128)}, f32[64,2,1,128]{3,2,1,0:T(1,128)S(1)}, u32[]{:S(2)}, u32[]{:S(2)}) collective-permute-start(f32[64,2,1,128]{3,2,1,0:T(1,128)} %get-tuple-element.62), channel_id=1, source_target_pairs={{0,1},{1,2},{2,3},{4,5},{5,6},{6,7},{8,9},{9,10},{10,11},{12,13},{... | collective-permute-start | bytes 196616 | tf_op jit(solution)/shard_map/ppermute | solution.py:207
  189.4 33.9 %collective-permute-start.26 = (f32[64,1,48,128]{3,2,1,0:T(8,128)}, f32[64,1,48,128]{3,2,1,0:T(8,128)}, u32[]{:S(2)}, u32[]{:S(2)}) collective-permute-start(f32[64,1,48,128]{3,2,1,0:T(8,128)} %get-tuple-element.24), channel_id=1, source_target_pairs={{4,0},{8,4},{12,8},{16,12},{20,16},{24,20},{28,24},{32,28},{36,32}... | collective-permute-start | bytes 4718600 | tf_op jit(solution)/shard_map/ppermute | solution.py:208
  192.7 35.2 %collective-permute-start.27 = (f32[64,1,48,128]{3,2,1,0:T(8,128)}, f32[64,1,48,128]{3,2,1,0:T(8,128)}, u32[]{:S(2)}, u32[]{:S(2)}) collective-permute-start(f32[64,1,48,128]{3,2,1,0:T(8,128)} %get-tuple-element.23), channel_id=1, source_target_pairs={{0,4},{4,8},{8,12},{12,16},{16,20},{20,24},{24,28},{28,32},{32,36}... | collective-permute-start | bytes 4718600 | tf_op jit(solution)/shard_map/ppermute | solution.py:207
  195.6 24.4 %collective-permute-start.28 = (f32[64,2,1,128]{3,2,1,0:T(1,128)}, f32[64,2,1,128]{3,2,1,0:T(1,128)S(1)}, u32[]{:S(2)}, u32[]{:S(2)}) collective-permute-start(f32[64,2,1,128]{3,2,1,0:T(1,128)} %get-tuple-element.27), channel_id=1, source_target_pairs={{1,0},{2,1},{3,2},{5,4},{6,5},{7,6},{9,8},{10,9},{11,10},{13,12},{... | collective-permute-start | bytes 196616 | tf_op jit(solution)/shard_map/ppermute | solution.py:208
  196.9 25.1 %collective-permute-start.29 = (f32[64,2,1,128]{3,2,1,0:T(1,128)}, f32[64,2,1,128]{3,2,1,0:T(1,128)S(1)}, u32[]{:S(2)}, u32[]{:S(2)}) collective-permute-start(f32[64,2,1,128]{3,2,1,0:T(1,128)} %get-tuple-element.28), channel_id=1, source_target_pairs={{0,1},{1,2},{2,3},{4,5},{5,6},{6,7},{8,9},{9,10},{10,11},{12,13},{... | collective-permute-start | bytes 196616 | tf_op jit(solution)/shard_map/ppermute | solution.py:207
  216.2 29.4 %collective-permute-start.10 = (f32[64,1,48,128]{3,2,1,0:T(8,128)}, f32[64,1,48,128]{3,2,1,0:T(8,128)}, u32[]{:S(2)}, u32[]{:S(2)}) collective-permute-start(f32[64,1,48,128]{3,2,1,0:T(8,128)} %get-tuple-element.52), channel_id=1, source_target_pairs={{4,0},{8,4},{12,8},{16,12},{20,16},{24,20},{28,24},{32,28},{36,32}... | collective-permute-start | bytes 4718600 | tf_op jit(solution)/shard_map/ppermute | solution.py:208
  220.0 29.8 %collective-permute-start.11 = (f32[64,1,48,128]{3,2,1,0:T(8,128)S(1)}, f32[64,1,48,128]{3,2,1,0:T(8,128)}, u32[]{:S(2)}, u32[]{:S(2)}) collective-permute-start(f32[64,1,48,128]{3,2,1,0:T(8,128)S(1)} %get-tuple-element.51), channel_id=1, source_target_pairs={{0,4},{4,8},{8,12},{12,16},{16,20},{20,24},{24,28},{28,32},{32,36}... | collective-permute-start | bytes 4718600 | tf_op jit(solution)/shard_map/ppermute | solution.py:207
  222.0 20.4 %collective-permute-start.12 = (f32[64,2,1,128]{3,2,1,0:T(1,128)}, f32[64,2,1,128]{3,2,1,0:T(1,128)S(1)}, u32[]{:S(2)}, u32[]{:S(2)}) collective-permute-start(f32[64,2,1,128]{3,2,1,0:T(1,128)} %get-tuple-element.55), channel_id=1, source_target_pairs={{1,0},{2,1},{3,2},{5,4},{6,5},{7,6},{9,8},{10,9},{11,10},{13,12},{... | collective-permute-start | bytes 196616 | tf_op jit(solution)/shard_map/ppermute | solution.py:208
  223.3 21.0 %collective-permute-start.13 = (f32[64,2,1,128]{3,2,1,0:T(1,128)}, f32[64,2,1,128]{3,2,1,0:T(1,128)}, u32[]{:S(2)}, u32[]{:S(2)}) collective-permute-start(f32[64,2,1,128]{3,2,1,0:T(1,128)} %get-tuple-element.56), channel_id=1, source_target_pairs={{0,1},{1,2},{2,3},{4,5},{5,6},{6,7},{8,9},{9,10},{10,11},{12,13},{... | collective-permute-start | bytes 196616 | tf_op jit(solution)/shard_map/ppermute | solution.py:207
  238.3 34.8 %collective-permute-start.30 = (f32[64,1,48,128]{3,2,1,0:T(8,128)}, f32[64,1,48,128]{3,2,1,0:T(8,128)}, u32[]{:S(2)}, u32[]{:S(2)}) collective-permute-start(f32[64,1,48,128]{3,2,1,0:T(8,128)} %get-tuple-element.22), channel_id=1, source_target_pairs={{4,0},{8,4},{12,8},{16,12},{20,16},{24,20},{28,24},{32,28},{36,32}... | collective-permute-start | bytes 4718600 | tf_op jit(solution)/shard_map/ppermute | solution.py:208
  242.4 35.3 %collective-permute-start.31 = (f32[64,1,48,128]{3,2,1,0:T(8,128)}, f32[64,1,48,128]{3,2,1,0:T(8,128)}, u32[]{:S(2)}, u32[]{:S(2)}) collective-permute-start(f32[64,1,48,128]{3,2,1,0:T(8,128)} %get-tuple-element.21), channel_id=1, source_target_pairs={{0,4},{4,8},{8,12},{12,16},{16,20},{20,24},{24,28},{28,32},{32,36}... | collective-permute-start | bytes 4718600 | tf_op jit(solution)/shard_map/ppermute | solution.py:207
  244.3 25.5 %collective-permute-start.32 = (f32[64,2,1,128]{3,2,1,0:T(1,128)}, f32[64,2,1,128]{3,2,1,0:T(1,128)S(1)}, u32[]{:S(2)}, u32[]{:S(2)}) collective-permute-start(f32[64,2,1,128]{3,2,1,0:T(1,128)} %get-tuple-element.18), channel_id=1, source_target_pairs={{1,0},{2,1},{3,2},{5,4},{6,5},{7,6},{9,8},{10,9},{11,10},{13,12},{... | collective-permute-start | bytes 196616 | tf_op jit(solution)/shard_map/ppermute | solution.py:208
  245.6 26.1 %collective-permute-start.33 = (f32[64,2,1,128]{3,2,1,0:T(1,128)}, f32[64,2,1,128]{3,2,1,0:T(1,128)S(1)}, u32[]{:S(2)}, u32[]{:S(2)}) collective-permute-start(f32[64,2,1,128]{3,2,1,0:T(1,128)} %get-tuple-element.17), channel_id=1, source_target_pairs={{0,1},{1,2},{2,3},{4,5},{5,6},{6,7},{8,9},{9,10},{10,11},{12,13},{... | collective-permute-start | bytes 196616 | tf_op jit(solution)/shard_map/ppermute | solution.py:207
  265.7 26.1 %collective-permute-start.14 = (f32[64,1,48,128]{3,2,1,0:T(8,128)}, f32[64,1,48,128]{3,2,1,0:T(8,128)}, u32[]{:S(2)}, u32[]{:S(2)}) collective-permute-start(f32[64,1,48,128]{3,2,1,0:T(8,128)} %get-tuple-element.50), channel_id=1, source_target_pairs={{4,0},{8,4},{12,8},{16,12},{20,16},{24,20},{28,24},{32,28},{36,32}... | collective-permute-start | bytes 4718600 | tf_op jit(solution)/shard_map/ppermute | solution.py:208
  269.8 22.0 %collective-permute-start.15 = (f32[64,1,48,128]{3,2,1,0:T(8,128)S(1)}, f32[64,1,48,128]{3,2,1,0:T(8,128)}, u32[]{:S(2)}, u32[]{:S(2)}) collective-permute-start(f32[64,1,48,128]{3,2,1,0:T(8,128)S(1)} %get-tuple-element.49), channel_id=1, source_target_pairs={{0,4},{4,8},{8,12},{12,16},{16,20},{20,24},{24,28},{28,32},{32,36}... | collective-permute-start | bytes 4718600 | tf_op jit(solution)/shard_map/ppermute | solution.py:207
  271.7 20.0 %collective-permute-start.16 = (f32[64,2,1,128]{3,2,1,0:T(1,128)}, f32[64,2,1,128]{3,2,1,0:T(1,128)S(1)}, u32[]{:S(2)}, u32[]{:S(2)}) collective-permute-start(f32[64,2,1,128]{3,2,1,0:T(1,128)} %get-tuple-element.46), channel_id=1, source_target_pairs={{1,0},{2,1},{3,2},{5,4},{6,5},{7,6},{9,8},{10,9},{11,10},{13,12},{... | collective-permute-start | bytes 196616 | tf_op jit(solution)/shard_map/ppermute | solution.py:208
  (23 other events, 266.9 us)

commit v6 on v3

--- a/solution.py
+++ b/solution.py
@@ -130,7 +130,7 @@
     )
 
 
-def gram(a, b, rows_per_step=16):
+def gram(a, b, rows_per_step=48):
     count, depth, rows, lanes = a.shape
     spec = pl.BlockSpec((count, 1, rows_per_step, lanes), lambda i, j: (0, i, j, 0))
     return pl.pallas_call(

time: 340 us -> 340 us (level)
  no operation moved by 1% of the time
where the time goes in v6:
time: 340 us; the launch traced here: 338 us
  starting transfers between devices  108 us (32%)
  other arithmetic  88.1 us (26%)
  local copies, waits for them, and re-layouts  46.4 us (14%)
  waiting for transfers between devices  44.4 us (13%)
  Pallas kernels  41.8 us (12%)
  between operations  9.03 us (3%)
    ppermute x16, starting transfers between devices, halo_pair(): lax.ppermute(lax.slice_in_dim(block, size - 1, None, axis=dim), axis, for...  54.2 us
    all_to_all x2, waiting for transfers between devices, windows(): received = lax.all_to_all(jnp.stack(parts), 'col', 0, 0, tiled=True)  44.3 us
    another operation x6, other arithmetic, run_segments(): return jnp.stack(factors)  42.1 us
    ppermute x16, starting transfers between devices, halo_pair(): high = lax.ppermute(lax.slice_in_dim(block, 0, 1, axis=dim), axis, backward)  37.6 us
    add x4, other arithmetic, solve_slabs(): rho_next * rho_now * direction + 2.0 * rho_next / half_span * residual  31.2 us
    pallas_call x1, Pallas kernels, reduce_scatter(): pl.pallas_call(reduce_kernel, out_shape=jax.ShapeDtypeStruct((1, 1, lanes...  28.1 us
    slice x14, local copies, waits for them, and re-layouts, shifted(): lax.slice_in_dim(block, 1, None, axis=dim)  24.9 us
    pallas_call x1, Pallas kernels, gram(): pl.pallas_call(gram_kernel, grid=(depth, rows // rows_per_step), in_specs...  13.7 us
  transfers between devices with their start and end apart: 36, of which 2 were waited for; matrix products, arithmetic and copies ran while one was open for 33% of the time, Pallas kernels for 0%

profile of v6, /device:TPU:1, one launch (start us, length us, event | category | flops | bytes accessed | tf_op | source)
XLA Modules:
  0.0 338.3 jit_solution(9133742983793041080)
XLA Ops:
  4.6 4.8 %all-to-all-start = ((f32[4,16,2,48,128]{4,3,2,1,0:T(8,128)}), f32[4,16,2,48,128]{4,3,2,1,0:T(8,128)S(1)}, u32[]{:S(2)}, u32[]{:S(2)}) async-start(f32[4,16,2,48,128]{4,3,2,1,0:T(8,128)} %pad_maximum_fusion.2), calls=%async_computation | async-start | bytes 6291456 | tf_op jit(solution)/shard_map/all_to_all | solution.py:186
  13.4 32.6 %all-to-all-done = f32[4,16,2,48,128]{4,3,2,1,0:T(8,128)S(1)} async-done(((f32[4,16,2,48,128]{4,3,2,1,0:T(8,128)}), f32[4,16,2,48,128]{4,3,2,1,0:T(8,128)S(1)}, u32[]{:S(2)}, u32[]{:S(2)}) %all-to-all-start) | async-done | bytes 3145760 | tf_op jit(solution)/shard_map/all_to_all | solution.py:186
  46.1 4.6 %all-to-all-start.1 = ((f32[4,16,2,48,128]{4,3,2,1,0:T(8,128)}), f32[4,16,2,48,128]{4,3,2,1,0:T(8,128)}, u32[]{:S(2)}, u32[]{:S(2)}) async-start(f32[4,16,2,48,128]{4,3,2,1,0:T(8,128)} %pad_maximum_fusion.3), calls=%async_computation.1 | async-start | bytes 6291456 | tf_op jit(solution)/shard_map/all_to_all | solution.py:186
  51.4 5.1 %select_add_fusion = f32[2,192,128]{2,1,0:T(8,128)S(1)} fusion(s32[2,192,128]{2,1,0:T(8,128)S(1)} %copy-done.13, f32[]{:T(128)} %bitcast.13, f32[]{:T(128)} %bitcast.12, f32[]{:T(128)} %bitcast.11, f32[]{:T(128)} %bitcast.10, f32[]{:T(128)} %bitcast.9, f32[]{:T(128)} %bitcast.8, f32[]{:T(128)} %bitcast.7, f32[]{:T(128)} %bitcast.6), kind=kLoop, calls=%fused_computation.210 | loop fusion | flops 1130496 | bytes 393248 | tf_op jit(solution)/shard_map/add | solution.py:151
  56.6 3.8 %collective-permute-start = (f32[1,50,128]{2,1,0:T(8,128)S(1)}, f32[1,50,128]{2,1,0:T(8,128)S(1)}, u32[]{:S(2)}, u32[]{:S(2)}) collective-permute-start(f32[1,50,128]{2,1,0:T(8,128)S(1)} %get-tuple-element.76), channel_id=1, source_target_pairs={{4,0},{8,4},{12,8},{16,12},{20,16},{24,20},{28,24},{32,28},{36,32}... | collective-permute-start | bytes 76808 | tf_op jit(solution)/shard_map/ppermute | solution.py:22
  74.8 11.7 %all-to-all-done.1 = f32[4,16,2,48,128]{4,3,2,1,0:T(8,128)} async-done(((f32[4,16,2,48,128]{4,3,2,1,0:T(8,128)}), f32[4,16,2,48,128]{4,3,2,1,0:T(8,128)}, u32[]{:S(2)}, u32[]{:S(2)}) %all-to-all-start.1) | async-done | bytes 3145760 | tf_op jit(solution)/shard_map/all_to_all | solution.py:186
  89.5 4.7 %collective-permute-start.18 = (f32[64,1,48,128]{3,2,1,0:T(8,128)S(1)}, f32[64,1,48,128]{3,2,1,0:T(8,128)S(1)}, u32[]{:S(2)}, u32[]{:S(2)}) collective-permute-start(f32[64,1,48,128]{3,2,1,0:T(8,128)S(1)} %get-tuple-element.36), channel_id=1, source_target_pairs={{4,0},{8,4},{12,8},{16,12},{20,16},{24,20},{28,24},{32,28},{36,32}... | collective-permute-start | bytes 4718600 | tf_op jit(solution)/shard_map/ppermute | solution.py:161
  99.0 4.0 %collective-permute-start.21 = (f32[64,2,1,128]{3,2,1,0:T(1,128)S(1)}, f32[64,2,1,128]{3,2,1,0:T(1,128)S(1)}, u32[]{:S(2)}, u32[]{:S(2)}) collective-permute-start(f32[64,2,1,128]{3,2,1,0:T(1,128)S(1)} %get-tuple-element.40), channel_id=1, source_target_pairs={{0,1},{1,2},{2,3},{4,5},{5,6},{6,7},{8,9},{9,10},{10,11},{12,13},{... | collective-permute-start | bytes 196616 | tf_op jit(solution)/shard_map/ppermute | solution.py:160
  110.0 3.6 %collective-permute-start.3 = (f32[64,1,48,128]{3,2,1,0:T(8,128)S(1)}, f32[64,1,48,128]{3,2,1,0:T(8,128)}, u32[]{:S(2)}, u32[]{:S(2)}) collective-permute-start(f32[64,1,48,128]{3,2,1,0:T(8,128)S(1)} %get-tuple-element.63), channel_id=1, source_target_pairs={{0,4},{4,8},{8,12},{12,16},{16,20},{20,24},{24,28},{28,32},{32,36}... | collective-permute-start | bytes 4718600 | tf_op jit(solution)/shard_map/ppermute | solution.py:160
  115.0 4.0 %collective-permute-start.5 = (f32[64,2,1,128]{3,2,1,0:T(1,128)}, f32[64,2,1,128]{3,2,1,0:T(1,128)S(1)}, u32[]{:S(2)}, u32[]{:S(2)}) collective-permute-start(f32[64,2,1,128]{3,2,1,0:T(1,128)} %get-tuple-element.68), channel_id=1, source_target_pairs={{0,1},{1,2},{2,3},{4,5},{5,6},{6,7},{8,9},{9,10},{10,11},{12,13},{... | collective-permute-start | bytes 196616 | tf_op jit(solution)/shard_map/ppermute | solution.py:160
  120.2 8.0 %multiply_add_fusion.1 = (f32[64,2,48,128]{3,2,1,0:T(8,128)S(1)}, f32[64,2,48,128]{3,2,1,0:T(8,128)}) fusion(f32[64,2,48,128]{3,2,1,0:T(8,128)S(1)} %get-tuple-element.92, f32[]{:T(128)S(6)} %div.73, f32[]{:T(128)S(6)} %mul.258, f32[]{:T(128)} %bitcast, f32[2,48,128]{2,1,0:T(8,128)S(1)} %get-tuple-element.78, f32[2,48,128]{2,1,0:T(8,128)S(1)} %copy-done.9, ...), kind=kLoop, calls=%fused_computation.196 | loop fusion | flops 21233664 | bytes 25460748 | tf_op jit(solution)/shard_map/add | solution.py:224
  138.4 4.0 %collective-permute-start.25 = (f32[64,2,1,128]{3,2,1,0:T(1,128)}, f32[64,2,1,128]{3,2,1,0:T(1,128)S(1)}, u32[]{:S(2)}, u32[]{:S(2)}) collective-permute-start(f32[64,2,1,128]{3,2,1,0:T(1,128)} %get-tuple-element.34), channel_id=1, source_target_pairs={{0,1},{1,2},{2,3},{4,5},{5,6},{6,7},{8,9},{9,10},{10,11},{12,13},{... | collective-permute-start | bytes 196616 | tf_op jit(solution)/shard_map/ppermute | solution.py:160
  142.4 7.6 %multiply_add_fusion.3 = (f32[64,2,48,128]{3,2,1,0:T(8,128)S(1)}, f32[64,2,48,128]{3,2,1,0:T(8,128)}) fusion(f32[64,2,48,128]{3,2,1,0:T(8,128)S(1)} %get-tuple-element.93, f32[]{:T(128)S(6)} %div.73, f32[]{:T(128)S(6)} %mul.258, f32[]{:T(128)} %bitcast, f32[2,48,128]{2,1,0:T(8,128)S(1)} %get-tuple-element.78, f32[2,48,128]{2,1,0:T(8,128)S(1)} %copy-done.9, ...), kind=kLoop, calls=%fused_computation.199 | loop fusion | flops 21233664 | bytes 25460748 | tf_op jit(solution)/shard_map/add | solution.py:224
  151.4 3.5 %fusion.165 = (f32[64,2,47,128]{3,2,1,0:T(8,128)}, f32[64,2,47,128]{3,2,1,0:T(8,128)}) fusion(f32[64,2,48,128]{3,2,1,0:T(8,128)S(1)} %get-tuple-element.7), kind=kLoop, calls=%fused_computation.242 | loop fusion | bytes 12320768 | tf_op jit(solution)/shard_map/slice | solution.py:167
  164.9 4.2 %collective-permute-start.9 = (f32[64,2,1,128]{3,2,1,0:T(1,128)}, f32[64,2,1,128]{3,2,1,0:T(1,128)S(1)}, u32[]{:S(2)}, u32[]{:S(2)}) collective-permute-start(f32[64,2,1,128]{3,2,1,0:T(1,128)} %get-tuple-element.62), channel_id=1, source_target_pairs={{0,1},{1,2},{2,3},{4,5},{5,6},{6,7},{8,9},{9,10},{10,11},{12,13},{... | collective-permute-start | bytes 196616 | tf_op jit(solution)/shard_map/ppermute | solution.py:160
  169.0 9.2 %multiply_bitcast_fusion = (f32[1,64,2,48,128]{4,3,2,1,0:T(8,128)}, f32[64,2,48,128]{3,2,1,0:T(8,128)S(1)}) fusion(f32[]{:T(128)S(6)} %sqrt.8, f32[64,2,48,128]{3,2,1,0:T(8,128)} %get-tuple-element.8, f32[64,2,48,128]{3,2,1,0:T(8,128)S(1)} %get-tuple-element.7, f32[]{:T(128)} %bitcast, f32[2,48,128]{2,1,0:T(8,128)S(1)} %get-tuple-element.78, ...), kind=kLoop, calls=%fused_computation.195 | loop fusion | flops 23592960 | bytes 28606480 | tf_op jit(solution)/shard_map/stack | solution.py:239
  188.2 4.0 %collective-permute-start.29 = (f32[64,2,1,128]{3,2,1,0:T(1,128)}, f32[64,2,1,128]{3,2,1,0:T(1,128)S(1)}, u32[]{:S(2)}, u32[]{:S(2)}) collective-permute-start(f32[64,2,1,128]{3,2,1,0:T(1,128)} %get-tuple-element.28), channel_id=1, source_target_pairs={{0,1},{1,2},{2,3},{4,5},{5,6},{6,7},{8,9},{9,10},{10,11},{12,13},{... | collective-permute-start | bytes 196616 | tf_op jit(solution)/shard_map/ppermute | solution.py:160
  192.2 8.3 %multiply_bitcast_fusion.1 = (f32[1,64,2,48,128]{4,3,2,1,0:T(8,128)}, f32[64,2,48,128]{3,2,1,0:T(8,128)S(1)}) fusion(f32[]{:T(128)S(6)} %sqrt.8, f32[64,2,48,128]{3,2,1,0:T(8,128)} %get-tuple-element.14, f32[64,2,48,128]{3,2,1,0:T(8,128)S(1)} %get-tuple-element.13, f32[]{:T(128)} %bitcast, f32[2,48,128]{2,1,0:T(8,128)S(1)} %get-tuple-element.78, ...), kind=kLoop, calls=%fused_computation.198 | loop fusion | flops 23592960 | bytes 28606480 | tf_op jit(solution)/shard_map/stack | solution.py:239
  207.5 3.8 %collective-permute-start.10 = (f32[64,1,48,128]{3,2,1,0:T(8,128)}, f32[64,1,48,128]{3,2,1,0:T(8,128)}, u32[]{:S(2)}, u32[]{:S(2)}) collective-permute-start(f32[64,1,48,128]{3,2,1,0:T(8,128)} %get-tuple-element.52), channel_id=1, source_target_pairs={{4,0},{8,4},{12,8},{16,12},{20,16},{24,20},{28,24},{32,28},{36,32}... | collective-permute-start | bytes 4718600 | tf_op jit(solution)/shard_map/ppermute | solution.py:161
  214.6 4.6 %collective-permute-start.13 = (f32[64,2,1,128]{3,2,1,0:T(1,128)}, f32[64,2,1,128]{3,2,1,0:T(1,128)}, u32[]{:S(2)}, u32[]{:S(2)}) collective-permute-start(f32[64,2,1,128]{3,2,1,0:T(1,128)} %get-tuple-element.56), channel_id=1, source_target_pairs={{0,1},{1,2},{2,3},{4,5},{5,6},{6,7},{8,9},{9,10},{10,11},{12,13},{... | collective-permute-start | bytes 196616 | tf_op jit(solution)/shard_map/ppermute | solution.py:160
  219.2 7.7 %multiply_add_fusion = (f32[64,2,48,128]{3,2,1,0:T(8,128)S(1)}, f32[64,2,48,128]{3,2,1,0:T(8,128)}) fusion(f32[]{:T(128)S(6)} %div.81, f32[]{:T(128)S(6)} %mul.607, f32[64,2,48,128]{3,2,1,0:T(8,128)S(1)} %get-tuple-element.4, f32[]{:T(128)S(6)} %mul.604, f32[64,2,48,128]{3,2,1,0:T(8,128)S(1)} %broadcast_divide_fusion, f32[]{:T(128)} %bitcast.15, ...), kind=kLoop, calls=%fused_computation.194 | loop fusion | flops 22020096 | bytes 25460752 | tf_op jit(solution)/shard_map/add | solution.py:224
  229.5 4.1 %collective-permute-start.30 = (f32[64,1,48,128]{3,2,1,0:T(8,128)}, f32[64,1,48,128]{3,2,1,0:T(8,128)}, u32[]{:S(2)}, u32[]{:S(2)}) collective-permute-start(f32[64,1,48,128]{3,2,1,0:T(8,128)} %get-tuple-element.22), channel_id=1, source_target_pairs={{4,0},{8,4},{12,8},{16,12},{20,16},{24,20},{28,24},{32,28},{36,32}... | collective-permute-start | bytes 4718600 | tf_op jit(solution)/shard_map/ppermute | solution.py:161
  236.9 4.0 %collective-permute-start.33 = (f32[64,2,1,128]{3,2,1,0:T(1,128)}, f32[64,2,1,128]{3,2,1,0:T(1,128)S(1)}, u32[]{:S(2)}, u32[]{:S(2)}) collective-permute-start(f32[64,2,1,128]{3,2,1,0:T(1,128)} %get-tuple-element.17), channel_id=1, source_target_pairs={{0,1},{1,2},{2,3},{4,5},{5,6},{6,7},{8,9},{9,10},{10,11},{12,13},{... | collective-permute-start | bytes 196616 | tf_op jit(solution)/shard_map/ppermute | solution.py:160
  240.9 7.8 %multiply_add_fusion.2 = (f32[64,2,48,128]{3,2,1,0:T(8,128)S(1)}, f32[64,2,48,128]{3,2,1,0:T(8,128)}) fusion(f32[]{:T(128)S(6)} %div.81, f32[]{:T(128)S(6)} %mul.607, f32[64,2,48,128]{3,2,1,0:T(8,128)S(1)} %get-tuple-element.10, f32[]{:T(128)S(6)} %mul.604, f32[64,2,48,128]{3,2,1,0:T(8,128)S(1)} %broadcast_divide_fusion.1, f32[]{:T(128)} %bitcast.15, ...), kind=kLoop, calls=%fused_computation.197 | loop fusion | flops 22020096 | bytes 25460752 | tf_op jit(solution)/shard_map/add | solution.py:224
  250.1 3.5 %fusion.159 = (f32[64,2,47,128]{3,2,1,0:T(8,128)}, f32[64,2,47,128]{3,2,1,0:T(8,128)}) fusion(f32[64,2,48,128]{3,2,1,0:T(8,128)S(1)} %get-tuple-element.5), kind=kLoop, calls=%fused_computation.236 | loop fusion | bytes 12320768 | tf_op jit(solution)/shard_map/slice | solution.py:168
  256.7 4.1 %collective-permute-start.14 = (f32[64,1,48,128]{3,2,1,0:T(8,128)}, f32[64,1,48,128]{3,2,1,0:T(8,128)}, u32[]{:S(2)}, u32[]{:S(2)}) collective-permute-start(f32[64,1,48,128]{3,2,1,0:T(8,128)} %get-tuple-element.50), channel_id=1, source_target_pairs={{4,0},{8,4},{12,8},{16,12},{20,16},{24,20},{28,24},{32,28},{36,32}... | collective-permute-start | bytes 4718600 | tf_op jit(solution)/shard_map/ppermute | solution.py:161
  264.1 4.6 %collective-permute-start.17 = (f32[64,2,1,128]{3,2,1,0:T(1,128)}, f32[64,2,1,128]{3,2,1,0:T(1,128)}, u32[]{:S(2)}, u32[]{:S(2)}) collective-permute-start(f32[64,2,1,128]{3,2,1,0:T(1,128)} %get-tuple-element.45), channel_id=1, source_target_pairs={{0,1},{1,2},{2,3},{4,5},{5,6},{6,7},{8,9},{9,10},{10,11},{12,13},{... | collective-permute-start | bytes 196616 | tf_op jit(solution)/shard_map/ppermute | solution.py:160
  268.7 8.8 %fusion.81 = f32[1,64,2,48,128]{4,3,2,1,0:T(8,128)} fusion(f32[64,2,48,128]{3,2,1,0:T(8,128)S(1)} %get-tuple-element.4, f32[64,2,48,128]{3,2,1,0:T(8,128)S(1)} %copy-done.1, f32[64,2,48,128]{3,2,1,0:T(8,128)S(1)} %get-tuple-element.5, f32[64,1,48,128]{3,2,1,0:T(8,128)} %collective-permute-done.30, f32[64,1,48,128]{3,2,1,0:T(8,128)} %get-tuple-element.21, ...), kind=kLoop, calls=%fused_computation.99 | loop fusion | flops 25952256 | bytes 25460760 | tf_op jit(solution)/shard_map/stack | solution.py:239
  277.5 5.3 %pad_maximum_fusion.1 = f32[2,64,2,48,128]{4,3,2,1,0:T(8,128)} fusion(f32[1,64,2,48,128]{4,3,2,1,0:T(8,128)} %fusion.81, f32[1,64,2,48,128]{4,3,2,1,0:T(8,128)S(1)} %copy-done.3), kind=kLoop, calls=%fused_computation.17 | loop fusion | flops 1572864 | bytes 12582912 | tf_op jit(solution)/shard_map/stack | solution.py:239
  282.9 7.2 %fusion.39 = f32[1,64,2,48,128]{4,3,2,1,0:T(8,128)S(1)} fusion(f32[64,2,48,128]{3,2,1,0:T(8,128)S(1)} %get-tuple-element.10, f32[64,2,48,128]{3,2,1,0:T(8,128)S(1)} %copy-done.2, f32[64,2,48,128]{3,2,1,0:T(8,128)S(1)} %get-tuple-element.11, f32[64,1,48,128]{3,2,1,0:T(8,128)} %collective-permute-done.14, f32[64,1,48,128]{3,2,1,0:T(8,128)S(1)} %get-tuple-element.49, ...), kind=kLoop, calls=%fused_computation.57 | loop fusion | flops 25952256 | bytes 25460760 | tf_op jit(solution)/shard_map/stack | solution.py:239
  293.3 13.7 %shard_map.76 = f32[128,128]{1,0:T(8,128)} custom-call(f32[128,2,48,128]{3,2,1,0:T(8,128)} %bitcast.48, f32[128,2,48,128]{3,2,1,0:T(8,128)} %bitcast.47), custom_call_target="tpu_custom_call" | custom-call | flops 402653184 | bytes 12582912 | tf_op jit(solution)/shard_map/pallas_call | solution.py:136
  308.9 28.1 %shard_map.77 = f32[1,1,128]{2,1,0:T(1,128)} custom-call(f32[4,32,128]{2,1,0:T(8,128)} %reshape.38.tiles_ref), custom_call_target="tpu_custom_call" | custom-call | tf_op jit(solution)/shard_map/pallas_call | solution.py:98
  (139 shorter events, 94.1 us)
Async XLA Ops:
  4.6 41.5 %all-to-all-start = ((f32[4,16,2,48,128]{4,3,2,1,0:T(8,128)}), f32[4,16,2,48,128]{4,3,2,1,0:T(8,128)S(1)}, u32[]{:S(2)}, u32[]{:S(2)}) async-start(f32[4,16,2,48,128]{4,3,2,1,0:T(8,128)} %pad_maximum_fusion.2), calls=%async_computation | async-start | bytes 6291456 | tf_op jit(solution)/shard_map/all_to_all | solution.py:186
  46.1 40.4 %all-to-all-start.1 = ((f32[4,16,2,48,128]{4,3,2,1,0:T(8,128)}), f32[4,16,2,48,128]{4,3,2,1,0:T(8,128)}, u32[]{:S(2)}, u32[]{:S(2)}) async-start(f32[4,16,2,48,128]{4,3,2,1,0:T(8,128)} %pad_maximum_fusion.3), calls=%async_computation.1 | async-start | bytes 6291456 | tf_op jit(solution)/shard_map/all_to_all | solution.py:186
  89.5 25.5 %collective-permute-start.18 = (f32[64,1,48,128]{3,2,1,0:T(8,128)S(1)}, f32[64,1,48,128]{3,2,1,0:T(8,128)S(1)}, u32[]{:S(2)}, u32[]{:S(2)}) collective-permute-start(f32[64,1,48,128]{3,2,1,0:T(8,128)S(1)} %get-tuple-element.36), channel_id=1, source_target_pairs={{4,0},{8,4},{12,8},{16,12},{20,16},{24,20},{28,24},{32,28},{36,32}... | collective-permute-start | bytes 4718600 | tf_op jit(solution)/shard_map/ppermute | solution.py:161
  94.2 24.9 %collective-permute-start.19 = (f32[64,1,48,128]{3,2,1,0:T(8,128)S(1)}, f32[64,1,48,128]{3,2,1,0:T(8,128)S(1)}, u32[]{:S(2)}, u32[]{:S(2)}) collective-permute-start(f32[64,1,48,128]{3,2,1,0:T(8,128)S(1)} %get-tuple-element.35), channel_id=1, source_target_pairs={{0,4},{4,8},{8,12},{12,16},{16,20},{20,24},{24,28},{28,32},{32,36}... | collective-permute-start | bytes 4718600 | tf_op jit(solution)/shard_map/ppermute | solution.py:160
  108.1 30.2 %collective-permute-start.1 = (f32[64,1,48,128]{3,2,1,0:T(8,128)}, f32[64,1,48,128]{3,2,1,0:T(8,128)}, u32[]{:S(2)}, u32[]{:S(2)}) collective-permute-start(f32[64,1,48,128]{3,2,1,0:T(8,128)} %get-tuple-element.64), channel_id=1, source_target_pairs={{4,0},{8,4},{12,8},{16,12},{20,16},{24,20},{28,24},{32,28},{36,32}... | collective-permute-start | bytes 4718600 | tf_op jit(solution)/shard_map/ppermute | solution.py:161
  110.0 32.3 %collective-permute-start.3 = (f32[64,1,48,128]{3,2,1,0:T(8,128)S(1)}, f32[64,1,48,128]{3,2,1,0:T(8,128)}, u32[]{:S(2)}, u32[]{:S(2)}) collective-permute-start(f32[64,1,48,128]{3,2,1,0:T(8,128)S(1)} %get-tuple-element.63), channel_id=1, source_target_pairs={{0,4},{4,8},{8,12},{12,16},{16,20},{20,24},{24,28},{28,32},{32,36}... | collective-permute-start | bytes 4718600 | tf_op jit(solution)/shard_map/ppermute | solution.py:160
  113.7 19.6 %collective-permute-start.4 = (f32[64,2,1,128]{3,2,1,0:T(1,128)}, f32[64,2,1,128]{3,2,1,0:T(1,128)S(1)}, u32[]{:S(2)}, u32[]{:S(2)}) collective-permute-start(f32[64,2,1,128]{3,2,1,0:T(1,128)} %get-tuple-element.67), channel_id=1, source_target_pairs={{1,0},{2,1},{3,2},{5,4},{6,5},{7,6},{9,8},{10,9},{11,10},{13,12},{... | collective-permute-start | bytes 196616 | tf_op jit(solution)/shard_map/ppermute | solution.py:161
  115.0 21.4 %collective-permute-start.5 = (f32[64,2,1,128]{3,2,1,0:T(1,128)}, f32[64,2,1,128]{3,2,1,0:T(1,128)S(1)}, u32[]{:S(2)}, u32[]{:S(2)}) collective-permute-start(f32[64,2,1,128]{3,2,1,0:T(1,128)} %get-tuple-element.68), channel_id=1, source_target_pairs={{0,1},{1,2},{2,3},{4,5},{5,6},{6,7},{8,9},{9,10},{10,11},{12,13},{... | collective-permute-start | bytes 196616 | tf_op jit(solution)/shard_map/ppermute | solution.py:160
  130.8 34.0 %collective-permute-start.22 = (f32[64,1,48,128]{3,2,1,0:T(8,128)}, f32[64,1,48,128]{3,2,1,0:T(8,128)}, u32[]{:S(2)}, u32[]{:S(2)}) collective-permute-start(f32[64,1,48,128]{3,2,1,0:T(8,128)} %get-tuple-element.30), channel_id=1, source_target_pairs={{4,0},{8,4},{12,8},{16,12},{20,16},{24,20},{28,24},{32,28},{36,32}... | collective-permute-start | bytes 4718600 | tf_op jit(solution)/shard_map/ppermute | solution.py:161
  133.3 35.8 %collective-permute-start.23 = (f32[64,1,48,128]{3,2,1,0:T(8,128)}, f32[64,1,48,128]{3,2,1,0:T(8,128)}, u32[]{:S(2)}, u32[]{:S(2)}) collective-permute-start(f32[64,1,48,128]{3,2,1,0:T(8,128)} %get-tuple-element.29), channel_id=1, source_target_pairs={{0,4},{4,8},{8,12},{12,16},{16,20},{20,24},{24,28},{28,32},{32,36}... | collective-permute-start | bytes 4718600 | tf_op jit(solution)/shard_map/ppermute | solution.py:160
  137.1 23.8 %collective-permute-start.24 = (f32[64,2,1,128]{3,2,1,0:T(1,128)}, f32[64,2,1,128]{3,2,1,0:T(1,128)S(1)}, u32[]{:S(2)}, u32[]{:S(2)}) collective-permute-start(f32[64,2,1,128]{3,2,1,0:T(1,128)} %get-tuple-element.33), channel_id=1, source_target_pairs={{1,0},{2,1},{3,2},{5,4},{6,5},{7,6},{9,8},{10,9},{11,10},{13,12},{... | collective-permute-start | bytes 196616 | tf_op jit(solution)/shard_map/ppermute | solution.py:161
  138.4 25.2 %collective-permute-start.25 = (f32[64,2,1,128]{3,2,1,0:T(1,128)}, f32[64,2,1,128]{3,2,1,0:T(1,128)S(1)}, u32[]{:S(2)}, u32[]{:S(2)}) collective-permute-start(f32[64,2,1,128]{3,2,1,0:T(1,128)} %get-tuple-element.34), channel_id=1, source_target_pairs={{0,1},{1,2},{2,3},{4,5},{5,6},{6,7},{8,9},{9,10},{10,11},{12,13},{... | collective-permute-start | bytes 196616 | tf_op jit(solution)/shard_map/ppermute | solution.py:160
  157.9 30.2 %collective-permute-start.6 = (f32[64,1,48,128]{3,2,1,0:T(8,128)}, f32[64,1,48,128]{3,2,1,0:T(8,128)}, u32[]{:S(2)}, u32[]{:S(2)}) collective-permute-start(f32[64,1,48,128]{3,2,1,0:T(8,128)} %get-tuple-element.58), channel_id=1, source_target_pairs={{4,0},{8,4},{12,8},{16,12},{20,16},{24,20},{28,24},{32,28},{36,32}... | collective-permute-start | bytes 4718600 | tf_op jit(solution)/shard_map/ppermute | solution.py:161
  160.8 31.3 %collective-permute-start.7 = (f32[64,1,48,128]{3,2,1,0:T(8,128)S(1)}, f32[64,1,48,128]{3,2,1,0:T(8,128)}, u32[]{:S(2)}, u32[]{:S(2)}) collective-permute-start(f32[64,1,48,128]{3,2,1,0:T(8,128)S(1)} %get-tuple-element.57), channel_id=1, source_target_pairs={{0,4},{4,8},{8,12},{12,16},{16,20},{20,24},{24,28},{28,32},{32,36}... | collective-permute-start | bytes 4718600 | tf_op jit(solution)/shard_map/ppermute | solution.py:160
  163.5 21.1 %collective-permute-start.8 = (f32[64,2,1,128]{3,2,1,0:T(1,128)}, f32[64,2,1,128]{3,2,1,0:T(1,128)S(1)}, u32[]{:S(2)}, u32[]{:S(2)}) collective-permute-start(f32[64,2,1,128]{3,2,1,0:T(1,128)} %get-tuple-element.61), channel_id=1, source_target_pairs={{1,0},{2,1},{3,2},{5,4},{6,5},{7,6},{9,8},{10,9},{11,10},{13,12},{... | collective-permute-start | bytes 196616 | tf_op jit(solution)/shard_map/ppermute | solution.py:161
  164.9 22.0 %collective-permute-start.9 = (f32[64,2,1,128]{3,2,1,0:T(1,128)}, f32[64,2,1,128]{3,2,1,0:T(1,128)S(1)}, u32[]{:S(2)}, u32[]{:S(2)}) collective-permute-start(f32[64,2,1,128]{3,2,1,0:T(1,128)} %get-tuple-element.62), channel_id=1, source_target_pairs={{0,1},{1,2},{2,3},{4,5},{5,6},{6,7},{8,9},{9,10},{10,11},{12,13},{... | collective-permute-start | bytes 196616 | tf_op jit(solution)/shard_map/ppermute | solution.py:160
  181.2 33.3 %collective-permute-start.26 = (f32[64,1,48,128]{3,2,1,0:T(8,128)}, f32[64,1,48,128]{3,2,1,0:T(8,128)}, u32[]{:S(2)}, u32[]{:S(2)}) collective-permute-start(f32[64,1,48,128]{3,2,1,0:T(8,128)} %get-tuple-element.24), channel_id=1, source_target_pairs={{4,0},{8,4},{12,8},{16,12},{20,16},{24,20},{28,24},{32,28},{36,32}... | collective-permute-start | bytes 4718600 | tf_op jit(solution)/shard_map/ppermute | solution.py:161
  184.6 34.6 %collective-permute-start.27 = (f32[64,1,48,128]{3,2,1,0:T(8,128)}, f32[64,1,48,128]{3,2,1,0:T(8,128)}, u32[]{:S(2)}, u32[]{:S(2)}) collective-permute-start(f32[64,1,48,128]{3,2,1,0:T(8,128)} %get-tuple-element.23), channel_id=1, source_target_pairs={{0,4},{4,8},{8,12},{12,16},{16,20},{20,24},{24,28},{28,32},{32,36}... | collective-permute-start | bytes 4718600 | tf_op jit(solution)/shard_map/ppermute | solution.py:160
  186.8 24.5 %collective-permute-start.28 = (f32[64,2,1,128]{3,2,1,0:T(1,128)}, f32[64,2,1,128]{3,2,1,0:T(1,128)S(1)}, u32[]{:S(2)}, u32[]{:S(2)}) collective-permute-start(f32[64,2,1,128]{3,2,1,0:T(1,128)} %get-tuple-element.27), channel_id=1, source_target_pairs={{1,0},{2,1},{3,2},{5,4},{6,5},{7,6},{9,8},{10,9},{11,10},{13,12},{... | collective-permute-start | bytes 196616 | tf_op jit(solution)/shard_map/ppermute | solution.py:161
  188.2 25.1 %collective-permute-start.29 = (f32[64,2,1,128]{3,2,1,0:T(1,128)}, f32[64,2,1,128]{3,2,1,0:T(1,128)S(1)}, u32[]{:S(2)}, u32[]{:S(2)}) collective-permute-start(f32[64,2,1,128]{3,2,1,0:T(1,128)} %get-tuple-element.28), channel_id=1, source_target_pairs={{0,1},{1,2},{2,3},{4,5},{5,6},{6,7},{8,9},{9,10},{10,11},{12,13},{... | collective-permute-start | bytes 196616 | tf_op jit(solution)/shard_map/ppermute | solution.py:160
  207.5 29.4 %collective-permute-start.10 = (f32[64,1,48,128]{3,2,1,0:T(8,128)}, f32[64,1,48,128]{3,2,1,0:T(8,128)}, u32[]{:S(2)}, u32[]{:S(2)}) collective-permute-start(f32[64,1,48,128]{3,2,1,0:T(8,128)} %get-tuple-element.52), channel_id=1, source_target_pairs={{4,0},{8,4},{12,8},{16,12},{20,16},{24,20},{28,24},{32,28},{36,32}... | collective-permute-start | bytes 4718600 | tf_op jit(solution)/shard_map/ppermute | solution.py:161
  211.3 29.5 %collective-permute-start.11 = (f32[64,1,48,128]{3,2,1,0:T(8,128)S(1)}, f32[64,1,48,128]{3,2,1,0:T(8,128)}, u32[]{:S(2)}, u32[]{:S(2)}) collective-permute-start(f32[64,1,48,128]{3,2,1,0:T(8,128)S(1)} %get-tuple-element.51), channel_id=1, source_target_pairs={{0,4},{4,8},{8,12},{12,16},{16,20},{20,24},{24,28},{28,32},{32,36}... | collective-permute-start | bytes 4718600 | tf_op jit(solution)/shard_map/ppermute | solution.py:160
  213.3 20.3 %collective-permute-start.12 = (f32[64,2,1,128]{3,2,1,0:T(1,128)}, f32[64,2,1,128]{3,2,1,0:T(1,128)S(1)}, u32[]{:S(2)}, u32[]{:S(2)}) collective-permute-start(f32[64,2,1,128]{3,2,1,0:T(1,128)} %get-tuple-element.55), channel_id=1, source_target_pairs={{1,0},{2,1},{3,2},{5,4},{6,5},{7,6},{9,8},{10,9},{11,10},{13,12},{... | collective-permute-start | bytes 196616 | tf_op jit(solution)/shard_map/ppermute | solution.py:161
  214.6 21.0 %collective-permute-start.13 = (f32[64,2,1,128]{3,2,1,0:T(1,128)}, f32[64,2,1,128]{3,2,1,0:T(1,128)}, u32[]{:S(2)}, u32[]{:S(2)}) collective-permute-start(f32[64,2,1,128]{3,2,1,0:T(1,128)} %get-tuple-element.56), channel_id=1, source_target_pairs={{0,1},{1,2},{2,3},{4,5},{5,6},{6,7},{8,9},{9,10},{10,11},{12,13},{... | collective-permute-start | bytes 196616 | tf_op jit(solution)/shard_map/ppermute | solution.py:160
  229.5 34.5 %collective-permute-start.30 = (f32[64,1,48,128]{3,2,1,0:T(8,128)}, f32[64,1,48,128]{3,2,1,0:T(8,128)}, u32[]{:S(2)}, u32[]{:S(2)}) collective-permute-start(f32[64,1,48,128]{3,2,1,0:T(8,128)} %get-tuple-element.22), channel_id=1, source_target_pairs={{4,0},{8,4},{12,8},{16,12},{20,16},{24,20},{28,24},{32,28},{36,32}... | collective-permute-start | bytes 4718600 | tf_op jit(solution)/shard_map/ppermute | solution.py:161
  233.6 35.1 %collective-permute-start.31 = (f32[64,1,48,128]{3,2,1,0:T(8,128)}, f32[64,1,48,128]{3,2,1,0:T(8,128)}, u32[]{:S(2)}, u32[]{:S(2)}) collective-permute-start(f32[64,1,48,128]{3,2,1,0:T(8,128)} %get-tuple-element.21), channel_id=1, source_target_pairs={{0,4},{4,8},{8,12},{12,16},{16,20},{20,24},{24,28},{28,32},{32,36}... | collective-permute-start | bytes 4718600 | tf_op jit(solution)/shard_map/ppermute | solution.py:160
  235.6 25.3 %collective-permute-start.32 = (f32[64,2,1,128]{3,2,1,0:T(1,128)}, f32[64,2,1,128]{3,2,1,0:T(1,128)S(1)}, u32[]{:S(2)}, u32[]{:S(2)}) collective-permute-start(f32[64,2,1,128]{3,2,1,0:T(1,128)} %get-tuple-element.18), channel_id=1, source_target_pairs={{1,0},{2,1},{3,2},{5,4},{6,5},{7,6},{9,8},{10,9},{11,10},{13,12},{... | collective-permute-start | bytes 196616 | tf_op jit(solution)/shard_map/ppermute | solution.py:161
  236.9 25.9 %collective-permute-start.33 = (f32[64,2,1,128]{3,2,1,0:T(1,128)}, f32[64,2,1,128]{3,2,1,0:T(1,128)S(1)}, u32[]{:S(2)}, u32[]{:S(2)}) collective-permute-start(f32[64,2,1,128]{3,2,1,0:T(1,128)} %get-tuple-element.17), channel_id=1, source_target_pairs={{0,1},{1,2},{2,3},{4,5},{5,6},{6,7},{8,9},{9,10},{10,11},{12,13},{... | collective-permute-start | bytes 196616 | tf_op jit(solution)/shard_map/ppermute | solution.py:160
  256.7 26.1 %collective-permute-start.14 = (f32[64,1,48,128]{3,2,1,0:T(8,128)}, f32[64,1,48,128]{3,2,1,0:T(8,128)}, u32[]{:S(2)}, u32[]{:S(2)}) collective-permute-start(f32[64,1,48,128]{3,2,1,0:T(8,128)} %get-tuple-element.50), channel_id=1, source_target_pairs={{4,0},{8,4},{12,8},{16,12},{20,16},{24,20},{28,24},{32,28},{36,32}... | collective-permute-start | bytes 4718600 | tf_op jit(solution)/shard_map/ppermute | solution.py:161
  260.8 22.0 %collective-permute-start.15 = (f32[64,1,48,128]{3,2,1,0:T(8,128)S(1)}, f32[64,1,48,128]{3,2,1,0:T(8,128)}, u32[]{:S(2)}, u32[]{:S(2)}) collective-permute-start(f32[64,1,48,128]{3,2,1,0:T(8,128)S(1)} %get-tuple-element.49), channel_id=1, source_target_pairs={{0,4},{4,8},{8,12},{12,16},{16,20},{20,24},{24,28},{28,32},{32,36}... | collective-permute-start | bytes 4718600 | tf_op jit(solution)/shard_map/ppermute | solution.py:160
  262.8 20.1 %collective-permute-start.16 = (f32[64,2,1,128]{3,2,1,0:T(1,128)}, f32[64,2,1,128]{3,2,1,0:T(1,128)S(1)}, u32[]{:S(2)}, u32[]{:S(2)}) collective-permute-start(f32[64,2,1,128]{3,2,1,0:T(1,128)} %get-tuple-element.46), channel_id=1, source_target_pairs={{1,0},{2,1},{3,2},{5,4},{6,5},{7,6},{9,8},{10,9},{11,10},{13,12},{... | collective-permute-start | bytes 196616 | tf_op jit(solution)/shard_map/ppermute | solution.py:161
  264.1 18.8 %collective-permute-start.17 = (f32[64,2,1,128]{3,2,1,0:T(1,128)}, f32[64,2,1,128]{3,2,1,0:T(1,128)}, u32[]{:S(2)}, u32[]{:S(2)}) collective-permute-start(f32[64,2,1,128]{3,2,1,0:T(1,128)} %get-tuple-element.45), channel_id=1, source_target_pairs={{0,1},{1,2},{2,3},{4,5},{5,6},{6,7},{8,9},{9,10},{10,11},{12,13},{... | collective-permute-start | bytes 196616 | tf_op jit(solution)/shard_map/ppermute | solution.py:160
  (25 other events, 312.9 us)

commit v7 on v3

--- a/solution.py
+++ b/solution.py
@@ -157,8 +157,12 @@
     forward = [(i, i + 1) for i in range(count - 1)]
     backward = [(target, source) for source, target in forward]
     size = block.shape[dim]
-    low = lax.ppermute(lax.slice_in_dim(block, size - 1, None, axis=dim), axis, forward)
-    high = lax.ppermute(lax.slice_in_dim(block, 0, 1, axis=dim), axis, backward)
+    last = lax.slice_in_dim(block, size - 1, None, axis=dim)
+    first = lax.slice_in_dim(block, 0, 1, axis=dim)
+    face_shape = last.shape
+    flat = (-1, block.shape[-1])
+    low = lax.ppermute(last.reshape(flat), axis, forward).reshape(face_shape)
+    high = lax.ppermute(first.reshape(flat), axis, backward).reshape(face_shape)
     return low, high
 
 

time: 340 us -> 340 us (level)
  no operation moved by 1% of the time
where the time goes in v7:
time: 340 us; the launch traced here: 338 us
  starting transfers between devices  109 us (32%)
  other arithmetic  88.3 us (26%)
  local copies, waits for them, and re-layouts  45.8 us (13%)
  waiting for transfers between devices  44.4 us (13%)
  Pallas kernels  41.3 us (12%)
  between operations  9.04 us (3%)
    ppermute x16, starting transfers between devices, halo_pair(): low = lax.ppermute(last.reshape(flat), axis, forward).reshape(face_shape)  55.1 us
    all_to_all x2, waiting for transfers between devices, windows(): received = lax.all_to_all(jnp.stack(parts), 'col', 0, 0, tiled=True)  44.3 us
    another operation x6, other arithmetic, run_segments(): return jnp.stack(factors)  42.1 us
    ppermute x16, starting transfers between devices, halo_pair(): high = lax.ppermute(first.reshape(flat), axis, backward).reshape(face_shape)  37.5 us
    add x4, other arithmetic, solve_slabs(): rho_next * rho_now * direction + 2.0 * rho_next / half_span * residual  31.2 us
    pallas_call x1, Pallas kernels, reduce_scatter(): pl.pallas_call(reduce_kernel, out_shape=jax.ShapeDtypeStruct((1, 1, lanes...  28.1 us
    slice x14, local copies, waits for them, and re-layouts, shifted(): lax.slice_in_dim(block, 1, None, axis=dim)  24.9 us
    pallas_call x1, Pallas kernels, gram(): pl.pallas_call(gram_kernel, grid=(depth, rows // rows_per_step), in_specs...  13.2 us
  transfers between devices with their start and end apart: 36, of which 2 were waited for; matrix products, arithmetic and copies ran while one was open for 33% of the time, Pallas kernels for 0%

profile of v7, /device:TPU:1, one launch (start us, length us, event | category | flops | bytes accessed | tf_op | source)
XLA Modules:
  0.0 338.0 jit_solution(15276785042547427447)
XLA Ops:
  4.7 4.8 %all-to-all-start = ((f32[4,16,2,48,128]{4,3,2,1,0:T(8,128)}), f32[4,16,2,48,128]{4,3,2,1,0:T(8,128)S(1)}, u32[]{:S(2)}, u32[]{:S(2)}) async-start(f32[4,16,2,48,128]{4,3,2,1,0:T(8,128)} %pad_maximum_fusion.2), calls=%async_computation | async-start | bytes 6291456 | tf_op jit(solution)/shard_map/all_to_all | solution.py:190
  13.5 32.6 %all-to-all-done = f32[4,16,2,48,128]{4,3,2,1,0:T(8,128)S(1)} async-done(((f32[4,16,2,48,128]{4,3,2,1,0:T(8,128)}), f32[4,16,2,48,128]{4,3,2,1,0:T(8,128)S(1)}, u32[]{:S(2)}, u32[]{:S(2)}) %all-to-all-start) | async-done | bytes 3145760 | tf_op jit(solution)/shard_map/all_to_all | solution.py:190
  46.2 4.7 %all-to-all-start.1 = ((f32[4,16,2,48,128]{4,3,2,1,0:T(8,128)}), f32[4,16,2,48,128]{4,3,2,1,0:T(8,128)}, u32[]{:S(2)}, u32[]{:S(2)}) async-start(f32[4,16,2,48,128]{4,3,2,1,0:T(8,128)} %pad_maximum_fusion.3), calls=%async_computation.1 | async-start | bytes 6291456 | tf_op jit(solution)/shard_map/all_to_all | solution.py:190
  51.5 5.2 %select_add_fusion = f32[2,192,128]{2,1,0:T(8,128)S(1)} fusion(s32[2,192,128]{2,1,0:T(8,128)S(1)} %copy-done.13, f32[]{:T(128)} %bitcast.13, f32[]{:T(128)} %bitcast.12, f32[]{:T(128)} %bitcast.11, f32[]{:T(128)} %bitcast.10, f32[]{:T(128)} %bitcast.9, f32[]{:T(128)} %bitcast.8, f32[]{:T(128)} %bitcast.7, f32[]{:T(128)} %bitcast.6), kind=kLoop, calls=%fused_computation.210 | loop fusion | flops 1130496 | bytes 393248 | tf_op jit(solution)/shard_map/add | solution.py:151
  56.7 3.8 %collective-permute-start = (f32[1,50,128]{2,1,0:T(8,128)S(1)}, f32[1,50,128]{2,1,0:T(8,128)S(1)}, u32[]{:S(2)}, u32[]{:S(2)}) collective-permute-start(f32[1,50,128]{2,1,0:T(8,128)S(1)} %get-tuple-element.76), channel_id=1, source_target_pairs={{4,0},{8,4},{12,8},{16,12},{20,16},{24,20},{28,24},{32,28},{36,32}... | collective-permute-start | bytes 76808 | tf_op jit(solution)/shard_map/ppermute | solution.py:22
  75.0 11.6 %all-to-all-done.1 = f32[4,16,2,48,128]{4,3,2,1,0:T(8,128)} async-done(((f32[4,16,2,48,128]{4,3,2,1,0:T(8,128)}), f32[4,16,2,48,128]{4,3,2,1,0:T(8,128)}, u32[]{:S(2)}, u32[]{:S(2)}) %all-to-all-start.1) | async-done | bytes 3145760 | tf_op jit(solution)/shard_map/all_to_all | solution.py:190
  89.6 4.7 %collective-permute-start.18 = (f32[3072,128]{1,0:T(8,128)S(1)}, f32[3072,128]{1,0:T(8,128)S(1)}, u32[]{:S(2)}, u32[]{:S(2)}) collective-permute-start(f32[3072,128]{1,0:T(8,128)S(1)} %bitcast.117), channel_id=1, source_target_pairs={{4,0},{8,4},{12,8},{16,12},{20,16},{24,20},{28,24},{32,28},{36,32}... | collective-permute-start | bytes 4718600 | tf_op jit(solution)/shard_map/ppermute | solution.py:165
  99.1 4.0 %collective-permute-start.21 = (f32[128,128]{1,0:T(8,128)S(1)}, f32[128,128]{1,0:T(8,128)S(1)}, u32[]{:S(2)}, u32[]{:S(2)}) collective-permute-start(f32[128,128]{1,0:T(8,128)S(1)} %bitcast.135), channel_id=1, source_target_pairs={{0,1},{1,2},{2,3},{4,5},{5,6},{6,7},{8,9},{9,10},{10,11},{12,13},{... | collective-permute-start | bytes 196616 | tf_op jit(solution)/shard_map/ppermute | solution.py:164
  110.2 3.6 %collective-permute-start.3 = (f32[3072,128]{1,0:T(8,128)S(1)}, f32[3072,128]{1,0:T(8,128)}, u32[]{:S(2)}, u32[]{:S(2)}) collective-permute-start(f32[3072,128]{1,0:T(8,128)S(1)} %bitcast.114), channel_id=1, source_target_pairs={{0,4},{4,8},{8,12},{12,16},{16,20},{20,24},{24,28},{28,32},{32,36}... | collective-permute-start | bytes 4718600 | tf_op jit(solution)/shard_map/ppermute | solution.py:164
  115.1 4.0 %collective-permute-start.5 = (f32[128,128]{1,0:T(8,128)}, f32[128,128]{1,0:T(8,128)S(1)}, u32[]{:S(2)}, u32[]{:S(2)}) collective-permute-start(f32[128,128]{1,0:T(8,128)} %bitcast.20), channel_id=1, source_target_pairs={{0,1},{1,2},{2,3},{4,5},{5,6},{6,7},{8,9},{9,10},{10,11},{12,13},{... | collective-permute-start | bytes 196616 | tf_op jit(solution)/shard_map/ppermute | solution.py:164
  120.3 8.0 %multiply_add_fusion.1 = (f32[64,2,48,128]{3,2,1,0:T(8,128)S(1)}, f32[64,2,48,128]{3,2,1,0:T(8,128)}) fusion(f32[64,2,48,128]{3,2,1,0:T(8,128)S(1)} %get-tuple-element.92, f32[]{:T(128)S(6)} %div.73, f32[]{:T(128)S(6)} %mul.258, f32[]{:T(128)} %bitcast, f32[2,48,128]{2,1,0:T(8,128)S(1)} %get-tuple-element.78, f32[2,48,128]{2,1,0:T(8,128)S(1)} %copy-done.9, ...), kind=kLoop, calls=%fused_computation.196 | loop fusion | flops 21233664 | bytes 25460748 | tf_op jit(solution)/shard_map/add | solution.py:228
  137.9 4.6 %collective-permute-start.25 = (f32[128,128]{1,0:T(8,128)}, f32[128,128]{1,0:T(8,128)}, u32[]{:S(2)}, u32[]{:S(2)}) collective-permute-start(f32[128,128]{1,0:T(8,128)} %bitcast.68), channel_id=1, source_target_pairs={{0,1},{1,2},{2,3},{4,5},{5,6},{6,7},{8,9},{9,10},{10,11},{12,13},{... | collective-permute-start | bytes 196616 | tf_op jit(solution)/shard_map/ppermute | solution.py:164
  142.5 7.6 %multiply_add_fusion.3 = (f32[64,2,48,128]{3,2,1,0:T(8,128)S(1)}, f32[64,2,48,128]{3,2,1,0:T(8,128)}) fusion(f32[64,2,48,128]{3,2,1,0:T(8,128)S(1)} %get-tuple-element.93, f32[]{:T(128)S(6)} %div.73, f32[]{:T(128)S(6)} %mul.258, f32[]{:T(128)} %bitcast, f32[2,48,128]{2,1,0:T(8,128)S(1)} %get-tuple-element.78, f32[2,48,128]{2,1,0:T(8,128)S(1)} %copy-done.9, ...), kind=kLoop, calls=%fused_computation.199 | loop fusion | flops 21233664 | bytes 25460748 | tf_op jit(solution)/shard_map/add | solution.py:228
  151.5 3.5 %fusion.165 = (f32[64,2,47,128]{3,2,1,0:T(8,128)}, f32[64,2,47,128]{3,2,1,0:T(8,128)}) fusion(f32[64,2,48,128]{3,2,1,0:T(8,128)S(1)} %get-tuple-element.7), kind=kLoop, calls=%fused_computation.242 | loop fusion | bytes 12320768 | tf_op jit(solution)/shard_map/slice | solution.py:171
  165.0 4.2 %collective-permute-start.9 = (f32[128,128]{1,0:T(8,128)}, f32[128,128]{1,0:T(8,128)S(1)}, u32[]{:S(2)}, u32[]{:S(2)}) collective-permute-start(f32[128,128]{1,0:T(8,128)} %bitcast.28), channel_id=1, source_target_pairs={{0,1},{1,2},{2,3},{4,5},{5,6},{6,7},{8,9},{9,10},{10,11},{12,13},{... | collective-permute-start | bytes 196616 | tf_op jit(solution)/shard_map/ppermute | solution.py:164
  169.2 9.2 %multiply_bitcast_fusion = (f32[1,64,2,48,128]{4,3,2,1,0:T(8,128)}, f32[64,2,48,128]{3,2,1,0:T(8,128)S(1)}) fusion(f32[]{:T(128)S(6)} %sqrt.8, f32[64,2,48,128]{3,2,1,0:T(8,128)} %get-tuple-element.8, f32[64,2,48,128]{3,2,1,0:T(8,128)S(1)} %get-tuple-element.7, f32[]{:T(128)} %bitcast, f32[2,48,128]{2,1,0:T(8,128)S(1)} %get-tuple-element.78, ...), kind=kLoop, calls=%fused_computation.195 | loop fusion | flops 23592960 | bytes 28606480 | tf_op jit(solution)/shard_map/stack | solution.py:243
  188.3 4.0 %collective-permute-start.29 = (f32[128,128]{1,0:T(8,128)}, f32[128,128]{1,0:T(8,128)S(1)}, u32[]{:S(2)}, u32[]{:S(2)}) collective-permute-start(f32[128,128]{1,0:T(8,128)} %bitcast.77), channel_id=1, source_target_pairs={{0,1},{1,2},{2,3},{4,5},{5,6},{6,7},{8,9},{9,10},{10,11},{12,13},{... | collective-permute-start | bytes 196616 | tf_op jit(solution)/shard_map/ppermute | solution.py:164
  192.3 8.3 %multiply_bitcast_fusion.1 = (f32[1,64,2,48,128]{4,3,2,1,0:T(8,128)}, f32[64,2,48,128]{3,2,1,0:T(8,128)S(1)}) fusion(f32[]{:T(128)S(6)} %sqrt.8, f32[64,2,48,128]{3,2,1,0:T(8,128)} %get-tuple-element.14, f32[64,2,48,128]{3,2,1,0:T(8,128)S(1)} %get-tuple-element.13, f32[]{:T(128)} %bitcast, f32[2,48,128]{2,1,0:T(8,128)S(1)} %get-tuple-element.78, ...), kind=kLoop, calls=%fused_computation.198 | loop fusion | flops 23592960 | bytes 28606480 | tf_op jit(solution)/shard_map/stack | solution.py:243
  207.6 3.8 %collective-permute-start.10 = (f32[3072,128]{1,0:T(8,128)}, f32[3072,128]{1,0:T(8,128)}, u32[]{:S(2)}, u32[]{:S(2)}) collective-permute-start(f32[3072,128]{1,0:T(8,128)} %bitcast.32), channel_id=1, source_target_pairs={{4,0},{8,4},{12,8},{16,12},{20,16},{24,20},{28,24},{32,28},{36,32}... | collective-permute-start | bytes 4718600 | tf_op jit(solution)/shard_map/ppermute | solution.py:165
  214.7 4.6 %collective-permute-start.13 = (f32[128,128]{1,0:T(8,128)}, f32[128,128]{1,0:T(8,128)}, u32[]{:S(2)}, u32[]{:S(2)}) collective-permute-start(f32[128,128]{1,0:T(8,128)} %bitcast.38), channel_id=1, source_target_pairs={{0,1},{1,2},{2,3},{4,5},{5,6},{6,7},{8,9},{9,10},{10,11},{12,13},{... | collective-permute-start | bytes 196616 | tf_op jit(solution)/shard_map/ppermute | solution.py:164
  219.3 7.7 %multiply_add_fusion = (f32[64,2,48,128]{3,2,1,0:T(8,128)S(1)}, f32[64,2,48,128]{3,2,1,0:T(8,128)}) fusion(f32[]{:T(128)S(6)} %div.81, f32[]{:T(128)S(6)} %mul.607, f32[64,2,48,128]{3,2,1,0:T(8,128)S(1)} %get-tuple-element.4, f32[]{:T(128)S(6)} %mul.604, f32[64,2,48,128]{3,2,1,0:T(8,128)S(1)} %broadcast_divide_fusion, f32[]{:T(128)} %bitcast.31, ...), kind=kLoop, calls=%fused_computation.194 | loop fusion | flops 22020096 | bytes 25460752 | tf_op jit(solution)/shard_map/add | solution.py:228
  229.7 4.1 %collective-permute-start.30 = (f32[3072,128]{1,0:T(8,128)}, f32[3072,128]{1,0:T(8,128)}, u32[]{:S(2)}, u32[]{:S(2)}) collective-permute-start(f32[3072,128]{1,0:T(8,128)} %bitcast.79), channel_id=1, source_target_pairs={{4,0},{8,4},{12,8},{16,12},{20,16},{24,20},{28,24},{32,28},{36,32}... | collective-permute-start | bytes 4718600 | tf_op jit(solution)/shard_map/ppermute | solution.py:165
  237.0 4.2 %collective-permute-start.33 = (f32[128,128]{1,0:T(8,128)}, f32[128,128]{1,0:T(8,128)S(1)}, u32[]{:S(2)}, u32[]{:S(2)}) collective-permute-start(f32[128,128]{1,0:T(8,128)} %bitcast.85), channel_id=1, source_target_pairs={{0,1},{1,2},{2,3},{4,5},{5,6},{6,7},{8,9},{9,10},{10,11},{12,13},{... | collective-permute-start | bytes 196616 | tf_op jit(solution)/shard_map/ppermute | solution.py:164
  241.3 7.8 %multiply_add_fusion.2 = (f32[64,2,48,128]{3,2,1,0:T(8,128)S(1)}, f32[64,2,48,128]{3,2,1,0:T(8,128)}) fusion(f32[]{:T(128)S(6)} %div.81, f32[]{:T(128)S(6)} %mul.607, f32[64,2,48,128]{3,2,1,0:T(8,128)S(1)} %get-tuple-element.10, f32[]{:T(128)S(6)} %mul.604, f32[64,2,48,128]{3,2,1,0:T(8,128)S(1)} %broadcast_divide_fusion.1, f32[]{:T(128)} %bitcast.31, ...), kind=kLoop, calls=%fused_computation.197 | loop fusion | flops 22020096 | bytes 25460752 | tf_op jit(solution)/shard_map/add | solution.py:228
  250.5 3.4 %fusion.159 = (f32[64,2,47,128]{3,2,1,0:T(8,128)}, f32[64,2,47,128]{3,2,1,0:T(8,128)}) fusion(f32[64,2,48,128]{3,2,1,0:T(8,128)S(1)} %get-tuple-element.5), kind=kLoop, calls=%fused_computation.236 | loop fusion | bytes 12320768 | tf_op jit(solution)/shard_map/slice | solution.py:172
  257.1 4.1 %collective-permute-start.14 = (f32[3072,128]{1,0:T(8,128)}, f32[3072,128]{1,0:T(8,128)}, u32[]{:S(2)}, u32[]{:S(2)}) collective-permute-start(f32[3072,128]{1,0:T(8,128)} %bitcast.40), channel_id=1, source_target_pairs={{4,0},{8,4},{12,8},{16,12},{20,16},{24,20},{28,24},{32,28},{36,32}... | collective-permute-start | bytes 4718600 | tf_op jit(solution)/shard_map/ppermute | solution.py:165
  264.4 4.6 %collective-permute-start.17 = (f32[128,128]{1,0:T(8,128)}, f32[128,128]{1,0:T(8,128)}, u32[]{:S(2)}, u32[]{:S(2)}) collective-permute-start(f32[128,128]{1,0:T(8,128)} %bitcast.46), channel_id=1, source_target_pairs={{0,1},{1,2},{2,3},{4,5},{5,6},{6,7},{8,9},{9,10},{10,11},{12,13},{... | collective-permute-start | bytes 196616 | tf_op jit(solution)/shard_map/ppermute | solution.py:164
  269.0 8.8 %fusion.81 = f32[1,64,2,48,128]{4,3,2,1,0:T(8,128)} fusion(f32[64,2,48,128]{3,2,1,0:T(8,128)S(1)} %get-tuple-element.4, f32[64,2,48,128]{3,2,1,0:T(8,128)S(1)} %copy-done.1, f32[64,2,48,128]{3,2,1,0:T(8,128)S(1)} %get-tuple-element.5, f32[64,1,48,128]{3,2,1,0:T(8,128)} %bitcast.80, f32[64,1,48,128]{3,2,1,0:T(8,128)} %get-tuple-element.21, ...), kind=kLoop, calls=%fused_computation.99 | loop fusion | flops 25952256 | bytes 25460760 | tf_op jit(solution)/shard_map/stack | solution.py:243
  277.9 5.3 %pad_maximum_fusion.1 = f32[2,64,2,48,128]{4,3,2,1,0:T(8,128)} fusion(f32[1,64,2,48,128]{4,3,2,1,0:T(8,128)} %fusion.81, f32[1,64,2,48,128]{4,3,2,1,0:T(8,128)S(1)} %copy-done.3), kind=kLoop, calls=%fused_computation.17 | loop fusion | flops 1572864 | bytes 12582912 | tf_op jit(solution)/shard_map/stack | solution.py:243
  283.2 7.3 %fusion.39 = f32[1,64,2,48,128]{4,3,2,1,0:T(8,128)S(1)} fusion(f32[64,2,48,128]{3,2,1,0:T(8,128)S(1)} %get-tuple-element.10, f32[64,2,48,128]{3,2,1,0:T(8,128)S(1)} %copy-done.2, f32[64,2,48,128]{3,2,1,0:T(8,128)S(1)} %get-tuple-element.11, f32[64,1,48,128]{3,2,1,0:T(8,128)} %bitcast.41, f32[64,1,48,128]{3,2,1,0:T(8,128)S(1)} %get-tuple-element.49, ...), kind=kLoop, calls=%fused_computation.57 | loop fusion | flops 25952256 | bytes 25460760 | tf_op jit(solution)/shard_map/stack | solution.py:243
  293.7 13.2 %shard_map.76 = f32[128,128]{1,0:T(8,128)} custom-call(f32[128,2,48,128]{3,2,1,0:T(8,128)} %bitcast.112, f32[128,2,48,128]{3,2,1,0:T(8,128)} %bitcast.111), custom_call_target="tpu_custom_call" | custom-call | flops 402653184 | bytes 12582912 | tf_op jit(solution)/shard_map/pallas_call | solution.py:136
  308.7 28.1 %shard_map.77 = f32[1,1,128]{2,1,0:T(1,128)} custom-call(f32[4,32,128]{2,1,0:T(8,128)} %reshape.294.tiles_ref), custom_call_target="tpu_custom_call" | custom-call | tf_op jit(solution)/shard_map/pallas_call | solution.py:98
  (135 shorter events, 93.5 us)
Async XLA Ops:
  4.7 41.5 %all-to-all-start = ((f32[4,16,2,48,128]{4,3,2,1,0:T(8,128)}), f32[4,16,2,48,128]{4,3,2,1,0:T(8,128)S(1)}, u32[]{:S(2)}, u32[]{:S(2)}) async-start(f32[4,16,2,48,128]{4,3,2,1,0:T(8,128)} %pad_maximum_fusion.2), calls=%async_computation | async-start | bytes 6291456 | tf_op jit(solution)/shard_map/all_to_all | solution.py:190
  46.2 40.5 %all-to-all-start.1 = ((f32[4,16,2,48,128]{4,3,2,1,0:T(8,128)}), f32[4,16,2,48,128]{4,3,2,1,0:T(8,128)}, u32[]{:S(2)}, u32[]{:S(2)}) async-start(f32[4,16,2,48,128]{4,3,2,1,0:T(8,128)} %pad_maximum_fusion.3), calls=%async_computation.1 | async-start | bytes 6291456 | tf_op jit(solution)/shard_map/all_to_all | solution.py:190
  89.6 25.5 %collective-permute-start.18 = (f32[3072,128]{1,0:T(8,128)S(1)}, f32[3072,128]{1,0:T(8,128)S(1)}, u32[]{:S(2)}, u32[]{:S(2)}) collective-permute-start(f32[3072,128]{1,0:T(8,128)S(1)} %bitcast.117), channel_id=1, source_target_pairs={{4,0},{8,4},{12,8},{16,12},{20,16},{24,20},{28,24},{32,28},{36,32}... | collective-permute-start | bytes 4718600 | tf_op jit(solution)/shard_map/ppermute | solution.py:165
  94.3 24.9 %collective-permute-start.19 = (f32[3072,128]{1,0:T(8,128)S(1)}, f32[3072,128]{1,0:T(8,128)S(1)}, u32[]{:S(2)}, u32[]{:S(2)}) collective-permute-start(f32[3072,128]{1,0:T(8,128)S(1)} %bitcast.116), channel_id=1, source_target_pairs={{0,4},{4,8},{8,12},{12,16},{16,20},{20,24},{24,28},{28,32},{32,36}... | collective-permute-start | bytes 4718600 | tf_op jit(solution)/shard_map/ppermute | solution.py:164
  108.2 29.7 %collective-permute-start.1 = (f32[3072,128]{1,0:T(8,128)}, f32[3072,128]{1,0:T(8,128)}, u32[]{:S(2)}, u32[]{:S(2)}) collective-permute-start(f32[3072,128]{1,0:T(8,128)} %bitcast.14), channel_id=1, source_target_pairs={{4,0},{8,4},{12,8},{16,12},{20,16},{24,20},{28,24},{32,28},{36,32}... | collective-permute-start | bytes 4718600 | tf_op jit(solution)/shard_map/ppermute | solution.py:165
  110.2 32.4 %collective-permute-start.3 = (f32[3072,128]{1,0:T(8,128)S(1)}, f32[3072,128]{1,0:T(8,128)}, u32[]{:S(2)}, u32[]{:S(2)}) collective-permute-start(f32[3072,128]{1,0:T(8,128)S(1)} %bitcast.114), channel_id=1, source_target_pairs={{0,4},{4,8},{8,12},{12,16},{16,20},{20,24},{24,28},{28,32},{32,36}... | collective-permute-start | bytes 4718600 | tf_op jit(solution)/shard_map/ppermute | solution.py:164
  113.8 19.6 %collective-permute-start.4 = (f32[128,128]{1,0:T(8,128)}, f32[128,128]{1,0:T(8,128)S(1)}, u32[]{:S(2)}, u32[]{:S(2)}) collective-permute-start(f32[128,128]{1,0:T(8,128)} %bitcast.18), channel_id=1, source_target_pairs={{1,0},{2,1},{3,2},{5,4},{6,5},{7,6},{9,8},{10,9},{11,10},{13,12},{... | collective-permute-start | bytes 196616 | tf_op jit(solution)/shard_map/ppermute | solution.py:165
  115.1 21.5 %collective-permute-start.5 = (f32[128,128]{1,0:T(8,128)}, f32[128,128]{1,0:T(8,128)S(1)}, u32[]{:S(2)}, u32[]{:S(2)}) collective-permute-start(f32[128,128]{1,0:T(8,128)} %bitcast.20), channel_id=1, source_target_pairs={{0,1},{1,2},{2,3},{4,5},{5,6},{6,7},{8,9},{9,10},{10,11},{12,13},{... | collective-permute-start | bytes 196616 | tf_op jit(solution)/shard_map/ppermute | solution.py:164
  131.0 34.0 %collective-permute-start.22 = (f32[3072,128]{1,0:T(8,128)}, f32[3072,128]{1,0:T(8,128)}, u32[]{:S(2)}, u32[]{:S(2)}) collective-permute-start(f32[3072,128]{1,0:T(8,128)} %bitcast.62), channel_id=1, source_target_pairs={{4,0},{8,4},{12,8},{16,12},{20,16},{24,20},{28,24},{32,28},{36,32}... | collective-permute-start | bytes 4718600 | tf_op jit(solution)/shard_map/ppermute | solution.py:165
  133.4 35.7 %collective-permute-start.23 = (f32[3072,128]{1,0:T(8,128)}, f32[3072,128]{1,0:T(8,128)}, u32[]{:S(2)}, u32[]{:S(2)}) collective-permute-start(f32[3072,128]{1,0:T(8,128)} %bitcast.64), channel_id=1, source_target_pairs={{0,4},{4,8},{8,12},{12,16},{16,20},{20,24},{24,28},{28,32},{32,36}... | collective-permute-start | bytes 4718600 | tf_op jit(solution)/shard_map/ppermute | solution.py:164
  136.6 24.3 %collective-permute-start.24 = (f32[128,128]{1,0:T(8,128)}, f32[128,128]{1,0:T(8,128)S(1)}, u32[]{:S(2)}, u32[]{:S(2)}) collective-permute-start(f32[128,128]{1,0:T(8,128)} %bitcast.66), channel_id=1, source_target_pairs={{1,0},{2,1},{3,2},{5,4},{6,5},{7,6},{9,8},{10,9},{11,10},{13,12},{... | collective-permute-start | bytes 196616 | tf_op jit(solution)/shard_map/ppermute | solution.py:165
  137.9 25.7 %collective-permute-start.25 = (f32[128,128]{1,0:T(8,128)}, f32[128,128]{1,0:T(8,128)}, u32[]{:S(2)}, u32[]{:S(2)}) collective-permute-start(f32[128,128]{1,0:T(8,128)} %bitcast.68), channel_id=1, source_target_pairs={{0,1},{1,2},{2,3},{4,5},{5,6},{6,7},{8,9},{9,10},{10,11},{12,13},{... | collective-permute-start | bytes 196616 | tf_op jit(solution)/shard_map/ppermute | solution.py:164
  158.1 30.2 %collective-permute-start.6 = (f32[3072,128]{1,0:T(8,128)}, f32[3072,128]{1,0:T(8,128)}, u32[]{:S(2)}, u32[]{:S(2)}) collective-permute-start(f32[3072,128]{1,0:T(8,128)} %bitcast.22), channel_id=1, source_target_pairs={{4,0},{8,4},{12,8},{16,12},{20,16},{24,20},{28,24},{32,28},{36,32}... | collective-permute-start | bytes 4718600 | tf_op jit(solution)/shard_map/ppermute | solution.py:165
  161.0 31.4 %collective-permute-start.7 = (f32[3072,128]{1,0:T(8,128)S(1)}, f32[3072,128]{1,0:T(8,128)}, u32[]{:S(2)}, u32[]{:S(2)}) collective-permute-start(f32[3072,128]{1,0:T(8,128)S(1)} %bitcast.113), channel_id=1, source_target_pairs={{0,4},{4,8},{8,12},{12,16},{16,20},{20,24},{24,28},{28,32},{32,36}... | collective-permute-start | bytes 4718600 | tf_op jit(solution)/shard_map/ppermute | solution.py:164
  163.7 21.1 %collective-permute-start.8 = (f32[128,128]{1,0:T(8,128)}, f32[128,128]{1,0:T(8,128)S(1)}, u32[]{:S(2)}, u32[]{:S(2)}) collective-permute-start(f32[128,128]{1,0:T(8,128)} %bitcast.26), channel_id=1, source_target_pairs={{1,0},{2,1},{3,2},{5,4},{6,5},{7,6},{9,8},{10,9},{11,10},{13,12},{... | collective-permute-start | bytes 196616 | tf_op jit(solution)/shard_map/ppermute | solution.py:165
  165.0 22.0 %collective-permute-start.9 = (f32[128,128]{1,0:T(8,128)}, f32[128,128]{1,0:T(8,128)S(1)}, u32[]{:S(2)}, u32[]{:S(2)}) collective-permute-start(f32[128,128]{1,0:T(8,128)} %bitcast.28), channel_id=1, source_target_pairs={{0,1},{1,2},{2,3},{4,5},{5,6},{6,7},{8,9},{9,10},{10,11},{12,13},{... | collective-permute-start | bytes 196616 | tf_op jit(solution)/shard_map/ppermute | solution.py:164
  181.4 33.3 %collective-permute-start.26 = (f32[3072,128]{1,0:T(8,128)}, f32[3072,128]{1,0:T(8,128)}, u32[]{:S(2)}, u32[]{:S(2)}) collective-permute-start(f32[3072,128]{1,0:T(8,128)} %bitcast.71), channel_id=1, source_target_pairs={{4,0},{8,4},{12,8},{16,12},{20,16},{24,20},{28,24},{32,28},{36,32}... | collective-permute-start | bytes 4718600 | tf_op jit(solution)/shard_map/ppermute | solution.py:165
  184.7 34.6 %collective-permute-start.27 = (f32[3072,128]{1,0:T(8,128)}, f32[3072,128]{1,0:T(8,128)}, u32[]{:S(2)}, u32[]{:S(2)}) collective-permute-start(f32[3072,128]{1,0:T(8,128)} %bitcast.73), channel_id=1, source_target_pairs={{0,4},{4,8},{8,12},{12,16},{16,20},{20,24},{24,28},{28,32},{32,36}... | collective-permute-start | bytes 4718600 | tf_op jit(solution)/shard_map/ppermute | solution.py:164
  187.0 24.4 %collective-permute-start.28 = (f32[128,128]{1,0:T(8,128)}, f32[128,128]{1,0:T(8,128)S(1)}, u32[]{:S(2)}, u32[]{:S(2)}) collective-permute-start(f32[128,128]{1,0:T(8,128)} %bitcast.75), channel_id=1, source_target_pairs={{1,0},{2,1},{3,2},{5,4},{6,5},{7,6},{9,8},{10,9},{11,10},{13,12},{... | collective-permute-start | bytes 196616 | tf_op jit(solution)/shard_map/ppermute | solution.py:165
  188.3 25.1 %collective-permute-start.29 = (f32[128,128]{1,0:T(8,128)}, f32[128,128]{1,0:T(8,128)S(1)}, u32[]{:S(2)}, u32[]{:S(2)}) collective-permute-start(f32[128,128]{1,0:T(8,128)} %bitcast.77), channel_id=1, source_target_pairs={{0,1},{1,2},{2,3},{4,5},{5,6},{6,7},{8,9},{9,10},{10,11},{12,13},{... | collective-permute-start | bytes 196616 | tf_op jit(solution)/shard_map/ppermute | solution.py:164
  207.6 29.4 %collective-permute-start.10 = (f32[3072,128]{1,0:T(8,128)}, f32[3072,128]{1,0:T(8,128)}, u32[]{:S(2)}, u32[]{:S(2)}) collective-permute-start(f32[3072,128]{1,0:T(8,128)} %bitcast.32), channel_id=1, source_target_pairs={{4,0},{8,4},{12,8},{16,12},{20,16},{24,20},{28,24},{32,28},{36,32}... | collective-permute-start | bytes 4718600 | tf_op jit(solution)/shard_map/ppermute | solution.py:165
  211.4 29.8 %collective-permute-start.11 = (f32[3072,128]{1,0:T(8,128)S(1)}, f32[3072,128]{1,0:T(8,128)}, u32[]{:S(2)}, u32[]{:S(2)}) collective-permute-start(f32[3072,128]{1,0:T(8,128)S(1)} %bitcast.115), channel_id=1, source_target_pairs={{0,4},{4,8},{8,12},{12,16},{16,20},{20,24},{24,28},{28,32},{32,36}... | collective-permute-start | bytes 4718600 | tf_op jit(solution)/shard_map/ppermute | solution.py:164
  213.4 20.4 %collective-permute-start.12 = (f32[128,128]{1,0:T(8,128)}, f32[128,128]{1,0:T(8,128)S(1)}, u32[]{:S(2)}, u32[]{:S(2)}) collective-permute-start(f32[128,128]{1,0:T(8,128)} %bitcast.36), channel_id=1, source_target_pairs={{1,0},{2,1},{3,2},{5,4},{6,5},{7,6},{9,8},{10,9},{11,10},{13,12},{... | collective-permute-start | bytes 196616 | tf_op jit(solution)/shard_map/ppermute | solution.py:165
  214.7 21.0 %collective-permute-start.13 = (f32[128,128]{1,0:T(8,128)}, f32[128,128]{1,0:T(8,128)}, u32[]{:S(2)}, u32[]{:S(2)}) collective-permute-start(f32[128,128]{1,0:T(8,128)} %bitcast.38), channel_id=1, source_target_pairs={{0,1},{1,2},{2,3},{4,5},{5,6},{6,7},{8,9},{9,10},{10,11},{12,13},{... | collective-permute-start | bytes 196616 | tf_op jit(solution)/shard_map/ppermute | solution.py:164
  229.7 34.7 %collective-permute-start.30 = (f32[3072,128]{1,0:T(8,128)}, f32[3072,128]{1,0:T(8,128)}, u32[]{:S(2)}, u32[]{:S(2)}) collective-permute-start(f32[3072,128]{1,0:T(8,128)} %bitcast.79), channel_id=1, source_target_pairs={{4,0},{8,4},{12,8},{16,12},{20,16},{24,20},{28,24},{32,28},{36,32}... | collective-permute-start | bytes 4718600 | tf_op jit(solution)/shard_map/ppermute | solution.py:165
  233.8 35.3 %collective-permute-start.31 = (f32[3072,128]{1,0:T(8,128)}, f32[3072,128]{1,0:T(8,128)}, u32[]{:S(2)}, u32[]{:S(2)}) collective-permute-start(f32[3072,128]{1,0:T(8,128)} %bitcast.81), channel_id=1, source_target_pairs={{0,4},{4,8},{8,12},{12,16},{16,20},{20,24},{24,28},{28,32},{32,36}... | collective-permute-start | bytes 4718600 | tf_op jit(solution)/shard_map/ppermute | solution.py:164
  235.7 25.5 %collective-permute-start.32 = (f32[128,128]{1,0:T(8,128)}, f32[128,128]{1,0:T(8,128)S(1)}, u32[]{:S(2)}, u32[]{:S(2)}) collective-permute-start(f32[128,128]{1,0:T(8,128)} %bitcast.83), channel_id=1, source_target_pairs={{1,0},{2,1},{3,2},{5,4},{6,5},{7,6},{9,8},{10,9},{11,10},{13,12},{... | collective-permute-start | bytes 196616 | tf_op jit(solution)/shard_map/ppermute | solution.py:165
  237.0 26.1 %collective-permute-start.33 = (f32[128,128]{1,0:T(8,128)}, f32[128,128]{1,0:T(8,128)S(1)}, u32[]{:S(2)}, u32[]{:S(2)}) collective-permute-start(f32[128,128]{1,0:T(8,128)} %bitcast.85), channel_id=1, source_target_pairs={{0,1},{1,2},{2,3},{4,5},{5,6},{6,7},{8,9},{9,10},{10,11},{12,13},{... | collective-permute-start | bytes 196616 | tf_op jit(solution)/shard_map/ppermute | solution.py:164
  257.1 26.1 %collective-permute-start.14 = (f32[3072,128]{1,0:T(8,128)}, f32[3072,128]{1,0:T(8,128)}, u32[]{:S(2)}, u32[]{:S(2)}) collective-permute-start(f32[3072,128]{1,0:T(8,128)} %bitcast.40), channel_id=1, source_target_pairs={{4,0},{8,4},{12,8},{16,12},{20,16},{24,20},{28,24},{32,28},{36,32}... | collective-permute-start | bytes 4718600 | tf_op jit(solution)/shard_map/ppermute | solution.py:165
  261.2 22.0 %collective-permute-start.15 = (f32[3072,128]{1,0:T(8,128)S(1)}, f32[3072,128]{1,0:T(8,128)}, u32[]{:S(2)}, u32[]{:S(2)}) collective-permute-start(f32[3072,128]{1,0:T(8,128)S(1)} %bitcast.118), channel_id=1, source_target_pairs={{0,4},{4,8},{8,12},{12,16},{16,20},{20,24},{24,28},{28,32},{32,36}... | collective-permute-start | bytes 4718600 | tf_op jit(solution)/shard_map/ppermute | solution.py:164
  263.1 20.0 %collective-permute-start.16 = (f32[128,128]{1,0:T(8,128)}, f32[128,128]{1,0:T(8,128)S(1)}, u32[]{:S(2)}, u32[]{:S(2)}) collective-permute-start(f32[128,128]{1,0:T(8,128)} %bitcast.44), channel_id=1, source_target_pairs={{1,0},{2,1},{3,2},{5,4},{6,5},{7,6},{9,8},{10,9},{11,10},{13,12},{... | collective-permute-start | bytes 196616 | tf_op jit(solution)/shard_map/ppermute | solution.py:165
  264.4 18.7 %collective-permute-start.17 = (f32[128,128]{1,0:T(8,128)}, f32[128,128]{1,0:T(8,128)}, u32[]{:S(2)}, u32[]{:S(2)}) collective-permute-start(f32[128,128]{1,0:T(8,128)} %bitcast.46), channel_id=1, source_target_pairs={{0,1},{1,2},{2,3},{4,5},{5,6},{6,7},{8,9},{9,10},{10,11},{12,13},{... | collective-permute-start | bytes 196616 | tf_op jit(solution)/shard_map/ppermute | solution.py:164
  (23 other events, 315.4 us)

commit v8 on v6

--- a/solution.py
+++ b/solution.py
@@ -113,36 +113,44 @@
     )(tiles)
 
 
-def gram_kernel(a_ref, b_ref, out_ref):
+def gram_kernel(c1_ref, c2_ref, o1_ref, o2_ref, out_ref, ctrl_ref, obsv_ref):
     @pl.when((pl.program_id(0) == 0) & (pl.program_id(1) == 0))
     def _():
         out_ref[...] = jnp.zeros_like(out_ref)
 
-    rows = a_ref.shape[2]
-    left = jnp.concatenate([a_ref[:, 0, row, :] for row in range(rows)], axis=1)
-    right = jnp.concatenate([b_ref[:, 0, row, :] for row in range(rows)], axis=1)
+    ctrl_ref[0] = c1_ref[...]
+    ctrl_ref[1] = c2_ref[...]
+    obsv_ref[0] = o1_ref[...]
+    obsv_ref[1] = o2_ref[...]
+    rows = c1_ref.shape[2]
+
+    def flat(first, second):
+        stacked = [jnp.concatenate([first[:, 0, row, :], second[:, 0, row, :]], axis=0) for row in range(rows)]
+        return jnp.concatenate(stacked, axis=1)
+
     out_ref[...] += lax.dot_general(
-        left,
-        right,
+        flat(c1_ref, c2_ref),
+        flat(o1_ref, o2_ref),
         (((1,), (1,)), ((), ())),
         precision=lax.Precision.HIGHEST,
         preferred_element_type=jnp.float32,
     )
 
 
-def gram(a, b, rows_per_step=48):
-    count, depth, rows, lanes = a.shape
+def gram(ctrl_parts, obsv_parts, rows_per_step=16):
+    count, depth, rows, lanes = ctrl_parts[0].shape
     spec = pl.BlockSpec((count, 1, rows_per_step, lanes), lambda i, j: (0, i, j, 0))
+    stack_spec = pl.BlockSpec((2, count, 1, rows_per_step, lanes), lambda i, j: (0, 0, i, j, 0))
+    stacked = jax.ShapeDtypeStruct((2,) + ctrl_parts[0].shape, jnp.float32)
+    cells = 4 * ctrl_parts[0].size
     return pl.pallas_call(
         gram_kernel,
         grid=(depth, rows // rows_per_step),
-        in_specs=[spec, spec],
-        out_specs=pl.BlockSpec((count, count), lambda i, j: (0, 0)),
-        out_shape=jax.ShapeDtypeStruct((count, count), jnp.float32),
-        cost_estimate=pl.CostEstimate(
-            flops=2 * count * count * a.size // count, bytes_accessed=8 * a.size, transcendentals=0
-        ),
-    )(a, b)
+        in_specs=[spec] * 4,
+        out_specs=[pl.BlockSpec((2 * count, 2 * count), lambda i, j: (0, 0)), stack_spec, stack_spec],
+        out_shape=[jax.ShapeDtypeStruct((2 * count, 2 * count), jnp.float32), stacked, stacked],
+        cost_estimate=pl.CostEstimate(flops=2 * count * cells, bytes_accessed=8 * cells, transcendentals=0),
+    )(*ctrl_parts, *obsv_parts)
 
 
 def lookup(region_ids, region_cond):
@@ -236,7 +244,7 @@
         else:
             current = current - (shifts[segment_idx - 1] + shift_val) * solver(current, shift_val)
         factors.append(jnp.sqrt(2.0 * shift_val) * current)
-    return jnp.stack(factors)
+    return factors
 
 
 def body(input_map, output_map, region_ids, region_cond, shift_ids):
@@ -257,11 +265,8 @@
     solver = lambda rhs, shift_val: solve_slabs(rhs, shift_val, cond_max, coeffs)
     ctrl_cols = run_segments(ctrl_in, shifts, solver)
     obsv_cols = run_segments(obsv_in, shifts, solver)
-    row_count = ctrl_cols.shape[0] * ctrl_cols.shape[1]
-    partial_value = gram(
-        ctrl_cols.reshape((row_count,) + ctrl_cols.shape[2:]),
-        obsv_cols.reshape((row_count,) + obsv_cols.shape[2:]),
-    )
+    partial_value, ctrl_cols, obsv_cols = gram(ctrl_cols, obsv_cols)
+    row_count = partial_value.shape[0]
     cells_total = total_x * region_ids.shape[1] * region_ids.shape[2]
     norm_scale = 1.0 / math.sqrt(cells_total)
     slab_count = lax.axis_size("slab")

time: 340 us -> 343 us (level)
  other arithmetic: 88.1 us -> 83.2 us
  Pallas kernels: 41.8 us -> 46.2 us
    another operation x6 -> x0, other arithmetic: 42.1 us -> none  [run_segments(): return jnp.stack(factors)]
    mul x0 -> x4, other arithmetic: none -> 21.6 us  [run_segments(): factors.append(jnp.sqrt(2.0 * shift_val) * current)]
    div x3, other arithmetic: 3.17 us -> 18.1 us  [solve_slabs(): direction = right_side / mid_eig]
  transfers between devices with their start and end apart: 36 -> 36, of which waited for: 2 -> 4; matrix products, arithmetic and copies ran while one was open for 33% -> 32% of each run, Pallas kernels for 0% -> 0%
where the time goes in v8:
time: 343 us; the launch traced here: 342 us
  starting transfers between devices  109 us (32%)
  other arithmetic  83.2 us (24%)
  local copies, waits for them, and re-layouts  48 us (14%)
  waiting for transfers between devices  46.4 us (14%)
  Pallas kernels  46.2 us (13%)
  between operations  9.05 us (3%)
    ppermute x16, starting transfers between devices, halo_pair(): lax.ppermute(lax.slice_in_dim(block, size - 1, None, axis=dim), axis, for...  54.3 us
    all_to_all x2, waiting for transfers between devices, windows(): received = lax.all_to_all(jnp.stack(parts), 'col', 0, 0, tiled=True)  44 us
    ppermute x16, starting transfers between devices, halo_pair(): high = lax.ppermute(lax.slice_in_dim(block, 0, 1, axis=dim), axis, backward)  37.6 us
    add x4, other arithmetic, solve_slabs(): rho_next * rho_now * direction + 2.0 * rho_next / half_span * residual  31.6 us
    pallas_call x1, Pallas kernels, reduce_scatter(): pl.pallas_call(reduce_kernel, out_shape=jax.ShapeDtypeStruct((1, 1, lanes...  30.8 us
    slice x14, local copies, waits for them, and re-layouts, shifted(): lax.slice_in_dim(block, 1, None, axis=dim)  26 us
    mul x4, other arithmetic, run_segments(): factors.append(jnp.sqrt(2.0 * shift_val) * current)  21.6 us
    div x3, other arithmetic, solve_slabs(): direction = right_side / mid_eig  18.1 us
  transfers between devices with their start and end apart: 36, of which 4 were waited for; matrix products, arithmetic and copies ran while one was open for 32% of the time, Pallas kernels for 0%

profile of v8, /device:TPU:1, one launch (start us, length us, event | category | flops | bytes accessed | tf_op | source)
XLA Modules:
  0.0 341.5 jit_solution(17360521754025719806)
XLA Ops:
  4.6 4.8 %all-to-all-start = ((f32[4,16,2,48,128]{4,3,2,1,0:T(8,128)}), f32[4,16,2,48,128]{4,3,2,1,0:T(8,128)S(1)}, u32[]{:S(2)}, u32[]{:S(2)}) async-start(f32[4,16,2,48,128]{4,3,2,1,0:T(8,128)} %pad_maximum_fusion), calls=%async_computation | async-start | bytes 6291456 | tf_op jit(solution)/shard_map/all_to_all | solution.py:194
  13.4 32.6 %all-to-all-done = f32[4,16,2,48,128]{4,3,2,1,0:T(8,128)S(1)} async-done(((f32[4,16,2,48,128]{4,3,2,1,0:T(8,128)}), f32[4,16,2,48,128]{4,3,2,1,0:T(8,128)S(1)}, u32[]{:S(2)}, u32[]{:S(2)}) %all-to-all-start) | async-done | bytes 3145760 | tf_op jit(solution)/shard_map/all_to_all | solution.py:194
  46.1 4.7 %all-to-all-start.1 = ((f32[4,16,2,48,128]{4,3,2,1,0:T(8,128)}), f32[4,16,2,48,128]{4,3,2,1,0:T(8,128)}, u32[]{:S(2)}, u32[]{:S(2)}) async-start(f32[4,16,2,48,128]{4,3,2,1,0:T(8,128)} %pad_maximum_fusion.1), calls=%async_computation.1 | async-start | bytes 6291456 | tf_op jit(solution)/shard_map/all_to_all | solution.py:194
  51.5 5.2 %select_add_fusion = f32[2,192,128]{2,1,0:T(8,128)S(1)} fusion(s32[2,192,128]{2,1,0:T(8,128)S(1)} %copy-done.8, f32[]{:T(128)} %bitcast.13, f32[]{:T(128)} %bitcast.12, f32[]{:T(128)} %bitcast.11, f32[]{:T(128)} %bitcast.10, f32[]{:T(128)} %bitcast.9, f32[]{:T(128)} %bitcast.8, f32[]{:T(128)} %bitcast.7, f32[]{:T(128)} %bitcast.6), kind=kLoop, calls=%fused_computation.206 | loop fusion | flops 1130496 | bytes 393248 | tf_op jit(solution)/shard_map/add | solution.py:159
  56.7 3.8 %collective-permute-start = (f32[1,50,128]{2,1,0:T(8,128)S(1)}, f32[1,50,128]{2,1,0:T(8,128)S(1)}, u32[]{:S(2)}, u32[]{:S(2)}) collective-permute-start(f32[1,50,128]{2,1,0:T(8,128)S(1)} %get-tuple-element.82), channel_id=1, source_target_pairs={{4,0},{8,4},{12,8},{16,12},{20,16},{24,20},{28,24},{32,28},{36,32}... | collective-permute-start | bytes 76808 | tf_op jit(solution)/shard_map/ppermute | solution.py:22
  75.1 11.4 %all-to-all-done.1 = f32[4,16,2,48,128]{4,3,2,1,0:T(8,128)} async-done(((f32[4,16,2,48,128]{4,3,2,1,0:T(8,128)}), f32[4,16,2,48,128]{4,3,2,1,0:T(8,128)}, u32[]{:S(2)}, u32[]{:S(2)}) %all-to-all-start.1) | async-done | bytes 3145760 | tf_op jit(solution)/shard_map/all_to_all | solution.py:194
  89.5 4.7 %collective-permute-start.18 = (f32[64,1,48,128]{3,2,1,0:T(8,128)S(1)}, f32[64,1,48,128]{3,2,1,0:T(8,128)S(1)}, u32[]{:S(2)}, u32[]{:S(2)}) collective-permute-start(f32[64,1,48,128]{3,2,1,0:T(8,128)S(1)} %get-tuple-element.42), channel_id=1, source_target_pairs={{4,0},{8,4},{12,8},{16,12},{20,16},{24,20},{28,24},{32,28},{36,32}... | collective-permute-start | bytes 4718600 | tf_op jit(solution)/shard_map/ppermute | solution.py:169
  99.1 4.0 %collective-permute-start.21 = (f32[64,2,1,128]{3,2,1,0:T(1,128)S(1)}, f32[64,2,1,128]{3,2,1,0:T(1,128)S(1)}, u32[]{:S(2)}, u32[]{:S(2)}) collective-permute-start(f32[64,2,1,128]{3,2,1,0:T(1,128)S(1)} %get-tuple-element.46), channel_id=1, source_target_pairs={{0,1},{1,2},{2,3},{4,5},{5,6},{6,7},{8,9},{9,10},{10,11},{12,13},{... | collective-permute-start | bytes 196616 | tf_op jit(solution)/shard_map/ppermute | solution.py:168
  110.7 3.6 %collective-permute-start.3 = (f32[64,1,48,128]{3,2,1,0:T(8,128)}, f32[64,1,48,128]{3,2,1,0:T(8,128)}, u32[]{:S(2)}, u32[]{:S(2)}) collective-permute-start(f32[64,1,48,128]{3,2,1,0:T(8,128)} %get-tuple-element.69), channel_id=1, source_target_pairs={{0,4},{4,8},{8,12},{12,16},{16,20},{20,24},{24,28},{28,32},{32,36}... | collective-permute-start | bytes 4718600 | tf_op jit(solution)/shard_map/ppermute | solution.py:168
  115.7 4.0 %collective-permute-start.5 = (f32[64,2,1,128]{3,2,1,0:T(1,128)}, f32[64,2,1,128]{3,2,1,0:T(1,128)S(1)}, u32[]{:S(2)}, u32[]{:S(2)}) collective-permute-start(f32[64,2,1,128]{3,2,1,0:T(1,128)} %get-tuple-element.74), channel_id=1, source_target_pairs={{0,1},{1,2},{2,3},{4,5},{5,6},{6,7},{8,9},{9,10},{10,11},{12,13},{... | collective-permute-start | bytes 196616 | tf_op jit(solution)/shard_map/ppermute | solution.py:168
  120.9 7.7 %multiply_add_fusion.1 = (f32[64,2,48,128]{3,2,1,0:T(8,128)S(1)}, f32[64,2,48,128]{3,2,1,0:T(8,128)}) fusion(f32[64,2,48,128]{3,2,1,0:T(8,128)S(1)} %get-tuple-element.98, f32[]{:T(128)S(6)} %div.73, f32[]{:T(128)S(6)} %mul.258, f32[]{:T(128)} %bitcast, f32[2,48,128]{2,1,0:T(8,128)S(1)} %get-tuple-element.84, f32[2,48,128]{2,1,0:T(8,128)S(1)} %copy-done.4, ...), kind=kLoop, calls=%fused_computation.191 | loop fusion | flops 21233664 | bytes 25460748 | tf_op jit(solution)/shard_map/add | solution.py:232
  138.2 4.0 %collective-permute-start.25 = (f32[64,2,1,128]{3,2,1,0:T(1,128)}, f32[64,2,1,128]{3,2,1,0:T(1,128)S(1)}, u32[]{:S(2)}, u32[]{:S(2)}) collective-permute-start(f32[64,2,1,128]{3,2,1,0:T(1,128)} %get-tuple-element.40), channel_id=1, source_target_pairs={{0,1},{1,2},{2,3},{4,5},{5,6},{6,7},{8,9},{9,10},{10,11},{12,13},{... | collective-permute-start | bytes 196616 | tf_op jit(solution)/shard_map/ppermute | solution.py:168
  142.2 7.9 %multiply_add_fusion.3 = (f32[64,2,48,128]{3,2,1,0:T(8,128)S(1)}, f32[64,2,48,128]{3,2,1,0:T(8,128)}) fusion(f32[64,2,48,128]{3,2,1,0:T(8,128)S(1)} %get-tuple-element.99, f32[]{:T(128)S(6)} %div.73, f32[]{:T(128)S(6)} %mul.258, f32[]{:T(128)} %bitcast, f32[2,48,128]{2,1,0:T(8,128)S(1)} %get-tuple-element.84, f32[2,48,128]{2,1,0:T(8,128)S(1)} %copy-done.4, ...), kind=kLoop, calls=%fused_computation.193 | loop fusion | flops 21233664 | bytes 25460748 | tf_op jit(solution)/shard_map/add | solution.py:232
  152.0 3.5 %fusion.163 = (f32[64,2,47,128]{3,2,1,0:T(8,128)}, f32[64,2,47,128]{3,2,1,0:T(8,128)}) fusion(f32[64,2,48,128]{3,2,1,0:T(8,128)S(1)} %get-tuple-element.13), kind=kLoop, calls=%fused_computation.238 | loop fusion | bytes 12320768 | tf_op jit(solution)/shard_map/slice | solution.py:175
  155.5 3.5 %fusion.175 = (f32[64,2,47,128]{3,2,1,0:T(8,128)}, f32[64,2,47,128]{3,2,1,0:T(8,128)}) fusion(f32[64,2,48,128]{3,2,1,0:T(8,128)S(1)} %get-tuple-element.19), kind=kLoop, calls=%fused_computation.250 | loop fusion | bytes 12320768 | tf_op jit(solution)/shard_map/slice | solution.py:175
  166.6 4.6 %collective-permute-start.9 = (f32[64,2,1,128]{3,2,1,0:T(1,128)}, f32[64,2,1,128]{3,2,1,0:T(1,128)}, u32[]{:S(2)}, u32[]{:S(2)}) collective-permute-start(f32[64,2,1,128]{3,2,1,0:T(1,128)} %get-tuple-element.68), channel_id=1, source_target_pairs={{0,1},{1,2},{2,3},{4,5},{5,6},{6,7},{8,9},{9,10},{10,11},{12,13},{... | collective-permute-start | bytes 196616 | tf_op jit(solution)/shard_map/ppermute | solution.py:168
  171.3 7.4 %broadcast_divide_fusion = (f32[64,2,48,128]{3,2,1,0:T(8,128)S(1)}, f32[64,2,48,128]{3,2,1,0:T(8,128)S(1)}) fusion(f32[]{:T(128)S(6)} %mul.604, f32[64,2,48,128]{3,2,1,0:T(8,128)} %get-tuple-element.14, f32[64,2,48,128]{3,2,1,0:T(8,128)S(1)} %get-tuple-element.13, f32[]{:T(128)} %bitcast, f32[2,48,128]{2,1,0:T(8,128)S(1)} %get-tuple-element.84, ...), kind=kLoop, calls=%fused_computation.194 | loop fusion | flops 23592960 | bytes 28606480 | tf_op jit(solution)/shard_map/div | solution.py:226
  187.7 4.0 %collective-permute-start.29 = (f32[64,2,1,128]{3,2,1,0:T(1,128)}, f32[64,2,1,128]{3,2,1,0:T(1,128)S(1)}, u32[]{:S(2)}, u32[]{:S(2)}) collective-permute-start(f32[64,2,1,128]{3,2,1,0:T(1,128)} %get-tuple-element.34), channel_id=1, source_target_pairs={{0,1},{1,2},{2,3},{4,5},{5,6},{6,7},{8,9},{9,10},{10,11},{12,13},{... | collective-permute-start | bytes 196616 | tf_op jit(solution)/shard_map/ppermute | solution.py:168
  191.8 7.9 %broadcast_divide_fusion.1 = (f32[64,2,48,128]{3,2,1,0:T(8,128)S(1)}, f32[64,2,48,128]{3,2,1,0:T(8,128)S(1)}) fusion(f32[]{:T(128)S(6)} %mul.604, f32[64,2,48,128]{3,2,1,0:T(8,128)} %get-tuple-element.20, f32[64,2,48,128]{3,2,1,0:T(8,128)S(1)} %get-tuple-element.19, f32[]{:T(128)} %bitcast, f32[2,48,128]{2,1,0:T(8,128)S(1)} %get-tuple-element.84, ...), kind=kLoop, calls=%fused_computation.195 | loop fusion | flops 23592960 | bytes 28606480 | tf_op jit(solution)/shard_map/div | solution.py:226
  201.6 3.8 %collective-permute-start.10 = (f32[64,1,48,128]{3,2,1,0:T(8,128)}, f32[64,1,48,128]{3,2,1,0:T(8,128)}, u32[]{:S(2)}, u32[]{:S(2)}) collective-permute-start(f32[64,1,48,128]{3,2,1,0:T(8,128)} %get-tuple-element.58), channel_id=1, source_target_pairs={{4,0},{8,4},{12,8},{16,12},{20,16},{24,20},{28,24},{32,28},{36,32}... | collective-permute-start | bytes 4718600 | tf_op jit(solution)/shard_map/ppermute | solution.py:169
  209.1 3.5 %fusion.160 = (f32[64,2,47,128]{3,2,1,0:T(8,128)}, f32[64,2,47,128]{3,2,1,0:T(8,128)}) fusion(f32[64,2,48,128]{3,2,1,0:T(8,128)S(1)} %get-tuple-element.11), kind=kLoop, calls=%fused_computation.235 | loop fusion | bytes 12320768 | tf_op jit(solution)/shard_map/slice | solution.py:175
  217.2 4.6 %collective-permute-start.13 = (f32[64,2,1,128]{3,2,1,0:T(1,128)}, f32[64,2,1,128]{3,2,1,0:T(1,128)}, u32[]{:S(2)}, u32[]{:S(2)}) collective-permute-start(f32[64,2,1,128]{3,2,1,0:T(1,128)} %get-tuple-element.62), channel_id=1, source_target_pairs={{0,1},{1,2},{2,3},{4,5},{5,6},{6,7},{8,9},{9,10},{10,11},{12,13},{... | collective-permute-start | bytes 196616 | tf_op jit(solution)/shard_map/ppermute | solution.py:168
  221.8 7.9 %multiply_add_fusion = (f32[64,2,48,128]{3,2,1,0:T(8,128)S(1)}, f32[64,2,48,128]{3,2,1,0:T(8,128)}) fusion(f32[]{:T(128)S(6)} %div.81, f32[]{:T(128)S(6)} %mul.607, f32[64,2,48,128]{3,2,1,0:T(8,128)S(1)} %get-tuple-element.12, f32[]{:T(128)S(6)} %mul.604, f32[64,2,48,128]{3,2,1,0:T(8,128)S(1)} %get-tuple-element.11, f32[]{:T(128)} %bitcast.14, ...), kind=kLoop, calls=%fused_computation.190 | loop fusion | flops 22020096 | bytes 25460752 | tf_op jit(solution)/shard_map/add | solution.py:232
  231.8 4.1 %collective-permute-start.30 = (f32[64,1,48,128]{3,2,1,0:T(8,128)}, f32[64,1,48,128]{3,2,1,0:T(8,128)}, u32[]{:S(2)}, u32[]{:S(2)}) collective-permute-start(f32[64,1,48,128]{3,2,1,0:T(8,128)} %get-tuple-element.28), channel_id=1, source_target_pairs={{4,0},{8,4},{12,8},{16,12},{20,16},{24,20},{28,24},{32,28},{36,32}... | collective-permute-start | bytes 4718600 | tf_op jit(solution)/shard_map/ppermute | solution.py:169
  239.4 8.1 %multiply_add_fusion.2 = (f32[64,2,48,128]{3,2,1,0:T(8,128)S(1)}, f32[64,2,48,128]{3,2,1,0:T(8,128)}) fusion(f32[]{:T(128)S(6)} %div.81, f32[]{:T(128)S(6)} %mul.607, f32[64,2,48,128]{3,2,1,0:T(8,128)S(1)} %get-tuple-element.18, f32[]{:T(128)S(6)} %mul.604, f32[64,2,48,128]{3,2,1,0:T(8,128)S(1)} %get-tuple-element.17, f32[]{:T(128)} %bitcast.14, ...), kind=kLoop, calls=%fused_computation.192 | loop fusion | flops 22020096 | bytes 25460752 | tf_op jit(solution)/shard_map/add | solution.py:232
  255.1 4.1 %collective-permute-start.33 = (f32[64,2,1,128]{3,2,1,0:T(1,128)S(1)}, f32[64,2,1,128]{3,2,1,0:T(1,128)S(1)}, u32[]{:S(2)}, u32[]{:S(2)}) collective-permute-start(f32[64,2,1,128]{3,2,1,0:T(1,128)S(1)} %get-tuple-element.23), channel_id=1, source_target_pairs={{0,1},{1,2},{2,3},{4,5},{5,6},{6,7},{8,9},{9,10},{10,11},{12,13},{... | collective-permute-start | bytes 196616 | tf_op jit(solution)/shard_map/ppermute | solution.py:168
  259.3 4.1 %collective-permute-start.14 = (f32[64,1,48,128]{3,2,1,0:T(8,128)}, f32[64,1,48,128]{3,2,1,0:T(8,128)}, u32[]{:S(2)}, u32[]{:S(2)}) collective-permute-start(f32[64,1,48,128]{3,2,1,0:T(8,128)} %get-tuple-element.56), channel_id=1, source_target_pairs={{4,0},{8,4},{12,8},{16,12},{20,16},{24,20},{28,24},{32,28},{36,32}... | collective-permute-start | bytes 4718600 | tf_op jit(solution)/shard_map/ppermute | solution.py:169
  268.0 4.0 %collective-permute-start.17 = (f32[64,2,1,128]{3,2,1,0:T(1,128)}, f32[64,2,1,128]{3,2,1,0:T(1,128)S(1)}, u32[]{:S(2)}, u32[]{:S(2)}) collective-permute-start(f32[64,2,1,128]{3,2,1,0:T(1,128)} %get-tuple-element.51), channel_id=1, source_target_pairs={{0,1},{1,2},{2,3},{4,5},{5,6},{6,7},{8,9},{9,10},{10,11},{12,13},{... | collective-permute-start | bytes 196616 | tf_op jit(solution)/shard_map/ppermute | solution.py:168
  272.0 8.7 %fusion.79.o2_ref = f32[64,2,48,128]{3,2,1,0:T(8,128)} fusion(f32[64,2,48,128]{3,2,1,0:T(8,128)S(1)} %get-tuple-element.12, f32[64,2,48,128]{3,2,1,0:T(8,128)S(1)} %copy-done, f32[64,2,48,128]{3,2,1,0:T(8,128)S(1)} %get-tuple-element.9, f32[64,1,48,128]{3,2,1,0:T(8,128)} %collective-permute-done.30, f32[64,1,48,128]{3,2,1,0:T(8,128)S(1)} %get-tuple-element.27, ...), kind=kLoop, calls=%fused_computation.95 | loop fusion | flops 25952256 | bytes 25460760 | tf_op jit(solution)/shard_map/mul | solution.py:246
  283.0 9.1 %fusion.38.c2_ref = f32[64,2,48,128]{3,2,1,0:T(8,128)} fusion(f32[64,2,48,128]{3,2,1,0:T(8,128)S(1)} %get-tuple-element.18, f32[64,2,48,128]{3,2,1,0:T(8,128)S(1)} %copy-done.1, f32[64,2,48,128]{3,2,1,0:T(8,128)S(1)} %get-tuple-element.15, f32[64,1,48,128]{3,2,1,0:T(8,128)} %collective-permute-done.14, f32[64,1,48,128]{3,2,1,0:T(8,128)} %get-tuple-element.55, ...), kind=kLoop, calls=%fused_computation.54 | loop fusion | flops 25952256 | bytes 25460760 | tf_op jit(solution)/shard_map/mul | solution.py:246
  292.1 15.4 %shard_map.76 = (f32[128,128]{1,0:T(8,128)}, f32[2,64,2,48,128]{4,3,2,1,0:T(8,128)}, f32[2,64,2,48,128]{4,3,2,1,0:T(8,128)}) custom-call(f32[64,2,48,128]{3,2,1,0:T(8,128)} %broadcast_multiply_fusion.1.c1_ref, f32[64,2,48,128]{3,2,1,0:T(8,128)} %fusion.38.c2_ref, f32[64,2,48,128]{3,2,1,0:T(8,128)} %broadcast_multiply_fusion.o1_ref, ...), custom_call_target="tpu_custom_call" | custom-call | flops 402653184 | bytes 25165824 | tf_op jit(solution)/shard_map/pallas_call | solution.py:146
  309.4 30.8 %shard_map.77 = f32[1,1,128]{2,1,0:T(1,128)} custom-call(f32[4,32,128]{2,1,0:T(8,128)} %reshape.30.tiles_ref), custom_call_target="tpu_custom_call" | custom-call | tf_op jit(solution)/shard_map/pallas_call | solution.py:98
  (125 shorter events, 94.9 us)
Async XLA Ops:
  4.6 41.5 %all-to-all-start = ((f32[4,16,2,48,128]{4,3,2,1,0:T(8,128)}), f32[4,16,2,48,128]{4,3,2,1,0:T(8,128)S(1)}, u32[]{:S(2)}, u32[]{:S(2)}) async-start(f32[4,16,2,48,128]{4,3,2,1,0:T(8,128)} %pad_maximum_fusion), calls=%async_computation | async-start | bytes 6291456 | tf_op jit(solution)/shard_map/all_to_all | solution.py:194
  46.1 40.5 %all-to-all-start.1 = ((f32[4,16,2,48,128]{4,3,2,1,0:T(8,128)}), f32[4,16,2,48,128]{4,3,2,1,0:T(8,128)}, u32[]{:S(2)}, u32[]{:S(2)}) async-start(f32[4,16,2,48,128]{4,3,2,1,0:T(8,128)} %pad_maximum_fusion.1), calls=%async_computation.1 | async-start | bytes 6291456 | tf_op jit(solution)/shard_map/all_to_all | solution.py:194
  56.7 16.3 %collective-permute-start = (f32[1,50,128]{2,1,0:T(8,128)S(1)}, f32[1,50,128]{2,1,0:T(8,128)S(1)}, u32[]{:S(2)}, u32[]{:S(2)}) collective-permute-start(f32[1,50,128]{2,1,0:T(8,128)S(1)} %get-tuple-element.82), channel_id=1, source_target_pairs={{4,0},{8,4},{12,8},{16,12},{20,16},{24,20},{28,24},{32,28},{36,32}... | collective-permute-start | bytes 76808 | tf_op jit(solution)/shard_map/ppermute | solution.py:22
  89.5 26.2 %collective-permute-start.18 = (f32[64,1,48,128]{3,2,1,0:T(8,128)S(1)}, f32[64,1,48,128]{3,2,1,0:T(8,128)S(1)}, u32[]{:S(2)}, u32[]{:S(2)}) collective-permute-start(f32[64,1,48,128]{3,2,1,0:T(8,128)S(1)} %get-tuple-element.42), channel_id=1, source_target_pairs={{4,0},{8,4},{12,8},{16,12},{20,16},{24,20},{28,24},{32,28},{36,32}... | collective-permute-start | bytes 4718600 | tf_op jit(solution)/shard_map/ppermute | solution.py:169
  94.2 25.5 %collective-permute-start.19 = (f32[64,1,48,128]{3,2,1,0:T(8,128)S(1)}, f32[64,1,48,128]{3,2,1,0:T(8,128)S(1)}, u32[]{:S(2)}, u32[]{:S(2)}) collective-permute-start(f32[64,1,48,128]{3,2,1,0:T(8,128)S(1)} %get-tuple-element.41), channel_id=1, source_target_pairs={{0,4},{4,8},{8,12},{12,16},{16,20},{20,24},{24,28},{28,32},{32,36}... | collective-permute-start | bytes 4718600 | tf_op jit(solution)/shard_map/ppermute | solution.py:168
  99.1 15.3 %collective-permute-start.21 = (f32[64,2,1,128]{3,2,1,0:T(1,128)S(1)}, f32[64,2,1,128]{3,2,1,0:T(1,128)S(1)}, u32[]{:S(2)}, u32[]{:S(2)}) collective-permute-start(f32[64,2,1,128]{3,2,1,0:T(1,128)S(1)} %get-tuple-element.46), channel_id=1, source_target_pairs={{0,1},{1,2},{2,3},{4,5},{5,6},{6,7},{8,9},{9,10},{10,11},{12,13},{... | collective-permute-start | bytes 196616 | tf_op jit(solution)/shard_map/ppermute | solution.py:168
  108.8 29.4 %collective-permute-start.1 = (f32[64,1,48,128]{3,2,1,0:T(8,128)}, f32[64,1,48,128]{3,2,1,0:T(8,128)}, u32[]{:S(2)}, u32[]{:S(2)}) collective-permute-start(f32[64,1,48,128]{3,2,1,0:T(8,128)} %get-tuple-element.70), channel_id=1, source_target_pairs={{4,0},{8,4},{12,8},{16,12},{20,16},{24,20},{28,24},{32,28},{36,32}... | collective-permute-start | bytes 4718600 | tf_op jit(solution)/shard_map/ppermute | solution.py:169
  110.7 31.5 %collective-permute-start.3 = (f32[64,1,48,128]{3,2,1,0:T(8,128)}, f32[64,1,48,128]{3,2,1,0:T(8,128)}, u32[]{:S(2)}, u32[]{:S(2)}) collective-permute-start(f32[64,1,48,128]{3,2,1,0:T(8,128)} %get-tuple-element.69), channel_id=1, source_target_pairs={{0,4},{4,8},{8,12},{12,16},{16,20},{20,24},{24,28},{28,32},{32,36}... | collective-permute-start | bytes 4718600 | tf_op jit(solution)/shard_map/ppermute | solution.py:168
  114.4 18.7 %collective-permute-start.4 = (f32[64,2,1,128]{3,2,1,0:T(1,128)}, f32[64,2,1,128]{3,2,1,0:T(1,128)S(1)}, u32[]{:S(2)}, u32[]{:S(2)}) collective-permute-start(f32[64,2,1,128]{3,2,1,0:T(1,128)} %get-tuple-element.73), channel_id=1, source_target_pairs={{1,0},{2,1},{3,2},{5,4},{6,5},{7,6},{9,8},{10,9},{11,10},{13,12},{... | collective-permute-start | bytes 196616 | tf_op jit(solution)/shard_map/ppermute | solution.py:169
  115.7 20.6 %collective-permute-start.5 = (f32[64,2,1,128]{3,2,1,0:T(1,128)}, f32[64,2,1,128]{3,2,1,0:T(1,128)S(1)}, u32[]{:S(2)}, u32[]{:S(2)}) collective-permute-start(f32[64,2,1,128]{3,2,1,0:T(1,128)} %get-tuple-element.74), channel_id=1, source_target_pairs={{0,1},{1,2},{2,3},{4,5},{5,6},{6,7},{8,9},{9,10},{10,11},{12,13},{... | collective-permute-start | bytes 196616 | tf_op jit(solution)/shard_map/ppermute | solution.py:168
  130.7 36.0 %collective-permute-start.22 = (f32[64,1,48,128]{3,2,1,0:T(8,128)}, f32[64,1,48,128]{3,2,1,0:T(8,128)}, u32[]{:S(2)}, u32[]{:S(2)}) collective-permute-start(f32[64,1,48,128]{3,2,1,0:T(8,128)} %get-tuple-element.36), channel_id=1, source_target_pairs={{4,0},{8,4},{12,8},{16,12},{20,16},{24,20},{28,24},{32,28},{36,32}... | collective-permute-start | bytes 4718600 | tf_op jit(solution)/shard_map/ppermute | solution.py:169
  133.1 38.2 %collective-permute-start.23 = (f32[64,1,48,128]{3,2,1,0:T(8,128)S(1)}, f32[64,1,48,128]{3,2,1,0:T(8,128)}, u32[]{:S(2)}, u32[]{:S(2)}) collective-permute-start(f32[64,1,48,128]{3,2,1,0:T(8,128)S(1)} %get-tuple-element.35), channel_id=1, source_target_pairs={{0,4},{4,8},{8,12},{12,16},{16,20},{20,24},{24,28},{28,32},{32,36}... | collective-permute-start | bytes 4718600 | tf_op jit(solution)/shard_map/ppermute | solution.py:168
  136.9 25.7 %collective-permute-start.24 = (f32[64,2,1,128]{3,2,1,0:T(1,128)}, f32[64,2,1,128]{3,2,1,0:T(1,128)S(1)}, u32[]{:S(2)}, u32[]{:S(2)}) collective-permute-start(f32[64,2,1,128]{3,2,1,0:T(1,128)} %get-tuple-element.39), channel_id=1, source_target_pairs={{1,0},{2,1},{3,2},{5,4},{6,5},{7,6},{9,8},{10,9},{11,10},{13,12},{... | collective-permute-start | bytes 196616 | tf_op jit(solution)/shard_map/ppermute | solution.py:169
  138.2 27.1 %collective-permute-start.25 = (f32[64,2,1,128]{3,2,1,0:T(1,128)}, f32[64,2,1,128]{3,2,1,0:T(1,128)S(1)}, u32[]{:S(2)}, u32[]{:S(2)}) collective-permute-start(f32[64,2,1,128]{3,2,1,0:T(1,128)} %get-tuple-element.40), channel_id=1, source_target_pairs={{0,1},{1,2},{2,3},{4,5},{5,6},{6,7},{8,9},{9,10},{10,11},{12,13},{... | collective-permute-start | bytes 196616 | tf_op jit(solution)/shard_map/ppermute | solution.py:168
  159.7 28.0 %collective-permute-start.6 = (f32[64,1,48,128]{3,2,1,0:T(8,128)}, f32[64,1,48,128]{3,2,1,0:T(8,128)}, u32[]{:S(2)}, u32[]{:S(2)}) collective-permute-start(f32[64,1,48,128]{3,2,1,0:T(8,128)} %get-tuple-element.64), channel_id=1, source_target_pairs={{4,0},{8,4},{12,8},{16,12},{20,16},{24,20},{28,24},{32,28},{36,32}... | collective-permute-start | bytes 4718600 | tf_op jit(solution)/shard_map/ppermute | solution.py:169
  162.6 29.2 %collective-permute-start.7 = (f32[64,1,48,128]{3,2,1,0:T(8,128)}, f32[64,1,48,128]{3,2,1,0:T(8,128)}, u32[]{:S(2)}, u32[]{:S(2)}) collective-permute-start(f32[64,1,48,128]{3,2,1,0:T(8,128)} %get-tuple-element.63), channel_id=1, source_target_pairs={{0,4},{4,8},{8,12},{12,16},{16,20},{20,24},{24,28},{28,32},{32,36}... | collective-permute-start | bytes 4718600 | tf_op jit(solution)/shard_map/ppermute | solution.py:168
  165.3 18.8 %collective-permute-start.8 = (f32[64,2,1,128]{3,2,1,0:T(1,128)}, f32[64,2,1,128]{3,2,1,0:T(1,128)S(1)}, u32[]{:S(2)}, u32[]{:S(2)}) collective-permute-start(f32[64,2,1,128]{3,2,1,0:T(1,128)} %get-tuple-element.67), channel_id=1, source_target_pairs={{1,0},{2,1},{3,2},{5,4},{6,5},{7,6},{9,8},{10,9},{11,10},{13,12},{... | collective-permute-start | bytes 196616 | tf_op jit(solution)/shard_map/ppermute | solution.py:169
  166.6 19.8 %collective-permute-start.9 = (f32[64,2,1,128]{3,2,1,0:T(1,128)}, f32[64,2,1,128]{3,2,1,0:T(1,128)}, u32[]{:S(2)}, u32[]{:S(2)}) collective-permute-start(f32[64,2,1,128]{3,2,1,0:T(1,128)} %get-tuple-element.68), channel_id=1, source_target_pairs={{0,1},{1,2},{2,3},{4,5},{5,6},{6,7},{8,9},{9,10},{10,11},{12,13},{... | collective-permute-start | bytes 196616 | tf_op jit(solution)/shard_map/ppermute | solution.py:168
  180.8 36.4 %collective-permute-start.26 = (f32[64,1,48,128]{3,2,1,0:T(8,128)}, f32[64,1,48,128]{3,2,1,0:T(8,128)}, u32[]{:S(2)}, u32[]{:S(2)}) collective-permute-start(f32[64,1,48,128]{3,2,1,0:T(8,128)} %get-tuple-element.30), channel_id=1, source_target_pairs={{4,0},{8,4},{12,8},{16,12},{20,16},{24,20},{28,24},{32,28},{36,32}... | collective-permute-start | bytes 4718600 | tf_op jit(solution)/shard_map/ppermute | solution.py:169
  184.2 37.7 %collective-permute-start.27 = (f32[64,1,48,128]{3,2,1,0:T(8,128)S(1)}, f32[64,1,48,128]{3,2,1,0:T(8,128)}, u32[]{:S(2)}, u32[]{:S(2)}) collective-permute-start(f32[64,1,48,128]{3,2,1,0:T(8,128)S(1)} %get-tuple-element.29), channel_id=1, source_target_pairs={{0,4},{4,8},{8,12},{12,16},{16,20},{20,24},{24,28},{28,32},{32,36}... | collective-permute-start | bytes 4718600 | tf_op jit(solution)/shard_map/ppermute | solution.py:168
  186.4 27.5 %collective-permute-start.28 = (f32[64,2,1,128]{3,2,1,0:T(1,128)}, f32[64,2,1,128]{3,2,1,0:T(1,128)S(1)}, u32[]{:S(2)}, u32[]{:S(2)}) collective-permute-start(f32[64,2,1,128]{3,2,1,0:T(1,128)} %get-tuple-element.33), channel_id=1, source_target_pairs={{1,0},{2,1},{3,2},{5,4},{6,5},{7,6},{9,8},{10,9},{11,10},{13,12},{... | collective-permute-start | bytes 196616 | tf_op jit(solution)/shard_map/ppermute | solution.py:169
  187.7 28.1 %collective-permute-start.29 = (f32[64,2,1,128]{3,2,1,0:T(1,128)}, f32[64,2,1,128]{3,2,1,0:T(1,128)S(1)}, u32[]{:S(2)}, u32[]{:S(2)}) collective-permute-start(f32[64,2,1,128]{3,2,1,0:T(1,128)} %get-tuple-element.34), channel_id=1, source_target_pairs={{0,1},{1,2},{2,3},{4,5},{5,6},{6,7},{8,9},{9,10},{10,11},{12,13},{... | collective-permute-start | bytes 196616 | tf_op jit(solution)/shard_map/ppermute | solution.py:168
  201.6 37.8 %collective-permute-start.10 = (f32[64,1,48,128]{3,2,1,0:T(8,128)}, f32[64,1,48,128]{3,2,1,0:T(8,128)}, u32[]{:S(2)}, u32[]{:S(2)}) collective-permute-start(f32[64,1,48,128]{3,2,1,0:T(8,128)} %get-tuple-element.58), channel_id=1, source_target_pairs={{4,0},{8,4},{12,8},{16,12},{20,16},{24,20},{28,24},{32,28},{36,32}... | collective-permute-start | bytes 4718600 | tf_op jit(solution)/shard_map/ppermute | solution.py:169
  214.0 25.4 %collective-permute-start.11 = (f32[64,1,48,128]{3,2,1,0:T(8,128)}, f32[64,1,48,128]{3,2,1,0:T(8,128)}, u32[]{:S(2)}, u32[]{:S(2)}) collective-permute-start(f32[64,1,48,128]{3,2,1,0:T(8,128)} %get-tuple-element.57), channel_id=1, source_target_pairs={{0,4},{4,8},{8,12},{12,16},{16,20},{20,24},{24,28},{28,32},{32,36}... | collective-permute-start | bytes 4718600 | tf_op jit(solution)/shard_map/ppermute | solution.py:168
  215.9 20.0 %collective-permute-start.12 = (f32[64,2,1,128]{3,2,1,0:T(1,128)}, f32[64,2,1,128]{3,2,1,0:T(1,128)S(1)}, u32[]{:S(2)}, u32[]{:S(2)}) collective-permute-start(f32[64,2,1,128]{3,2,1,0:T(1,128)} %get-tuple-element.61), channel_id=1, source_target_pairs={{1,0},{2,1},{3,2},{5,4},{6,5},{7,6},{9,8},{10,9},{11,10},{13,12},{... | collective-permute-start | bytes 196616 | tf_op jit(solution)/shard_map/ppermute | solution.py:169
  217.2 20.6 %collective-permute-start.13 = (f32[64,2,1,128]{3,2,1,0:T(1,128)}, f32[64,2,1,128]{3,2,1,0:T(1,128)}, u32[]{:S(2)}, u32[]{:S(2)}) collective-permute-start(f32[64,2,1,128]{3,2,1,0:T(1,128)} %get-tuple-element.62), channel_id=1, source_target_pairs={{0,1},{1,2},{2,3},{4,5},{5,6},{6,7},{8,9},{9,10},{10,11},{12,13},{... | collective-permute-start | bytes 196616 | tf_op jit(solution)/shard_map/ppermute | solution.py:168
  231.8 36.2 %collective-permute-start.30 = (f32[64,1,48,128]{3,2,1,0:T(8,128)}, f32[64,1,48,128]{3,2,1,0:T(8,128)}, u32[]{:S(2)}, u32[]{:S(2)}) collective-permute-start(f32[64,1,48,128]{3,2,1,0:T(8,128)} %get-tuple-element.28), channel_id=1, source_target_pairs={{4,0},{8,4},{12,8},{16,12},{20,16},{24,20},{28,24},{32,28},{36,32}... | collective-permute-start | bytes 4718600 | tf_op jit(solution)/shard_map/ppermute | solution.py:169
  235.9 36.1 %collective-permute-start.31 = (f32[64,1,48,128]{3,2,1,0:T(8,128)S(1)}, f32[64,1,48,128]{3,2,1,0:T(8,128)}, u32[]{:S(2)}, u32[]{:S(2)}) collective-permute-start(f32[64,1,48,128]{3,2,1,0:T(8,128)S(1)} %get-tuple-element.27), channel_id=1, source_target_pairs={{0,4},{4,8},{8,12},{12,16},{16,20},{20,24},{24,28},{28,32},{32,36}... | collective-permute-start | bytes 4718600 | tf_op jit(solution)/shard_map/ppermute | solution.py:168
  237.8 25.6 %collective-permute-start.32 = (f32[64,2,1,128]{3,2,1,0:T(1,128)}, f32[64,2,1,128]{3,2,1,0:T(1,128)S(1)}, u32[]{:S(2)}, u32[]{:S(2)}) collective-permute-start(f32[64,2,1,128]{3,2,1,0:T(1,128)} %get-tuple-element.24), channel_id=1, source_target_pairs={{1,0},{2,1},{3,2},{5,4},{6,5},{7,6},{9,8},{10,9},{11,10},{13,12},{... | collective-permute-start | bytes 196616 | tf_op jit(solution)/shard_map/ppermute | solution.py:169
  259.3 22.1 %collective-permute-start.14 = (f32[64,1,48,128]{3,2,1,0:T(8,128)}, f32[64,1,48,128]{3,2,1,0:T(8,128)}, u32[]{:S(2)}, u32[]{:S(2)}) collective-permute-start(f32[64,1,48,128]{3,2,1,0:T(8,128)} %get-tuple-element.56), channel_id=1, source_target_pairs={{4,0},{8,4},{12,8},{16,12},{20,16},{24,20},{28,24},{32,28},{36,32}... | collective-permute-start | bytes 4718600 | tf_op jit(solution)/shard_map/ppermute | solution.py:169
  263.4 19.6 %collective-permute-start.15 = (f32[64,1,48,128]{3,2,1,0:T(8,128)}, f32[64,1,48,128]{3,2,1,0:T(8,128)}, u32[]{:S(2)}, u32[]{:S(2)}) collective-permute-start(f32[64,1,48,128]{3,2,1,0:T(8,128)} %get-tuple-element.55), channel_id=1, source_target_pairs={{0,4},{4,8},{8,12},{12,16},{16,20},{20,24},{24,28},{28,32},{32,36}... | collective-permute-start | bytes 4718600 | tf_op jit(solution)/shard_map/ppermute | solution.py:168
  266.7 14.0 %collective-permute-start.16 = (f32[64,2,1,128]{3,2,1,0:T(1,128)}, f32[64,2,1,128]{3,2,1,0:T(1,128)S(1)}, u32[]{:S(2)}, u32[]{:S(2)}) collective-permute-start(f32[64,2,1,128]{3,2,1,0:T(1,128)} %get-tuple-element.52), channel_id=1, source_target_pairs={{1,0},{2,1},{3,2},{5,4},{6,5},{7,6},{9,8},{10,9},{11,10},{13,12},{... | collective-permute-start | bytes 196616 | tf_op jit(solution)/shard_map/ppermute | solution.py:169
  (19 other events, 264.7 us)

commit v9 on v6

--- a/solution.py
+++ b/solution.py
@@ -130,7 +130,7 @@
     )
 
 
-def gram(a, b, rows_per_step=48):
+def gram(a, b, rows_per_step=8):
     count, depth, rows, lanes = a.shape
     spec = pl.BlockSpec((count, 1, rows_per_step, lanes), lambda i, j: (0, i, j, 0))
     return pl.pallas_call(

time: 340 us -> 342 us (level)
  no operation moved by 1% of the time
where the time goes in v9:
time: 342 us; the launch traced here: 340 us
  starting transfers between devices  109 us (32%)
  other arithmetic  88.1 us (26%)
  local copies, waits for them, and re-layouts  46.4 us (14%)
  waiting for transfers between devices  44.4 us (13%)
  Pallas kernels  43 us (13%)
  between operations  9.03 us (3%)
    ppermute x16, starting transfers between devices, halo_pair(): lax.ppermute(lax.slice_in_dim(block, size - 1, None, axis=dim), axis, for...  54.4 us
    all_to_all x2, waiting for transfers between devices, windows(): received = lax.all_to_all(jnp.stack(parts), 'col', 0, 0, tiled=True)  44.3 us
    another operation x6, other arithmetic, run_segments(): return jnp.stack(factors)  42.1 us
    ppermute x16, starting transfers between devices, halo_pair(): high = lax.ppermute(lax.slice_in_dim(block, 0, 1, axis=dim), axis, backward)  37.6 us
    add x4, other arithmetic, solve_slabs(): rho_next * rho_now * direction + 2.0 * rho_next / half_span * residual  31.2 us
    pallas_call x1, Pallas kernels, reduce_scatter(): pl.pallas_call(reduce_kernel, out_shape=jax.ShapeDtypeStruct((1, 1, lanes...  28 us
    slice x14, local copies, waits for them, and re-layouts, shifted(): lax.slice_in_dim(block, 1, None, axis=dim)  24.9 us
    pallas_call x1, Pallas kernels, gram(): pl.pallas_call(gram_kernel, grid=(depth, rows // rows_per_step), in_specs...  15 us
  transfers between devices with their start and end apart: 36, of which 2 were waited for; matrix products, arithmetic and copies ran while one was open for 33% of the time, Pallas kernels for 0%

profile of v9, /device:TPU:1, one launch (start us, length us, event | category | flops | bytes accessed | tf_op | source)
XLA Modules:
  0.0 339.7 jit_solution(10830226538777836548)
XLA Ops:
  4.6 4.8 %all-to-all-start = ((f32[4,16,2,48,128]{4,3,2,1,0:T(8,128)}), f32[4,16,2,48,128]{4,3,2,1,0:T(8,128)S(1)}, u32[]{:S(2)}, u32[]{:S(2)}) async-start(f32[4,16,2,48,128]{4,3,2,1,0:T(8,128)} %pad_maximum_fusion.2), calls=%async_computation | async-start | bytes 6291456 | tf_op jit(solution)/shard_map/all_to_all | solution.py:186
  13.4 32.6 %all-to-all-done = f32[4,16,2,48,128]{4,3,2,1,0:T(8,128)S(1)} async-done(((f32[4,16,2,48,128]{4,3,2,1,0:T(8,128)}), f32[4,16,2,48,128]{4,3,2,1,0:T(8,128)S(1)}, u32[]{:S(2)}, u32[]{:S(2)}) %all-to-all-start) | async-done | bytes 3145760 | tf_op jit(solution)/shard_map/all_to_all | solution.py:186
  46.1 4.6 %all-to-all-start.1 = ((f32[4,16,2,48,128]{4,3,2,1,0:T(8,128)}), f32[4,16,2,48,128]{4,3,2,1,0:T(8,128)}, u32[]{:S(2)}, u32[]{:S(2)}) async-start(f32[4,16,2,48,128]{4,3,2,1,0:T(8,128)} %pad_maximum_fusion.3), calls=%async_computation.1 | async-start | bytes 6291456 | tf_op jit(solution)/shard_map/all_to_all | solution.py:186
  51.4 5.1 %select_add_fusion = f32[2,192,128]{2,1,0:T(8,128)S(1)} fusion(s32[2,192,128]{2,1,0:T(8,128)S(1)} %copy-done.13, f32[]{:T(128)} %bitcast.13, f32[]{:T(128)} %bitcast.12, f32[]{:T(128)} %bitcast.11, f32[]{:T(128)} %bitcast.10, f32[]{:T(128)} %bitcast.9, f32[]{:T(128)} %bitcast.8, f32[]{:T(128)} %bitcast.7, f32[]{:T(128)} %bitcast.6), kind=kLoop, calls=%fused_computation.210 | loop fusion | flops 1130496 | bytes 393248 | tf_op jit(solution)/shard_map/add | solution.py:151
  56.6 3.8 %collective-permute-start = (f32[1,50,128]{2,1,0:T(8,128)S(1)}, f32[1,50,128]{2,1,0:T(8,128)S(1)}, u32[]{:S(2)}, u32[]{:S(2)}) collective-permute-start(f32[1,50,128]{2,1,0:T(8,128)S(1)} %get-tuple-element.76), channel_id=1, source_target_pairs={{4,0},{8,4},{12,8},{16,12},{20,16},{24,20},{28,24},{32,28},{36,32}... | collective-permute-start | bytes 76808 | tf_op jit(solution)/shard_map/ppermute | solution.py:22
  74.8 11.7 %all-to-all-done.1 = f32[4,16,2,48,128]{4,3,2,1,0:T(8,128)} async-done(((f32[4,16,2,48,128]{4,3,2,1,0:T(8,128)}), f32[4,16,2,48,128]{4,3,2,1,0:T(8,128)}, u32[]{:S(2)}, u32[]{:S(2)}) %all-to-all-start.1) | async-done | bytes 3145760 | tf_op jit(solution)/shard_map/all_to_all | solution.py:186
  89.5 4.7 %collective-permute-start.18 = (f32[64,1,48,128]{3,2,1,0:T(8,128)S(1)}, f32[64,1,48,128]{3,2,1,0:T(8,128)S(1)}, u32[]{:S(2)}, u32[]{:S(2)}) collective-permute-start(f32[64,1,48,128]{3,2,1,0:T(8,128)S(1)} %get-tuple-element.36), channel_id=1, source_target_pairs={{4,0},{8,4},{12,8},{16,12},{20,16},{24,20},{28,24},{32,28},{36,32}... | collective-permute-start | bytes 4718600 | tf_op jit(solution)/shard_map/ppermute | solution.py:161
  99.0 4.0 %collective-permute-start.21 = (f32[64,2,1,128]{3,2,1,0:T(1,128)S(1)}, f32[64,2,1,128]{3,2,1,0:T(1,128)S(1)}, u32[]{:S(2)}, u32[]{:S(2)}) collective-permute-start(f32[64,2,1,128]{3,2,1,0:T(1,128)S(1)} %get-tuple-element.40), channel_id=1, source_target_pairs={{0,1},{1,2},{2,3},{4,5},{5,6},{6,7},{8,9},{9,10},{10,11},{12,13},{... | collective-permute-start | bytes 196616 | tf_op jit(solution)/shard_map/ppermute | solution.py:160
  110.0 3.6 %collective-permute-start.3 = (f32[64,1,48,128]{3,2,1,0:T(8,128)S(1)}, f32[64,1,48,128]{3,2,1,0:T(8,128)}, u32[]{:S(2)}, u32[]{:S(2)}) collective-permute-start(f32[64,1,48,128]{3,2,1,0:T(8,128)S(1)} %get-tuple-element.63), channel_id=1, source_target_pairs={{0,4},{4,8},{8,12},{12,16},{16,20},{20,24},{24,28},{28,32},{32,36}... | collective-permute-start | bytes 4718600 | tf_op jit(solution)/shard_map/ppermute | solution.py:160
  115.0 4.0 %collective-permute-start.5 = (f32[64,2,1,128]{3,2,1,0:T(1,128)}, f32[64,2,1,128]{3,2,1,0:T(1,128)S(1)}, u32[]{:S(2)}, u32[]{:S(2)}) collective-permute-start(f32[64,2,1,128]{3,2,1,0:T(1,128)} %get-tuple-element.68), channel_id=1, source_target_pairs={{0,1},{1,2},{2,3},{4,5},{5,6},{6,7},{8,9},{9,10},{10,11},{12,13},{... | collective-permute-start | bytes 196616 | tf_op jit(solution)/shard_map/ppermute | solution.py:160
  120.2 8.0 %multiply_add_fusion.1 = (f32[64,2,48,128]{3,2,1,0:T(8,128)S(1)}, f32[64,2,48,128]{3,2,1,0:T(8,128)}) fusion(f32[64,2,48,128]{3,2,1,0:T(8,128)S(1)} %get-tuple-element.92, f32[]{:T(128)S(6)} %div.73, f32[]{:T(128)S(6)} %mul.258, f32[]{:T(128)} %bitcast, f32[2,48,128]{2,1,0:T(8,128)S(1)} %get-tuple-element.78, f32[2,48,128]{2,1,0:T(8,128)S(1)} %copy-done.9, ...), kind=kLoop, calls=%fused_computation.196 | loop fusion | flops 21233664 | bytes 25460748 | tf_op jit(solution)/shard_map/add | solution.py:224
  138.4 4.0 %collective-permute-start.25 = (f32[64,2,1,128]{3,2,1,0:T(1,128)}, f32[64,2,1,128]{3,2,1,0:T(1,128)S(1)}, u32[]{:S(2)}, u32[]{:S(2)}) collective-permute-start(f32[64,2,1,128]{3,2,1,0:T(1,128)} %get-tuple-element.34), channel_id=1, source_target_pairs={{0,1},{1,2},{2,3},{4,5},{5,6},{6,7},{8,9},{9,10},{10,11},{12,13},{... | collective-permute-start | bytes 196616 | tf_op jit(solution)/shard_map/ppermute | solution.py:160
  142.4 7.6 %multiply_add_fusion.3 = (f32[64,2,48,128]{3,2,1,0:T(8,128)S(1)}, f32[64,2,48,128]{3,2,1,0:T(8,128)}) fusion(f32[64,2,48,128]{3,2,1,0:T(8,128)S(1)} %get-tuple-element.93, f32[]{:T(128)S(6)} %div.73, f32[]{:T(128)S(6)} %mul.258, f32[]{:T(128)} %bitcast, f32[2,48,128]{2,1,0:T(8,128)S(1)} %get-tuple-element.78, f32[2,48,128]{2,1,0:T(8,128)S(1)} %copy-done.9, ...), kind=kLoop, calls=%fused_computation.199 | loop fusion | flops 21233664 | bytes 25460748 | tf_op jit(solution)/shard_map/add | solution.py:224
  151.4 3.5 %fusion.165 = (f32[64,2,47,128]{3,2,1,0:T(8,128)}, f32[64,2,47,128]{3,2,1,0:T(8,128)}) fusion(f32[64,2,48,128]{3,2,1,0:T(8,128)S(1)} %get-tuple-element.7), kind=kLoop, calls=%fused_computation.242 | loop fusion | bytes 12320768 | tf_op jit(solution)/shard_map/slice | solution.py:167
  164.9 4.2 %collective-permute-start.9 = (f32[64,2,1,128]{3,2,1,0:T(1,128)}, f32[64,2,1,128]{3,2,1,0:T(1,128)S(1)}, u32[]{:S(2)}, u32[]{:S(2)}) collective-permute-start(f32[64,2,1,128]{3,2,1,0:T(1,128)} %get-tuple-element.62), channel_id=1, source_target_pairs={{0,1},{1,2},{2,3},{4,5},{5,6},{6,7},{8,9},{9,10},{10,11},{12,13},{... | collective-permute-start | bytes 196616 | tf_op jit(solution)/shard_map/ppermute | solution.py:160
  169.0 9.2 %multiply_bitcast_fusion = (f32[1,64,2,48,128]{4,3,2,1,0:T(8,128)}, f32[64,2,48,128]{3,2,1,0:T(8,128)S(1)}) fusion(f32[]{:T(128)S(6)} %sqrt.8, f32[64,2,48,128]{3,2,1,0:T(8,128)} %get-tuple-element.8, f32[64,2,48,128]{3,2,1,0:T(8,128)S(1)} %get-tuple-element.7, f32[]{:T(128)} %bitcast, f32[2,48,128]{2,1,0:T(8,128)S(1)} %get-tuple-element.78, ...), kind=kLoop, calls=%fused_computation.195 | loop fusion | flops 23592960 | bytes 28606480 | tf_op jit(solution)/shard_map/stack | solution.py:239
  188.2 4.0 %collective-permute-start.29 = (f32[64,2,1,128]{3,2,1,0:T(1,128)}, f32[64,2,1,128]{3,2,1,0:T(1,128)S(1)}, u32[]{:S(2)}, u32[]{:S(2)}) collective-permute-start(f32[64,2,1,128]{3,2,1,0:T(1,128)} %get-tuple-element.28), channel_id=1, source_target_pairs={{0,1},{1,2},{2,3},{4,5},{5,6},{6,7},{8,9},{9,10},{10,11},{12,13},{... | collective-permute-start | bytes 196616 | tf_op jit(solution)/shard_map/ppermute | solution.py:160
  192.2 8.3 %multiply_bitcast_fusion.1 = (f32[1,64,2,48,128]{4,3,2,1,0:T(8,128)}, f32[64,2,48,128]{3,2,1,0:T(8,128)S(1)}) fusion(f32[]{:T(128)S(6)} %sqrt.8, f32[64,2,48,128]{3,2,1,0:T(8,128)} %get-tuple-element.14, f32[64,2,48,128]{3,2,1,0:T(8,128)S(1)} %get-tuple-element.13, f32[]{:T(128)} %bitcast, f32[2,48,128]{2,1,0:T(8,128)S(1)} %get-tuple-element.78, ...), kind=kLoop, calls=%fused_computation.198 | loop fusion | flops 23592960 | bytes 28606480 | tf_op jit(solution)/shard_map/stack | solution.py:239
  207.5 3.8 %collective-permute-start.10 = (f32[64,1,48,128]{3,2,1,0:T(8,128)}, f32[64,1,48,128]{3,2,1,0:T(8,128)}, u32[]{:S(2)}, u32[]{:S(2)}) collective-permute-start(f32[64,1,48,128]{3,2,1,0:T(8,128)} %get-tuple-element.52), channel_id=1, source_target_pairs={{4,0},{8,4},{12,8},{16,12},{20,16},{24,20},{28,24},{32,28},{36,32}... | collective-permute-start | bytes 4718600 | tf_op jit(solution)/shard_map/ppermute | solution.py:161
  214.6 4.6 %collective-permute-start.13 = (f32[64,2,1,128]{3,2,1,0:T(1,128)}, f32[64,2,1,128]{3,2,1,0:T(1,128)}, u32[]{:S(2)}, u32[]{:S(2)}) collective-permute-start(f32[64,2,1,128]{3,2,1,0:T(1,128)} %get-tuple-element.56), channel_id=1, source_target_pairs={{0,1},{1,2},{2,3},{4,5},{5,6},{6,7},{8,9},{9,10},{10,11},{12,13},{... | collective-permute-start | bytes 196616 | tf_op jit(solution)/shard_map/ppermute | solution.py:160
  219.2 7.7 %multiply_add_fusion = (f32[64,2,48,128]{3,2,1,0:T(8,128)S(1)}, f32[64,2,48,128]{3,2,1,0:T(8,128)}) fusion(f32[]{:T(128)S(6)} %div.81, f32[]{:T(128)S(6)} %mul.607, f32[64,2,48,128]{3,2,1,0:T(8,128)S(1)} %get-tuple-element.4, f32[]{:T(128)S(6)} %mul.604, f32[64,2,48,128]{3,2,1,0:T(8,128)S(1)} %broadcast_divide_fusion, f32[]{:T(128)} %bitcast.15, ...), kind=kLoop, calls=%fused_computation.194 | loop fusion | flops 22020096 | bytes 25460752 | tf_op jit(solution)/shard_map/add | solution.py:224
  229.5 4.1 %collective-permute-start.30 = (f32[64,1,48,128]{3,2,1,0:T(8,128)}, f32[64,1,48,128]{3,2,1,0:T(8,128)}, u32[]{:S(2)}, u32[]{:S(2)}) collective-permute-start(f32[64,1,48,128]{3,2,1,0:T(8,128)} %get-tuple-element.22), channel_id=1, source_target_pairs={{4,0},{8,4},{12,8},{16,12},{20,16},{24,20},{28,24},{32,28},{36,32}... | collective-permute-start | bytes 4718600 | tf_op jit(solution)/shard_map/ppermute | solution.py:161
  236.9 4.2 %collective-permute-start.33 = (f32[64,2,1,128]{3,2,1,0:T(1,128)}, f32[64,2,1,128]{3,2,1,0:T(1,128)S(1)}, u32[]{:S(2)}, u32[]{:S(2)}) collective-permute-start(f32[64,2,1,128]{3,2,1,0:T(1,128)} %get-tuple-element.17), channel_id=1, source_target_pairs={{0,1},{1,2},{2,3},{4,5},{5,6},{6,7},{8,9},{9,10},{10,11},{12,13},{... | collective-permute-start | bytes 196616 | tf_op jit(solution)/shard_map/ppermute | solution.py:160
  241.1 7.8 %multiply_add_fusion.2 = (f32[64,2,48,128]{3,2,1,0:T(8,128)S(1)}, f32[64,2,48,128]{3,2,1,0:T(8,128)}) fusion(f32[]{:T(128)S(6)} %div.81, f32[]{:T(128)S(6)} %mul.607, f32[64,2,48,128]{3,2,1,0:T(8,128)S(1)} %get-tuple-element.10, f32[]{:T(128)S(6)} %mul.604, f32[64,2,48,128]{3,2,1,0:T(8,128)S(1)} %broadcast_divide_fusion.1, f32[]{:T(128)} %bitcast.15, ...), kind=kLoop, calls=%fused_computation.197 | loop fusion | flops 22020096 | bytes 25460752 | tf_op jit(solution)/shard_map/add | solution.py:224
  250.3 3.5 %fusion.159 = (f32[64,2,47,128]{3,2,1,0:T(8,128)}, f32[64,2,47,128]{3,2,1,0:T(8,128)}) fusion(f32[64,2,48,128]{3,2,1,0:T(8,128)S(1)} %get-tuple-element.5), kind=kLoop, calls=%fused_computation.236 | loop fusion | bytes 12320768 | tf_op jit(solution)/shard_map/slice | solution.py:168
  256.9 4.1 %collective-permute-start.14 = (f32[64,1,48,128]{3,2,1,0:T(8,128)}, f32[64,1,48,128]{3,2,1,0:T(8,128)}, u32[]{:S(2)}, u32[]{:S(2)}) collective-permute-start(f32[64,1,48,128]{3,2,1,0:T(8,128)} %get-tuple-element.50), channel_id=1, source_target_pairs={{4,0},{8,4},{12,8},{16,12},{20,16},{24,20},{28,24},{32,28},{36,32}... | collective-permute-start | bytes 4718600 | tf_op jit(solution)/shard_map/ppermute | solution.py:161
  264.3 4.6 %collective-permute-start.17 = (f32[64,2,1,128]{3,2,1,0:T(1,128)}, f32[64,2,1,128]{3,2,1,0:T(1,128)}, u32[]{:S(2)}, u32[]{:S(2)}) collective-permute-start(f32[64,2,1,128]{3,2,1,0:T(1,128)} %get-tuple-element.45), channel_id=1, source_target_pairs={{0,1},{1,2},{2,3},{4,5},{5,6},{6,7},{8,9},{9,10},{10,11},{12,13},{... | collective-permute-start | bytes 196616 | tf_op jit(solution)/shard_map/ppermute | solution.py:160
  268.9 8.8 %fusion.81 = f32[1,64,2,48,128]{4,3,2,1,0:T(8,128)} fusion(f32[64,2,48,128]{3,2,1,0:T(8,128)S(1)} %get-tuple-element.4, f32[64,2,48,128]{3,2,1,0:T(8,128)S(1)} %copy-done.1, f32[64,2,48,128]{3,2,1,0:T(8,128)S(1)} %get-tuple-element.5, f32[64,1,48,128]{3,2,1,0:T(8,128)} %collective-permute-done.30, f32[64,1,48,128]{3,2,1,0:T(8,128)} %get-tuple-element.21, ...), kind=kLoop, calls=%fused_computation.99 | loop fusion | flops 25952256 | bytes 25460760 | tf_op jit(solution)/shard_map/stack | solution.py:239
  277.8 5.3 %pad_maximum_fusion.1 = f32[2,64,2,48,128]{4,3,2,1,0:T(8,128)} fusion(f32[1,64,2,48,128]{4,3,2,1,0:T(8,128)} %fusion.81, f32[1,64,2,48,128]{4,3,2,1,0:T(8,128)S(1)} %copy-done.3), kind=kLoop, calls=%fused_computation.17 | loop fusion | flops 1572864 | bytes 12582912 | tf_op jit(solution)/shard_map/stack | solution.py:239
  283.1 7.2 %fusion.39 = f32[1,64,2,48,128]{4,3,2,1,0:T(8,128)S(1)} fusion(f32[64,2,48,128]{3,2,1,0:T(8,128)S(1)} %get-tuple-element.10, f32[64,2,48,128]{3,2,1,0:T(8,128)S(1)} %copy-done.2, f32[64,2,48,128]{3,2,1,0:T(8,128)S(1)} %get-tuple-element.11, f32[64,1,48,128]{3,2,1,0:T(8,128)} %collective-permute-done.14, f32[64,1,48,128]{3,2,1,0:T(8,128)S(1)} %get-tuple-element.49, ...), kind=kLoop, calls=%fused_computation.57 | loop fusion | flops 25952256 | bytes 25460760 | tf_op jit(solution)/shard_map/stack | solution.py:239
  293.5 15.0 %shard_map.76 = f32[128,128]{1,0:T(8,128)} custom-call(f32[128,2,48,128]{3,2,1,0:T(8,128)} %bitcast.48, f32[128,2,48,128]{3,2,1,0:T(8,128)} %bitcast.47), custom_call_target="tpu_custom_call" | custom-call | flops 402653184 | bytes 12582912 | tf_op jit(solution)/shard_map/pallas_call | solution.py:136
  310.4 28.0 %shard_map.77 = f32[1,1,128]{2,1,0:T(1,128)} custom-call(f32[4,32,128]{2,1,0:T(8,128)} %reshape.38.tiles_ref), custom_call_target="tpu_custom_call" | custom-call | tf_op jit(solution)/shard_map/pallas_call | solution.py:98
  (139 shorter events, 94.1 us)
Async XLA Ops:
  4.6 41.5 %all-to-all-start = ((f32[4,16,2,48,128]{4,3,2,1,0:T(8,128)}), f32[4,16,2,48,128]{4,3,2,1,0:T(8,128)S(1)}, u32[]{:S(2)}, u32[]{:S(2)}) async-start(f32[4,16,2,48,128]{4,3,2,1,0:T(8,128)} %pad_maximum_fusion.2), calls=%async_computation | async-start | bytes 6291456 | tf_op jit(solution)/shard_map/all_to_all | solution.py:186
  46.1 40.4 %all-to-all-start.1 = ((f32[4,16,2,48,128]{4,3,2,1,0:T(8,128)}), f32[4,16,2,48,128]{4,3,2,1,0:T(8,128)}, u32[]{:S(2)}, u32[]{:S(2)}) async-start(f32[4,16,2,48,128]{4,3,2,1,0:T(8,128)} %pad_maximum_fusion.3), calls=%async_computation.1 | async-start | bytes 6291456 | tf_op jit(solution)/shard_map/all_to_all | solution.py:186
  89.5 25.5 %collective-permute-start.18 = (f32[64,1,48,128]{3,2,1,0:T(8,128)S(1)}, f32[64,1,48,128]{3,2,1,0:T(8,128)S(1)}, u32[]{:S(2)}, u32[]{:S(2)}) collective-permute-start(f32[64,1,48,128]{3,2,1,0:T(8,128)S(1)} %get-tuple-element.36), channel_id=1, source_target_pairs={{4,0},{8,4},{12,8},{16,12},{20,16},{24,20},{28,24},{32,28},{36,32}... | collective-permute-start | bytes 4718600 | tf_op jit(solution)/shard_map/ppermute | solution.py:161
  94.2 24.9 %collective-permute-start.19 = (f32[64,1,48,128]{3,2,1,0:T(8,128)S(1)}, f32[64,1,48,128]{3,2,1,0:T(8,128)S(1)}, u32[]{:S(2)}, u32[]{:S(2)}) collective-permute-start(f32[64,1,48,128]{3,2,1,0:T(8,128)S(1)} %get-tuple-element.35), channel_id=1, source_target_pairs={{0,4},{4,8},{8,12},{12,16},{16,20},{20,24},{24,28},{28,32},{32,36}... | collective-permute-start | bytes 4718600 | tf_op jit(solution)/shard_map/ppermute | solution.py:160
  108.1 30.2 %collective-permute-start.1 = (f32[64,1,48,128]{3,2,1,0:T(8,128)}, f32[64,1,48,128]{3,2,1,0:T(8,128)}, u32[]{:S(2)}, u32[]{:S(2)}) collective-permute-start(f32[64,1,48,128]{3,2,1,0:T(8,128)} %get-tuple-element.64), channel_id=1, source_target_pairs={{4,0},{8,4},{12,8},{16,12},{20,16},{24,20},{28,24},{32,28},{36,32}... | collective-permute-start | bytes 4718600 | tf_op jit(solution)/shard_map/ppermute | solution.py:161
  110.0 32.3 %collective-permute-start.3 = (f32[64,1,48,128]{3,2,1,0:T(8,128)S(1)}, f32[64,1,48,128]{3,2,1,0:T(8,128)}, u32[]{:S(2)}, u32[]{:S(2)}) collective-permute-start(f32[64,1,48,128]{3,2,1,0:T(8,128)S(1)} %get-tuple-element.63), channel_id=1, source_target_pairs={{0,4},{4,8},{8,12},{12,16},{16,20},{20,24},{24,28},{28,32},{32,36}... | collective-permute-start | bytes 4718600 | tf_op jit(solution)/shard_map/ppermute | solution.py:160
  113.7 19.6 %collective-permute-start.4 = (f32[64,2,1,128]{3,2,1,0:T(1,128)}, f32[64,2,1,128]{3,2,1,0:T(1,128)S(1)}, u32[]{:S(2)}, u32[]{:S(2)}) collective-permute-start(f32[64,2,1,128]{3,2,1,0:T(1,128)} %get-tuple-element.67), channel_id=1, source_target_pairs={{1,0},{2,1},{3,2},{5,4},{6,5},{7,6},{9,8},{10,9},{11,10},{13,12},{... | collective-permute-start | bytes 196616 | tf_op jit(solution)/shard_map/ppermute | solution.py:161
  115.0 21.4 %collective-permute-start.5 = (f32[64,2,1,128]{3,2,1,0:T(1,128)}, f32[64,2,1,128]{3,2,1,0:T(1,128)S(1)}, u32[]{:S(2)}, u32[]{:S(2)}) collective-permute-start(f32[64,2,1,128]{3,2,1,0:T(1,128)} %get-tuple-element.68), channel_id=1, source_target_pairs={{0,1},{1,2},{2,3},{4,5},{5,6},{6,7},{8,9},{9,10},{10,11},{12,13},{... | collective-permute-start | bytes 196616 | tf_op jit(solution)/shard_map/ppermute | solution.py:160
  130.8 34.0 %collective-permute-start.22 = (f32[64,1,48,128]{3,2,1,0:T(8,128)}, f32[64,1,48,128]{3,2,1,0:T(8,128)}, u32[]{:S(2)}, u32[]{:S(2)}) collective-permute-start(f32[64,1,48,128]{3,2,1,0:T(8,128)} %get-tuple-element.30), channel_id=1, source_target_pairs={{4,0},{8,4},{12,8},{16,12},{20,16},{24,20},{28,24},{32,28},{36,32}... | collective-permute-start | bytes 4718600 | tf_op jit(solution)/shard_map/ppermute | solution.py:161
  133.3 35.8 %collective-permute-start.23 = (f32[64,1,48,128]{3,2,1,0:T(8,128)}, f32[64,1,48,128]{3,2,1,0:T(8,128)}, u32[]{:S(2)}, u32[]{:S(2)}) collective-permute-start(f32[64,1,48,128]{3,2,1,0:T(8,128)} %get-tuple-element.29), channel_id=1, source_target_pairs={{0,4},{4,8},{8,12},{12,16},{16,20},{20,24},{24,28},{28,32},{32,36}... | collective-permute-start | bytes 4718600 | tf_op jit(solution)/shard_map/ppermute | solution.py:160
  137.1 23.8 %collective-permute-start.24 = (f32[64,2,1,128]{3,2,1,0:T(1,128)}, f32[64,2,1,128]{3,2,1,0:T(1,128)S(1)}, u32[]{:S(2)}, u32[]{:S(2)}) collective-permute-start(f32[64,2,1,128]{3,2,1,0:T(1,128)} %get-tuple-element.33), channel_id=1, source_target_pairs={{1,0},{2,1},{3,2},{5,4},{6,5},{7,6},{9,8},{10,9},{11,10},{13,12},{... | collective-permute-start | bytes 196616 | tf_op jit(solution)/shard_map/ppermute | solution.py:161
  138.4 25.2 %collective-permute-start.25 = (f32[64,2,1,128]{3,2,1,0:T(1,128)}, f32[64,2,1,128]{3,2,1,0:T(1,128)S(1)}, u32[]{:S(2)}, u32[]{:S(2)}) collective-permute-start(f32[64,2,1,128]{3,2,1,0:T(1,128)} %get-tuple-element.34), channel_id=1, source_target_pairs={{0,1},{1,2},{2,3},{4,5},{5,6},{6,7},{8,9},{9,10},{10,11},{12,13},{... | collective-permute-start | bytes 196616 | tf_op jit(solution)/shard_map/ppermute | solution.py:160
  157.9 30.2 %collective-permute-start.6 = (f32[64,1,48,128]{3,2,1,0:T(8,128)}, f32[64,1,48,128]{3,2,1,0:T(8,128)}, u32[]{:S(2)}, u32[]{:S(2)}) collective-permute-start(f32[64,1,48,128]{3,2,1,0:T(8,128)} %get-tuple-element.58), channel_id=1, source_target_pairs={{4,0},{8,4},{12,8},{16,12},{20,16},{24,20},{28,24},{32,28},{36,32}... | collective-permute-start | bytes 4718600 | tf_op jit(solution)/shard_map/ppermute | solution.py:161
  160.8 31.3 %collective-permute-start.7 = (f32[64,1,48,128]{3,2,1,0:T(8,128)S(1)}, f32[64,1,48,128]{3,2,1,0:T(8,128)}, u32[]{:S(2)}, u32[]{:S(2)}) collective-permute-start(f32[64,1,48,128]{3,2,1,0:T(8,128)S(1)} %get-tuple-element.57), channel_id=1, source_target_pairs={{0,4},{4,8},{8,12},{12,16},{16,20},{20,24},{24,28},{28,32},{32,36}... | collective-permute-start | bytes 4718600 | tf_op jit(solution)/shard_map/ppermute | solution.py:160
  163.5 21.1 %collective-permute-start.8 = (f32[64,2,1,128]{3,2,1,0:T(1,128)}, f32[64,2,1,128]{3,2,1,0:T(1,128)S(1)}, u32[]{:S(2)}, u32[]{:S(2)}) collective-permute-start(f32[64,2,1,128]{3,2,1,0:T(1,128)} %get-tuple-element.61), channel_id=1, source_target_pairs={{1,0},{2,1},{3,2},{5,4},{6,5},{7,6},{9,8},{10,9},{11,10},{13,12},{... | collective-permute-start | bytes 196616 | tf_op jit(solution)/shard_map/ppermute | solution.py:161
  164.9 22.0 %collective-permute-start.9 = (f32[64,2,1,128]{3,2,1,0:T(1,128)}, f32[64,2,1,128]{3,2,1,0:T(1,128)S(1)}, u32[]{:S(2)}, u32[]{:S(2)}) collective-permute-start(f32[64,2,1,128]{3,2,1,0:T(1,128)} %get-tuple-element.62), channel_id=1, source_target_pairs={{0,1},{1,2},{2,3},{4,5},{5,6},{6,7},{8,9},{9,10},{10,11},{12,13},{... | collective-permute-start | bytes 196616 | tf_op jit(solution)/shard_map/ppermute | solution.py:160
  181.2 33.3 %collective-permute-start.26 = (f32[64,1,48,128]{3,2,1,0:T(8,128)}, f32[64,1,48,128]{3,2,1,0:T(8,128)}, u32[]{:S(2)}, u32[]{:S(2)}) collective-permute-start(f32[64,1,48,128]{3,2,1,0:T(8,128)} %get-tuple-element.24), channel_id=1, source_target_pairs={{4,0},{8,4},{12,8},{16,12},{20,16},{24,20},{28,24},{32,28},{36,32}... | collective-permute-start | bytes 4718600 | tf_op jit(solution)/shard_map/ppermute | solution.py:161
  184.6 34.6 %collective-permute-start.27 = (f32[64,1,48,128]{3,2,1,0:T(8,128)}, f32[64,1,48,128]{3,2,1,0:T(8,128)}, u32[]{:S(2)}, u32[]{:S(2)}) collective-permute-start(f32[64,1,48,128]{3,2,1,0:T(8,128)} %get-tuple-element.23), channel_id=1, source_target_pairs={{0,4},{4,8},{8,12},{12,16},{16,20},{20,24},{24,28},{28,32},{32,36}... | collective-permute-start | bytes 4718600 | tf_op jit(solution)/shard_map/ppermute | solution.py:160
  186.8 24.5 %collective-permute-start.28 = (f32[64,2,1,128]{3,2,1,0:T(1,128)}, f32[64,2,1,128]{3,2,1,0:T(1,128)S(1)}, u32[]{:S(2)}, u32[]{:S(2)}) collective-permute-start(f32[64,2,1,128]{3,2,1,0:T(1,128)} %get-tuple-element.27), channel_id=1, source_target_pairs={{1,0},{2,1},{3,2},{5,4},{6,5},{7,6},{9,8},{10,9},{11,10},{13,12},{... | collective-permute-start | bytes 196616 | tf_op jit(solution)/shard_map/ppermute | solution.py:161
  188.2 25.1 %collective-permute-start.29 = (f32[64,2,1,128]{3,2,1,0:T(1,128)}, f32[64,2,1,128]{3,2,1,0:T(1,128)S(1)}, u32[]{:S(2)}, u32[]{:S(2)}) collective-permute-start(f32[64,2,1,128]{3,2,1,0:T(1,128)} %get-tuple-element.28), channel_id=1, source_target_pairs={{0,1},{1,2},{2,3},{4,5},{5,6},{6,7},{8,9},{9,10},{10,11},{12,13},{... | collective-permute-start | bytes 196616 | tf_op jit(solution)/shard_map/ppermute | solution.py:160
  207.5 29.4 %collective-permute-start.10 = (f32[64,1,48,128]{3,2,1,0:T(8,128)}, f32[64,1,48,128]{3,2,1,0:T(8,128)}, u32[]{:S(2)}, u32[]{:S(2)}) collective-permute-start(f32[64,1,48,128]{3,2,1,0:T(8,128)} %get-tuple-element.52), channel_id=1, source_target_pairs={{4,0},{8,4},{12,8},{16,12},{20,16},{24,20},{28,24},{32,28},{36,32}... | collective-permute-start | bytes 4718600 | tf_op jit(solution)/shard_map/ppermute | solution.py:161
  211.3 29.8 %collective-permute-start.11 = (f32[64,1,48,128]{3,2,1,0:T(8,128)S(1)}, f32[64,1,48,128]{3,2,1,0:T(8,128)}, u32[]{:S(2)}, u32[]{:S(2)}) collective-permute-start(f32[64,1,48,128]{3,2,1,0:T(8,128)S(1)} %get-tuple-element.51), channel_id=1, source_target_pairs={{0,4},{4,8},{8,12},{12,16},{16,20},{20,24},{24,28},{28,32},{32,36}... | collective-permute-start | bytes 4718600 | tf_op jit(solution)/shard_map/ppermute | solution.py:160
  213.3 20.3 %collective-permute-start.12 = (f32[64,2,1,128]{3,2,1,0:T(1,128)}, f32[64,2,1,128]{3,2,1,0:T(1,128)S(1)}, u32[]{:S(2)}, u32[]{:S(2)}) collective-permute-start(f32[64,2,1,128]{3,2,1,0:T(1,128)} %get-tuple-element.55), channel_id=1, source_target_pairs={{1,0},{2,1},{3,2},{5,4},{6,5},{7,6},{9,8},{10,9},{11,10},{13,12},{... | collective-permute-start | bytes 196616 | tf_op jit(solution)/shard_map/ppermute | solution.py:161
  214.6 21.0 %collective-permute-start.13 = (f32[64,2,1,128]{3,2,1,0:T(1,128)}, f32[64,2,1,128]{3,2,1,0:T(1,128)}, u32[]{:S(2)}, u32[]{:S(2)}) collective-permute-start(f32[64,2,1,128]{3,2,1,0:T(1,128)} %get-tuple-element.56), channel_id=1, source_target_pairs={{0,1},{1,2},{2,3},{4,5},{5,6},{6,7},{8,9},{9,10},{10,11},{12,13},{... | collective-permute-start | bytes 196616 | tf_op jit(solution)/shard_map/ppermute | solution.py:160
  229.5 34.8 %collective-permute-start.30 = (f32[64,1,48,128]{3,2,1,0:T(8,128)}, f32[64,1,48,128]{3,2,1,0:T(8,128)}, u32[]{:S(2)}, u32[]{:S(2)}) collective-permute-start(f32[64,1,48,128]{3,2,1,0:T(8,128)} %get-tuple-element.22), channel_id=1, source_target_pairs={{4,0},{8,4},{12,8},{16,12},{20,16},{24,20},{28,24},{32,28},{36,32}... | collective-permute-start | bytes 4718600 | tf_op jit(solution)/shard_map/ppermute | solution.py:161
  233.6 35.3 %collective-permute-start.31 = (f32[64,1,48,128]{3,2,1,0:T(8,128)}, f32[64,1,48,128]{3,2,1,0:T(8,128)}, u32[]{:S(2)}, u32[]{:S(2)}) collective-permute-start(f32[64,1,48,128]{3,2,1,0:T(8,128)} %get-tuple-element.21), channel_id=1, source_target_pairs={{0,4},{4,8},{8,12},{12,16},{16,20},{20,24},{24,28},{28,32},{32,36}... | collective-permute-start | bytes 4718600 | tf_op jit(solution)/shard_map/ppermute | solution.py:160
  235.6 25.5 %collective-permute-start.32 = (f32[64,2,1,128]{3,2,1,0:T(1,128)}, f32[64,2,1,128]{3,2,1,0:T(1,128)S(1)}, u32[]{:S(2)}, u32[]{:S(2)}) collective-permute-start(f32[64,2,1,128]{3,2,1,0:T(1,128)} %get-tuple-element.18), channel_id=1, source_target_pairs={{1,0},{2,1},{3,2},{5,4},{6,5},{7,6},{9,8},{10,9},{11,10},{13,12},{... | collective-permute-start | bytes 196616 | tf_op jit(solution)/shard_map/ppermute | solution.py:161
  236.9 26.1 %collective-permute-start.33 = (f32[64,2,1,128]{3,2,1,0:T(1,128)}, f32[64,2,1,128]{3,2,1,0:T(1,128)S(1)}, u32[]{:S(2)}, u32[]{:S(2)}) collective-permute-start(f32[64,2,1,128]{3,2,1,0:T(1,128)} %get-tuple-element.17), channel_id=1, source_target_pairs={{0,1},{1,2},{2,3},{4,5},{5,6},{6,7},{8,9},{9,10},{10,11},{12,13},{... | collective-permute-start | bytes 196616 | tf_op jit(solution)/shard_map/ppermute | solution.py:160
  256.9 26.1 %collective-permute-start.14 = (f32[64,1,48,128]{3,2,1,0:T(8,128)}, f32[64,1,48,128]{3,2,1,0:T(8,128)}, u32[]{:S(2)}, u32[]{:S(2)}) collective-permute-start(f32[64,1,48,128]{3,2,1,0:T(8,128)} %get-tuple-element.50), channel_id=1, source_target_pairs={{4,0},{8,4},{12,8},{16,12},{20,16},{24,20},{28,24},{32,28},{36,32}... | collective-permute-start | bytes 4718600 | tf_op jit(solution)/shard_map/ppermute | solution.py:161
  261.0 22.0 %collective-permute-start.15 = (f32[64,1,48,128]{3,2,1,0:T(8,128)S(1)}, f32[64,1,48,128]{3,2,1,0:T(8,128)}, u32[]{:S(2)}, u32[]{:S(2)}) collective-permute-start(f32[64,1,48,128]{3,2,1,0:T(8,128)S(1)} %get-tuple-element.49), channel_id=1, source_target_pairs={{0,4},{4,8},{8,12},{12,16},{16,20},{20,24},{24,28},{28,32},{32,36}... | collective-permute-start | bytes 4718600 | tf_op jit(solution)/shard_map/ppermute | solution.py:160
  263.0 20.1 %collective-permute-start.16 = (f32[64,2,1,128]{3,2,1,0:T(1,128)}, f32[64,2,1,128]{3,2,1,0:T(1,128)S(1)}, u32[]{:S(2)}, u32[]{:S(2)}) collective-permute-start(f32[64,2,1,128]{3,2,1,0:T(1,128)} %get-tuple-element.46), channel_id=1, source_target_pairs={{1,0},{2,1},{3,2},{5,4},{6,5},{7,6},{9,8},{10,9},{11,10},{13,12},{... | collective-permute-start | bytes 196616 | tf_op jit(solution)/shard_map/ppermute | solution.py:161
  264.3 18.8 %collective-permute-start.17 = (f32[64,2,1,128]{3,2,1,0:T(1,128)}, f32[64,2,1,128]{3,2,1,0:T(1,128)}, u32[]{:S(2)}, u32[]{:S(2)}) collective-permute-start(f32[64,2,1,128]{3,2,1,0:T(1,128)} %get-tuple-element.45), channel_id=1, source_target_pairs={{0,1},{1,2},{2,3},{4,5},{5,6},{6,7},{8,9},{9,10},{10,11},{12,13},{... | collective-permute-start | bytes 196616 | tf_op jit(solution)/shard_map/ppermute | solution.py:160
  (25 other events, 313.1 us)

commit v10 on v5

--- a/solution.py
+++ b/solution.py
@@ -289,6 +289,7 @@
 def body(input_map, output_map, region_ids, region_cond, shift_ids):
     col_count = lax.axis_size("col")
     ctrl_in = exchange(input_map, col_count)
+    ctrl_in, output_map = lax.optimization_barrier((ctrl_in, output_map))
     obsv_in = windows(output_map, output_map.shape[2] // col_count, col_count)
     col_local = ctrl_in.shape[0]
     rows = ctrl_in.shape[2]

time: 349 us -> 340 us (0.974)
  Pallas kernels: 101 us -> 80.8 us
  waiting for transfers between devices: 0.09 us -> 13.2 us
    pallas_call x1, Pallas kernels: 58.3 us -> 38.8 us  [exchange(): pl.pallas_call(exchange_kernel, out_shape=jax.ShapeDtypeStruct((cols * nc...]
    all_to_all x1, waiting for transfers between devices: 0.01 us -> 13.1 us  [windows(): received = lax.all_to_all(jnp.stack(parts), 'col', 0, 0, tiled=True)]
  transfers between devices with their start and end apart: 35 -> 35, of which waited for: 0 -> 1; matrix products, arithmetic and copies ran while one was open for 32% -> 32% of each run, Pallas kernels for 17% -> 0%
where the time goes in v10:
time: 340 us; the launch traced here: 338 us
  starting transfers between devices  103 us (30%)
  other arithmetic  86.5 us (25%)
  Pallas kernels  80.8 us (24%)
  local copies, waits for them, and re-layouts  46.4 us (14%)
  waiting for transfers between devices  13.2 us (4%)
  between operations  8.65 us (3%)
    ppermute x16, starting transfers between devices, halo_pair(): lax.ppermute(lax.slice_in_dim(block, size - 1, None, axis=dim), axis, for...  55.3 us
    another operation x6, other arithmetic, run_segments(): return jnp.stack(factors)  41.9 us
    pallas_call x1, Pallas kernels, exchange(): pl.pallas_call(exchange_kernel, out_shape=jax.ShapeDtypeStruct((cols * nc...  38.8 us
    ppermute x16, starting transfers between devices, halo_pair(): high = lax.ppermute(lax.slice_in_dim(block, 0, 1, axis=dim), axis, backward)  36.7 us
    add x4, other arithmetic, solve_slabs(): rho_next * rho_now * direction + 2.0 * rho_next / half_span * residual  31.2 us
    pallas_call x1, Pallas kernels, reduce_scatter(): pl.pallas_call(reduce_kernel, out_shape=jax.ShapeDtypeStruct((1, 1, lanes...  28.8 us
    slice x14, local copies, waits for them, and re-layouts, shifted(): lax.slice_in_dim(block, 1, None, axis=dim)  25.7 us
    pallas_call x1, Pallas kernels, gram(): pl.pallas_call(gram_kernel, grid=(depth, rows // rows_per_step), in_specs...  13.2 us
  transfers between devices with their start and end apart: 35, of which 1 were waited for; matrix products, arithmetic and copies ran while one was open for 32% of the time, Pallas kernels for 0%

profile of v10, /device:TPU:1, one launch (start us, length us, event | category | flops | bytes accessed | tf_op | source)
XLA Modules:
  0.0 338.3 jit_solution(5006560951464988364)
XLA Ops:
  0.6 38.8 %shard_map.76 = f32[64,2,48,128]{3,2,1,0:T(8,128)} custom-call(f32[16,2,192,128]{3,2,1,0:T(8,128)} %x_ref.1), custom_call_target="tpu_custom_call" | custom-call | tf_op jit(solution)/shard_map/pallas_call | solution.py:150
  44.0 4.2 %all-to-all-start = ((f32[4,16,2,48,128]{4,3,2,1,0:T(8,128)}), f32[4,16,2,48,128]{4,3,2,1,0:T(8,128)S(1)}, u32[]{:S(2)}, u32[]{:S(2)}) async-start(f32[4,16,2,48,128]{4,3,2,1,0:T(8,128)} %pad_maximum_fusion.2), calls=%async_computation | async-start | bytes 6291456 | tf_op jit(solution)/shard_map/all_to_all | solution.py:233
  48.8 5.3 %select_add_fusion = f32[2,192,128]{2,1,0:T(8,128)S(1)} fusion(s32[2,192,128]{2,1,0:T(8,128)S(1)} %copy-done.15, f32[]{:T(128)} %bitcast.8, f32[]{:T(128)} %bitcast.7, f32[]{:T(128)} %bitcast.6, f32[]{:T(128)} %bitcast.5, f32[]{:T(128)} %bitcast.4, f32[]{:T(128)} %bitcast.3, f32[]{:T(128)} %bitcast.2, f32[]{:T(128)} %bitcast.1), kind=kLoop, calls=%fused_computation.206 | loop fusion | flops 1130496 | bytes 393248 | tf_op jit(solution)/shard_map/add | solution.py:198
  57.3 3.4 %collective-permute-start.2 = (f32[1,50,128]{2,1,0:T(8,128)S(1)}, f32[1,50,128]{2,1,0:T(8,128)S(1)}, u32[]{:S(2)}, u32[]{:S(2)}) collective-permute-start(f32[1,50,128]{2,1,0:T(8,128)S(1)} %get-tuple-element.75), channel_id=1, source_target_pairs={{0,4},{4,8},{8,12},{12,16},{16,20},{20,24},{24,28},{28,32},{32,36}... | collective-permute-start | bytes 76808 | tf_op jit(solution)/shard_map/ppermute | solution.py:19
  71.4 13.1 %all-to-all-done = f32[4,16,2,48,128]{4,3,2,1,0:T(8,128)S(1)} async-done(((f32[4,16,2,48,128]{4,3,2,1,0:T(8,128)}), f32[4,16,2,48,128]{4,3,2,1,0:T(8,128)S(1)}, u32[]{:S(2)}, u32[]{:S(2)}) %all-to-all-start) | async-done | bytes 3145760 | tf_op jit(solution)/shard_map/all_to_all | solution.py:233
  87.7 4.0 %collective-permute-start.18 = (f32[64,1,48,128]{3,2,1,0:T(8,128)S(1)}, f32[64,1,48,128]{3,2,1,0:T(8,128)S(1)}, u32[]{:S(2)}, u32[]{:S(2)}) collective-permute-start(f32[64,1,48,128]{3,2,1,0:T(8,128)S(1)} %get-tuple-element.40), channel_id=1, source_target_pairs={{4,0},{8,4},{12,8},{16,12},{20,16},{24,20},{28,24},{32,28},{36,32}... | collective-permute-start | bytes 4718600 | tf_op jit(solution)/shard_map/ppermute | solution.py:208
  91.7 3.4 %collective-permute-start.19 = (f32[64,1,48,128]{3,2,1,0:T(8,128)S(1)}, f32[64,1,48,128]{3,2,1,0:T(8,128)S(1)}, u32[]{:S(2)}, u32[]{:S(2)}) collective-permute-start(f32[64,1,48,128]{3,2,1,0:T(8,128)S(1)} %get-tuple-element.39), channel_id=1, source_target_pairs={{0,4},{4,8},{8,12},{12,16},{16,20},{20,24},{24,28},{28,32},{32,36}... | collective-permute-start | bytes 4718600 | tf_op jit(solution)/shard_map/ppermute | solution.py:207
  96.6 4.0 %collective-permute-start.21 = (f32[64,2,1,128]{3,2,1,0:T(1,128)S(1)}, f32[64,2,1,128]{3,2,1,0:T(1,128)S(1)}, u32[]{:S(2)}, u32[]{:S(2)}) collective-permute-start(f32[64,2,1,128]{3,2,1,0:T(1,128)S(1)} %get-tuple-element.44), channel_id=1, source_target_pairs={{0,1},{1,2},{2,3},{4,5},{5,6},{6,7},{8,9},{9,10},{10,11},{12,13},{... | collective-permute-start | bytes 196616 | tf_op jit(solution)/shard_map/ppermute | solution.py:207
  108.4 3.6 %collective-permute-start.3 = (f32[64,1,48,128]{3,2,1,0:T(8,128)}, f32[64,1,48,128]{3,2,1,0:T(8,128)}, u32[]{:S(2)}, u32[]{:S(2)}) collective-permute-start(f32[64,1,48,128]{3,2,1,0:T(8,128)} %get-tuple-element.67), channel_id=1, source_target_pairs={{0,4},{4,8},{8,12},{12,16},{16,20},{20,24},{24,28},{28,32},{32,36}... | collective-permute-start | bytes 4718600 | tf_op jit(solution)/shard_map/ppermute | solution.py:207
  113.4 4.6 %collective-permute-start.5 = (f32[64,2,1,128]{3,2,1,0:T(1,128)}, f32[64,2,1,128]{3,2,1,0:T(1,128)}, u32[]{:S(2)}, u32[]{:S(2)}) collective-permute-start(f32[64,2,1,128]{3,2,1,0:T(1,128)} %get-tuple-element.72), channel_id=1, source_target_pairs={{0,1},{1,2},{2,3},{4,5},{5,6},{6,7},{8,9},{9,10},{10,11},{12,13},{... | collective-permute-start | bytes 196616 | tf_op jit(solution)/shard_map/ppermute | solution.py:207
  119.2 7.7 %multiply_add_fusion.1 = (f32[64,2,48,128]{3,2,1,0:T(8,128)S(1)}, f32[64,2,48,128]{3,2,1,0:T(8,128)}) fusion(f32[64,2,48,128]{3,2,1,0:T(8,128)S(1)} %get-tuple-element.92, f32[]{:T(128)S(6)} %div.73, f32[]{:T(128)S(6)} %mul.262, f32[]{:T(128)} %bitcast, f32[2,48,128]{2,1,0:T(8,128)S(1)} %get-tuple-element.78, f32[2,48,128]{2,1,0:T(8,128)S(1)} %copy-done.10, ...), kind=kLoop, calls=%fused_computation.194 | loop fusion | flops 21233664 | bytes 25460748 | tf_op jit(solution)/shard_map/add | solution.py:271
  136.6 4.0 %collective-permute-start.25 = (f32[64,2,1,128]{3,2,1,0:T(1,128)}, f32[64,2,1,128]{3,2,1,0:T(1,128)S(1)}, u32[]{:S(2)}, u32[]{:S(2)}) collective-permute-start(f32[64,2,1,128]{3,2,1,0:T(1,128)} %get-tuple-element.38), channel_id=1, source_target_pairs={{0,1},{1,2},{2,3},{4,5},{5,6},{6,7},{8,9},{9,10},{10,11},{12,13},{... | collective-permute-start | bytes 196616 | tf_op jit(solution)/shard_map/ppermute | solution.py:207
  140.6 7.9 %multiply_add_fusion.3 = (f32[64,2,48,128]{3,2,1,0:T(8,128)S(1)}, f32[64,2,48,128]{3,2,1,0:T(8,128)}) fusion(f32[64,2,48,128]{3,2,1,0:T(8,128)S(1)} %get-tuple-element.93, f32[]{:T(128)S(6)} %div.73, f32[]{:T(128)S(6)} %mul.262, f32[64,2,48,128]{3,2,1,0:T(8,128)S(1)} %copy-done, f32[]{:T(128)} %bitcast, f32[2,48,128]{2,1,0:T(8,128)S(1)} %get-tuple-element.78, ...), kind=kLoop, calls=%fused_computation.197 | loop fusion | flops 21233664 | bytes 25460748 | tf_op jit(solution)/shard_map/add | solution.py:271
  149.9 3.5 %fusion.165 = (f32[64,2,47,128]{3,2,1,0:T(8,128)}, f32[64,2,47,128]{3,2,1,0:T(8,128)}) fusion(f32[64,2,48,128]{3,2,1,0:T(8,128)S(1)} %get-tuple-element.11), kind=kLoop, calls=%fused_computation.238 | loop fusion | bytes 12320768 | tf_op jit(solution)/shard_map/slice | solution.py:214
  164.0 4.2 %collective-permute-start.9 = (f32[64,2,1,128]{3,2,1,0:T(1,128)}, f32[64,2,1,128]{3,2,1,0:T(1,128)S(1)}, u32[]{:S(2)}, u32[]{:S(2)}) collective-permute-start(f32[64,2,1,128]{3,2,1,0:T(1,128)} %get-tuple-element.66), channel_id=1, source_target_pairs={{0,1},{1,2},{2,3},{4,5},{5,6},{6,7},{8,9},{9,10},{10,11},{12,13},{... | collective-permute-start | bytes 196616 | tf_op jit(solution)/shard_map/ppermute | solution.py:207
  168.2 9.1 %multiply_bitcast_fusion = (f32[1,64,2,48,128]{4,3,2,1,0:T(8,128)}, f32[64,2,48,128]{3,2,1,0:T(8,128)S(1)}) fusion(f32[]{:T(128)S(6)} %sqrt.8, f32[64,2,48,128]{3,2,1,0:T(8,128)} %get-tuple-element.12, f32[64,2,48,128]{3,2,1,0:T(8,128)S(1)} %get-tuple-element.11, f32[]{:T(128)} %bitcast, f32[2,48,128]{2,1,0:T(8,128)S(1)} %get-tuple-element.78, ...), kind=kLoop, calls=%fused_computation.193 | loop fusion | flops 23592960 | bytes 28606480 | tf_op jit(solution)/shard_map/stack | solution.py:286
  187.9 4.0 %collective-permute-start.29 = (f32[64,2,1,128]{3,2,1,0:T(1,128)}, f32[64,2,1,128]{3,2,1,0:T(1,128)S(1)}, u32[]{:S(2)}, u32[]{:S(2)}) collective-permute-start(f32[64,2,1,128]{3,2,1,0:T(1,128)} %get-tuple-element.32), channel_id=1, source_target_pairs={{0,1},{1,2},{2,3},{4,5},{5,6},{6,7},{8,9},{9,10},{10,11},{12,13},{... | collective-permute-start | bytes 196616 | tf_op jit(solution)/shard_map/ppermute | solution.py:207
  191.9 8.2 %multiply_bitcast_fusion.1 = (f32[1,64,2,48,128]{4,3,2,1,0:T(8,128)}, f32[64,2,48,128]{3,2,1,0:T(8,128)S(1)}) fusion(f32[]{:T(128)S(6)} %sqrt.8, f32[64,2,48,128]{3,2,1,0:T(8,128)} %get-tuple-element.18, f32[64,2,48,128]{3,2,1,0:T(8,128)S(1)} %get-tuple-element.17, f32[]{:T(128)} %bitcast, f32[2,48,128]{2,1,0:T(8,128)S(1)} %get-tuple-element.78, ...), kind=kLoop, calls=%fused_computation.196 | loop fusion | flops 23592960 | bytes 28606480 | tf_op jit(solution)/shard_map/stack | solution.py:286
  207.1 3.8 %collective-permute-start.10 = (f32[64,1,48,128]{3,2,1,0:T(8,128)}, f32[64,1,48,128]{3,2,1,0:T(8,128)}, u32[]{:S(2)}, u32[]{:S(2)}) collective-permute-start(f32[64,1,48,128]{3,2,1,0:T(8,128)} %get-tuple-element.56), channel_id=1, source_target_pairs={{4,0},{8,4},{12,8},{16,12},{20,16},{24,20},{28,24},{32,28},{36,32}... | collective-permute-start | bytes 4718600 | tf_op jit(solution)/shard_map/ppermute | solution.py:208
  214.1 4.6 %collective-permute-start.13 = (f32[64,2,1,128]{3,2,1,0:T(1,128)}, f32[64,2,1,128]{3,2,1,0:T(1,128)}, u32[]{:S(2)}, u32[]{:S(2)}) collective-permute-start(f32[64,2,1,128]{3,2,1,0:T(1,128)} %get-tuple-element.60), channel_id=1, source_target_pairs={{0,1},{1,2},{2,3},{4,5},{5,6},{6,7},{8,9},{9,10},{10,11},{12,13},{... | collective-permute-start | bytes 196616 | tf_op jit(solution)/shard_map/ppermute | solution.py:207
  218.7 7.7 %multiply_add_fusion = (f32[64,2,48,128]{3,2,1,0:T(8,128)S(1)}, f32[64,2,48,128]{3,2,1,0:T(8,128)}) fusion(f32[]{:T(128)S(6)} %div.81, f32[]{:T(128)S(6)} %mul.612, f32[64,2,48,128]{3,2,1,0:T(8,128)S(1)} %get-tuple-element.8, f32[]{:T(128)S(6)} %mul.609, f32[64,2,48,128]{3,2,1,0:T(8,128)S(1)} %broadcast_divide_fusion, f32[]{:T(128)} %bitcast.10, ...), kind=kLoop, calls=%fused_computation.192 | loop fusion | flops 22020096 | bytes 25460752 | tf_op jit(solution)/shard_map/add | solution.py:271
  229.1 4.1 %collective-permute-start.30 = (f32[64,1,48,128]{3,2,1,0:T(8,128)}, f32[64,1,48,128]{3,2,1,0:T(8,128)}, u32[]{:S(2)}, u32[]{:S(2)}) collective-permute-start(f32[64,1,48,128]{3,2,1,0:T(8,128)} %get-tuple-element.26), channel_id=1, source_target_pairs={{4,0},{8,4},{12,8},{16,12},{20,16},{24,20},{28,24},{32,28},{36,32}... | collective-permute-start | bytes 4718600 | tf_op jit(solution)/shard_map/ppermute | solution.py:208
  236.5 4.2 %collective-permute-start.33 = (f32[64,2,1,128]{3,2,1,0:T(1,128)}, f32[64,2,1,128]{3,2,1,0:T(1,128)S(1)}, u32[]{:S(2)}, u32[]{:S(2)}) collective-permute-start(f32[64,2,1,128]{3,2,1,0:T(1,128)} %get-tuple-element.21), channel_id=1, source_target_pairs={{0,1},{1,2},{2,3},{4,5},{5,6},{6,7},{8,9},{9,10},{10,11},{12,13},{... | collective-permute-start | bytes 196616 | tf_op jit(solution)/shard_map/ppermute | solution.py:207
  240.7 7.8 %multiply_add_fusion.2 = (f32[64,2,48,128]{3,2,1,0:T(8,128)S(1)}, f32[64,2,48,128]{3,2,1,0:T(8,128)}) fusion(f32[]{:T(128)S(6)} %div.81, f32[]{:T(128)S(6)} %mul.612, f32[64,2,48,128]{3,2,1,0:T(8,128)S(1)} %get-tuple-element.14, f32[]{:T(128)S(6)} %mul.609, f32[64,2,48,128]{3,2,1,0:T(8,128)S(1)} %broadcast_divide_fusion.1, f32[]{:T(128)} %bitcast.10, ...), kind=kLoop, calls=%fused_computation.195 | loop fusion | flops 22020096 | bytes 25460752 | tf_op jit(solution)/shard_map/add | solution.py:271
  249.9 3.5 %fusion.159 = (f32[64,2,47,128]{3,2,1,0:T(8,128)}, f32[64,2,47,128]{3,2,1,0:T(8,128)}) fusion(f32[64,2,48,128]{3,2,1,0:T(8,128)S(1)} %get-tuple-element.9), kind=kLoop, calls=%fused_computation.232 | loop fusion | bytes 12320768 | tf_op jit(solution)/shard_map/slice | solution.py:215
  256.5 4.1 %collective-permute-start.14 = (f32[64,1,48,128]{3,2,1,0:T(8,128)}, f32[64,1,48,128]{3,2,1,0:T(8,128)}, u32[]{:S(2)}, u32[]{:S(2)}) collective-permute-start(f32[64,1,48,128]{3,2,1,0:T(8,128)} %get-tuple-element.54), channel_id=1, source_target_pairs={{4,0},{8,4},{12,8},{16,12},{20,16},{24,20},{28,24},{32,28},{36,32}... | collective-permute-start | bytes 4718600 | tf_op jit(solution)/shard_map/ppermute | solution.py:208
  263.9 4.6 %collective-permute-start.17 = (f32[64,2,1,128]{3,2,1,0:T(1,128)}, f32[64,2,1,128]{3,2,1,0:T(1,128)}, u32[]{:S(2)}, u32[]{:S(2)}) collective-permute-start(f32[64,2,1,128]{3,2,1,0:T(1,128)} %get-tuple-element.49), channel_id=1, source_target_pairs={{0,1},{1,2},{2,3},{4,5},{5,6},{6,7},{8,9},{9,10},{10,11},{12,13},{... | collective-permute-start | bytes 196616 | tf_op jit(solution)/shard_map/ppermute | solution.py:207
  268.5 8.8 %fusion.81 = f32[1,64,2,48,128]{4,3,2,1,0:T(8,128)} fusion(f32[64,2,48,128]{3,2,1,0:T(8,128)S(1)} %get-tuple-element.8, f32[64,2,48,128]{3,2,1,0:T(8,128)S(1)} %copy-done.2, f32[64,2,48,128]{3,2,1,0:T(8,128)S(1)} %get-tuple-element.9, f32[64,1,48,128]{3,2,1,0:T(8,128)} %collective-permute-done.30, f32[64,1,48,128]{3,2,1,0:T(8,128)} %get-tuple-element.25, ...), kind=kLoop, calls=%fused_computation.99 | loop fusion | flops 25952256 | bytes 25460760 | tf_op jit(solution)/shard_map/stack | solution.py:286
  277.3 5.3 %pad_maximum_fusion.1 = f32[2,64,2,48,128]{4,3,2,1,0:T(8,128)} fusion(f32[1,64,2,48,128]{4,3,2,1,0:T(8,128)} %fusion.81, f32[1,64,2,48,128]{4,3,2,1,0:T(8,128)S(1)} %copy-done.4), kind=kLoop, calls=%fused_computation.17 | loop fusion | flops 1572864 | bytes 12582912 | tf_op jit(solution)/shard_map/stack | solution.py:286
  282.7 7.3 %fusion.39 = f32[1,64,2,48,128]{4,3,2,1,0:T(8,128)S(1)} fusion(f32[64,2,48,128]{3,2,1,0:T(8,128)S(1)} %get-tuple-element.14, f32[64,2,48,128]{3,2,1,0:T(8,128)S(1)} %copy-done.3, f32[64,2,48,128]{3,2,1,0:T(8,128)S(1)} %get-tuple-element.15, f32[64,1,48,128]{3,2,1,0:T(8,128)} %collective-permute-done.14, f32[64,1,48,128]{3,2,1,0:T(8,128)S(1)} %get-tuple-element.53, ...), kind=kLoop, calls=%fused_computation.57 | loop fusion | flops 25952256 | bytes 25460760 | tf_op jit(solution)/shard_map/stack | solution.py:286
  293.1 13.2 %shard_map.77 = f32[128,128]{1,0:T(8,128)} custom-call(f32[128,2,48,128]{3,2,1,0:T(8,128)} %bitcast.36, f32[128,2,48,128]{3,2,1,0:T(8,128)} %bitcast.35), custom_call_target="tpu_custom_call" | custom-call | flops 402653184 | bytes 12582912 | tf_op jit(solution)/shard_map/pallas_call | solution.py:183
  308.1 28.8 %shard_map.78 = f32[1,1,128]{2,1,0:T(1,128)} custom-call(f32[4,32,128]{2,1,0:T(8,128)} %reshape.34.tiles_ref), custom_call_target="tpu_custom_call" | custom-call | tf_op jit(solution)/shard_map/pallas_call | solution.py:98
  (137 shorter events, 88.8 us)
Async XLA Ops:
  44.0 40.6 %all-to-all-start = ((f32[4,16,2,48,128]{4,3,2,1,0:T(8,128)}), f32[4,16,2,48,128]{4,3,2,1,0:T(8,128)S(1)}, u32[]{:S(2)}, u32[]{:S(2)}) async-start(f32[4,16,2,48,128]{4,3,2,1,0:T(8,128)} %pad_maximum_fusion.2), calls=%async_computation | async-start | bytes 6291456 | tf_op jit(solution)/shard_map/all_to_all | solution.py:233
  87.7 25.7 %collective-permute-start.18 = (f32[64,1,48,128]{3,2,1,0:T(8,128)S(1)}, f32[64,1,48,128]{3,2,1,0:T(8,128)S(1)}, u32[]{:S(2)}, u32[]{:S(2)}) collective-permute-start(f32[64,1,48,128]{3,2,1,0:T(8,128)S(1)} %get-tuple-element.40), channel_id=1, source_target_pairs={{4,0},{8,4},{12,8},{16,12},{20,16},{24,20},{28,24},{32,28},{36,32}... | collective-permute-start | bytes 4718600 | tf_op jit(solution)/shard_map/ppermute | solution.py:208
  91.7 26.3 %collective-permute-start.19 = (f32[64,1,48,128]{3,2,1,0:T(8,128)S(1)}, f32[64,1,48,128]{3,2,1,0:T(8,128)S(1)}, u32[]{:S(2)}, u32[]{:S(2)}) collective-permute-start(f32[64,1,48,128]{3,2,1,0:T(8,128)S(1)} %get-tuple-element.39), channel_id=1, source_target_pairs={{0,4},{4,8},{8,12},{12,16},{16,20},{20,24},{24,28},{28,32},{32,36}... | collective-permute-start | bytes 4718600 | tf_op jit(solution)/shard_map/ppermute | solution.py:207
  96.6 15.5 %collective-permute-start.21 = (f32[64,2,1,128]{3,2,1,0:T(1,128)S(1)}, f32[64,2,1,128]{3,2,1,0:T(1,128)S(1)}, u32[]{:S(2)}, u32[]{:S(2)}) collective-permute-start(f32[64,2,1,128]{3,2,1,0:T(1,128)S(1)} %get-tuple-element.44), channel_id=1, source_target_pairs={{0,1},{1,2},{2,3},{4,5},{5,6},{6,7},{8,9},{9,10},{10,11},{12,13},{... | collective-permute-start | bytes 196616 | tf_op jit(solution)/shard_map/ppermute | solution.py:207
  106.5 30.0 %collective-permute-start.1 = (f32[64,1,48,128]{3,2,1,0:T(8,128)}, f32[64,1,48,128]{3,2,1,0:T(8,128)}, u32[]{:S(2)}, u32[]{:S(2)}) collective-permute-start(f32[64,1,48,128]{3,2,1,0:T(8,128)} %get-tuple-element.68), channel_id=1, source_target_pairs={{4,0},{8,4},{12,8},{16,12},{20,16},{24,20},{28,24},{32,28},{36,32}... | collective-permute-start | bytes 4718600 | tf_op jit(solution)/shard_map/ppermute | solution.py:208
  108.4 32.1 %collective-permute-start.3 = (f32[64,1,48,128]{3,2,1,0:T(8,128)}, f32[64,1,48,128]{3,2,1,0:T(8,128)}, u32[]{:S(2)}, u32[]{:S(2)}) collective-permute-start(f32[64,1,48,128]{3,2,1,0:T(8,128)} %get-tuple-element.67), channel_id=1, source_target_pairs={{0,4},{4,8},{8,12},{12,16},{16,20},{20,24},{24,28},{28,32},{32,36}... | collective-permute-start | bytes 4718600 | tf_op jit(solution)/shard_map/ppermute | solution.py:207
  112.1 19.9 %collective-permute-start.4 = (f32[64,2,1,128]{3,2,1,0:T(1,128)}, f32[64,2,1,128]{3,2,1,0:T(1,128)S(1)}, u32[]{:S(2)}, u32[]{:S(2)}) collective-permute-start(f32[64,2,1,128]{3,2,1,0:T(1,128)} %get-tuple-element.71), channel_id=1, source_target_pairs={{1,0},{2,1},{3,2},{5,4},{6,5},{7,6},{9,8},{10,9},{11,10},{13,12},{... | collective-permute-start | bytes 196616 | tf_op jit(solution)/shard_map/ppermute | solution.py:208
  113.4 21.8 %collective-permute-start.5 = (f32[64,2,1,128]{3,2,1,0:T(1,128)}, f32[64,2,1,128]{3,2,1,0:T(1,128)}, u32[]{:S(2)}, u32[]{:S(2)}) collective-permute-start(f32[64,2,1,128]{3,2,1,0:T(1,128)} %get-tuple-element.72), channel_id=1, source_target_pairs={{0,1},{1,2},{2,3},{4,5},{5,6},{6,7},{8,9},{9,10},{10,11},{12,13},{... | collective-permute-start | bytes 196616 | tf_op jit(solution)/shard_map/ppermute | solution.py:207
  129.5 34.5 %collective-permute-start.22 = (f32[64,1,48,128]{3,2,1,0:T(8,128)}, f32[64,1,48,128]{3,2,1,0:T(8,128)}, u32[]{:S(2)}, u32[]{:S(2)}) collective-permute-start(f32[64,1,48,128]{3,2,1,0:T(8,128)} %get-tuple-element.34), channel_id=1, source_target_pairs={{4,0},{8,4},{12,8},{16,12},{20,16},{24,20},{28,24},{32,28},{36,32}... | collective-permute-start | bytes 4718600 | tf_op jit(solution)/shard_map/ppermute | solution.py:208
  132.0 36.1 %collective-permute-start.23 = (f32[64,1,48,128]{3,2,1,0:T(8,128)}, f32[64,1,48,128]{3,2,1,0:T(8,128)}, u32[]{:S(2)}, u32[]{:S(2)}) collective-permute-start(f32[64,1,48,128]{3,2,1,0:T(8,128)} %get-tuple-element.33), channel_id=1, source_target_pairs={{0,4},{4,8},{8,12},{12,16},{16,20},{20,24},{24,28},{28,32},{32,36}... | collective-permute-start | bytes 4718600 | tf_op jit(solution)/shard_map/ppermute | solution.py:207
  135.2 24.0 %collective-permute-start.24 = (f32[64,2,1,128]{3,2,1,0:T(1,128)}, f32[64,2,1,128]{3,2,1,0:T(1,128)S(1)}, u32[]{:S(2)}, u32[]{:S(2)}) collective-permute-start(f32[64,2,1,128]{3,2,1,0:T(1,128)} %get-tuple-element.37), channel_id=1, source_target_pairs={{1,0},{2,1},{3,2},{5,4},{6,5},{7,6},{9,8},{10,9},{11,10},{13,12},{... | collective-permute-start | bytes 196616 | tf_op jit(solution)/shard_map/ppermute | solution.py:208
  136.6 25.5 %collective-permute-start.25 = (f32[64,2,1,128]{3,2,1,0:T(1,128)}, f32[64,2,1,128]{3,2,1,0:T(1,128)S(1)}, u32[]{:S(2)}, u32[]{:S(2)}) collective-permute-start(f32[64,2,1,128]{3,2,1,0:T(1,128)} %get-tuple-element.38), channel_id=1, source_target_pairs={{0,1},{1,2},{2,3},{4,5},{5,6},{6,7},{8,9},{9,10},{10,11},{12,13},{... | collective-permute-start | bytes 196616 | tf_op jit(solution)/shard_map/ppermute | solution.py:207
  156.5 31.4 %collective-permute-start.6 = (f32[64,1,48,128]{3,2,1,0:T(8,128)}, f32[64,1,48,128]{3,2,1,0:T(8,128)}, u32[]{:S(2)}, u32[]{:S(2)}) collective-permute-start(f32[64,1,48,128]{3,2,1,0:T(8,128)} %get-tuple-element.62), channel_id=1, source_target_pairs={{4,0},{8,4},{12,8},{16,12},{20,16},{24,20},{28,24},{32,28},{36,32}... | collective-permute-start | bytes 4718600 | tf_op jit(solution)/shard_map/ppermute | solution.py:208
  159.3 32.6 %collective-permute-start.7 = (f32[64,1,48,128]{3,2,1,0:T(8,128)S(1)}, f32[64,1,48,128]{3,2,1,0:T(8,128)}, u32[]{:S(2)}, u32[]{:S(2)}) collective-permute-start(f32[64,1,48,128]{3,2,1,0:T(8,128)S(1)} %get-tuple-element.61), channel_id=1, source_target_pairs={{0,4},{4,8},{8,12},{12,16},{16,20},{20,24},{24,28},{28,32},{32,36}... | collective-permute-start | bytes 4718600 | tf_op jit(solution)/shard_map/ppermute | solution.py:207
  162.7 20.9 %collective-permute-start.8 = (f32[64,2,1,128]{3,2,1,0:T(1,128)}, f32[64,2,1,128]{3,2,1,0:T(1,128)S(1)}, u32[]{:S(2)}, u32[]{:S(2)}) collective-permute-start(f32[64,2,1,128]{3,2,1,0:T(1,128)} %get-tuple-element.65), channel_id=1, source_target_pairs={{1,0},{2,1},{3,2},{5,4},{6,5},{7,6},{9,8},{10,9},{11,10},{13,12},{... | collective-permute-start | bytes 196616 | tf_op jit(solution)/shard_map/ppermute | solution.py:208
  164.0 21.9 %collective-permute-start.9 = (f32[64,2,1,128]{3,2,1,0:T(1,128)}, f32[64,2,1,128]{3,2,1,0:T(1,128)S(1)}, u32[]{:S(2)}, u32[]{:S(2)}) collective-permute-start(f32[64,2,1,128]{3,2,1,0:T(1,128)} %get-tuple-element.66), channel_id=1, source_target_pairs={{0,1},{1,2},{2,3},{4,5},{5,6},{6,7},{8,9},{9,10},{10,11},{12,13},{... | collective-permute-start | bytes 196616 | tf_op jit(solution)/shard_map/ppermute | solution.py:207
  180.3 33.8 %collective-permute-start.26 = (f32[64,1,48,128]{3,2,1,0:T(8,128)}, f32[64,1,48,128]{3,2,1,0:T(8,128)}, u32[]{:S(2)}, u32[]{:S(2)}) collective-permute-start(f32[64,1,48,128]{3,2,1,0:T(8,128)} %get-tuple-element.28), channel_id=1, source_target_pairs={{4,0},{8,4},{12,8},{16,12},{20,16},{24,20},{28,24},{32,28},{36,32}... | collective-permute-start | bytes 4718600 | tf_op jit(solution)/shard_map/ppermute | solution.py:208
  183.6 35.1 %collective-permute-start.27 = (f32[64,1,48,128]{3,2,1,0:T(8,128)}, f32[64,1,48,128]{3,2,1,0:T(8,128)}, u32[]{:S(2)}, u32[]{:S(2)}) collective-permute-start(f32[64,1,48,128]{3,2,1,0:T(8,128)} %get-tuple-element.27), channel_id=1, source_target_pairs={{0,4},{4,8},{8,12},{12,16},{16,20},{20,24},{24,28},{28,32},{32,36}... | collective-permute-start | bytes 4718600 | tf_op jit(solution)/shard_map/ppermute | solution.py:207
  186.6 24.3 %collective-permute-start.28 = (f32[64,2,1,128]{3,2,1,0:T(1,128)}, f32[64,2,1,128]{3,2,1,0:T(1,128)S(1)}, u32[]{:S(2)}, u32[]{:S(2)}) collective-permute-start(f32[64,2,1,128]{3,2,1,0:T(1,128)} %get-tuple-element.31), channel_id=1, source_target_pairs={{1,0},{2,1},{3,2},{5,4},{6,5},{7,6},{9,8},{10,9},{11,10},{13,12},{... | collective-permute-start | bytes 196616 | tf_op jit(solution)/shard_map/ppermute | solution.py:208
  187.9 24.9 %collective-permute-start.29 = (f32[64,2,1,128]{3,2,1,0:T(1,128)}, f32[64,2,1,128]{3,2,1,0:T(1,128)S(1)}, u32[]{:S(2)}, u32[]{:S(2)}) collective-permute-start(f32[64,2,1,128]{3,2,1,0:T(1,128)} %get-tuple-element.32), channel_id=1, source_target_pairs={{0,1},{1,2},{2,3},{4,5},{5,6},{6,7},{8,9},{9,10},{10,11},{12,13},{... | collective-permute-start | bytes 196616 | tf_op jit(solution)/shard_map/ppermute | solution.py:207
  207.1 29.4 %collective-permute-start.10 = (f32[64,1,48,128]{3,2,1,0:T(8,128)}, f32[64,1,48,128]{3,2,1,0:T(8,128)}, u32[]{:S(2)}, u32[]{:S(2)}) collective-permute-start(f32[64,1,48,128]{3,2,1,0:T(8,128)} %get-tuple-element.56), channel_id=1, source_target_pairs={{4,0},{8,4},{12,8},{16,12},{20,16},{24,20},{28,24},{32,28},{36,32}... | collective-permute-start | bytes 4718600 | tf_op jit(solution)/shard_map/ppermute | solution.py:208
  210.9 29.8 %collective-permute-start.11 = (f32[64,1,48,128]{3,2,1,0:T(8,128)S(1)}, f32[64,1,48,128]{3,2,1,0:T(8,128)}, u32[]{:S(2)}, u32[]{:S(2)}) collective-permute-start(f32[64,1,48,128]{3,2,1,0:T(8,128)S(1)} %get-tuple-element.55), channel_id=1, source_target_pairs={{0,4},{4,8},{8,12},{12,16},{16,20},{20,24},{24,28},{28,32},{32,36}... | collective-permute-start | bytes 4718600 | tf_op jit(solution)/shard_map/ppermute | solution.py:207
  212.8 20.4 %collective-permute-start.12 = (f32[64,2,1,128]{3,2,1,0:T(1,128)}, f32[64,2,1,128]{3,2,1,0:T(1,128)S(1)}, u32[]{:S(2)}, u32[]{:S(2)}) collective-permute-start(f32[64,2,1,128]{3,2,1,0:T(1,128)} %get-tuple-element.59), channel_id=1, source_target_pairs={{1,0},{2,1},{3,2},{5,4},{6,5},{7,6},{9,8},{10,9},{11,10},{13,12},{... | collective-permute-start | bytes 196616 | tf_op jit(solution)/shard_map/ppermute | solution.py:208
  214.1 21.0 %collective-permute-start.13 = (f32[64,2,1,128]{3,2,1,0:T(1,128)}, f32[64,2,1,128]{3,2,1,0:T(1,128)}, u32[]{:S(2)}, u32[]{:S(2)}) collective-permute-start(f32[64,2,1,128]{3,2,1,0:T(1,128)} %get-tuple-element.60), channel_id=1, source_target_pairs={{0,1},{1,2},{2,3},{4,5},{5,6},{6,7},{8,9},{9,10},{10,11},{12,13},{... | collective-permute-start | bytes 196616 | tf_op jit(solution)/shard_map/ppermute | solution.py:207
  229.1 34.8 %collective-permute-start.30 = (f32[64,1,48,128]{3,2,1,0:T(8,128)}, f32[64,1,48,128]{3,2,1,0:T(8,128)}, u32[]{:S(2)}, u32[]{:S(2)}) collective-permute-start(f32[64,1,48,128]{3,2,1,0:T(8,128)} %get-tuple-element.26), channel_id=1, source_target_pairs={{4,0},{8,4},{12,8},{16,12},{20,16},{24,20},{28,24},{32,28},{36,32}... | collective-permute-start | bytes 4718600 | tf_op jit(solution)/shard_map/ppermute | solution.py:208
  233.2 35.3 %collective-permute-start.31 = (f32[64,1,48,128]{3,2,1,0:T(8,128)}, f32[64,1,48,128]{3,2,1,0:T(8,128)}, u32[]{:S(2)}, u32[]{:S(2)}) collective-permute-start(f32[64,1,48,128]{3,2,1,0:T(8,128)} %get-tuple-element.25), channel_id=1, source_target_pairs={{0,4},{4,8},{8,12},{12,16},{16,20},{20,24},{24,28},{28,32},{32,36}... | collective-permute-start | bytes 4718600 | tf_op jit(solution)/shard_map/ppermute | solution.py:207
  235.2 25.5 %collective-permute-start.32 = (f32[64,2,1,128]{3,2,1,0:T(1,128)}, f32[64,2,1,128]{3,2,1,0:T(1,128)S(1)}, u32[]{:S(2)}, u32[]{:S(2)}) collective-permute-start(f32[64,2,1,128]{3,2,1,0:T(1,128)} %get-tuple-element.22), channel_id=1, source_target_pairs={{1,0},{2,1},{3,2},{5,4},{6,5},{7,6},{9,8},{10,9},{11,10},{13,12},{... | collective-permute-start | bytes 196616 | tf_op jit(solution)/shard_map/ppermute | solution.py:208
  236.5 26.1 %collective-permute-start.33 = (f32[64,2,1,128]{3,2,1,0:T(1,128)}, f32[64,2,1,128]{3,2,1,0:T(1,128)S(1)}, u32[]{:S(2)}, u32[]{:S(2)}) collective-permute-start(f32[64,2,1,128]{3,2,1,0:T(1,128)} %get-tuple-element.21), channel_id=1, source_target_pairs={{0,1},{1,2},{2,3},{4,5},{5,6},{6,7},{8,9},{9,10},{10,11},{12,13},{... | collective-permute-start | bytes 196616 | tf_op jit(solution)/shard_map/ppermute | solution.py:207
  256.5 26.1 %collective-permute-start.14 = (f32[64,1,48,128]{3,2,1,0:T(8,128)}, f32[64,1,48,128]{3,2,1,0:T(8,128)}, u32[]{:S(2)}, u32[]{:S(2)}) collective-permute-start(f32[64,1,48,128]{3,2,1,0:T(8,128)} %get-tuple-element.54), channel_id=1, source_target_pairs={{4,0},{8,4},{12,8},{16,12},{20,16},{24,20},{28,24},{32,28},{36,32}... | collective-permute-start | bytes 4718600 | tf_op jit(solution)/shard_map/ppermute | solution.py:208
  260.6 22.0 %collective-permute-start.15 = (f32[64,1,48,128]{3,2,1,0:T(8,128)S(1)}, f32[64,1,48,128]{3,2,1,0:T(8,128)}, u32[]{:S(2)}, u32[]{:S(2)}) collective-permute-start(f32[64,1,48,128]{3,2,1,0:T(8,128)S(1)} %get-tuple-element.53), channel_id=1, source_target_pairs={{0,4},{4,8},{8,12},{12,16},{16,20},{20,24},{24,28},{28,32},{32,36}... | collective-permute-start | bytes 4718600 | tf_op jit(solution)/shard_map/ppermute | solution.py:207
  262.6 20.0 %collective-permute-start.16 = (f32[64,2,1,128]{3,2,1,0:T(1,128)}, f32[64,2,1,128]{3,2,1,0:T(1,128)S(1)}, u32[]{:S(2)}, u32[]{:S(2)}) collective-permute-start(f32[64,2,1,128]{3,2,1,0:T(1,128)} %get-tuple-element.50), channel_id=1, source_target_pairs={{1,0},{2,1},{3,2},{5,4},{6,5},{7,6},{9,8},{10,9},{11,10},{13,12},{... | collective-permute-start | bytes 196616 | tf_op jit(solution)/shard_map/ppermute | solution.py:208
  263.9 18.7 %collective-permute-start.17 = (f32[64,2,1,128]{3,2,1,0:T(1,128)}, f32[64,2,1,128]{3,2,1,0:T(1,128)}, u32[]{:S(2)}, u32[]{:S(2)}) collective-permute-start(f32[64,2,1,128]{3,2,1,0:T(1,128)} %get-tuple-element.49), channel_id=1, source_target_pairs={{0,1},{1,2},{2,3},{4,5},{5,6},{6,7},{8,9},{9,10},{10,11},{12,13},{... | collective-permute-start | bytes 196616 | tf_op jit(solution)/shard_map/ppermute | solution.py:207
  (24 other events, 253.1 us)

commit v11 on v3

--- a/solution.py
+++ b/solution.py
@@ -241,8 +241,10 @@
 
 def body(input_map, output_map, region_ids, region_cond, shift_ids):
     col_count = lax.axis_size("col")
-    ctrl_in = windows(input_map, input_map.shape[2] // col_count, col_count)
-    obsv_in = windows(output_map, output_map.shape[2] // col_count, col_count)
+    both = windows(jnp.concatenate([input_map, output_map], 0), input_map.shape[2] // col_count, col_count)
+    both = both.reshape((col_count, 2, input_map.shape[0]) + both.shape[1:])
+    ctrl_in = both[:, 0].reshape((-1,) + both.shape[3:])
+    obsv_in = both[:, 1].reshape((-1,) + both.shape[3:])
     col_local = ctrl_in.shape[0]
     rows = ctrl_in.shape[2]
     local_x = input_map.shape[1]

time: 340 us -> 339 us (level)
  starting transfers between devices: 109 us -> 102 us
  waiting for transfers between devices: 44.4 us -> 49.6 us
  other arithmetic: 88.1 us -> 83.1 us
  local copies, waits for them, and re-layouts: 46.4 us -> 50 us
    all_to_all x2 -> x1, waiting for transfers between devices: 44.3 us -> 49.5 us  [windows(): received = lax.all_to_all(jnp.stack(parts), 'col', 0, 0, tiled=True)]
    all_to_all x2 -> x1, starting transfers between devices: 9.48 us -> 5.36 us  [windows(): received = lax.all_to_all(jnp.stack(parts), 'col', 0, 0, tiled=True)]
  transfers between devices with their start and end apart: 36 -> 35, of which waited for: 2 -> 1; matrix products, arithmetic and copies ran while one was open for 33% -> 32% of each run, Pallas kernels for 0% -> 0%
where the time goes in v11:
time: 339 us; the launch traced here: 337 us
  starting transfers between devices  102 us (30%)
  other arithmetic  83.1 us (25%)
  local copies, waits for them, and re-layouts  50 us (15%)
  waiting for transfers between devices  49.6 us (15%)
  Pallas kernels  43.7 us (13%)
  between operations  9.04 us (3%)
    ppermute x16, starting transfers between devices, halo_pair(): lax.ppermute(lax.slice_in_dim(block, size - 1, None, axis=dim), axis, for...  53.3 us
    all_to_all x1, waiting for transfers between devices, windows(): received = lax.all_to_all(jnp.stack(parts), 'col', 0, 0, tiled=True)  49.5 us
    another operation x6, other arithmetic, run_segments(): return jnp.stack(factors)  42 us
    ppermute x16, starting transfers between devices, halo_pair(): high = lax.ppermute(lax.slice_in_dim(block, 0, 1, axis=dim), axis, backward)  36.3 us
    pallas_call x1, Pallas kernels, reduce_scatter(): pl.pallas_call(reduce_kernel, out_shape=jax.ShapeDtypeStruct((1, 1, lanes...  30.5 us
    add x4, other arithmetic, solve_slabs(): rho_next * rho_now * direction + 2.0 * rho_next / half_span * residual  30.4 us
    slice x14, local copies, waits for them, and re-layouts, shifted(): lax.slice_in_dim(block, 1, None, axis=dim)  26.5 us
    pallas_call x1, Pallas kernels, gram(): pl.pallas_call(gram_kernel, grid=(depth, rows // rows_per_step), in_specs...  13.2 us
  transfers between devices with their start and end apart: 35, of which 1 were waited for; matrix products, arithmetic and copies ran while one was open for 32% of the time, Pallas kernels for 0%

profile of v11, /device:TPU:1, one launch (start us, length us, event | category | flops | bytes accessed | tf_op | source)
XLA Modules:
  0.0 337.2 jit_solution(16246682812436202414)
XLA Ops:
  7.6 5.4 %all-to-all-start = ((f32[4,32,2,48,128]{4,3,2,1,0:T(8,128)}), f32[4,32,2,48,128]{4,3,2,1,0:T(8,128)}, u32[]{:S(2)}, u32[]{:S(2)}) async-start(f32[4,32,2,48,128]{4,3,2,1,0:T(8,128)} %pad_maximum_fusion), calls=%async_computation | async-start | bytes 12582912 | tf_op jit(solution)/shard_map/all_to_all | solution.py:186
  13.7 5.2 %select_add_fusion = f32[2,192,128]{2,1,0:T(8,128)S(1)} fusion(s32[2,192,128]{2,1,0:T(8,128)S(1)} %copy-done.12, f32[]{:T(128)} %bitcast.14, f32[]{:T(128)} %bitcast.13, f32[]{:T(128)} %bitcast.12, f32[]{:T(128)} %bitcast.11, f32[]{:T(128)} %bitcast.10, f32[]{:T(128)} %bitcast.9, f32[]{:T(128)} %bitcast.8, f32[]{:T(128)} %bitcast.7), kind=kLoop, calls=%fused_computation.205 | loop fusion | flops 1130496 | bytes 393248 | tf_op jit(solution)/shard_map/add | solution.py:151
  18.9 3.3 collective-permute-start
  22.3 3.5 %collective-permute-start.2 = (f32[1,50,128]{2,1,0:T(8,128)S(1)}, f32[1,50,128]{2,1,0:T(8,128)S(1)}, u32[]{:S(2)}, u32[]{:S(2)}) collective-permute-start(f32[1,50,128]{2,1,0:T(8,128)S(1)} %get-tuple-element.73), channel_id=1, source_target_pairs={{0,4},{4,8},{8,12},{12,16},{16,20},{20,24},{24,28},{28,32},{32,36}... | collective-permute-start | bytes 76808 | tf_op jit(solution)/shard_map/ppermute | solution.py:19
  34.8 49.5 %all-to-all-done = f32[4,32,2,48,128]{4,3,2,1,0:T(8,128)} async-done(((f32[4,32,2,48,128]{4,3,2,1,0:T(8,128)}), f32[4,32,2,48,128]{4,3,2,1,0:T(8,128)}, u32[]{:S(2)}, u32[]{:S(2)}) %all-to-all-start) | async-done | bytes 6291488 | tf_op jit(solution)/shard_map/all_to_all | solution.py:186
  88.5 3.5 %collective-permute-start.18 = (f32[64,1,48,128]{3,2,1,0:T(8,128)S(1)}, f32[64,1,48,128]{3,2,1,0:T(8,128)S(1)}, u32[]{:S(2)}, u32[]{:S(2)}) collective-permute-start(f32[64,1,48,128]{3,2,1,0:T(8,128)S(1)} %get-tuple-element.42), channel_id=1, source_target_pairs={{4,0},{8,4},{12,8},{16,12},{20,16},{24,20},{28,24},{32,28},{36,32}... | collective-permute-start | bytes 4718600 | tf_op jit(solution)/shard_map/ppermute | solution.py:161
  92.1 3.6 %collective-permute-start.19 = (f32[64,1,48,128]{3,2,1,0:T(8,128)S(1)}, f32[64,1,48,128]{3,2,1,0:T(8,128)S(1)}, u32[]{:S(2)}, u32[]{:S(2)}) collective-permute-start(f32[64,1,48,128]{3,2,1,0:T(8,128)S(1)} %get-tuple-element.41), channel_id=1, source_target_pairs={{0,4},{4,8},{8,12},{12,16},{16,20},{20,24},{24,28},{28,32},{32,36}... | collective-permute-start | bytes 4718600 | tf_op jit(solution)/shard_map/ppermute | solution.py:160
  97.1 4.0 %collective-permute-start.21 = (f32[64,2,1,128]{3,2,1,0:T(1,128)S(1)}, f32[64,2,1,128]{3,2,1,0:T(1,128)S(1)}, u32[]{:S(2)}, u32[]{:S(2)}) collective-permute-start(f32[64,2,1,128]{3,2,1,0:T(1,128)S(1)} %get-tuple-element.46), channel_id=1, source_target_pairs={{0,1},{1,2},{2,3},{4,5},{5,6},{6,7},{8,9},{9,10},{10,11},{12,13},{... | collective-permute-start | bytes 196616 | tf_op jit(solution)/shard_map/ppermute | solution.py:160
  109.8 3.6 %collective-permute-start.3 = (f32[64,1,48,128]{3,2,1,0:T(8,128)S(1)}, f32[64,1,48,128]{3,2,1,0:T(8,128)}, u32[]{:S(2)}, u32[]{:S(2)}) collective-permute-start(f32[64,1,48,128]{3,2,1,0:T(8,128)S(1)} %get-tuple-element.65), channel_id=1, source_target_pairs={{0,4},{4,8},{8,12},{12,16},{16,20},{20,24},{24,28},{28,32},{32,36}... | collective-permute-start | bytes 4718600 | tf_op jit(solution)/shard_map/ppermute | solution.py:160
  114.8 4.0 %collective-permute-start.5 = (f32[64,2,1,128]{3,2,1,0:T(1,128)}, f32[64,2,1,128]{3,2,1,0:T(1,128)S(1)}, u32[]{:S(2)}, u32[]{:S(2)}) collective-permute-start(f32[64,2,1,128]{3,2,1,0:T(1,128)} %get-tuple-element.70), channel_id=1, source_target_pairs={{0,1},{1,2},{2,3},{4,5},{5,6},{6,7},{8,9},{9,10},{10,11},{12,13},{... | collective-permute-start | bytes 196616 | tf_op jit(solution)/shard_map/ppermute | solution.py:160
  120.0 7.3 %multiply_add_fusion.1 = (f32[64,2,48,128]{3,2,1,0:T(8,128)S(1)}, f32[64,2,48,128]{3,2,1,0:T(8,128)}) fusion(f32[64,2,48,128]{3,2,1,0:T(8,128)S(1)} %get-tuple-element.90, f32[]{:T(128)S(6)} %div.73, f32[]{:T(128)S(6)} %mul.258, f32[]{:T(128)} %bitcast, f32[2,48,128]{2,1,0:T(8,128)S(1)} %get-tuple-element.76, f32[2,48,128]{2,1,0:T(8,128)S(1)} %get-tuple-element.79, ...), kind=kLoop, calls=%fused_computation.195 | loop fusion | flops 21233664 | bytes 25460748 | tf_op jit(solution)/shard_map/add | solution.py:224
  136.9 4.0 %collective-permute-start.25 = (f32[64,2,1,128]{3,2,1,0:T(1,128)}, f32[64,2,1,128]{3,2,1,0:T(1,128)S(1)}, u32[]{:S(2)}, u32[]{:S(2)}) collective-permute-start(f32[64,2,1,128]{3,2,1,0:T(1,128)} %get-tuple-element.40), channel_id=1, source_target_pairs={{0,1},{1,2},{2,3},{4,5},{5,6},{6,7},{8,9},{9,10},{10,11},{12,13},{... | collective-permute-start | bytes 196616 | tf_op jit(solution)/shard_map/ppermute | solution.py:160
  140.9 7.6 %multiply_add_fusion.3 = (f32[64,2,48,128]{3,2,1,0:T(8,128)S(1)}, f32[64,2,48,128]{3,2,1,0:T(8,128)}) fusion(f32[64,2,48,128]{3,2,1,0:T(8,128)S(1)} %get-tuple-element.91, f32[]{:T(128)S(6)} %div.73, f32[]{:T(128)S(6)} %mul.258, f32[]{:T(128)} %bitcast, f32[2,48,128]{2,1,0:T(8,128)S(1)} %get-tuple-element.76, f32[2,48,128]{2,1,0:T(8,128)S(1)} %get-tuple-element.79, ...), kind=kLoop, calls=%fused_computation.198 | loop fusion | flops 21233664 | bytes 25460748 | tf_op jit(solution)/shard_map/add | solution.py:224
  149.9 3.5 %fusion.166 = (f32[64,2,47,128]{3,2,1,0:T(8,128)}, f32[64,2,47,128]{3,2,1,0:T(8,128)}) fusion(f32[64,2,48,128]{3,2,1,0:T(8,128)S(1)} %get-tuple-element.7), kind=kLoop, calls=%fused_computation.240 | loop fusion | bytes 12320768 | tf_op jit(solution)/shard_map/slice | solution.py:167
  163.3 4.0 %collective-permute-start.9 = (f32[64,2,1,128]{3,2,1,0:T(1,128)}, f32[64,2,1,128]{3,2,1,0:T(1,128)S(1)}, u32[]{:S(2)}, u32[]{:S(2)}) collective-permute-start(f32[64,2,1,128]{3,2,1,0:T(1,128)} %get-tuple-element.64), channel_id=1, source_target_pairs={{0,1},{1,2},{2,3},{4,5},{5,6},{6,7},{8,9},{9,10},{10,11},{12,13},{... | collective-permute-start | bytes 196616 | tf_op jit(solution)/shard_map/ppermute | solution.py:160
  167.3 9.2 %multiply_bitcast_fusion = (f32[1,64,2,48,128]{4,3,2,1,0:T(8,128)}, f32[64,2,48,128]{3,2,1,0:T(8,128)S(1)}) fusion(f32[]{:T(128)S(6)} %sqrt.8, f32[64,2,48,128]{3,2,1,0:T(8,128)} %get-tuple-element.8, f32[64,2,48,128]{3,2,1,0:T(8,128)S(1)} %get-tuple-element.7, f32[]{:T(128)} %bitcast, f32[2,48,128]{2,1,0:T(8,128)S(1)} %get-tuple-element.76, ...), kind=kLoop, calls=%fused_computation.194 | loop fusion | flops 23592960 | bytes 28606480 | tf_op jit(solution)/shard_map/stack | solution.py:239
  186.4 4.0 %collective-permute-start.29 = (f32[64,2,1,128]{3,2,1,0:T(1,128)}, f32[64,2,1,128]{3,2,1,0:T(1,128)S(1)}, u32[]{:S(2)}, u32[]{:S(2)}) collective-permute-start(f32[64,2,1,128]{3,2,1,0:T(1,128)} %get-tuple-element.34), channel_id=1, source_target_pairs={{0,1},{1,2},{2,3},{4,5},{5,6},{6,7},{8,9},{9,10},{10,11},{12,13},{... | collective-permute-start | bytes 196616 | tf_op jit(solution)/shard_map/ppermute | solution.py:160
  190.4 8.3 %multiply_bitcast_fusion.1 = (f32[1,64,2,48,128]{4,3,2,1,0:T(8,128)}, f32[64,2,48,128]{3,2,1,0:T(8,128)S(1)}) fusion(f32[]{:T(128)S(6)} %sqrt.8, f32[64,2,48,128]{3,2,1,0:T(8,128)} %get-tuple-element.14, f32[64,2,48,128]{3,2,1,0:T(8,128)S(1)} %get-tuple-element.13, f32[]{:T(128)} %bitcast, f32[2,48,128]{2,1,0:T(8,128)S(1)} %get-tuple-element.76, ...), kind=kLoop, calls=%fused_computation.197 | loop fusion | flops 23592960 | bytes 28606480 | tf_op jit(solution)/shard_map/stack | solution.py:239
  205.7 3.8 %collective-permute-start.10 = (f32[64,1,48,128]{3,2,1,0:T(8,128)}, f32[64,1,48,128]{3,2,1,0:T(8,128)}, u32[]{:S(2)}, u32[]{:S(2)}) collective-permute-start(f32[64,1,48,128]{3,2,1,0:T(8,128)} %get-tuple-element.54), channel_id=1, source_target_pairs={{4,0},{8,4},{12,8},{16,12},{20,16},{24,20},{28,24},{32,28},{36,32}... | collective-permute-start | bytes 4718600 | tf_op jit(solution)/shard_map/ppermute | solution.py:161
  212.7 4.0 %collective-permute-start.13 = (f32[64,2,1,128]{3,2,1,0:T(1,128)}, f32[64,2,1,128]{3,2,1,0:T(1,128)S(1)}, u32[]{:S(2)}, u32[]{:S(2)}) collective-permute-start(f32[64,2,1,128]{3,2,1,0:T(1,128)} %get-tuple-element.58), channel_id=1, source_target_pairs={{0,1},{1,2},{2,3},{4,5},{5,6},{6,7},{8,9},{9,10},{10,11},{12,13},{... | collective-permute-start | bytes 196616 | tf_op jit(solution)/shard_map/ppermute | solution.py:160
  216.7 7.8 %multiply_add_fusion = (f32[64,2,48,128]{3,2,1,0:T(8,128)S(1)}, f32[64,2,48,128]{3,2,1,0:T(8,128)}) fusion(f32[]{:T(128)S(6)} %div.81, f32[]{:T(128)S(6)} %mul.607, f32[64,2,48,128]{3,2,1,0:T(8,128)S(1)} %get-tuple-element.4, f32[]{:T(128)S(6)} %mul.604, f32[64,2,48,128]{3,2,1,0:T(8,128)S(1)} %broadcast_divide_fusion, f32[]{:T(128)} %bitcast.16, ...), kind=kLoop, calls=%fused_computation.193 | loop fusion | flops 22020096 | bytes 25460752 | tf_op jit(solution)/shard_map/add | solution.py:224
  227.1 4.2 %collective-permute-start.30 = (f32[64,1,48,128]{3,2,1,0:T(8,128)}, f32[64,1,48,128]{3,2,1,0:T(8,128)}, u32[]{:S(2)}, u32[]{:S(2)}) collective-permute-start(f32[64,1,48,128]{3,2,1,0:T(8,128)} %get-tuple-element.28), channel_id=1, source_target_pairs={{4,0},{8,4},{12,8},{16,12},{20,16},{24,20},{28,24},{32,28},{36,32}... | collective-permute-start | bytes 4718600 | tf_op jit(solution)/shard_map/ppermute | solution.py:161
  234.5 4.2 %collective-permute-start.33 = (f32[64,2,1,128]{3,2,1,0:T(1,128)}, f32[64,2,1,128]{3,2,1,0:T(1,128)S(1)}, u32[]{:S(2)}, u32[]{:S(2)}) collective-permute-start(f32[64,2,1,128]{3,2,1,0:T(1,128)} %get-tuple-element.23), channel_id=1, source_target_pairs={{0,1},{1,2},{2,3},{4,5},{5,6},{6,7},{8,9},{9,10},{10,11},{12,13},{... | collective-permute-start | bytes 196616 | tf_op jit(solution)/shard_map/ppermute | solution.py:160
  238.8 7.8 %multiply_add_fusion.2 = (f32[64,2,48,128]{3,2,1,0:T(8,128)S(1)}, f32[64,2,48,128]{3,2,1,0:T(8,128)}) fusion(f32[]{:T(128)S(6)} %div.81, f32[]{:T(128)S(6)} %mul.607, f32[64,2,48,128]{3,2,1,0:T(8,128)S(1)} %get-tuple-element.10, f32[]{:T(128)S(6)} %mul.604, f32[64,2,48,128]{3,2,1,0:T(8,128)S(1)} %broadcast_divide_fusion.1, f32[]{:T(128)} %bitcast.16, ...), kind=kLoop, calls=%fused_computation.196 | loop fusion | flops 22020096 | bytes 25460752 | tf_op jit(solution)/shard_map/add | solution.py:224
  247.9 3.4 %fusion.160 = (f32[64,2,47,128]{3,2,1,0:T(8,128)}, f32[64,2,47,128]{3,2,1,0:T(8,128)}) fusion(f32[64,2,48,128]{3,2,1,0:T(8,128)S(1)} %get-tuple-element.5), kind=kLoop, calls=%fused_computation.234 | loop fusion | bytes 12320768 | tf_op jit(solution)/shard_map/slice | solution.py:168
  254.5 4.1 %collective-permute-start.14 = (f32[64,1,48,128]{3,2,1,0:T(8,128)}, f32[64,1,48,128]{3,2,1,0:T(8,128)}, u32[]{:S(2)}, u32[]{:S(2)}) collective-permute-start(f32[64,1,48,128]{3,2,1,0:T(8,128)} %get-tuple-element.52), channel_id=1, source_target_pairs={{4,0},{8,4},{12,8},{16,12},{20,16},{24,20},{28,24},{32,28},{36,32}... | collective-permute-start | bytes 4718600 | tf_op jit(solution)/shard_map/ppermute | solution.py:161
  261.9 4.0 %collective-permute-start.17 = (f32[64,2,1,128]{3,2,1,0:T(1,128)}, f32[64,2,1,128]{3,2,1,0:T(1,128)S(1)}, u32[]{:S(2)}, u32[]{:S(2)}) collective-permute-start(f32[64,2,1,128]{3,2,1,0:T(1,128)} %get-tuple-element.47), channel_id=1, source_target_pairs={{0,1},{1,2},{2,3},{4,5},{5,6},{6,7},{8,9},{9,10},{10,11},{12,13},{... | collective-permute-start | bytes 196616 | tf_op jit(solution)/shard_map/ppermute | solution.py:160
  265.9 8.8 %fusion.81 = f32[1,64,2,48,128]{4,3,2,1,0:T(8,128)} fusion(f32[64,2,48,128]{3,2,1,0:T(8,128)S(1)} %get-tuple-element.4, f32[64,2,48,128]{3,2,1,0:T(8,128)S(1)} %copy-done.1, f32[64,2,48,128]{3,2,1,0:T(8,128)S(1)} %get-tuple-element.5, f32[64,1,48,128]{3,2,1,0:T(8,128)} %collective-permute-done.30, f32[64,1,48,128]{3,2,1,0:T(8,128)} %get-tuple-element.27, ...), kind=kLoop, calls=%fused_computation.100 | loop fusion | flops 25952256 | bytes 25460760 | tf_op jit(solution)/shard_map/stack | solution.py:239
  274.7 5.3 %pad_maximum_fusion.2 = f32[2,64,2,48,128]{4,3,2,1,0:T(8,128)} fusion(f32[1,64,2,48,128]{4,3,2,1,0:T(8,128)} %fusion.81, f32[1,64,2,48,128]{4,3,2,1,0:T(8,128)S(1)} %copy-done.3), kind=kLoop, calls=%fused_computation.18 | loop fusion | flops 1572864 | bytes 12582912 | tf_op jit(solution)/shard_map/stack | solution.py:239
  280.0 7.2 %fusion.39 = f32[1,64,2,48,128]{4,3,2,1,0:T(8,128)S(1)} fusion(f32[64,2,48,128]{3,2,1,0:T(8,128)S(1)} %get-tuple-element.10, f32[64,2,48,128]{3,2,1,0:T(8,128)S(1)} %copy-done.2, f32[64,2,48,128]{3,2,1,0:T(8,128)S(1)} %get-tuple-element.11, f32[64,1,48,128]{3,2,1,0:T(8,128)} %collective-permute-done.14, f32[64,1,48,128]{3,2,1,0:T(8,128)S(1)} %get-tuple-element.51, ...), kind=kLoop, calls=%fused_computation.58 | loop fusion | flops 25952256 | bytes 25460760 | tf_op jit(solution)/shard_map/stack | solution.py:239
  290.4 13.2 %shard_map.76 = f32[128,128]{1,0:T(8,128)} custom-call(f32[128,2,48,128]{3,2,1,0:T(8,128)} %bitcast.45, f32[128,2,48,128]{3,2,1,0:T(8,128)} %bitcast.44), custom_call_target="tpu_custom_call" | custom-call | flops 402653184 | bytes 12582912 | tf_op jit(solution)/shard_map/pallas_call | solution.py:136
  305.4 30.5 %shard_map.77 = f32[1,1,128]{2,1,0:T(1,128)} custom-call(f32[4,32,128]{2,1,0:T(8,128)} %reshape.30.tiles_ref), custom_call_target="tpu_custom_call" | custom-call | tf_op jit(solution)/shard_map/pallas_call | solution.py:98
  (126 shorter events, 86.5 us)
Async XLA Ops:
  7.6 76.7 %all-to-all-start = ((f32[4,32,2,48,128]{4,3,2,1,0:T(8,128)}), f32[4,32,2,48,128]{4,3,2,1,0:T(8,128)}, u32[]{:S(2)}, u32[]{:S(2)}) async-start(f32[4,32,2,48,128]{4,3,2,1,0:T(8,128)} %pad_maximum_fusion), calls=%async_computation | async-start | bytes 12582912 | tf_op jit(solution)/shard_map/all_to_all | solution.py:186
  88.5 26.2 %collective-permute-start.18 = (f32[64,1,48,128]{3,2,1,0:T(8,128)S(1)}, f32[64,1,48,128]{3,2,1,0:T(8,128)S(1)}, u32[]{:S(2)}, u32[]{:S(2)}) collective-permute-start(f32[64,1,48,128]{3,2,1,0:T(8,128)S(1)} %get-tuple-element.42), channel_id=1, source_target_pairs={{4,0},{8,4},{12,8},{16,12},{20,16},{24,20},{28,24},{32,28},{36,32}... | collective-permute-start | bytes 4718600 | tf_op jit(solution)/shard_map/ppermute | solution.py:161
  92.1 26.7 %collective-permute-start.19 = (f32[64,1,48,128]{3,2,1,0:T(8,128)S(1)}, f32[64,1,48,128]{3,2,1,0:T(8,128)S(1)}, u32[]{:S(2)}, u32[]{:S(2)}) collective-permute-start(f32[64,1,48,128]{3,2,1,0:T(8,128)S(1)} %get-tuple-element.41), channel_id=1, source_target_pairs={{0,4},{4,8},{8,12},{12,16},{16,20},{20,24},{24,28},{28,32},{32,36}... | collective-permute-start | bytes 4718600 | tf_op jit(solution)/shard_map/ppermute | solution.py:160
  97.1 16.4 %collective-permute-start.21 = (f32[64,2,1,128]{3,2,1,0:T(1,128)S(1)}, f32[64,2,1,128]{3,2,1,0:T(1,128)S(1)}, u32[]{:S(2)}, u32[]{:S(2)}) collective-permute-start(f32[64,2,1,128]{3,2,1,0:T(1,128)S(1)} %get-tuple-element.46), channel_id=1, source_target_pairs={{0,1},{1,2},{2,3},{4,5},{5,6},{6,7},{8,9},{9,10},{10,11},{12,13},{... | collective-permute-start | bytes 196616 | tf_op jit(solution)/shard_map/ppermute | solution.py:160
  107.9 29.0 %collective-permute-start.1 = (f32[64,1,48,128]{3,2,1,0:T(8,128)}, f32[64,1,48,128]{3,2,1,0:T(8,128)}, u32[]{:S(2)}, u32[]{:S(2)}) collective-permute-start(f32[64,1,48,128]{3,2,1,0:T(8,128)} %get-tuple-element.66), channel_id=1, source_target_pairs={{4,0},{8,4},{12,8},{16,12},{20,16},{24,20},{28,24},{32,28},{36,32}... | collective-permute-start | bytes 4718600 | tf_op jit(solution)/shard_map/ppermute | solution.py:161
  109.8 31.1 %collective-permute-start.3 = (f32[64,1,48,128]{3,2,1,0:T(8,128)S(1)}, f32[64,1,48,128]{3,2,1,0:T(8,128)}, u32[]{:S(2)}, u32[]{:S(2)}) collective-permute-start(f32[64,1,48,128]{3,2,1,0:T(8,128)S(1)} %get-tuple-element.65), channel_id=1, source_target_pairs={{0,4},{4,8},{8,12},{12,16},{16,20},{20,24},{24,28},{28,32},{32,36}... | collective-permute-start | bytes 4718600 | tf_op jit(solution)/shard_map/ppermute | solution.py:160
  113.5 18.9 %collective-permute-start.4 = (f32[64,2,1,128]{3,2,1,0:T(1,128)}, f32[64,2,1,128]{3,2,1,0:T(1,128)S(1)}, u32[]{:S(2)}, u32[]{:S(2)}) collective-permute-start(f32[64,2,1,128]{3,2,1,0:T(1,128)} %get-tuple-element.69), channel_id=1, source_target_pairs={{1,0},{2,1},{3,2},{5,4},{6,5},{7,6},{9,8},{10,9},{11,10},{13,12},{... | collective-permute-start | bytes 196616 | tf_op jit(solution)/shard_map/ppermute | solution.py:161
  114.8 20.8 %collective-permute-start.5 = (f32[64,2,1,128]{3,2,1,0:T(1,128)}, f32[64,2,1,128]{3,2,1,0:T(1,128)S(1)}, u32[]{:S(2)}, u32[]{:S(2)}) collective-permute-start(f32[64,2,1,128]{3,2,1,0:T(1,128)} %get-tuple-element.70), channel_id=1, source_target_pairs={{0,1},{1,2},{2,3},{4,5},{5,6},{6,7},{8,9},{9,10},{10,11},{12,13},{... | collective-permute-start | bytes 196616 | tf_op jit(solution)/shard_map/ppermute | solution.py:160
  130.0 33.3 %collective-permute-start.22 = (f32[64,1,48,128]{3,2,1,0:T(8,128)}, f32[64,1,48,128]{3,2,1,0:T(8,128)}, u32[]{:S(2)}, u32[]{:S(2)}) collective-permute-start(f32[64,1,48,128]{3,2,1,0:T(8,128)} %get-tuple-element.36), channel_id=1, source_target_pairs={{4,0},{8,4},{12,8},{16,12},{20,16},{24,20},{28,24},{32,28},{36,32}... | collective-permute-start | bytes 4718600 | tf_op jit(solution)/shard_map/ppermute | solution.py:161
  132.4 34.9 %collective-permute-start.23 = (f32[64,1,48,128]{3,2,1,0:T(8,128)}, f32[64,1,48,128]{3,2,1,0:T(8,128)}, u32[]{:S(2)}, u32[]{:S(2)}) collective-permute-start(f32[64,1,48,128]{3,2,1,0:T(8,128)} %get-tuple-element.35), channel_id=1, source_target_pairs={{0,4},{4,8},{8,12},{12,16},{16,20},{20,24},{24,28},{28,32},{32,36}... | collective-permute-start | bytes 4718600 | tf_op jit(solution)/shard_map/ppermute | solution.py:160
  135.6 23.6 %collective-permute-start.24 = (f32[64,2,1,128]{3,2,1,0:T(1,128)}, f32[64,2,1,128]{3,2,1,0:T(1,128)S(1)}, u32[]{:S(2)}, u32[]{:S(2)}) collective-permute-start(f32[64,2,1,128]{3,2,1,0:T(1,128)} %get-tuple-element.39), channel_id=1, source_target_pairs={{1,0},{2,1},{3,2},{5,4},{6,5},{7,6},{9,8},{10,9},{11,10},{13,12},{... | collective-permute-start | bytes 196616 | tf_op jit(solution)/shard_map/ppermute | solution.py:161
  136.9 25.1 %collective-permute-start.25 = (f32[64,2,1,128]{3,2,1,0:T(1,128)}, f32[64,2,1,128]{3,2,1,0:T(1,128)S(1)}, u32[]{:S(2)}, u32[]{:S(2)}) collective-permute-start(f32[64,2,1,128]{3,2,1,0:T(1,128)} %get-tuple-element.40), channel_id=1, source_target_pairs={{0,1},{1,2},{2,3},{4,5},{5,6},{6,7},{8,9},{9,10},{10,11},{12,13},{... | collective-permute-start | bytes 196616 | tf_op jit(solution)/shard_map/ppermute | solution.py:160
  156.4 30.0 %collective-permute-start.6 = (f32[64,1,48,128]{3,2,1,0:T(8,128)}, f32[64,1,48,128]{3,2,1,0:T(8,128)}, u32[]{:S(2)}, u32[]{:S(2)}) collective-permute-start(f32[64,1,48,128]{3,2,1,0:T(8,128)} %get-tuple-element.60), channel_id=1, source_target_pairs={{4,0},{8,4},{12,8},{16,12},{20,16},{24,20},{28,24},{32,28},{36,32}... | collective-permute-start | bytes 4718600 | tf_op jit(solution)/shard_map/ppermute | solution.py:161
  159.2 31.2 %collective-permute-start.7 = (f32[64,1,48,128]{3,2,1,0:T(8,128)S(1)}, f32[64,1,48,128]{3,2,1,0:T(8,128)}, u32[]{:S(2)}, u32[]{:S(2)}) collective-permute-start(f32[64,1,48,128]{3,2,1,0:T(8,128)S(1)} %get-tuple-element.59), channel_id=1, source_target_pairs={{0,4},{4,8},{8,12},{12,16},{16,20},{20,24},{24,28},{28,32},{32,36}... | collective-permute-start | bytes 4718600 | tf_op jit(solution)/shard_map/ppermute | solution.py:160
  162.0 20.8 %collective-permute-start.8 = (f32[64,2,1,128]{3,2,1,0:T(1,128)}, f32[64,2,1,128]{3,2,1,0:T(1,128)S(1)}, u32[]{:S(2)}, u32[]{:S(2)}) collective-permute-start(f32[64,2,1,128]{3,2,1,0:T(1,128)} %get-tuple-element.63), channel_id=1, source_target_pairs={{1,0},{2,1},{3,2},{5,4},{6,5},{7,6},{9,8},{10,9},{11,10},{13,12},{... | collective-permute-start | bytes 196616 | tf_op jit(solution)/shard_map/ppermute | solution.py:161
  163.3 21.8 %collective-permute-start.9 = (f32[64,2,1,128]{3,2,1,0:T(1,128)}, f32[64,2,1,128]{3,2,1,0:T(1,128)S(1)}, u32[]{:S(2)}, u32[]{:S(2)}) collective-permute-start(f32[64,2,1,128]{3,2,1,0:T(1,128)} %get-tuple-element.64), channel_id=1, source_target_pairs={{0,1},{1,2},{2,3},{4,5},{5,6},{6,7},{8,9},{9,10},{10,11},{12,13},{... | collective-permute-start | bytes 196616 | tf_op jit(solution)/shard_map/ppermute | solution.py:160
  179.5 33.2 %collective-permute-start.26 = (f32[64,1,48,128]{3,2,1,0:T(8,128)}, f32[64,1,48,128]{3,2,1,0:T(8,128)}, u32[]{:S(2)}, u32[]{:S(2)}) collective-permute-start(f32[64,1,48,128]{3,2,1,0:T(8,128)} %get-tuple-element.30), channel_id=1, source_target_pairs={{4,0},{8,4},{12,8},{16,12},{20,16},{24,20},{28,24},{32,28},{36,32}... | collective-permute-start | bytes 4718600 | tf_op jit(solution)/shard_map/ppermute | solution.py:161
  182.8 33.9 %collective-permute-start.27 = (f32[64,1,48,128]{3,2,1,0:T(8,128)}, f32[64,1,48,128]{3,2,1,0:T(8,128)}, u32[]{:S(2)}, u32[]{:S(2)}) collective-permute-start(f32[64,1,48,128]{3,2,1,0:T(8,128)} %get-tuple-element.29), channel_id=1, source_target_pairs={{0,4},{4,8},{8,12},{12,16},{16,20},{20,24},{24,28},{28,32},{32,36}... | collective-permute-start | bytes 4718600 | tf_op jit(solution)/shard_map/ppermute | solution.py:160
  185.1 24.4 %collective-permute-start.28 = (f32[64,2,1,128]{3,2,1,0:T(1,128)}, f32[64,2,1,128]{3,2,1,0:T(1,128)S(1)}, u32[]{:S(2)}, u32[]{:S(2)}) collective-permute-start(f32[64,2,1,128]{3,2,1,0:T(1,128)} %get-tuple-element.33), channel_id=1, source_target_pairs={{1,0},{2,1},{3,2},{5,4},{6,5},{7,6},{9,8},{10,9},{11,10},{13,12},{... | collective-permute-start | bytes 196616 | tf_op jit(solution)/shard_map/ppermute | solution.py:161
  186.4 25.0 %collective-permute-start.29 = (f32[64,2,1,128]{3,2,1,0:T(1,128)}, f32[64,2,1,128]{3,2,1,0:T(1,128)S(1)}, u32[]{:S(2)}, u32[]{:S(2)}) collective-permute-start(f32[64,2,1,128]{3,2,1,0:T(1,128)} %get-tuple-element.34), channel_id=1, source_target_pairs={{0,1},{1,2},{2,3},{4,5},{5,6},{6,7},{8,9},{9,10},{10,11},{12,13},{... | collective-permute-start | bytes 196616 | tf_op jit(solution)/shard_map/ppermute | solution.py:160
  205.7 28.9 %collective-permute-start.10 = (f32[64,1,48,128]{3,2,1,0:T(8,128)}, f32[64,1,48,128]{3,2,1,0:T(8,128)}, u32[]{:S(2)}, u32[]{:S(2)}) collective-permute-start(f32[64,1,48,128]{3,2,1,0:T(8,128)} %get-tuple-element.54), channel_id=1, source_target_pairs={{4,0},{8,4},{12,8},{16,12},{20,16},{24,20},{28,24},{32,28},{36,32}... | collective-permute-start | bytes 4718600 | tf_op jit(solution)/shard_map/ppermute | solution.py:161
  209.5 29.3 %collective-permute-start.11 = (f32[64,1,48,128]{3,2,1,0:T(8,128)S(1)}, f32[64,1,48,128]{3,2,1,0:T(8,128)}, u32[]{:S(2)}, u32[]{:S(2)}) collective-permute-start(f32[64,1,48,128]{3,2,1,0:T(8,128)S(1)} %get-tuple-element.53), channel_id=1, source_target_pairs={{0,4},{4,8},{8,12},{12,16},{16,20},{20,24},{24,28},{28,32},{32,36}... | collective-permute-start | bytes 4718600 | tf_op jit(solution)/shard_map/ppermute | solution.py:160
  211.4 19.9 %collective-permute-start.12 = (f32[64,2,1,128]{3,2,1,0:T(1,128)}, f32[64,2,1,128]{3,2,1,0:T(1,128)S(1)}, u32[]{:S(2)}, u32[]{:S(2)}) collective-permute-start(f32[64,2,1,128]{3,2,1,0:T(1,128)} %get-tuple-element.57), channel_id=1, source_target_pairs={{1,0},{2,1},{3,2},{5,4},{6,5},{7,6},{9,8},{10,9},{11,10},{13,12},{... | collective-permute-start | bytes 196616 | tf_op jit(solution)/shard_map/ppermute | solution.py:161
  212.7 20.5 %collective-permute-start.13 = (f32[64,2,1,128]{3,2,1,0:T(1,128)}, f32[64,2,1,128]{3,2,1,0:T(1,128)S(1)}, u32[]{:S(2)}, u32[]{:S(2)}) collective-permute-start(f32[64,2,1,128]{3,2,1,0:T(1,128)} %get-tuple-element.58), channel_id=1, source_target_pairs={{0,1},{1,2},{2,3},{4,5},{5,6},{6,7},{8,9},{9,10},{10,11},{12,13},{... | collective-permute-start | bytes 196616 | tf_op jit(solution)/shard_map/ppermute | solution.py:160
  227.1 34.8 %collective-permute-start.30 = (f32[64,1,48,128]{3,2,1,0:T(8,128)}, f32[64,1,48,128]{3,2,1,0:T(8,128)}, u32[]{:S(2)}, u32[]{:S(2)}) collective-permute-start(f32[64,1,48,128]{3,2,1,0:T(8,128)} %get-tuple-element.28), channel_id=1, source_target_pairs={{4,0},{8,4},{12,8},{16,12},{20,16},{24,20},{28,24},{32,28},{36,32}... | collective-permute-start | bytes 4718600 | tf_op jit(solution)/shard_map/ppermute | solution.py:161
  231.3 34.6 %collective-permute-start.31 = (f32[64,1,48,128]{3,2,1,0:T(8,128)}, f32[64,1,48,128]{3,2,1,0:T(8,128)}, u32[]{:S(2)}, u32[]{:S(2)}) collective-permute-start(f32[64,1,48,128]{3,2,1,0:T(8,128)} %get-tuple-element.27), channel_id=1, source_target_pairs={{0,4},{4,8},{8,12},{12,16},{16,20},{20,24},{24,28},{28,32},{32,36}... | collective-permute-start | bytes 4718600 | tf_op jit(solution)/shard_map/ppermute | solution.py:160
  233.2 25.4 %collective-permute-start.32 = (f32[64,2,1,128]{3,2,1,0:T(1,128)}, f32[64,2,1,128]{3,2,1,0:T(1,128)S(1)}, u32[]{:S(2)}, u32[]{:S(2)}) collective-permute-start(f32[64,2,1,128]{3,2,1,0:T(1,128)} %get-tuple-element.24), channel_id=1, source_target_pairs={{1,0},{2,1},{3,2},{5,4},{6,5},{7,6},{9,8},{10,9},{11,10},{13,12},{... | collective-permute-start | bytes 196616 | tf_op jit(solution)/shard_map/ppermute | solution.py:161
  234.5 26.0 %collective-permute-start.33 = (f32[64,2,1,128]{3,2,1,0:T(1,128)}, f32[64,2,1,128]{3,2,1,0:T(1,128)S(1)}, u32[]{:S(2)}, u32[]{:S(2)}) collective-permute-start(f32[64,2,1,128]{3,2,1,0:T(1,128)} %get-tuple-element.23), channel_id=1, source_target_pairs={{0,1},{1,2},{2,3},{4,5},{5,6},{6,7},{8,9},{9,10},{10,11},{12,13},{... | collective-permute-start | bytes 196616 | tf_op jit(solution)/shard_map/ppermute | solution.py:160
  254.5 25.5 %collective-permute-start.14 = (f32[64,1,48,128]{3,2,1,0:T(8,128)}, f32[64,1,48,128]{3,2,1,0:T(8,128)}, u32[]{:S(2)}, u32[]{:S(2)}) collective-permute-start(f32[64,1,48,128]{3,2,1,0:T(8,128)} %get-tuple-element.52), channel_id=1, source_target_pairs={{4,0},{8,4},{12,8},{16,12},{20,16},{24,20},{28,24},{32,28},{36,32}... | collective-permute-start | bytes 4718600 | tf_op jit(solution)/shard_map/ppermute | solution.py:161
  258.6 21.4 %collective-permute-start.15 = (f32[64,1,48,128]{3,2,1,0:T(8,128)S(1)}, f32[64,1,48,128]{3,2,1,0:T(8,128)}, u32[]{:S(2)}, u32[]{:S(2)}) collective-permute-start(f32[64,1,48,128]{3,2,1,0:T(8,128)S(1)} %get-tuple-element.51), channel_id=1, source_target_pairs={{0,4},{4,8},{8,12},{12,16},{16,20},{20,24},{24,28},{28,32},{32,36}... | collective-permute-start | bytes 4718600 | tf_op jit(solution)/shard_map/ppermute | solution.py:160
  260.6 19.4 %collective-permute-start.16 = (f32[64,2,1,128]{3,2,1,0:T(1,128)}, f32[64,2,1,128]{3,2,1,0:T(1,128)S(1)}, u32[]{:S(2)}, u32[]{:S(2)}) collective-permute-start(f32[64,2,1,128]{3,2,1,0:T(1,128)} %get-tuple-element.48), channel_id=1, source_target_pairs={{1,0},{2,1},{3,2},{5,4},{6,5},{7,6},{9,8},{10,9},{11,10},{13,12},{... | collective-permute-start | bytes 196616 | tf_op jit(solution)/shard_map/ppermute | solution.py:161
  261.9 18.1 %collective-permute-start.17 = (f32[64,2,1,128]{3,2,1,0:T(1,128)}, f32[64,2,1,128]{3,2,1,0:T(1,128)S(1)}, u32[]{:S(2)}, u32[]{:S(2)}) collective-permute-start(f32[64,2,1,128]{3,2,1,0:T(1,128)} %get-tuple-element.47), channel_id=1, source_target_pairs={{0,1},{1,2},{2,3},{4,5},{5,6},{6,7},{8,9},{9,10},{10,11},{12,13},{... | collective-permute-start | bytes 196616 | tf_op jit(solution)/shard_map/ppermute | solution.py:160
  (18 other events, 176.9 us)
